TPU v7x, 256 devices: a whole 4x4x8 slice. The times are simulated.
256 devices in a mesh: space: 32 (over z_hi, x, core), tm: 8 (over z_lo, y).
Axes of the slice: x: 4, y: 4, z: 8 (z_hi: 4, z_lo: 2; z = z_hi * 2 + z_lo), core: 2. Of those that a mesh axis runs over, the one named last changes fastest.
Arguments:
- start_state: float32 [1024, 8192], P('space'), may hold values from -6 to 6
- old_starts: float32 [8, 1024, 8192], P('tm', 'space'), may hold values from -6 to 6
- conductivity: float32 [1024, 8192], P('space'), may hold values from 0.1 to 0.7
- velocity: float32 [2, 1024, 8192], P(None, 'space'), may hold values from -0.2 to 0.2
- coarse_gain: float32 [8, 1024, 8192], P('tm', 'space'), may hold values from 0.4 to 0.99
- targets: float32 [8, 1024, 8192], P('tm', 'space'), may hold values from -6 to 6
Outputs:
- new_ends: float32 [8, 1024, 8192], P('tm', 'space')
- gradient: float32 [1024, 8192], P('space')
All inputs are finite; a program needn't handle non-finite values.
Results may differ from a plain program's by a relative error of at most 0.00002.
Values sent between devices are 32-bit elements; how exact they have to be, the bound alone decides.
A program may use at most 128 MiB of HBM per device.

v0:
```python
import jax
import jax.numpy as jnp
from jax import lax
from jax.sharding import PartitionSpec as P

STEPS = 4


time_step = 0.25


def with_halo(cells, sides, width):
    for axis, dim in sides:
        count = lax.axis_size(axis)
        ends = count - 1
        head = lax.slice_in_dim(cells, 0, width, axis=dim)
        tail = lax.slice_in_dim(cells, cells.shape[dim] - width, cells.shape[dim], axis=dim)
        cells = jnp.concatenate(
            [
                lax.ppermute(tail, axis, [(i, (i + 1) % count) for i in range(ends)]),
                cells,
                lax.ppermute(head, axis, [((i + 1) % count, i) for i in range(ends)]),
            ],
            axis=dim,
        )
    return cells


def from_behind(block, axis, distance):
    devices = range(lax.axis_size(axis))
    route = [(i - distance, i) for i in devices if i - distance in devices]
    return lax.ppermute(block, axis, route)


def potential(field):
    return field + 0.25 * jnp.tanh(field)


def advance(padded, kappa, velocity):
    wide = jnp.pad(padded, ((0, 0), (1, 1)))
    shaped = potential(wide)
    centre = wide[1:-1, 1:-1]
    spread = (
        shaped[:-2, 1:-1]
        + shaped[2:, 1:-1]
        + shaped[1:-1, :-2]
        + shaped[1:-1, 2:]
        - 4.0 * shaped[1:-1, 1:-1]
    )
    along_rows = velocity[0]
    along_cols = velocity[1]
    transport = (
        jnp.maximum(along_rows, 0.0) * (centre - wide[:-2, 1:-1])
        + jnp.minimum(along_rows, 0.0) * (wide[2:, 1:-1] - centre)
        + jnp.maximum(along_cols, 0.0) * (centre - wide[1:-1, :-2])
        + jnp.minimum(along_cols, 0.0) * (wide[1:-1, 2:] - centre)
    )
    return centre + time_step * (kappa * spread - transport)


def on_device(start_state, old_starts, conductivity, velocity, coarse_gain, targets):
    anchor = old_starts[0]
    gain = coarse_gain[0]
    target = targets[0]
    rows = anchor.shape[0]
    pullbacks = []
    field = anchor
    for step in range(STEPS):
        padded = with_halo(field, (("space", 0),), 1)
        field, pullback = jax.vjp(
            lambda edged, kappa: advance(edged, kappa, velocity), padded, conductivity
        )
        pullbacks.append(pullback)
    carried = field - gain * anchor
    slab = lax.axis_index("tm")
    slab_count = lax.axis_size("tm")
    begin = start_state
    new_end = gain * begin + carried
    for turn in range(slab_count - 1):
        arrived = from_behind(new_end, "tm", 1)
        begin = jnp.where(slab == turn + 1, arrived, begin)
        new_end = gain * begin + carried
    misfit = new_end - target
    incoming = jnp.zeros_like(misfit)
    adjoint = misfit
    outgoing = gain * adjoint
    for turn in range(slab_count - 1):
        arrived = from_behind(outgoing, "tm", -1)
        incoming = jnp.where(slab == slab_count - 2 - turn, arrived, incoming)
        adjoint = misfit + incoming
        outgoing = gain * adjoint
    cotangent = adjoint
    partial_grad = jnp.zeros_like(conductivity)
    for step in range(STEPS - 1, -1, -1):
        field_part, kappa_part = pullbacks[step](cotangent)
        partial_grad = partial_grad + kappa_part
        if step > 0:
            from_below = from_behind(field_part[:1], "space", -1)
            from_above = from_behind(field_part[-1:], "space", 1)
            cotangent = field_part[1:-1].at[:1].add(from_above).at[rows - 1 :].add(from_below)
    gradient = lax.psum(partial_grad, "tm")
    return (new_end[None], gradient)


def solution(mesh):
    in_specs = (
        P("space", None),
        P("tm", "space", None),
        P("space", None),
        P(None, "space", None),
        P("tm", "space", None),
        P("tm", "space", None),
    )
    out_specs = (P("tm", "space", None), P("space", None))
    return jax.shard_map(
        on_device, mesh=mesh, in_specs=in_specs, out_specs=out_specs, check_vma=False
    )
```

profile of v0, /device:TPU:160, one launch (start us, length us, event | category | flops | bytes accessed | tf_op | source)
XLA Modules:
  0.0 618.1 jit_solution(7258317410066099021)
XLA Ops:
  10.2 7.9 %collective-permute-start.1 = (f32[1,8192]{1,0:T(1,128)S(1)}, f32[1,8192]{1,0:T(1,128)S(1)}, u32[]{:S(2)}, u32[]{:S(2)}) collective-permute-start(f32[1,8192]{1,0:T(1,128)S(1)} %get-tuple-element.147), channel_id=1, source_target_pairs={{8,0},{16,8},{24,16},{32,24},{40,32},{48,40},{56,48},{64,56},{72,6... | collective-permute-start | bytes 98312 | tf_op jit(solution)/shard_map/ppermute | solution.py:22
  21.8 4.1 fusion.45
  27.9 7.9 %collective-permute-start.3 = (f32[1,8192]{1,0:T(1,128)S(1)}, f32[1,8192]{1,0:T(1,128)S(1)}, u32[]{:S(2)}, u32[]{:S(2)}) collective-permute-start(f32[1,8192]{1,0:T(1,128)S(1)} %get-tuple-element.145), channel_id=1, source_target_pairs={{8,0},{16,8},{24,16},{32,24},{40,32},{48,40},{56,48},{64,56},{72,6... | collective-permute-start | bytes 98312 | tf_op jit(solution)/shard_map/ppermute | solution.py:22
  42.6 7.9 %collective-permute-start.5 = (f32[1,8192]{1,0:T(1,128)S(1)}, f32[1,8192]{1,0:T(1,128)S(1)}, u32[]{:S(2)}, u32[]{:S(2)}) collective-permute-start(f32[1,8192]{1,0:T(1,128)S(1)} %get-tuple-element.143), channel_id=1, source_target_pairs={{8,0},{16,8},{24,16},{32,24},{40,32},{48,40},{56,48},{64,56},{72,6... | collective-permute-start | bytes 98312 | tf_op jit(solution)/shard_map/ppermute | solution.py:22
  57.4 8.1 %collective-permute-start.7 = (f32[1,8192]{1,0:T(1,128)S(1)}, f32[1,8192]{1,0:T(1,128)S(1)}, u32[]{:S(2)}, u32[]{:S(2)}) collective-permute-start(f32[1,8192]{1,0:T(1,128)S(1)} %get-tuple-element.141), channel_id=1, source_target_pairs={{8,0},{16,8},{24,16},{32,24},{40,32},{48,40},{56,48},{64,56},{72,6... | collective-permute-start | bytes 98312 | tf_op jit(solution)/shard_map/ppermute | solution.py:22
  70.8 3.5 collective-permute-start.8
  74.3 19.7 %collective-permute-done.8 = f32[32,8192]{1,0:T(8,128)} collective-permute-done((f32[32,8192]{1,0:T(8,128)}, f32[32,8192]{1,0:T(8,128)}, u32[]{:S(2)}, u32[]{:S(2)}) %collective-permute-start.8) | collective-permute-done | bytes 1048608 | tf_op jit(solution)/shard_map/ppermute | solution.py:32
  99.0 20.4 %collective-permute-done.9 = f32[32,8192]{1,0:T(8,128)} collective-permute-done((f32[32,8192]{1,0:T(8,128)}, f32[32,8192]{1,0:T(8,128)}, u32[]{:S(2)}, u32[]{:S(2)}) %collective-permute-start.9) | collective-permute-done | bytes 1048608 | tf_op jit(solution)/shard_map/ppermute | solution.py:32
  124.1 19.5 %collective-permute-done.10 = f32[32,8192]{1,0:T(8,128)} collective-permute-done((f32[32,8192]{1,0:T(8,128)}, f32[32,8192]{1,0:T(8,128)}, u32[]{:S(2)}, u32[]{:S(2)}) %collective-permute-start.10) | collective-permute-done | bytes 1048608 | tf_op jit(solution)/shard_map/ppermute | solution.py:32
  148.6 18.7 %collective-permute-done.11 = f32[32,8192]{1,0:T(8,128)} collective-permute-done((f32[32,8192]{1,0:T(8,128)}, f32[32,8192]{1,0:T(8,128)}, u32[]{:S(2)}, u32[]{:S(2)}) %collective-permute-start.11) | collective-permute-done | bytes 1048608 | tf_op jit(solution)/shard_map/ppermute | solution.py:32
  172.0 18.3 %collective-permute-done.12 = f32[32,8192]{1,0:T(8,128)} collective-permute-done((f32[32,8192]{1,0:T(8,128)}, f32[32,8192]{1,0:T(8,128)}, u32[]{:S(2)}, u32[]{:S(2)}) %collective-permute-start.12) | collective-permute-done | bytes 1048608 | tf_op jit(solution)/shard_map/ppermute | solution.py:32
  195.3 19.2 %collective-permute-done.13 = f32[32,8192]{1,0:T(8,128)} collective-permute-done((f32[32,8192]{1,0:T(8,128)}, f32[32,8192]{1,0:T(8,128)}, u32[]{:S(2)}, u32[]{:S(2)}) %collective-permute-start.13) | collective-permute-done | bytes 1048608 | tf_op jit(solution)/shard_map/ppermute | solution.py:32
  219.1 17.2 %collective-permute-done.14 = f32[32,8192]{1,0:T(8,128)} collective-permute-done((f32[32,8192]{1,0:T(8,128)}, f32[32,8192]{1,0:T(8,128)}, u32[]{:S(2)}, u32[]{:S(2)}) %collective-permute-start.14) | collective-permute-done | bytes 1048608 | tf_op jit(solution)/shard_map/ppermute | solution.py:32
  236.3 3.1 bitcast_multiply_fusion.18
  241.4 24.0 %collective-permute-done.15 = f32[32,8192]{1,0:T(8,128)S(1)} collective-permute-done((f32[32,8192]{1,0:T(8,128)S(1)}, f32[32,8192]{1,0:T(8,128)S(1)}, u32[]{:S(2)}, u32[]{:S(2)}) %collective-permute-start.15) | collective-permute-done | bytes 1048608 | tf_op jit(solution)/shard_map/ppermute | solution.py:32
  267.5 25.1 %collective-permute-done.16 = f32[32,8192]{1,0:T(8,128)S(1)} collective-permute-done((f32[32,8192]{1,0:T(8,128)S(1)}, f32[32,8192]{1,0:T(8,128)S(1)}, u32[]{:S(2)}, u32[]{:S(2)}) %collective-permute-start.16) | collective-permute-done | bytes 1048608 | tf_op jit(solution)/shard_map/ppermute | solution.py:32
  294.7 25.8 %collective-permute-done.17 = f32[32,8192]{1,0:T(8,128)S(1)} collective-permute-done((f32[32,8192]{1,0:T(8,128)S(1)}, f32[32,8192]{1,0:T(8,128)S(1)}, u32[]{:S(2)}, u32[]{:S(2)}) %collective-permute-start.17) | collective-permute-done | bytes 1048608 | tf_op jit(solution)/shard_map/ppermute | solution.py:32
  323.1 24.6 %collective-permute-done.18 = f32[32,8192]{1,0:T(8,128)S(1)} collective-permute-done((f32[32,8192]{1,0:T(8,128)S(1)}, f32[32,8192]{1,0:T(8,128)S(1)}, u32[]{:S(2)}, u32[]{:S(2)}) %collective-permute-start.18) | collective-permute-done | bytes 1048608 | tf_op jit(solution)/shard_map/ppermute | solution.py:32
  348.0 4.7 collective-permute-start.19
  352.7 23.3 %collective-permute-done.19 = f32[32,8192]{1,0:T(8,128)S(1)} collective-permute-done((f32[32,8192]{1,0:T(8,128)S(1)}, f32[32,8192]{1,0:T(8,128)S(1)}, u32[]{:S(2)}, u32[]{:S(2)}) %collective-permute-start.19) | collective-permute-done | bytes 1048608 | tf_op jit(solution)/shard_map/ppermute | solution.py:32
  376.3 6.7 %collective-permute-start.20 = (f32[32,8192]{1,0:T(8,128)S(1)}, f32[32,8192]{1,0:T(8,128)S(1)}, u32[]{:S(2)}, u32[]{:S(2)}) collective-permute-start(f32[32,8192]{1,0:T(8,128)S(1)} %bitcast_multiply_fusion.13), channel_id=1, source_target_pairs={{1,0},{2,1},{3,2},{4,3},{5,4},{6,5},{7,6},{9,8},{10,9},{11,10},{12... | collective-permute-start | bytes 3145736 | tf_op jit(solution)/shard_map/ppermute | solution.py:32
  382.9 23.1 %collective-permute-done.20 = f32[32,8192]{1,0:T(8,128)S(1)} collective-permute-done((f32[32,8192]{1,0:T(8,128)S(1)}, f32[32,8192]{1,0:T(8,128)S(1)}, u32[]{:S(2)}, u32[]{:S(2)}) %collective-permute-start.20) | collective-permute-done | bytes 1048608 | tf_op jit(solution)/shard_map/ppermute | solution.py:32
  407.8 6.5 %collective-permute-start.21 = (f32[32,8192]{1,0:T(8,128)}, f32[32,8192]{1,0:T(8,128)S(1)}, u32[]{:S(2)}, u32[]{:S(2)}) collective-permute-start(f32[32,8192]{1,0:T(8,128)} %get-tuple-element.82), channel_id=1, source_target_pairs={{1,0},{2,1},{3,2},{4,3},{5,4},{6,5},{7,6},{9,8},{10,9},{11,10},{12... | collective-permute-start | bytes 3145736 | tf_op jit(solution)/shard_map/ppermute | solution.py:32
  414.3 12.6 %collective-permute-done.21 = f32[32,8192]{1,0:T(8,128)S(1)} collective-permute-done((f32[32,8192]{1,0:T(8,128)}, f32[32,8192]{1,0:T(8,128)S(1)}, u32[]{:S(2)}, u32[]{:S(2)}) %collective-permute-start.21) | collective-permute-done | bytes 1048608 | tf_op jit(solution)/shard_map/ppermute | solution.py:32
  431.3 3.6 multiply_add_fusion.2
  438.4 31.8 %collective-permute-start.23 = (f32[1,8192]{1,0:T(1,128)S(1)}, f32[1,8192]{1,0:T(1,128)S(1)}, u32[]{:S(2)}, u32[]{:S(2)}) collective-permute-start(f32[1,8192]{1,0:T(1,128)S(1)} %get-tuple-element.124), channel_id=1, source_target_pairs={{8,0},{16,8},{24,16},{32,24},{40,32},{48,40},{56,48},{64,56},{72,6... | collective-permute-start | bytes 98312 | tf_op jit(solution)/shard_map/ppermute | solution.py:32
  477.3 3.7 multiply_add_fusion.1
  484.5 9.6 %collective-permute-start.25 = (f32[1,8192]{1,0:T(1,128)S(1)}, f32[1,8192]{1,0:T(1,128)S(1)}, u32[]{:S(2)}, u32[]{:S(2)}) collective-permute-start(f32[1,8192]{1,0:T(1,128)S(1)} %get-tuple-element.122), channel_id=1, source_target_pairs={{8,0},{16,8},{24,16},{32,24},{40,32},{48,40},{56,48},{64,56},{72,6... | collective-permute-start | bytes 98312 | tf_op jit(solution)/shard_map/ppermute | solution.py:32
  501.2 3.7 multiply_add_fusion
  508.4 7.8 %collective-permute-start.27 = (f32[1,8192]{1,0:T(1,128)S(1)}, f32[1,8192]{1,0:T(1,128)S(1)}, u32[]{:S(2)}, u32[]{:S(2)}) collective-permute-start(f32[1,8192]{1,0:T(1,128)S(1)} %get-tuple-element.120), channel_id=1, source_target_pairs={{8,0},{16,8},{24,16},{32,24},{40,32},{48,40},{56,48},{64,56},{72,6... | collective-permute-start | bytes 98312 | tf_op jit(solution)/shard_map/ppermute | solution.py:32
  521.0 3.9 multiply_add_fusion.7
  524.9 84.1 %all-reduce.36.cloned.1.call-done = f32[32,8192]{1,0:T(8,128)} async-done(((f32[32,8192]{1,0:T(8,128)}), f32[32,8192]{1,0:T(8,128)}) %all-reduce.36.cloned.1.call-update) | async-done | bytes 1048592 | tf_op jit(solution)/shard_map/psum | solution.py:101
  (115 shorter events, 103.6 us)
Async XLA Ops:
  7.2 601.8 %all-reduce.36.cloned.1.call-start = ((), (), s32[]{:S(2)}) async-start(), calls=%async_computation | async-start | bytes 2097152 | tf_op jit(solution)/shard_map/psum | solution.py:101
  8.3 9.8 %collective-permute-start = (f32[1,8192]{1,0:T(1,128)S(1)}, f32[1,8192]{1,0:T(1,128)S(1)}, u32[]{:S(2)}, u32[]{:S(2)}) collective-permute-start(f32[1,8192]{1,0:T(1,128)S(1)} %get-tuple-element.146), channel_id=1, source_target_pairs={{0,8},{8,16},{16,24},{24,32},{32,40},{40,48},{48,56},{56,64},{64,7... | collective-permute-start | bytes 98312 | tf_op jit(solution)/shard_map/ppermute | solution.py:20
  10.2 9.4 %collective-permute-start.1 = (f32[1,8192]{1,0:T(1,128)S(1)}, f32[1,8192]{1,0:T(1,128)S(1)}, u32[]{:S(2)}, u32[]{:S(2)}) collective-permute-start(f32[1,8192]{1,0:T(1,128)S(1)} %get-tuple-element.147), channel_id=1, source_target_pairs={{8,0},{16,8},{24,16},{32,24},{40,32},{48,40},{56,48},{64,56},{72,6... | collective-permute-start | bytes 98312 | tf_op jit(solution)/shard_map/ppermute | solution.py:22
  26.0 9.8 %collective-permute-start.2 = (f32[1,8192]{1,0:T(1,128)S(1)}, f32[1,8192]{1,0:T(1,128)S(1)}, u32[]{:S(2)}, u32[]{:S(2)}) collective-permute-start(f32[1,8192]{1,0:T(1,128)S(1)} %get-tuple-element.144), channel_id=1, source_target_pairs={{0,8},{8,16},{16,24},{24,32},{32,40},{40,48},{48,56},{56,64},{64,7... | collective-permute-start | bytes 98312 | tf_op jit(solution)/shard_map/ppermute | solution.py:20
  27.9 9.5 %collective-permute-start.3 = (f32[1,8192]{1,0:T(1,128)S(1)}, f32[1,8192]{1,0:T(1,128)S(1)}, u32[]{:S(2)}, u32[]{:S(2)}) collective-permute-start(f32[1,8192]{1,0:T(1,128)S(1)} %get-tuple-element.145), channel_id=1, source_target_pairs={{8,0},{16,8},{24,16},{32,24},{40,32},{48,40},{56,48},{64,56},{72,6... | collective-permute-start | bytes 98312 | tf_op jit(solution)/shard_map/ppermute | solution.py:22
  40.7 9.8 %collective-permute-start.4 = (f32[1,8192]{1,0:T(1,128)S(1)}, f32[1,8192]{1,0:T(1,128)S(1)}, u32[]{:S(2)}, u32[]{:S(2)}) collective-permute-start(f32[1,8192]{1,0:T(1,128)S(1)} %get-tuple-element.142), channel_id=1, source_target_pairs={{0,8},{8,16},{16,24},{24,32},{32,40},{40,48},{48,56},{56,64},{64,7... | collective-permute-start | bytes 98312 | tf_op jit(solution)/shard_map/ppermute | solution.py:20
  42.6 9.5 %collective-permute-start.5 = (f32[1,8192]{1,0:T(1,128)S(1)}, f32[1,8192]{1,0:T(1,128)S(1)}, u32[]{:S(2)}, u32[]{:S(2)}) collective-permute-start(f32[1,8192]{1,0:T(1,128)S(1)} %get-tuple-element.143), channel_id=1, source_target_pairs={{8,0},{16,8},{24,16},{32,24},{40,32},{48,40},{56,48},{64,56},{72,6... | collective-permute-start | bytes 98312 | tf_op jit(solution)/shard_map/ppermute | solution.py:22
  55.4 10.1 %collective-permute-start.6 = (f32[1,8192]{1,0:T(1,128)S(1)}, f32[1,8192]{1,0:T(1,128)S(1)}, u32[]{:S(2)}, u32[]{:S(2)}) collective-permute-start(f32[1,8192]{1,0:T(1,128)S(1)} %get-tuple-element.140), channel_id=1, source_target_pairs={{0,8},{8,16},{16,24},{24,32},{32,40},{40,48},{48,56},{56,64},{64,7... | collective-permute-start | bytes 98312 | tf_op jit(solution)/shard_map/ppermute | solution.py:20
  57.4 9.7 %collective-permute-start.7 = (f32[1,8192]{1,0:T(1,128)S(1)}, f32[1,8192]{1,0:T(1,128)S(1)}, u32[]{:S(2)}, u32[]{:S(2)}) collective-permute-start(f32[1,8192]{1,0:T(1,128)S(1)} %get-tuple-element.141), channel_id=1, source_target_pairs={{8,0},{16,8},{24,16},{32,24},{40,32},{48,40},{56,48},{64,56},{72,6... | collective-permute-start | bytes 98312 | tf_op jit(solution)/shard_map/ppermute | solution.py:22
  70.8 23.2 %collective-permute-start.8 = (f32[32,8192]{1,0:T(8,128)}, f32[32,8192]{1,0:T(8,128)}, u32[]{:S(2)}, u32[]{:S(2)}) collective-permute-start(f32[32,8192]{1,0:T(8,128)} %get-tuple-element.97), channel_id=1, source_target_pairs={{0,1},{1,2},{2,3},{3,4},{4,5},{5,6},{6,7},{8,9},{9,10},{10,11},{11... | collective-permute-start | bytes 3145736 | tf_op jit(solution)/shard_map/ppermute | solution.py:32
  97.1 22.3 %collective-permute-start.9 = (f32[32,8192]{1,0:T(8,128)}, f32[32,8192]{1,0:T(8,128)}, u32[]{:S(2)}, u32[]{:S(2)}) collective-permute-start(f32[32,8192]{1,0:T(8,128)} %get-tuple-element.95), channel_id=1, source_target_pairs={{0,1},{1,2},{2,3},{3,4},{4,5},{5,6},{6,7},{8,9},{9,10},{10,11},{11... | collective-permute-start | bytes 3145736 | tf_op jit(solution)/shard_map/ppermute | solution.py:32
  122.1 21.5 %collective-permute-start.10 = (f32[32,8192]{1,0:T(8,128)}, f32[32,8192]{1,0:T(8,128)}, u32[]{:S(2)}, u32[]{:S(2)}) collective-permute-start(f32[32,8192]{1,0:T(8,128)} %fusion.56), channel_id=1, source_target_pairs={{0,1},{1,2},{2,3},{3,4},{4,5},{5,6},{6,7},{8,9},{9,10},{10,11},{11... | collective-permute-start | bytes 3145736 | tf_op jit(solution)/shard_map/ppermute | solution.py:32
  146.7 20.6 %collective-permute-start.11 = (f32[32,8192]{1,0:T(8,128)}, f32[32,8192]{1,0:T(8,128)}, u32[]{:S(2)}, u32[]{:S(2)}) collective-permute-start(f32[32,8192]{1,0:T(8,128)} %get-tuple-element.93), channel_id=1, source_target_pairs={{0,1},{1,2},{2,3},{3,4},{4,5},{5,6},{6,7},{8,9},{9,10},{10,11},{11... | collective-permute-start | bytes 3145736 | tf_op jit(solution)/shard_map/ppermute | solution.py:32
  170.1 20.2 %collective-permute-start.12 = (f32[32,8192]{1,0:T(8,128)}, f32[32,8192]{1,0:T(8,128)}, u32[]{:S(2)}, u32[]{:S(2)}) collective-permute-start(f32[32,8192]{1,0:T(8,128)} %fusion.58), channel_id=1, source_target_pairs={{0,1},{1,2},{2,3},{3,4},{4,5},{5,6},{6,7},{8,9},{9,10},{10,11},{11... | collective-permute-start | bytes 3145736 | tf_op jit(solution)/shard_map/ppermute | solution.py:32
  193.4 21.1 %collective-permute-start.13 = (f32[32,8192]{1,0:T(8,128)}, f32[32,8192]{1,0:T(8,128)}, u32[]{:S(2)}, u32[]{:S(2)}) collective-permute-start(f32[32,8192]{1,0:T(8,128)} %get-tuple-element.91), channel_id=1, source_target_pairs={{0,1},{1,2},{2,3},{3,4},{4,5},{5,6},{6,7},{8,9},{9,10},{10,11},{11... | collective-permute-start | bytes 3145736 | tf_op jit(solution)/shard_map/ppermute | solution.py:32
  217.2 19.1 %collective-permute-start.14 = (f32[32,8192]{1,0:T(8,128)}, f32[32,8192]{1,0:T(8,128)}, u32[]{:S(2)}, u32[]{:S(2)}) collective-permute-start(f32[32,8192]{1,0:T(8,128)} %fusion.60), channel_id=1, source_target_pairs={{0,1},{1,2},{2,3},{3,4},{4,5},{5,6},{6,7},{8,9},{9,10},{10,11},{11... | collective-permute-start | bytes 3145736 | tf_op jit(solution)/shard_map/ppermute | solution.py:32
  239.4 166.6 %copy-start.2 = (f32[32,8192]{1,0:T(8,128)}, f32[32,8192]{1,0:T(8,128)S(1)}, u32[]{:S(2)}) copy-start(f32[32,8192]{1,0:T(8,128)S(1)} %get-tuple-element.89) | copy-start | bytes 3145732
  239.4 25.9 %collective-permute-start.15 = (f32[32,8192]{1,0:T(8,128)S(1)}, f32[32,8192]{1,0:T(8,128)S(1)}, u32[]{:S(2)}, u32[]{:S(2)}) collective-permute-start(f32[32,8192]{1,0:T(8,128)S(1)} %get-tuple-element.88), channel_id=1, source_target_pairs={{1,0},{2,1},{3,2},{4,3},{5,4},{6,5},{7,6},{9,8},{10,9},{11,10},{12... | collective-permute-start | bytes 3145736 | tf_op jit(solution)/shard_map/ppermute | solution.py:32
  265.5 27.0 %collective-permute-start.16 = (f32[32,8192]{1,0:T(8,128)S(1)}, f32[32,8192]{1,0:T(8,128)S(1)}, u32[]{:S(2)}, u32[]{:S(2)}) collective-permute-start(f32[32,8192]{1,0:T(8,128)S(1)} %bitcast_multiply_fusion.17), channel_id=1, source_target_pairs={{1,0},{2,1},{3,2},{4,3},{5,4},{6,5},{7,6},{9,8},{10,9},{11,10},{12... | collective-permute-start | bytes 3145736 | tf_op jit(solution)/shard_map/ppermute | solution.py:32
  292.8 27.7 %collective-permute-start.17 = (f32[32,8192]{1,0:T(8,128)S(1)}, f32[32,8192]{1,0:T(8,128)S(1)}, u32[]{:S(2)}, u32[]{:S(2)}) collective-permute-start(f32[32,8192]{1,0:T(8,128)S(1)} %get-tuple-element.86), channel_id=1, source_target_pairs={{1,0},{2,1},{3,2},{4,3},{5,4},{6,5},{7,6},{9,8},{10,9},{11,10},{12... | collective-permute-start | bytes 3145736 | tf_op jit(solution)/shard_map/ppermute | solution.py:32
  320.8 26.9 %collective-permute-start.18 = (f32[32,8192]{1,0:T(8,128)S(1)}, f32[32,8192]{1,0:T(8,128)S(1)}, u32[]{:S(2)}, u32[]{:S(2)}) collective-permute-start(f32[32,8192]{1,0:T(8,128)S(1)} %bitcast_multiply_fusion.15), channel_id=1, source_target_pairs={{1,0},{2,1},{3,2},{4,3},{5,4},{6,5},{7,6},{9,8},{10,9},{11,10},{12... | collective-permute-start | bytes 3145736 | tf_op jit(solution)/shard_map/ppermute | solution.py:32
  348.0 28.0 %collective-permute-start.19 = (f32[32,8192]{1,0:T(8,128)S(1)}, f32[32,8192]{1,0:T(8,128)S(1)}, u32[]{:S(2)}, u32[]{:S(2)}) collective-permute-start(f32[32,8192]{1,0:T(8,128)S(1)} %get-tuple-element.84), channel_id=1, source_target_pairs={{1,0},{2,1},{3,2},{4,3},{5,4},{6,5},{7,6},{9,8},{10,9},{11,10},{12... | collective-permute-start | bytes 3145736 | tf_op jit(solution)/shard_map/ppermute | solution.py:32
  376.3 29.8 %collective-permute-start.20 = (f32[32,8192]{1,0:T(8,128)S(1)}, f32[32,8192]{1,0:T(8,128)S(1)}, u32[]{:S(2)}, u32[]{:S(2)}) collective-permute-start(f32[32,8192]{1,0:T(8,128)S(1)} %bitcast_multiply_fusion.13), channel_id=1, source_target_pairs={{1,0},{2,1},{3,2},{4,3},{5,4},{6,5},{7,6},{9,8},{10,9},{11,10},{12... | collective-permute-start | bytes 3145736 | tf_op jit(solution)/shard_map/ppermute | solution.py:32
  407.8 19.1 %collective-permute-start.21 = (f32[32,8192]{1,0:T(8,128)}, f32[32,8192]{1,0:T(8,128)S(1)}, u32[]{:S(2)}, u32[]{:S(2)}) collective-permute-start(f32[32,8192]{1,0:T(8,128)} %get-tuple-element.82), channel_id=1, source_target_pairs={{1,0},{2,1},{3,2},{4,3},{5,4},{6,5},{7,6},{9,8},{10,9},{11,10},{12... | collective-permute-start | bytes 3145736 | tf_op jit(solution)/shard_map/ppermute | solution.py:32
  435.2 35.0 %collective-permute-start.22 = (f32[1,8192]{1,0:T(1,128)S(1)}, f32[1,8192]{1,0:T(1,128)S(1)}, u32[]{:S(2)}, u32[]{:S(2)}) collective-permute-start(f32[1,8192]{1,0:T(1,128)S(1)} %get-tuple-element.125), channel_id=1, source_target_pairs={{0,8},{8,16},{16,24},{24,32},{32,40},{40,48},{48,56},{56,64},{64,7... | collective-permute-start | bytes 98312 | tf_op jit(solution)/shard_map/ppermute | solution.py:32
  438.4 33.7 %collective-permute-start.23 = (f32[1,8192]{1,0:T(1,128)S(1)}, f32[1,8192]{1,0:T(1,128)S(1)}, u32[]{:S(2)}, u32[]{:S(2)}) collective-permute-start(f32[1,8192]{1,0:T(1,128)S(1)} %get-tuple-element.124), channel_id=1, source_target_pairs={{8,0},{16,8},{24,16},{32,24},{40,32},{48,40},{56,48},{64,56},{72,6... | collective-permute-start | bytes 98312 | tf_op jit(solution)/shard_map/ppermute | solution.py:32
  481.2 12.9 %collective-permute-start.24 = (f32[1,8192]{1,0:T(1,128)S(1)}, f32[1,8192]{1,0:T(1,128)S(1)}, u32[]{:S(2)}, u32[]{:S(2)}) collective-permute-start(f32[1,8192]{1,0:T(1,128)S(1)} %get-tuple-element.123), channel_id=1, source_target_pairs={{0,8},{8,16},{16,24},{24,32},{32,40},{40,48},{48,56},{56,64},{64,7... | collective-permute-start | bytes 98312 | tf_op jit(solution)/shard_map/ppermute | solution.py:32
  484.5 11.6 %collective-permute-start.25 = (f32[1,8192]{1,0:T(1,128)S(1)}, f32[1,8192]{1,0:T(1,128)S(1)}, u32[]{:S(2)}, u32[]{:S(2)}) collective-permute-start(f32[1,8192]{1,0:T(1,128)S(1)} %get-tuple-element.122), channel_id=1, source_target_pairs={{8,0},{16,8},{24,16},{32,24},{40,32},{48,40},{56,48},{64,56},{72,6... | collective-permute-start | bytes 98312 | tf_op jit(solution)/shard_map/ppermute | solution.py:32
  501.2 19.8 %copy-start.15 = (f32[32,8192]{1,0:T(8,128)S(1)}, f32[32,8192]{1,0:T(8,128)}, u32[]{:S(2)}) copy-start(f32[32,8192]{1,0:T(8,128)} %copy-done.14) | copy-start | bytes 3145732
  504.9 16.1 %copy-start.12 = (f32[32,8192]{1,0:T(8,128)S(1)}, f32[32,8192]{1,0:T(8,128)}, u32[]{:S(2)}) copy-start(f32[32,8192]{1,0:T(8,128)} %scatter-add.21) | copy-start | bytes 3145732
  505.1 11.2 %collective-permute-start.26 = (f32[1,8192]{1,0:T(1,128)S(1)}, f32[1,8192]{1,0:T(1,128)S(1)}, u32[]{:S(2)}, u32[]{:S(2)}) collective-permute-start(f32[1,8192]{1,0:T(1,128)S(1)} %get-tuple-element.121), channel_id=1, source_target_pairs={{0,8},{8,16},{16,24},{24,32},{32,40},{40,48},{48,56},{56,64},{64,7... | collective-permute-start | bytes 98312 | tf_op jit(solution)/shard_map/ppermute | solution.py:32
  508.4 9.8 %collective-permute-start.27 = (f32[1,8192]{1,0:T(1,128)S(1)}, f32[1,8192]{1,0:T(1,128)S(1)}, u32[]{:S(2)}, u32[]{:S(2)}) collective-permute-start(f32[1,8192]{1,0:T(1,128)S(1)} %get-tuple-element.120), channel_id=1, source_target_pairs={{8,0},{16,8},{24,16},{32,24},{40,32},{48,40},{56,48},{64,56},{72,6... | collective-permute-start | bytes 98312 | tf_op jit(solution)/shard_map/ppermute | solution.py:32
  (15 other events, 97.8 us)
Sparse Core Ops, SparseCore 0:
  525.0 83.9 all-reduce.35
where the time goes:
time: 622 us; the launch traced here: 618 us
  waiting for transfers between devices  382 us (61%)
  starting transfers between devices  135 us (22%)
  other arithmetic  65.6 us (11%)
  local copies, waits for them, and re-layouts  20.6 us (3%)
  between operations  14.7 us (2%)
    ppermute x20, waiting for transfers between devices, from_behind(): return lax.ppermute(block, axis, route)  291 us
    ppermute x20, starting transfers between devices, from_behind(): return lax.ppermute(block, axis, route)  95.9 us
    psum x1, waiting for transfers between devices, on_device(): gradient = lax.psum(partial_grad, 'tm')  84.1 us
    ppermute x4, starting transfers between devices, with_halo(): lax.ppermute(head, axis, [((i + 1) % count, i) for i in range(ends)])  31.7 us
    add x7, other arithmetic, on_device(): new_end = gain * begin + carried  20.6 us
  transfers between devices with their start and end apart: 29, of which 19 were waited for; matrix products, arithmetic and copies ran while one was open for 2% of the time, Pallas kernels for 0%

commit v1 on v0

v1 whole, which is shorter than its diff:
```python
import jax
import jax.numpy as jnp
from jax import lax
from jax.sharding import PartitionSpec as P

STEPS = 4
HALO = 8


time_step = 0.25


def with_halo(cells, axis, dim):
    count = lax.axis_size(axis)
    ends = count - 1
    head = lax.slice_in_dim(cells, 0, 1, axis=dim)
    tail = lax.slice_in_dim(cells, cells.shape[dim] - 1, cells.shape[dim], axis=dim)
    return jnp.concatenate(
        [
            lax.ppermute(tail, axis, [(i, (i + 1) % count) for i in range(ends)]),
            cells,
            lax.ppermute(head, axis, [((i + 1) % count, i) for i in range(ends)]),
        ],
        axis=dim,
    )


def potential(field):
    return field + 0.25 * jnp.tanh(field)


def advance(padded, kappa, along_rows, along_cols):
    wide = jnp.pad(padded, ((0, 0), (0, 0), (1, 1)))
    shaped = potential(wide)
    centre = wide[:, 1:-1, 1:-1]
    spread = (
        shaped[:, :-2, 1:-1]
        + shaped[:, 2:, 1:-1]
        + shaped[:, 1:-1, :-2]
        + shaped[:, 1:-1, 2:]
        - 4.0 * shaped[:, 1:-1, 1:-1]
    )
    transport = (
        jnp.maximum(along_rows, 0.0) * (centre - wide[:, :-2, 1:-1])
        + jnp.minimum(along_rows, 0.0) * (wide[:, 2:, 1:-1] - centre)
        + jnp.maximum(along_cols, 0.0) * (centre - wide[:, 1:-1, :-2])
        + jnp.minimum(along_cols, 0.0) * (wide[:, 1:-1, 2:] - centre)
    )
    return centre + time_step * (kappa * spread - transport)


def fine(field, kappa, along_rows, along_cols, inside):
    for step in range(STEPS):
        padded = with_halo(field, "space", 1)
        field = jnp.where(inside, advance(padded, kappa, along_rows, along_cols), 0.0)
    return field


def pad_cols(x):
    return jnp.pad(x, [(0, 0)] * (x.ndim - 1) + [(HALO, HALO)])


def own_window(x, start, width):
    return lax.dynamic_slice_in_dim(pad_cols(x), start, width, axis=x.ndim - 1)


def on_device(start_state, old_starts, conductivity, velocity, coarse_gain, targets):
    blocks = lax.axis_size("tm")
    block = lax.axis_index("tm")
    rows, cols = start_state.shape
    width = cols // blocks
    wide = width + 2 * HALO

    def send_windows(x):
        padded = pad_cols(x)
        return jnp.stack([padded[:, k * width : k * width + wide] for k in range(blocks)])

    def to_blocks(x):
        return lax.all_to_all(send_windows(x), "tm", 0, 0, tiled=True)

    old = to_blocks(old_starts[0])
    gain = to_blocks(coarse_gain[0])
    target = to_blocks(targets[0])

    first = block * width
    kappa = own_window(conductivity, first, wide)
    flow = own_window(velocity, first, wide)
    begin = own_window(start_state, first, wide)
    column = first - HALO + lax.broadcasted_iota(jnp.int32, (1, 1, wide), 2)
    inside = (column >= 0) & (column < cols)

    fine_ends, pullback = jax.vjp(
        lambda k: fine(old, k, flow[0], flow[1], inside), kappa
    )
    carried = fine_ends - gain * old
    ends = []
    for slab in range(blocks):
        begin = gain[slab] * begin + carried[slab]
        ends.append(begin)
    new_ends = jnp.stack(ends)
    misfit = new_ends - target
    adjoints = [misfit[blocks - 1]]
    for slab in range(blocks - 2, -1, -1):
        adjoints.insert(0, misfit[slab] + gain[slab + 1] * adjoints[0])
    adjoint = jnp.stack(adjoints)
    (grad_window,) = pullback(adjoint)

    interior = new_ends[:, :, HALO : HALO + width]
    new_end = lax.all_to_all(interior, "tm", 0, 2, tiled=True)
    gradient = lax.all_gather(grad_window[:, HALO : HALO + width], "tm", axis=1, tiled=True)
    return (new_end, gradient)


def solution(mesh):
    in_specs = (
        P("space", None),
        P("tm", "space", None),
        P("space", None),
        P(None, "space", None),
        P("tm", "space", None),
        P("tm", "space", None),
    )
    out_specs = (P("tm", "space", None), P("space", None))
    return jax.shard_map(
        on_device, mesh=mesh, in_specs=in_specs, out_specs=out_specs, check_vma=False
    )
```

time: 622 us -> 242 us (0.39)
  waiting for transfers between devices: 382 us -> 68.2 us
  starting transfers between devices: 135 us -> 79.7 us
  other arithmetic: 65.6 us -> 46.5 us
  local copies, waits for them, and re-layouts: 20.6 us -> 30.2 us
    ppermute x20 -> x0, waiting for transfers between devices: 291 us -> none  [from_behind(): return lax.ppermute(block, axis, route)]
    ppermute x20 -> x0, starting transfers between devices: 95.9 us -> none  [from_behind(): return lax.ppermute(block, axis, route)]
    psum x1 -> x0, waiting for transfers between devices: 84.1 us -> none  [on_device(): gradient = lax.psum(partial_grad, 'tm')]
    add x17 -> x0, other arithmetic: 37.3 us -> none  [the longest x7 20.6 us: on_device(): new_end = gain * begin + carried]
    all_gather x0 -> x1, waiting for transfers between devices: none -> 31 us  [on_device(): lax.all_gather(grad_window[:, HALO:HALO + width], 'tm', axis=1, tiled=True)]
    all_to_all x0 -> x4, starting transfers between devices: none -> 21.5 us  [the longest x3 17.2 us: to_blocks(): return lax.all_to_all(send_windows(x), 'tm', 0, 0, tiled=True)]
    unnamed x37 -> x97, local copies, waits for them, and re-layouts: 4.14 us -> 23.5 us
    ppermute x4 -> x7, waiting for transfers between devices: 6.26 us -> 22.8 us  [with_halo(): lax.ppermute(head, axis, [((i + 1) % count, i) for i in range(ends)])]
  transfers between devices with their start and end apart: 29 -> 19, of which waited for: 19 -> 11; matrix products, arithmetic and copies ran while one was open for 2% -> 18% of each run, Pallas kernels for 0% -> 0%
where the time goes in v1:
time: 242 us; the launch traced here: 239 us
  starting transfers between devices  79.7 us (33%)
  waiting for transfers between devices  68.2 us (28%)
  other arithmetic  46.5 us (19%)
  local copies, waits for them, and re-layouts  30.2 us (12%)
  between operations  14.6 us (6%)
    ppermute x7, starting transfers between devices, with_halo(): lax.ppermute(head, axis, [((i + 1) % count, i) for i in range(ends)])  38.6 us
    all_gather x1, waiting for transfers between devices, on_device(): lax.all_gather(grad_window[:, HALO:HALO + width], 'tm', axis=1, tiled=True)  31 us
    unnamed x97, local copies, waits for them, and re-layouts  23.5 us
    ppermute x7, waiting for transfers between devices, with_halo(): lax.ppermute(head, axis, [((i + 1) % count, i) for i in range(ends)])  22.8 us
    ppermute x7, starting transfers between devices, with_halo(): lax.ppermute(tail, axis, [(i, (i + 1) % count) for i in range(ends)])  19.6 us
    all_to_all x3, starting transfers between devices, to_blocks(): return lax.all_to_all(send_windows(x), 'tm', 0, 0, tiled=True)  17.2 us
    add_any x3, other arithmetic, potential(): return field + 0.25 * jnp.tanh(field)  13.8 us
    select_n x3, other arithmetic, fine(): jnp.where(inside, advance(padded, kappa, along_rows, along_cols), 0.0)  8.96 us
  transfers between devices with their start and end apart: 19, of which 11 were waited for; matrix products, arithmetic and copies ran while one was open for 18% of the time, Pallas kernels for 0%

profile of v1, /device:TPU:160, one launch (start us, length us, event | category | flops | bytes accessed | tf_op | source)
XLA Modules:
  0.0 239.2 jit_solution(3339310915675040073)
XLA Ops:
  14.3 6.1 %all-to-all-start.1 = ((f32[8,32,1040]{2,1,0:T(8,128)}), f32[8,32,1040]{2,1,0:T(8,128)S(1)}, u32[]{:S(2)}, u32[]{:S(2)}) async-start(f32[8,32,1040]{2,1,0:T(8,128)} %fusion.80), calls=%async_computation.1 | async-start | bytes 2359296 | tf_op jit(solution)/shard_map/all_to_all | solution.py:79
  32.9 3.1 %all-to-all-done.1 = f32[8,32,1040]{2,1,0:T(8,128)S(1)} async-done(((f32[8,32,1040]{2,1,0:T(8,128)}), f32[8,32,1040]{2,1,0:T(8,128)S(1)}, u32[]{:S(2)}, u32[]{:S(2)}) %all-to-all-start.1) | async-done | bytes 1064992 | tf_op jit(solution)/shard_map/all_to_all | solution.py:79
  36.0 4.2 %all-to-all-start = ((f32[8,32,1040]{2,1,0:T(8,128)}), f32[8,32,1040]{2,1,0:T(8,128)S(1)}, u32[]{:S(2)}, u32[]{:S(2)}) async-start(f32[8,32,1040]{2,1,0:T(8,128)} %fusion.76), calls=%async_computation | async-start | bytes 2359296 | tf_op jit(solution)/shard_map/all_to_all | solution.py:79
  42.2 7.9 %collective-permute-start.1 = (f32[8,1,1040]{2,1,0:T(1,128)S(1)}, f32[8,1,1040]{2,1,0:T(1,128)S(1)}, u32[]{:S(2)}, u32[]{:S(2)}) collective-permute-start(f32[8,1,1040]{2,1,0:T(1,128)S(1)} %get-tuple-element.76), channel_id=1, source_target_pairs={{8,0},{16,8},{24,16},{32,24},{40,32},{48,40},{56,48},{64,56},{72,6... | collective-permute-start | bytes 99848 | tf_op jit(solution)/shard_map/jvp()/ppermute | solution.py:22
  50.1 3.7 %collective-permute-done.1 = f32[8,1,1040]{2,1,0:T(1,128)S(1)} collective-permute-done((f32[8,1,1040]{2,1,0:T(1,128)S(1)}, f32[8,1,1040]{2,1,0:T(1,128)S(1)}, u32[]{:S(2)}, u32[]{:S(2)}) %collective-permute-start.1) | collective-permute-done | bytes 33312 | tf_op jit(solution)/shard_map/jvp()/ppermute | solution.py:22
  54.5 3.0 %fusion.58 = (f32[8,32,1040]{2,1,0:T(8,128)S(1)}, f32[8,32,1040]{2,1,0:T(8,128)}) fusion(f32[8,32,1040]{2,1,0:T(8,128)S(1)} %all-to-all-done.1, f32[8,34,1042]{2,1,0:T(8,128)S(1)} %get-tuple-element.66, f32[8,1,1040]{2,1,0:T(1,128)S(1)} %collective-permute-done.1, f32[8,1,1040]{2,1,0:T(1,128)S(1)} %collective-permute-done, ...), kind=kLoop, calls=%fused_computation.105 | loop fusion | flops 6123520 | bytes 11382800 | tf_op jit(solution)/shard_map/jvp(jit(_where))/select_n | solution.py:55
  57.5 1.9 collective-permute-start.2
  59.4 8.0 %collective-permute-start.3 = (f32[8,1,1040]{2,1,0:T(1,128)S(1)}, f32[8,1,1040]{2,1,0:T(1,128)S(1)}, u32[]{:S(2)}, u32[]{:S(2)}) collective-permute-start(f32[8,1,1040]{2,1,0:T(1,128)S(1)} %get-tuple-element.74), channel_id=1, source_target_pairs={{8,0},{16,8},{24,16},{32,24},{40,32},{48,40},{56,48},{64,56},{72,6... | collective-permute-start | bytes 99848 | tf_op jit(solution)/shard_map/jvp()/ppermute | solution.py:22
  69.8 3.0 %fusion.44 = (f32[8,32,1040]{2,1,0:T(8,128)S(1)}, f32[8,32,1040]{2,1,0:T(8,128)}) fusion(f32[8,32,1040]{2,1,0:T(8,128)S(1)} %get-tuple-element.32, f32[8,34,1042]{2,1,0:T(8,128)S(1)} %get-tuple-element.64, f32[8,1,1040]{2,1,0:T(1,128)S(1)} %collective-permute-done.3, f32[8,1,1040]{2,1,0:T(1,128)S(1)} %collective-permute-done.2, ...), kind=kLoop, calls=%fused_computation.83 | loop fusion | flops 6123520 | bytes 11382800 | tf_op jit(solution)/shard_map/jvp(jit(_where))/select_n | solution.py:55
  72.8 1.9 collective-permute-start.4
  74.8 7.9 %collective-permute-start.5 = (f32[8,1,1040]{2,1,0:T(1,128)S(1)}, f32[8,1,1040]{2,1,0:T(1,128)S(1)}, u32[]{:S(2)}, u32[]{:S(2)}) collective-permute-start(f32[8,1,1040]{2,1,0:T(1,128)S(1)} %get-tuple-element.72), channel_id=1, source_target_pairs={{8,0},{16,8},{24,16},{32,24},{40,32},{48,40},{56,48},{64,56},{72,6... | collective-permute-start | bytes 99848 | tf_op jit(solution)/shard_map/jvp()/ppermute | solution.py:22
  85.0 3.0 %fusion.30 = (f32[8,32,1040]{2,1,0:T(8,128)S(1)}, f32[8,32,1040]{2,1,0:T(8,128)}) fusion(f32[8,32,1040]{2,1,0:T(8,128)S(1)} %get-tuple-element.30, f32[8,34,1042]{2,1,0:T(8,128)S(1)} %get-tuple-element.62, f32[8,1,1040]{2,1,0:T(1,128)S(1)} %collective-permute-done.5, f32[8,1,1040]{2,1,0:T(1,128)S(1)} %collective-permute-done.4, ...), kind=kLoop, calls=%fused_computation.61 | loop fusion | flops 6123520 | bytes 11382800 | tf_op jit(solution)/shard_map/jvp(jit(_where))/select_n | solution.py:55
  88.0 1.9 collective-permute-start.6
  89.9 7.9 %collective-permute-start.7 = (f32[8,1,1040]{2,1,0:T(1,128)S(1)}, f32[8,1,1040]{2,1,0:T(1,128)S(1)}, u32[]{:S(2)}, u32[]{:S(2)}) collective-permute-start(f32[8,1,1040]{2,1,0:T(1,128)S(1)} %get-tuple-element.70), channel_id=1, source_target_pairs={{8,0},{16,8},{24,16},{32,24},{40,32},{48,40},{56,48},{64,56},{72,6... | collective-permute-start | bytes 99848 | tf_op jit(solution)/shard_map/jvp()/ppermute | solution.py:22
  101.9 7.0 %all-to-all-start.3 = ((f32[8,32,1040]{2,1,0:T(8,128)}), f32[8,32,1040]{2,1,0:T(8,128)}, u32[]{:S(2)}, u32[]{:S(2)}) async-start(f32[8,32,1040]{2,1,0:T(8,128)} %fusion.84), calls=%async_computation.3 | async-start | bytes 2359296 | tf_op jit(solution)/shard_map/all_to_all | solution.py:79
  108.8 6.1 %fusion.16 = (f32[8,32,1040]{2,1,0:T(8,128)S(1)}, f32[8,32,1040]{2,1,0:T(8,128)}) fusion(f32[8,32,1040]{2,1,0:T(8,128)} %copy-done.4, f32[8,34,1042]{2,1,0:T(8,128)} %get-tuple-element.60, f32[8,1,1040]{2,1,0:T(1,128)} %copy-done.32, f32[8,1,1040]{2,1,0:T(1,128)} %copy-done.30, f32[8,32,1040]{2,1,0:T(8,128)S(1)} %all-to-all-done, ...), kind=kLoop, calls=%fused_computation.39 | loop fusion | flops 6656000 | bytes 13512720 | tf_op jit(solution)/shard_map/sub | solution.py:95
  115.3 4.4 %all-to-all-done.3 = f32[8,32,1040]{2,1,0:T(8,128)} async-done(((f32[8,32,1040]{2,1,0:T(8,128)}), f32[8,32,1040]{2,1,0:T(8,128)}, u32[]{:S(2)}, u32[]{:S(2)}) %all-to-all-start.3) | async-done | bytes 1064992 | tf_op jit(solution)/shard_map/all_to_all | solution.py:79
  123.1 4.6 %multiply_add_fusion.2 = f32[8,34,1042]{2,1,0:T(8,128)S(1)} fusion(f32[8,32,1040]{2,1,0:T(8,128)S(1)} %get-tuple-element.68, f32[8,32,1040]{2,1,0:T(8,128)S(1)} %get-tuple-element.67, f32[8,32,1040]{2,1,0:T(8,128)S(1)} %get-tuple-element.55, f32[8,32,1040]{2,1,0:T(8,128)S(1)} %get-tuple-element.56, f32[8,32,1040]{2,1,0:T(8,128)S(1)} %get-tuple-element.57, ...), kind=kLoop, calls=%fused_computation.14 | loop fusion | flops 6518752 | bytes 9719936 | tf_op jit(solution)/shard_map/transpose(jvp())/add_any | solution.py:29
  127.9 8.0 %collective-permute-start.8 = (f32[8,1,1040]{2,1,0:T(1,128)S(1)}, f32[8,1,1040]{2,1,0:T(1,128)S(1)}, u32[]{:S(2)}, u32[]{:S(2)}) collective-permute-start(f32[8,1,1040]{2,1,0:T(1,128)S(1)} %get-tuple-element.52), channel_id=1, source_target_pairs={{8,0},{16,8},{24,16},{32,24},{40,32},{48,40},{56,48},{64,56},{72,6... | collective-permute-start | bytes 99848 | tf_op jit(solution)/shard_map/transpose(jvp())/ppermute | solution.py:20
  136.0 1.9 collective-permute-start.9
  137.9 7.9 %collective-permute-done.9 = f32[8,1,1040]{2,1,0:T(1,128)S(1)} collective-permute-done((f32[8,1,1040]{2,1,0:T(1,128)S(1)}, f32[8,1,1040]{2,1,0:T(1,128)S(1)}, u32[]{:S(2)}, u32[]{:S(2)}) %collective-permute-start.9) | collective-permute-done | bytes 33312 | tf_op jit(solution)/shard_map/transpose(jvp())/ppermute | solution.py:22
  147.8 4.6 %multiply_add_fusion.1 = f32[8,34,1042]{2,1,0:T(8,128)S(1)} fusion(f32[8,32,1040]{2,1,0:T(8,128)S(1)} %get-tuple-element.9, f32[8,32,1040]{2,1,0:T(8,128)S(1)} %get-tuple-element.8, f32[8,32,1040]{2,1,0:T(8,128)S(1)} %get-tuple-element.43, f32[8,32,1040]{2,1,0:T(8,128)S(1)} %get-tuple-element.44, f32[8,32,1040]{2,1,0:T(8,128)S(1)} %get-tuple-element.45, ...), kind=kLoop, calls=%fused_computation.13 | loop fusion | flops 6518752 | bytes 9719936 | tf_op jit(solution)/shard_map/transpose(jvp())/add_any | solution.py:29
  154.5 2.6 %collective-permute-start.11 = (f32[8,1,1040]{2,1,0:T(1,128)S(1)}, f32[8,1,1040]{2,1,0:T(1,128)S(1)}, u32[]{:S(2)}, u32[]{:S(2)}) collective-permute-start(f32[8,1,1040]{2,1,0:T(1,128)S(1)} %get-tuple-element.51), channel_id=1, source_target_pairs={{0,8},{8,16},{16,24},{24,32},{32,40},{40,48},{48,56},{56,64},{64,7... | collective-permute-start | bytes 99848 | tf_op jit(solution)/shard_map/transpose(jvp())/ppermute | solution.py:22
  157.2 6.9 %collective-permute-done.11 = f32[8,1,1040]{2,1,0:T(1,128)S(1)} collective-permute-done((f32[8,1,1040]{2,1,0:T(1,128)S(1)}, f32[8,1,1040]{2,1,0:T(1,128)S(1)}, u32[]{:S(2)}, u32[]{:S(2)}) %collective-permute-start.11) | collective-permute-done | bytes 33312 | tf_op jit(solution)/shard_map/transpose(jvp())/ppermute | solution.py:22
  166.0 4.6 %multiply_add_fusion = f32[8,34,1042]{2,1,0:T(8,128)S(1)} fusion(f32[8,32,1040]{2,1,0:T(8,128)S(1)} %get-tuple-element.7, f32[8,32,1040]{2,1,0:T(8,128)S(1)} %get-tuple-element.6, f32[8,32,1040]{2,1,0:T(8,128)S(1)} %get-tuple-element.39, f32[8,32,1040]{2,1,0:T(8,128)S(1)} %get-tuple-element.40, f32[8,32,1040]{2,1,0:T(8,128)S(1)} %get-tuple-element.41, ...), kind=kLoop, calls=%fused_computation.12 | loop fusion | flops 6518752 | bytes 9719936 | tf_op jit(solution)/shard_map/transpose(jvp())/add_any | solution.py:29
  173.9 2.4 %collective-permute-start.13 = (f32[8,1,1040]{2,1,0:T(1,128)S(1)}, f32[8,1,1040]{2,1,0:T(1,128)S(1)}, u32[]{:S(2)}, u32[]{:S(2)}) collective-permute-start(f32[8,1,1040]{2,1,0:T(1,128)S(1)} %get-tuple-element.49), channel_id=1, source_target_pairs={{0,8},{8,16},{16,24},{24,32},{32,40},{40,48},{48,56},{56,64},{64,7... | collective-permute-start | bytes 99848 | tf_op jit(solution)/shard_map/transpose(jvp())/ppermute | solution.py:22
  177.6 4.3 %all-to-all-start.2 = ((f32[8,32,1024]{2,1,0:T(8,128)}), f32[8,32,1024]{2,1,0:T(8,128)}, u32[]{:S(2)}, u32[]{:S(2)}) async-start(f32[8,32,1024]{2,1,0:T(8,128)} %slice.509), calls=%async_computation.2 | async-start | bytes 2097152 | tf_op jit(solution)/shard_map/all_to_all | solution.py:109
  184.3 4.6 %multiply_reduce_fusion.2 = (f32[32,1040]{1,0:T(8,128)S(1)}, f32[32,1040]{1,0:T(8,128)S(1)}, f32[32,1040]{1,0:T(8,128)S(1)}, f32[32,1040]{1,0:T(8,128)S(1)}) fusion(f32[8,32,1040]{2,1,0:T(8,128)} %get-tuple-element.27, f32[8,32,1040]{2,1,0:T(8,128)} %copy-done.11, pred[1040]{0:T(1024)(128)(4,1)S(1)} %fusion.117, f32[8,32,1040]{2,1,0:T(8,128)} %get-tuple-element.29, ...), kind=kLoop, calls=%fused_computation.129 | loop fusion | flops 5724160 | bytes 9252880 | tf_op jit(solution)/shard_map/transpose(jvp())/reduce_sum | solution.py:49
  189.8 7.0 %all-to-all-done.2 = f32[8,32,1024]{2,1,0:T(8,128)} async-done(((f32[8,32,1024]{2,1,0:T(8,128)}), f32[8,32,1024]{2,1,0:T(8,128)}, u32[]{:S(2)}, u32[]{:S(2)}) %all-to-all-start.2) | async-done | bytes 1048608 | tf_op jit(solution)/shard_map/all_to_all | solution.py:109
  196.7 2.3 copy.9
  199.1 31.0 %all-gather.2.cloned.1.call-done = f32[32,8192]{1,0:T(8,128)} async-done(((f32[32,1024]{1,0:T(8,128)}), f32[32,8192]{1,0:T(8,128)}) %all-gather.2.cloned.1.call-update) | async-done | bytes 1048592 | tf_op jit(solution)/shard_map/all_gather | solution.py:110
  230.1 2.3 copy.46
  (151 shorter events, 48.7 us)
Async XLA Ops:
  14.3 6.1 %copy-start.8 = (f32[1,32,8192]{2,1,0:T(8,128)S(1)}, f32[1,32,8192]{2,1,0:T(8,128)}, u32[]{:S(2)}) copy-start(f32[1,32,8192]{2,1,0:T(8,128)} %param.10) | copy-start | bytes 3145732
  14.3 21.7 %all-to-all-start.1 = ((f32[8,32,1040]{2,1,0:T(8,128)}), f32[8,32,1040]{2,1,0:T(8,128)S(1)}, u32[]{:S(2)}, u32[]{:S(2)}) async-start(f32[8,32,1040]{2,1,0:T(8,128)} %fusion.80), calls=%async_computation.1 | async-start | bytes 2359296 | tf_op jit(solution)/shard_map/all_to_all | solution.py:79
  27.5 118.4 %copy-start.15 = (f32[32,1040]{1,0:T(8,128)}, f32[32,1040]{1,0:T(8,128)S(1)}, u32[]{:S(2)}) copy-start(f32[32,1040]{1,0:T(8,128)S(1)} %get-tuple-element.12) | copy-start | bytes 399364
  36.0 18.4 %copy-start.6 = (f32[8,32,1040]{2,1,0:T(8,128)}, f32[8,32,1040]{2,1,0:T(8,128)S(1)}, u32[]{:S(2)}) copy-start(f32[8,32,1040]{2,1,0:T(8,128)S(1)} %all-to-all-done.1) | copy-start | bytes 3194884
  36.0 65.8 %all-to-all-start = ((f32[8,32,1040]{2,1,0:T(8,128)}), f32[8,32,1040]{2,1,0:T(8,128)S(1)}, u32[]{:S(2)}, u32[]{:S(2)}) async-start(f32[8,32,1040]{2,1,0:T(8,128)} %fusion.76), calls=%async_computation | async-start | bytes 2359296 | tf_op jit(solution)/shard_map/all_to_all | solution.py:79
  40.3 9.8 %collective-permute-start = (f32[8,1,1040]{2,1,0:T(1,128)S(1)}, f32[8,1,1040]{2,1,0:T(1,128)S(1)}, u32[]{:S(2)}, u32[]{:S(2)}) collective-permute-start(f32[8,1,1040]{2,1,0:T(1,128)S(1)} %get-tuple-element.75), channel_id=1, source_target_pairs={{0,8},{8,16},{16,24},{24,32},{32,40},{40,48},{48,56},{56,64},{64,7... | collective-permute-start | bytes 99848 | tf_op jit(solution)/shard_map/jvp()/ppermute | solution.py:20
  42.2 11.6 %collective-permute-start.1 = (f32[8,1,1040]{2,1,0:T(1,128)S(1)}, f32[8,1,1040]{2,1,0:T(1,128)S(1)}, u32[]{:S(2)}, u32[]{:S(2)}) collective-permute-start(f32[8,1,1040]{2,1,0:T(1,128)S(1)} %get-tuple-element.76), channel_id=1, source_target_pairs={{8,0},{16,8},{24,16},{32,24},{40,32},{48,40},{56,48},{64,56},{72,6... | collective-permute-start | bytes 99848 | tf_op jit(solution)/shard_map/jvp()/ppermute | solution.py:22
  54.4 13.0 %copy-start.10 = (f32[1,32,8192]{2,1,0:T(8,128)S(1)}, f32[1,32,8192]{2,1,0:T(8,128)}, u32[]{:S(2)}) copy-start(f32[1,32,8192]{2,1,0:T(8,128)} %param.11) | copy-start | bytes 3145732
  57.5 12.3 %copy-start = (f32[8,32,1040]{2,1,0:T(8,128)}, f32[8,32,1040]{2,1,0:T(8,128)S(1)}, u32[]{:S(2)}) copy-start(f32[8,32,1040]{2,1,0:T(8,128)S(1)} %get-tuple-element.32) | copy-start | bytes 3194884
  57.5 10.7 %collective-permute-start.2 = (f32[8,1,1040]{2,1,0:T(1,128)S(1)}, f32[8,1,1040]{2,1,0:T(1,128)S(1)}, u32[]{:S(2)}, u32[]{:S(2)}) collective-permute-start(f32[8,1,1040]{2,1,0:T(1,128)S(1)} %get-tuple-element.73), channel_id=1, source_target_pairs={{0,8},{8,16},{16,24},{24,32},{32,40},{40,48},{48,56},{56,64},{64,7... | collective-permute-start | bytes 99848 | tf_op jit(solution)/shard_map/jvp()/ppermute | solution.py:20
  59.4 9.7 %collective-permute-start.3 = (f32[8,1,1040]{2,1,0:T(1,128)S(1)}, f32[8,1,1040]{2,1,0:T(1,128)S(1)}, u32[]{:S(2)}, u32[]{:S(2)}) collective-permute-start(f32[8,1,1040]{2,1,0:T(1,128)S(1)} %get-tuple-element.74), channel_id=1, source_target_pairs={{8,0},{16,8},{24,16},{32,24},{40,32},{48,40},{56,48},{64,56},{72,6... | collective-permute-start | bytes 99848 | tf_op jit(solution)/shard_map/jvp()/ppermute | solution.py:22
  72.8 12.2 %copy-start.2 = (f32[8,32,1040]{2,1,0:T(8,128)}, f32[8,32,1040]{2,1,0:T(8,128)S(1)}, u32[]{:S(2)}) copy-start(f32[8,32,1040]{2,1,0:T(8,128)S(1)} %get-tuple-element.30) | copy-start | bytes 3194884
  72.8 10.6 %collective-permute-start.4 = (f32[8,1,1040]{2,1,0:T(1,128)S(1)}, f32[8,1,1040]{2,1,0:T(1,128)S(1)}, u32[]{:S(2)}, u32[]{:S(2)}) collective-permute-start(f32[8,1,1040]{2,1,0:T(1,128)S(1)} %get-tuple-element.71), channel_id=1, source_target_pairs={{0,8},{8,16},{16,24},{24,32},{32,40},{40,48},{48,56},{56,64},{64,7... | collective-permute-start | bytes 99848 | tf_op jit(solution)/shard_map/jvp()/ppermute | solution.py:20
  74.8 9.5 %collective-permute-start.5 = (f32[8,1,1040]{2,1,0:T(1,128)S(1)}, f32[8,1,1040]{2,1,0:T(1,128)S(1)}, u32[]{:S(2)}, u32[]{:S(2)}) collective-permute-start(f32[8,1,1040]{2,1,0:T(1,128)S(1)} %get-tuple-element.72), channel_id=1, source_target_pairs={{8,0},{16,8},{24,16},{32,24},{40,32},{48,40},{56,48},{64,56},{72,6... | collective-permute-start | bytes 99848 | tf_op jit(solution)/shard_map/jvp()/ppermute | solution.py:22
  87.9 11.5 %copy-start.4 = (f32[8,32,1040]{2,1,0:T(8,128)}, f32[8,32,1040]{2,1,0:T(8,128)S(1)}, u32[]{:S(2)}) copy-start(f32[8,32,1040]{2,1,0:T(8,128)S(1)} %get-tuple-element.28) | copy-start | bytes 3194884
  88.0 10.6 %collective-permute-start.6 = (f32[8,1,1040]{2,1,0:T(1,128)S(1)}, f32[8,1,1040]{2,1,0:T(1,128)S(1)}, u32[]{:S(2)}, u32[]{:S(2)}) collective-permute-start(f32[8,1,1040]{2,1,0:T(1,128)S(1)} %get-tuple-element.69), channel_id=1, source_target_pairs={{0,8},{8,16},{16,24},{24,32},{32,40},{40,48},{48,56},{56,64},{64,7... | collective-permute-start | bytes 99848 | tf_op jit(solution)/shard_map/jvp()/ppermute | solution.py:20
  89.9 9.5 %collective-permute-start.7 = (f32[8,1,1040]{2,1,0:T(1,128)S(1)}, f32[8,1,1040]{2,1,0:T(1,128)S(1)}, u32[]{:S(2)}, u32[]{:S(2)}) collective-permute-start(f32[8,1,1040]{2,1,0:T(1,128)S(1)} %get-tuple-element.70), channel_id=1, source_target_pairs={{8,0},{16,8},{24,16},{32,24},{40,32},{48,40},{56,48},{64,56},{72,6... | collective-permute-start | bytes 99848 | tf_op jit(solution)/shard_map/jvp()/ppermute | solution.py:22
  101.9 17.8 %all-to-all-start.3 = ((f32[8,32,1040]{2,1,0:T(8,128)}), f32[8,32,1040]{2,1,0:T(8,128)}, u32[]{:S(2)}, u32[]{:S(2)}) async-start(f32[8,32,1040]{2,1,0:T(8,128)} %fusion.84), calls=%async_computation.3 | async-start | bytes 2359296 | tf_op jit(solution)/shard_map/all_to_all | solution.py:79
  108.8 6.1 %copy-start.17 = (f32[32,8192]{1,0:T(8,128)S(1)}, f32[32,8192]{1,0:T(8,128)}, u32[]{:S(2)}) copy-start(f32[32,8192]{1,0:T(8,128)} %param.6) | copy-start | bytes 3145732
  115.3 5.8 %copy-start.13 = (f32[8,32,1040]{2,1,0:T(8,128)}, f32[8,32,1040]{2,1,0:T(8,128)S(1)}, u32[]{:S(2)}) copy-start(f32[8,32,1040]{2,1,0:T(8,128)S(1)} %fusion.96) | copy-start | bytes 3194884
  127.9 10.0 %collective-permute-start.8 = (f32[8,1,1040]{2,1,0:T(1,128)S(1)}, f32[8,1,1040]{2,1,0:T(1,128)S(1)}, u32[]{:S(2)}, u32[]{:S(2)}) collective-permute-start(f32[8,1,1040]{2,1,0:T(1,128)S(1)} %get-tuple-element.52), channel_id=1, source_target_pairs={{8,0},{16,8},{24,16},{32,24},{40,32},{48,40},{56,48},{64,56},{72,6... | collective-permute-start | bytes 99848 | tf_op jit(solution)/shard_map/transpose(jvp())/ppermute | solution.py:20
  136.0 9.9 %collective-permute-start.9 = (f32[8,1,1040]{2,1,0:T(1,128)S(1)}, f32[8,1,1040]{2,1,0:T(1,128)S(1)}, u32[]{:S(2)}, u32[]{:S(2)}) collective-permute-start(f32[8,1,1040]{2,1,0:T(1,128)S(1)} %get-tuple-element.53), channel_id=1, source_target_pairs={{0,8},{8,16},{16,24},{24,32},{32,40},{40,48},{48,56},{56,64},{64,7... | collective-permute-start | bytes 99848 | tf_op jit(solution)/shard_map/transpose(jvp())/ppermute | solution.py:22
  137.9 8.5 %copy-start.18 = (f32[8,1,1040]{2,1,0:T(1,128)}, f32[8,1,1040]{2,1,0:T(1,128)S(1)}, u32[]{:S(2)}) copy-start(f32[8,1,1040]{2,1,0:T(1,128)S(1)} %collective-permute-done.8) | copy-start | bytes 99844
  147.8 16.3 %copy-start.16 = (f32[32,1040]{1,0:T(8,128)S(1)}, f32[32,1040]{1,0:T(8,128)}, u32[]{:S(2)}) copy-start(f32[32,1040]{1,0:T(8,128)} %copy-done.15) | copy-start | bytes 399364
  152.6 4.6 %collective-permute-start.10 = (f32[8,1,1040]{2,1,0:T(1,128)S(1)}, f32[8,1,1040]{2,1,0:T(1,128)S(1)}, u32[]{:S(2)}, u32[]{:S(2)}) collective-permute-start(f32[8,1,1040]{2,1,0:T(1,128)S(1)} %get-tuple-element.50), channel_id=1, source_target_pairs={{8,0},{16,8},{24,16},{32,24},{40,32},{48,40},{56,48},{64,56},{72,6... | collective-permute-start | bytes 99848 | tf_op jit(solution)/shard_map/transpose(jvp())/ppermute | solution.py:20
  154.5 9.5 %collective-permute-start.11 = (f32[8,1,1040]{2,1,0:T(1,128)S(1)}, f32[8,1,1040]{2,1,0:T(1,128)S(1)}, u32[]{:S(2)}, u32[]{:S(2)}) collective-permute-start(f32[8,1,1040]{2,1,0:T(1,128)S(1)} %get-tuple-element.51), channel_id=1, source_target_pairs={{0,8},{8,16},{16,24},{24,32},{32,40},{40,48},{48,56},{56,64},{64,7... | collective-permute-start | bytes 99848 | tf_op jit(solution)/shard_map/transpose(jvp())/ppermute | solution.py:22
  157.2 7.5 %copy-start.20 = (f32[8,1,1040]{2,1,0:T(1,128)}, f32[8,1,1040]{2,1,0:T(1,128)S(1)}, u32[]{:S(2)}) copy-start(f32[8,1,1040]{2,1,0:T(1,128)S(1)} %collective-permute-done.10) | copy-start | bytes 99844
  166.0 10.3 %copy-start.14 = (f32[8,32,1040]{2,1,0:T(8,128)S(1)}, f32[8,32,1040]{2,1,0:T(8,128)}, u32[]{:S(2)}) copy-start(f32[8,32,1040]{2,1,0:T(8,128)} %copy-done.13) | copy-start | bytes 3194884
  172.0 10.0 %collective-permute-start.12 = (f32[8,1,1040]{2,1,0:T(1,128)S(1)}, f32[8,1,1040]{2,1,0:T(1,128)S(1)}, u32[]{:S(2)}, u32[]{:S(2)}) collective-permute-start(f32[8,1,1040]{2,1,0:T(1,128)S(1)} %get-tuple-element.48), channel_id=1, source_target_pairs={{8,0},{16,8},{24,16},{32,24},{40,32},{48,40},{56,48},{64,56},{72,6... | collective-permute-start | bytes 99848 | tf_op jit(solution)/shard_map/transpose(jvp())/ppermute | solution.py:20
  173.9 9.8 %collective-permute-start.13 = (f32[8,1,1040]{2,1,0:T(1,128)S(1)}, f32[8,1,1040]{2,1,0:T(1,128)S(1)}, u32[]{:S(2)}, u32[]{:S(2)}) collective-permute-start(f32[8,1,1040]{2,1,0:T(1,128)S(1)} %get-tuple-element.49), channel_id=1, source_target_pairs={{0,8},{8,16},{16,24},{24,32},{32,40},{40,48},{48,56},{56,64},{64,7... | collective-permute-start | bytes 99848 | tf_op jit(solution)/shard_map/transpose(jvp())/ppermute | solution.py:22
  177.6 19.1 %all-to-all-start.2 = ((f32[8,32,1024]{2,1,0:T(8,128)}), f32[8,32,1024]{2,1,0:T(8,128)}, u32[]{:S(2)}, u32[]{:S(2)}) async-start(f32[8,32,1024]{2,1,0:T(8,128)} %slice.509), calls=%async_computation.2 | async-start | bytes 2097152 | tf_op jit(solution)/shard_map/all_to_all | solution.py:109
  181.9 48.2 %all-gather.2.cloned.1.call-start = ((), (), s32[]{:S(2)}) async-start(), calls=%async_computation.4 | async-start | bytes 1179648 | tf_op jit(solution)/shard_map/all_gather | solution.py:110
  (23 other events, 27.8 us)
Sparse Core Ops, SparseCore 0:
  189.9 40.1 all-gather.1

commit v2 on v1

--- a/solution.py
+++ b/solution.py
@@ -10,11 +10,11 @@
 time_step = 0.25
 
 
-def with_halo(cells, axis, dim):
+def with_halo(cells, axis, dim, width):
     count = lax.axis_size(axis)
     ends = count - 1
-    head = lax.slice_in_dim(cells, 0, 1, axis=dim)
-    tail = lax.slice_in_dim(cells, cells.shape[dim] - 1, cells.shape[dim], axis=dim)
+    head = lax.slice_in_dim(cells, 0, width, axis=dim)
+    tail = lax.slice_in_dim(cells, cells.shape[dim] - width, cells.shape[dim], axis=dim)
     return jnp.concatenate(
         [
             lax.ppermute(tail, axis, [(i, (i + 1) % count) for i in range(ends)]),
@@ -29,8 +29,8 @@
     return field + 0.25 * jnp.tanh(field)
 
 
-def advance(padded, kappa, along_rows, along_cols):
-    wide = jnp.pad(padded, ((0, 0), (0, 0), (1, 1)))
+def advance(field, kappa, along_rows, along_cols):
+    wide = jnp.pad(field, ((0, 0), (1, 1), (1, 1)))
     shaped = potential(wide)
     centre = wide[:, 1:-1, 1:-1]
     spread = (
@@ -50,10 +50,10 @@
 
 
 def fine(field, kappa, along_rows, along_cols, inside):
+    kappa = with_halo(kappa, "space", 0, STEPS)
     for step in range(STEPS):
-        padded = with_halo(field, "space", 1)
-        field = jnp.where(inside, advance(padded, kappa, along_rows, along_cols), 0.0)
-    return field
+        field = jnp.where(inside, advance(field, kappa, along_rows, along_cols), 0.0)
+    return field[:, STEPS:-STEPS]
 
 
 def pad_cols(x):
@@ -87,10 +87,14 @@
     flow = own_window(velocity, first, wide)
     begin = own_window(start_state, first, wide)
     column = first - HALO + lax.broadcasted_iota(jnp.int32, (1, 1, wide), 2)
-    inside = (column >= 0) & (column < cols)
+    strip = lax.axis_index("space")
+    row = strip * rows - STEPS + lax.broadcasted_iota(jnp.int32, (1, rows + 2 * STEPS, 1), 1)
+    inside = (column >= 0) & (column < cols) & (row >= 0) & (row < rows * lax.axis_size("space"))
+    old_rows = with_halo(old, "space", 1, STEPS)
+    flow_rows = with_halo(flow, "space", 1, STEPS)
 
     fine_ends, pullback = jax.vjp(
-        lambda k: fine(old, k, flow[0], flow[1], inside), kappa
+        lambda k: fine(old_rows, k, flow_rows[0], flow_rows[1], inside), kappa
     )
     carried = fine_ends - gain * old
     ends = []
@@ -107,7 +111,9 @@
 
     interior = new_ends[:, :, HALO : HALO + width]
     new_end = lax.all_to_all(interior, "tm", 0, 2, tiled=True)
-    gradient = lax.all_gather(grad_window[:, HALO : HALO + width], "tm", axis=1, tiled=True)
+    own = grad_window[:, HALO : HALO + width]
+    copies = jnp.broadcast_to(own[None], (blocks,) + own.shape)
+    gradient = lax.all_to_all(copies, "tm", 0, 2, tiled=True)[0]
     return (new_end, gradient)
 
 

time: 242 us -> 166 us (0.69)
  waiting for transfers between devices: 68.2 us -> 17.1 us
  between operations: 14.6 us -> 1.24 us
  starting transfers between devices: 79.7 us -> 67.9 us
  other arithmetic: 46.5 us -> 49.2 us
    all_gather x1 -> x0, waiting for transfers between devices: 31 us -> none  [on_device(): lax.all_gather(grad_window[:, HALO:HALO + width], 'tm', axis=1, tiled=True)]
    add_any x3 -> x1, other arithmetic: 13.8 us -> 0.12 us  [with_halo(): head = lax.slice_in_dim(cells, 0, width, axis=dim)]
    ppermute x7 -> x4, waiting for transfers between devices: 22.8 us -> 9.14 us  [with_halo(): lax.ppermute(head, axis, [((i + 1) % count, i) for i in range(ends)])]
    ppermute x7 -> x4, starting transfers between devices: 38.6 us -> 25.5 us  [with_halo(): lax.ppermute(head, axis, [((i + 1) % count, i) for i in range(ends)])]
    unnamed x11, other arithmetic: 0.62 us -> 11.3 us
    ppermute x7 -> x4, starting transfers between devices: 19.6 us -> 11.3 us  [with_halo(): lax.ppermute(tail, axis, [(i, (i + 1) % count) for i in range(ends)])]
    all_to_all x0 -> x1, waiting for transfers between devices: none -> 7.73 us  [on_device(): gradient = lax.all_to_all(copies, 'tm', 0, 2, tiled=True)[0]]
    all_to_all x3, waiting for transfers between devices: 7.43 us -> 0.01 us  [to_blocks(): return lax.all_to_all(send_windows(x), 'tm', 0, 0, tiled=True)]
  transfers between devices with their start and end apart: 19 -> 13, of which waited for: 11 -> 4; matrix products, arithmetic and copies ran while one was open for 18% -> 42% of each run, Pallas kernels for 0% -> 0%
where the time goes in v2:
time: 166 us; the launch traced here: 165 us
  starting transfers between devices  67.9 us (41%)
  other arithmetic  49.2 us (30%)
  local copies, waits for them, and re-layouts  29.7 us (18%)
  waiting for transfers between devices  17.1 us (10%)
    ppermute x4, starting transfers between devices, with_halo(): lax.ppermute(head, axis, [((i + 1) % count, i) for i in range(ends)])  25.5 us
    all_to_all x3, starting transfers between devices, to_blocks(): return lax.all_to_all(send_windows(x), 'tm', 0, 0, tiled=True)  19.5 us
    unnamed x69, local copies, waits for them, and re-layouts  18.5 us
    unnamed x11, other arithmetic  11.3 us
    ppermute x4, starting transfers between devices, with_halo(): lax.ppermute(tail, axis, [(i, (i + 1) % count) for i in range(ends)])  11.3 us
    select_n x3, other arithmetic, fine(): jnp.where(inside, advance(field, kappa, along_rows, along_cols), 0.0)  10.2 us
    ppermute x4, waiting for transfers between devices, with_halo(): lax.ppermute(head, axis, [((i + 1) % count, i) for i in range(ends)])  9.14 us
    reduce_sum x3, other arithmetic, advance(): return centre + time_step * (kappa * spread - transport)  9.06 us
  transfers between devices with their start and end apart: 13, of which 4 were waited for; matrix products, arithmetic and copies ran while one was open for 42% of the time, Pallas kernels for 0%

profile of v2, /device:TPU:160, one launch (start us, length us, event | category | flops | bytes accessed | tf_op | source)
XLA Modules:
  0.0 165.1 jit_solution(989754349141749460)
XLA Ops:
  1.6 1.9 %collective-permute-start.2 = (f32[4,1040]{1,0:T(4,128)S(1)}, f32[4,1040]{1,0:T(4,128)S(1)}, u32[]{:S(2)}, u32[]{:S(2)}) collective-permute-start(f32[4,1040]{1,0:T(4,128)S(1)} %get-tuple-element.60), channel_id=1, source_target_pairs={{0,8},{8,16},{16,24},{24,32},{32,40},{40,48},{48,56},{56,64},{64,7... | collective-permute-start | bytes 49928 | tf_op jit(solution)/shard_map/jvp()/ppermute | solution.py:20
  3.6 7.9 %collective-permute-start.3 = (f32[4,1040]{1,0:T(4,128)S(1)}, f32[4,1040]{1,0:T(4,128)S(1)}, u32[]{:S(2)}, u32[]{:S(2)}) collective-permute-start(f32[4,1040]{1,0:T(4,128)S(1)} %get-tuple-element.61), channel_id=1, source_target_pairs={{8,0},{16,8},{24,16},{32,24},{40,32},{48,40},{56,48},{64,56},{72,6... | collective-permute-start | bytes 49928 | tf_op jit(solution)/shard_map/jvp()/ppermute | solution.py:22
  11.4 1.0 pad_dynamic-slice_fusion.1
  12.5 1.9 %collective-permute-start.4 = (f32[2,4,1040]{2,1,0:T(4,128)S(1)}, f32[2,4,1040]{2,1,0:T(4,128)S(1)}, u32[]{:S(2)}, u32[]{:S(2)}) collective-permute-start(f32[2,4,1040]{2,1,0:T(4,128)S(1)} %get-tuple-element.30), channel_id=1, source_target_pairs={{0,8},{8,16},{16,24},{24,32},{32,40},{40,48},{48,56},{56,64},{64,7... | collective-permute-start | bytes 99848 | tf_op jit(solution)/shard_map/ppermute | solution.py:20
  14.4 7.9 %collective-permute-start.5 = (f32[2,4,1040]{2,1,0:T(4,128)S(1)}, f32[2,4,1040]{2,1,0:T(4,128)S(1)}, u32[]{:S(2)}, u32[]{:S(2)}) collective-permute-start(f32[2,4,1040]{2,1,0:T(4,128)S(1)} %get-tuple-element.31), channel_id=1, source_target_pairs={{8,0},{16,8},{24,16},{32,24},{40,32},{48,40},{56,48},{64,56},{72,6... | collective-permute-start | bytes 99848 | tf_op jit(solution)/shard_map/ppermute | solution.py:22
  28.4 6.1 %all-to-all-start.1 = ((f32[8,32,1040]{2,1,0:T(8,128)}), f32[8,32,1040]{2,1,0:T(8,128)S(1)}, u32[]{:S(2)}, u32[]{:S(2)}) async-start(f32[8,32,1040]{2,1,0:T(8,128)} %fusion.109), calls=%async_computation.1 | async-start | bytes 2359296 | tf_op jit(solution)/shard_map/all_to_all | solution.py:79
  34.6 1.2 pad_dynamic-slice_fusion.2
  45.6 5.7 %all-to-all-start = ((f32[8,32,1040]{2,1,0:T(8,128)}), f32[8,32,1040]{2,1,0:T(8,128)}, u32[]{:S(2)}, u32[]{:S(2)}) async-start(f32[8,32,1040]{2,1,0:T(8,128)} %fusion.105), calls=%async_computation | async-start | bytes 2359296 | tf_op jit(solution)/shard_map/all_to_all | solution.py:79
  51.4 1.9 %collective-permute-start = (f32[8,4,1040]{2,1,0:T(4,128)S(1)}, f32[8,4,1040]{2,1,0:T(4,128)S(1)}, u32[]{:S(2)}, u32[]{:S(2)}) collective-permute-start(f32[8,4,1040]{2,1,0:T(4,128)S(1)} %get-tuple-element.58), channel_id=1, source_target_pairs={{0,8},{8,16},{16,24},{24,32},{32,40},{40,48},{48,56},{56,64},{64,7... | collective-permute-start | bytes 399368 | tf_op jit(solution)/shard_map/ppermute | solution.py:20
  53.3 7.9 %collective-permute-start.1 = (f32[8,4,1040]{2,1,0:T(4,128)S(1)}, f32[8,4,1040]{2,1,0:T(4,128)S(1)}, u32[]{:S(2)}, u32[]{:S(2)}) collective-permute-start(f32[8,4,1040]{2,1,0:T(4,128)S(1)} %get-tuple-element.59), channel_id=1, source_target_pairs={{8,0},{16,8},{24,16},{32,24},{40,32},{48,40},{56,48},{64,56},{72,6... | collective-permute-start | bytes 399368 | tf_op jit(solution)/shard_map/ppermute | solution.py:22
  62.1 1.7 %collective-permute-done.1 = f32[8,4,1040]{2,1,0:T(4,128)S(1)} collective-permute-done((f32[8,4,1040]{2,1,0:T(4,128)S(1)}, f32[8,4,1040]{2,1,0:T(4,128)S(1)}, u32[]{:S(2)}, u32[]{:S(2)}) %collective-permute-start.1) | collective-permute-done | bytes 133152 | tf_op jit(solution)/shard_map/ppermute | solution.py:22
  64.6 3.4 %fusion.24 = (f32[8,40,1040]{2,1,0:T(8,128)S(1)}, f32[8,40,1040]{2,1,0:T(8,128)}) fusion(f32[8,40,1040]{2,1,0:T(8,128)S(1)} %pad_maximum_fusion, f32[40,1040]{1,0:T(8,128)S(1)} %get-tuple-element.64, f32[40,1040]{1,0:T(8,128)S(1)} %get-tuple-element.65, f32[40,1040]{1,0:T(8,128)S(1)} %get-tuple-element.63, f32[40,1040]{1,0:T(8,128)S(1)} %get-tuple-element.62, ...), kind=kLoop, calls=%fused_computation.60 | loop fusion | flops 6988800 | bytes 11523200 | tf_op jit(solution)/shard_map/jvp(jit(_where))/select_n | solution.py:55
  69.1 3.4 %fusion.39 = (f32[8,40,1040]{2,1,0:T(8,128)S(1)}, f32[8,40,1040]{2,1,0:T(8,128)}) fusion(f32[8,40,1040]{2,1,0:T(8,128)S(1)} %get-tuple-element.28, f32[40,1040]{1,0:T(8,128)S(1)} %get-tuple-element.64, f32[40,1040]{1,0:T(8,128)S(1)} %get-tuple-element.65, f32[40,1040]{1,0:T(8,128)S(1)} %get-tuple-element.63, f32[40,1040]{1,0:T(8,128)S(1)} %get-tuple-element.62, ...), kind=kLoop, calls=%fused_computation.75 | loop fusion | flops 6988800 | bytes 11523200 | tf_op jit(solution)/shard_map/jvp(jit(_where))/select_n | solution.py:55
  73.7 3.4 %fusion.55 = (f32[8,40,1040]{2,1,0:T(8,128)S(1)}, f32[8,40,1040]{2,1,0:T(8,128)}) fusion(f32[8,40,1040]{2,1,0:T(8,128)S(1)} %get-tuple-element.26, f32[40,1040]{1,0:T(8,128)S(1)} %get-tuple-element.64, f32[40,1040]{1,0:T(8,128)S(1)} %get-tuple-element.65, f32[40,1040]{1,0:T(8,128)S(1)} %get-tuple-element.63, f32[40,1040]{1,0:T(8,128)S(1)} %get-tuple-element.62, ...), kind=kLoop, calls=%fused_computation.91 | loop fusion | flops 6988800 | bytes 11523200 | tf_op jit(solution)/shard_map/jvp(jit(_where))/select_n | solution.py:55
  77.6 2.8 %fusion.84 = f32[8,40,1040]{2,1,0:T(8,128)} fusion(f32[8,42,1042]{2,1,0:T(8,128)S(1)} %pad_add_fusion), kind=kLoop, calls=%fused_computation.133 | loop fusion | flops 1664000 | bytes 7987200 | tf_op jit(solution)/shard_map/jvp()/sub | solution.py:37
  80.5 2.9 %fusion.65 = (f32[8,40,1040]{2,1,0:T(8,128)}, f32[8,40,1040]{2,1,0:T(8,128)}, f32[8,40,1040]{2,1,0:T(8,128)}) fusion(f32[8,40,1040]{2,1,0:T(8,128)S(1)} %get-tuple-element.24, f32[40,1040]{1,0:T(8,128)S(1)} %get-tuple-element.63, f32[40,1040]{1,0:T(8,128)S(1)} %get-tuple-element.62, f32[40,1040]{1,0:T(8,128)S(1)} %get-tuple-element.65), kind=kLoop, calls=%fused_computation.101 | loop fusion | flops 2662400 | bytes 5824000 | tf_op jit(solution)/shard_map/jvp()/add | solution.py:44
  83.4 7.7 %all-to-all-start.3 = ((f32[8,32,1040]{2,1,0:T(8,128)}), f32[8,32,1040]{2,1,0:T(8,128)}, u32[]{:S(2)}, u32[]{:S(2)}) async-start(f32[8,32,1040]{2,1,0:T(8,128)} %copy-done.20), calls=%async_computation.3 | async-start | bytes 2359296 | tf_op jit(solution)/shard_map/all_to_all | solution.py:79
  91.2 4.3 %fusion.98 = f32[8,32,1040]{2,1,0:T(8,128)S(1)} fusion(f32[8,40,1040]{2,1,0:T(8,128)S(1)} %get-tuple-element.24, f32[8,40,1040]{2,1,0:T(8,128)} %fusion.84, f32[8,40,1040]{2,1,0:T(8,128)} %get-tuple-element.47, f32[8,40,1040]{2,1,0:T(8,128)} %get-tuple-element.48, f32[8,40,1040]{2,1,0:T(8,128)} %get-tuple-element.46, f32[8,32,1040]{2,1,0:T(8,128)} %all-to-all-done, ...), kind=kLoop, calls=%fused_computation.182 | loop fusion | flops 2662400 | bytes 8819200 | tf_op jit(solution)/shard_map/sub | solution.py:99
  104.5 1.3 slice.472
  105.9 5.7 %all-to-all-start.2 = ((f32[8,32,1024]{2,1,0:T(8,128)}), f32[8,32,1024]{2,1,0:T(8,128)}, u32[]{:S(2)}, u32[]{:S(2)}) async-start(f32[8,32,1024]{2,1,0:T(8,128)} %slice.472), calls=%async_computation.2 | async-start | bytes 2097152 | tf_op jit(solution)/shard_map/all_to_all | solution.py:113
  111.6 1.7 %sub.120 = f32[8,32,1040]{2,1,0:T(8,128)S(1)} subtract(f32[8,32,1040]{2,1,0:T(8,128)} %copy-done.17, f32[8,32,1040]{2,1,0:T(8,128)} %all-to-all-done.3) | non-fusion elementwise | flops 266240 | bytes 3194880 | tf_op jit(solution)/shard_map/sub | solution.py:105
  113.3 1.4 fusion.116
  119.2 2.7 %multiply_reduce_fusion.1 = (f32[40,1040]{1,0:T(8,128)S(1)}, f32[8,40,1040]{2,1,0:T(8,128)S(1)}) fusion(f32[8,40,1040]{2,1,0:T(8,128)S(1)} %copy-done.15, f32[8,40,1040]{2,1,0:T(8,128)S(1)} %get-tuple-element.24, f32[8,40,1040]{2,1,0:T(8,128)S(1)} %get-tuple-element.56, f32[8,40,1040]{2,1,0:T(8,128)S(1)} %get-tuple-element.57, ...), kind=kLoop, calls=%fused_computation.158 | loop fusion | flops 6281600 | bytes 13520000 | tf_op jit(solution)/shard_map/transpose(jvp())/reduce_sum | solution.py:49
  123.7 2.7 %multiply_reduce_fusion = (f32[40,1040]{1,0:T(8,128)S(1)}, f32[8,40,1040]{2,1,0:T(8,128)S(1)}) fusion(f32[8,40,1040]{2,1,0:T(8,128)S(1)} %copy-done.14, f32[8,40,1040]{2,1,0:T(8,128)S(1)} %copy-done.1, f32[8,40,1040]{2,1,0:T(8,128)S(1)} %get-tuple-element.45, f32[8,40,1040]{2,1,0:T(8,128)S(1)} %get-tuple-element.44, ...), kind=kLoop, calls=%fused_computation.155 | loop fusion | flops 6281600 | bytes 13520000 | tf_op jit(solution)/shard_map/transpose(jvp())/reduce_sum | solution.py:49
  128.3 3.6 %multiply_reduce_fusion.2 = (f32[40,1040]{1,0:T(8,128)S(1)}, f32[40,1040]{1,0:T(8,128)S(1)}) fusion(f32[8,32,1040]{2,1,0:T(8,128)S(1)} %slice_dynamic-update-slice_fusion, pred[40,1040]{1,0:T(8,128)(4,1)S(1)} %and_and_fusion, f32[8,40,1040]{2,1,0:T(8,128)S(1)} %copy-done.16, f32[8,40,1040]{2,1,0:T(8,128)S(1)} %copy-done.3, ...), kind=kLoop, calls=%fused_computation.161 | loop fusion | flops 9235200 | bytes 20076160 | tf_op jit(solution)/shard_map/transpose(jvp())/reduce_sum | solution.py:49
  131.9 5.5 %collective-permute-start.6 = (f32[4,1040]{1,0:T(4,128)S(1)}, f32[4,1040]{1,0:T(4,128)S(1)}, u32[]{:S(2)}, u32[]{:S(2)}) collective-permute-start(f32[4,1040]{1,0:T(4,128)S(1)} %get-tuple-element.66), channel_id=1, source_target_pairs={{8,0},{16,8},{24,16},{32,24},{40,32},{48,40},{56,48},{64,56},{72,6... | collective-permute-start | bytes 49928 | tf_op jit(solution)/shard_map/transpose(jvp())/ppermute | solution.py:20
  137.5 1.9 %collective-permute-start.7 = (f32[4,1040]{1,0:T(4,128)S(1)}, f32[4,1040]{1,0:T(4,128)S(1)}, u32[]{:S(2)}, u32[]{:S(2)}) collective-permute-start(f32[4,1040]{1,0:T(4,128)S(1)} %get-tuple-element.67), channel_id=1, source_target_pairs={{0,8},{8,16},{16,24},{24,32},{32,40},{40,48},{48,56},{56,64},{64,7... | collective-permute-start | bytes 49928 | tf_op jit(solution)/shard_map/transpose(jvp())/ppermute | solution.py:22
  139.4 7.4 %collective-permute-done.7 = f32[4,1040]{1,0:T(4,128)S(1)} collective-permute-done((f32[4,1040]{1,0:T(4,128)S(1)}, f32[4,1040]{1,0:T(4,128)S(1)}, u32[]{:S(2)}, u32[]{:S(2)}) %collective-permute-start.7) | collective-permute-done | bytes 16672 | tf_op jit(solution)/shard_map/transpose(jvp())/ppermute | solution.py:22
  147.0 1.1 broadcast_in_dim.33
  148.1 5.9 %all-to-all-start.4 = ((f32[8,32,1024]{2,1,0:T(8,128)}), f32[8,32,1024]{2,1,0:T(8,128)S(1)}, u32[]{:S(2)}, u32[]{:S(2)}) async-start(f32[8,32,1024]{2,1,0:T(8,128)} %broadcast_in_dim.33), calls=%async_computation.4 | async-start | bytes 2097152 | tf_op jit(solution)/shard_map/all_to_all | solution.py:116
  154.0 2.3 %copy.12 = f32[1,8,4,8,1024]{4,3,1,2,0:T(8,128)} copy(f32[1,8,4,8,1024]{4,3,2,1,0:T(8,128)} %bitcast.61) | data formatting | bytes 2097152 | tf_op jit(solution)/shard_map/all_to_all | solution.py:113
  156.3 7.7 %all-to-all-done.4 = f32[8,32,1024]{2,1,0:T(8,128)S(1)} async-done(((f32[8,32,1024]{2,1,0:T(8,128)}), f32[8,32,1024]{2,1,0:T(8,128)S(1)}, u32[]{:S(2)}, u32[]{:S(2)}) %all-to-all-start.4) | async-done | bytes 1048608 | tf_op jit(solution)/shard_map/all_to_all | solution.py:116
  (118 shorter events, 39.5 us)
Async XLA Ops:
  0.6 21.7 %copy-start.11 = (f32[1,32,8192]{2,1,0:T(8,128)S(1)}, f32[1,32,8192]{2,1,0:T(8,128)}, u32[]{:S(2)}) copy-start(f32[1,32,8192]{2,1,0:T(8,128)} %param.7) | copy-start | bytes 3145732
  1.6 41.5 %collective-permute-start.2 = (f32[4,1040]{1,0:T(4,128)S(1)}, f32[4,1040]{1,0:T(4,128)S(1)}, u32[]{:S(2)}, u32[]{:S(2)}) collective-permute-start(f32[4,1040]{1,0:T(4,128)S(1)} %get-tuple-element.60), channel_id=1, source_target_pairs={{0,8},{8,16},{16,24},{24,32},{32,40},{40,48},{48,56},{56,64},{64,7... | collective-permute-start | bytes 49928 | tf_op jit(solution)/shard_map/jvp()/ppermute | solution.py:20
  3.6 40.6 %collective-permute-start.3 = (f32[4,1040]{1,0:T(4,128)S(1)}, f32[4,1040]{1,0:T(4,128)S(1)}, u32[]{:S(2)}, u32[]{:S(2)}) collective-permute-start(f32[4,1040]{1,0:T(4,128)S(1)} %get-tuple-element.61), channel_id=1, source_target_pairs={{8,0},{16,8},{24,16},{32,24},{40,32},{48,40},{56,48},{64,56},{72,6... | collective-permute-start | bytes 49928 | tf_op jit(solution)/shard_map/jvp()/ppermute | solution.py:22
  12.5 33.0 %collective-permute-start.4 = (f32[2,4,1040]{2,1,0:T(4,128)S(1)}, f32[2,4,1040]{2,1,0:T(4,128)S(1)}, u32[]{:S(2)}, u32[]{:S(2)}) collective-permute-start(f32[2,4,1040]{2,1,0:T(4,128)S(1)} %get-tuple-element.30), channel_id=1, source_target_pairs={{0,8},{8,16},{16,24},{24,32},{32,40},{40,48},{48,56},{56,64},{64,7... | collective-permute-start | bytes 99848 | tf_op jit(solution)/shard_map/ppermute | solution.py:20
  14.4 31.1 %collective-permute-start.5 = (f32[2,4,1040]{2,1,0:T(4,128)S(1)}, f32[2,4,1040]{2,1,0:T(4,128)S(1)}, u32[]{:S(2)}, u32[]{:S(2)}) collective-permute-start(f32[2,4,1040]{2,1,0:T(4,128)S(1)} %get-tuple-element.31), channel_id=1, source_target_pairs={{8,0},{16,8},{24,16},{32,24},{40,32},{48,40},{56,48},{64,56},{72,6... | collective-permute-start | bytes 99848 | tf_op jit(solution)/shard_map/ppermute | solution.py:22
  28.4 6.1 %copy-start.18 = (f32[32,8192]{1,0:T(8,128)S(1)}, f32[32,8192]{1,0:T(8,128)}, u32[]{:S(2)}) copy-start(f32[32,8192]{1,0:T(8,128)} %param.8) | copy-start | bytes 3145732
  28.4 17.1 %all-to-all-start.1 = ((f32[8,32,1040]{2,1,0:T(8,128)}), f32[8,32,1040]{2,1,0:T(8,128)S(1)}, u32[]{:S(2)}, u32[]{:S(2)}) async-start(f32[8,32,1040]{2,1,0:T(8,128)} %fusion.109), calls=%async_computation.1 | async-start | bytes 2359296 | tf_op jit(solution)/shard_map/all_to_all | solution.py:79
  34.6 1.3 copy-start.12
  35.9 5.4 %copy-start.13 = (f32[1,32,8192]{2,1,0:T(8,128)S(1)}, f32[1,32,8192]{2,1,0:T(8,128)}, u32[]{:S(2)}) copy-start(f32[1,32,8192]{2,1,0:T(8,128)} %param.11) | copy-start | bytes 3145732
  45.6 18.3 %copy-start.4 = (f32[8,32,1040]{2,1,0:T(8,128)}, f32[8,32,1040]{2,1,0:T(8,128)S(1)}, u32[]{:S(2)}) copy-start(f32[8,32,1040]{2,1,0:T(8,128)S(1)} %all-to-all-done.1) | copy-start | bytes 3194884
  45.6 37.8 %all-to-all-start = ((f32[8,32,1040]{2,1,0:T(8,128)}), f32[8,32,1040]{2,1,0:T(8,128)}, u32[]{:S(2)}, u32[]{:S(2)}) async-start(f32[8,32,1040]{2,1,0:T(8,128)} %fusion.105), calls=%async_computation | async-start | bytes 2359296 | tf_op jit(solution)/shard_map/all_to_all | solution.py:79
  51.4 10.8 %collective-permute-start = (f32[8,4,1040]{2,1,0:T(4,128)S(1)}, f32[8,4,1040]{2,1,0:T(4,128)S(1)}, u32[]{:S(2)}, u32[]{:S(2)}) collective-permute-start(f32[8,4,1040]{2,1,0:T(4,128)S(1)} %get-tuple-element.58), channel_id=1, source_target_pairs={{0,8},{8,16},{16,24},{24,32},{32,40},{40,48},{48,56},{56,64},{64,7... | collective-permute-start | bytes 399368 | tf_op jit(solution)/shard_map/ppermute | solution.py:20
  53.3 10.6 %collective-permute-start.1 = (f32[8,4,1040]{2,1,0:T(4,128)S(1)}, f32[8,4,1040]{2,1,0:T(4,128)S(1)}, u32[]{:S(2)}, u32[]{:S(2)}) collective-permute-start(f32[8,4,1040]{2,1,0:T(4,128)S(1)} %get-tuple-element.59), channel_id=1, source_target_pairs={{8,0},{16,8},{24,16},{32,24},{40,32},{48,40},{56,48},{64,56},{72,6... | collective-permute-start | bytes 399368 | tf_op jit(solution)/shard_map/ppermute | solution.py:22
  61.2 11.9 %copy-start.9 = (f32[40,1040]{1,0:T(8,128)}, f32[40,1040]{1,0:T(8,128)S(1)}, u32[]{:S(2)}) copy-start(f32[40,1040]{1,0:T(8,128)S(1)} %get-tuple-element.64) | copy-start | bytes 499204
  61.2 19.2 %copy-start.5 = (f32[40,1040]{1,0:T(8,128)}, f32[40,1040]{1,0:T(8,128)S(1)}, u32[]{:S(2)}) copy-start(f32[40,1040]{1,0:T(8,128)S(1)} %get-tuple-element.63) | copy-start | bytes 499204
  61.2 19.2 %copy-start.7 = (f32[40,1040]{1,0:T(8,128)}, f32[40,1040]{1,0:T(8,128)S(1)}, u32[]{:S(2)}) copy-start(f32[40,1040]{1,0:T(8,128)S(1)} %get-tuple-element.65) | copy-start | bytes 499204
  72.5 1.2 copy-start
  83.4 22.4 %all-to-all-start.3 = ((f32[8,32,1040]{2,1,0:T(8,128)}), f32[8,32,1040]{2,1,0:T(8,128)}, u32[]{:S(2)}, u32[]{:S(2)}) async-start(f32[8,32,1040]{2,1,0:T(8,128)} %copy-done.20), calls=%async_computation.3 | async-start | bytes 2359296 | tf_op jit(solution)/shard_map/all_to_all | solution.py:79
  91.2 4.3 %copy-start.21 = (f32[32,8192]{1,0:T(8,128)S(1)}, f32[32,8192]{1,0:T(8,128)}, u32[]{:S(2)}) copy-start(f32[32,8192]{1,0:T(8,128)} %param.6) | copy-start | bytes 3145732
  105.9 41.1 %all-to-all-start.2 = ((f32[8,32,1024]{2,1,0:T(8,128)}), f32[8,32,1024]{2,1,0:T(8,128)}, u32[]{:S(2)}, u32[]{:S(2)}) async-start(f32[8,32,1024]{2,1,0:T(8,128)} %slice.472), calls=%async_computation.2 | async-start | bytes 2097152 | tf_op jit(solution)/shard_map/all_to_all | solution.py:113
  114.7 3.0 %copy-start.6 = (f32[40,1040]{1,0:T(8,128)S(1)}, f32[40,1040]{1,0:T(8,128)}, u32[]{:S(2)}) copy-start(f32[40,1040]{1,0:T(8,128)} %copy-done.5) | copy-start | bytes 499204
  114.7 3.0 %copy-start.8 = (f32[40,1040]{1,0:T(8,128)S(1)}, f32[40,1040]{1,0:T(8,128)}, u32[]{:S(2)}) copy-start(f32[40,1040]{1,0:T(8,128)} %copy-done.7) | copy-start | bytes 499204
  114.7 3.0 %copy-start.10 = (f32[40,1040]{1,0:T(8,128)S(1)}, f32[40,1040]{1,0:T(8,128)}, u32[]{:S(2)}) copy-start(f32[40,1040]{1,0:T(8,128)} %copy-done.9) | copy-start | bytes 499204
  114.7 3.0 %copy-start.19 = (f32[40,1040]{1,0:T(8,128)S(1)}, f32[40,1040]{1,0:T(8,128)}, u32[]{:S(2)}) copy-start(f32[40,1040]{1,0:T(8,128)} %get-tuple-element.68) | copy-start | bytes 499204
  117.8 1.4 copy-start.15
  121.9 1.4 copy-start.1
  121.9 1.8 %copy-start.14 = (f32[8,40,1040]{2,1,0:T(8,128)S(1)}, f32[8,40,1040]{2,1,0:T(8,128)}, u32[]{:S(2)}) copy-start(f32[8,40,1040]{2,1,0:T(8,128)} %get-tuple-element.27) | copy-start | bytes 3993604
  126.4 1.4 copy-start.3
  126.5 1.8 %copy-start.16 = (f32[8,40,1040]{2,1,0:T(8,128)S(1)}, f32[8,40,1040]{2,1,0:T(8,128)}, u32[]{:S(2)}) copy-start(f32[8,40,1040]{2,1,0:T(8,128)} %get-tuple-element.29) | copy-start | bytes 3993604
  131.9 7.5 %collective-permute-start.6 = (f32[4,1040]{1,0:T(4,128)S(1)}, f32[4,1040]{1,0:T(4,128)S(1)}, u32[]{:S(2)}, u32[]{:S(2)}) collective-permute-start(f32[4,1040]{1,0:T(4,128)S(1)} %get-tuple-element.66), channel_id=1, source_target_pairs={{8,0},{16,8},{24,16},{32,24},{40,32},{48,40},{56,48},{64,56},{72,6... | collective-permute-start | bytes 49928 | tf_op jit(solution)/shard_map/transpose(jvp())/ppermute | solution.py:20
  137.5 9.4 %collective-permute-start.7 = (f32[4,1040]{1,0:T(4,128)S(1)}, f32[4,1040]{1,0:T(4,128)S(1)}, u32[]{:S(2)}, u32[]{:S(2)}) collective-permute-start(f32[4,1040]{1,0:T(4,128)S(1)} %get-tuple-element.67), channel_id=1, source_target_pairs={{0,8},{8,16},{16,24},{24,32},{32,40},{40,48},{48,56},{56,64},{64,7... | collective-permute-start | bytes 49928 | tf_op jit(solution)/shard_map/transpose(jvp())/ppermute | solution.py:22
  148.1 15.9 %all-to-all-start.4 = ((f32[8,32,1024]{2,1,0:T(8,128)}), f32[8,32,1024]{2,1,0:T(8,128)S(1)}, u32[]{:S(2)}, u32[]{:S(2)}) async-start(f32[8,32,1024]{2,1,0:T(8,128)} %broadcast_in_dim.33), calls=%async_computation.4 | async-start | bytes 2097152 | tf_op jit(solution)/shard_map/all_to_all | solution.py:116
  (3 other events, 3.2 us)

commit v3 on v2

--- a/solution.py
+++ b/solution.py
@@ -1,6 +1,7 @@
 import jax
 import jax.numpy as jnp
 from jax import lax
+from jax.experimental import pallas as pl
 from jax.sharding import PartitionSpec as P
 
 STEPS = 4
@@ -64,6 +65,35 @@
     return lax.dynamic_slice_in_dim(pad_cols(x), start, width, axis=x.ndim - 1)
 
 
+def scan_kernel(fine_ref, old_ref, gain_ref, target_ref, begin_ref, ends_ref, adjoint_ref):
+    slabs = fine_ref.shape[0]
+    begin = begin_ref[...]
+    for slab in range(slabs):
+        carried = fine_ref[slab] - gain_ref[slab] * old_ref[slab]
+        begin = gain_ref[slab] * begin + carried
+        ends_ref[slab] = begin
+    adjoint = ends_ref[slabs - 1] - target_ref[slabs - 1]
+    adjoint_ref[slabs - 1] = adjoint
+    for slab in range(slabs - 2, -1, -1):
+        adjoint = (ends_ref[slab] - target_ref[slab]) + gain_ref[slab + 1] * adjoint
+        adjoint_ref[slab] = adjoint
+
+
+def scans(fine_ends, old, gain, target, begin):
+    slabs, rows, wide = fine_ends.shape
+    tile = 8
+    stacked = pl.BlockSpec((slabs, tile, wide), lambda i: (0, i, 0))
+    single = pl.BlockSpec((tile, wide), lambda i: (i, 0))
+    shape = jax.ShapeDtypeStruct(fine_ends.shape, fine_ends.dtype)
+    return pl.pallas_call(
+        scan_kernel,
+        grid=(rows // tile,),
+        in_specs=[stacked, stacked, stacked, stacked, single],
+        out_specs=[stacked, stacked],
+        out_shape=[shape, shape],
+    )(fine_ends, old, gain, target, begin)
+
+
 def on_device(start_state, old_starts, conductivity, velocity, coarse_gain, targets):
     blocks = lax.axis_size("tm")
     block = lax.axis_index("tm")
@@ -72,8 +102,10 @@
     wide = width + 2 * HALO
 
     def send_windows(x):
-        padded = pad_cols(x)
-        return jnp.stack([padded[:, k * width : k * width + wide] for k in range(blocks)])
+        main = x.reshape(rows, blocks, width).transpose(1, 0, 2)
+        left = jnp.pad(main[:-1, :, width - HALO :], ((1, 0), (0, 0), (0, 0)))
+        right = jnp.pad(main[1:, :, :HALO], ((0, 1), (0, 0), (0, 0)))
+        return jnp.concatenate([left, main, right], axis=2)
 
     def to_blocks(x):
         return lax.all_to_all(send_windows(x), "tm", 0, 0, tiled=True)
@@ -96,17 +128,7 @@
     fine_ends, pullback = jax.vjp(
         lambda k: fine(old_rows, k, flow_rows[0], flow_rows[1], inside), kappa
     )
-    carried = fine_ends - gain * old
-    ends = []
-    for slab in range(blocks):
-        begin = gain[slab] * begin + carried[slab]
-        ends.append(begin)
-    new_ends = jnp.stack(ends)
-    misfit = new_ends - target
-    adjoints = [misfit[blocks - 1]]
-    for slab in range(blocks - 2, -1, -1):
-        adjoints.insert(0, misfit[slab] + gain[slab + 1] * adjoints[0])
-    adjoint = jnp.stack(adjoints)
+    new_ends, adjoint = scans(fine_ends, old, gain, target, begin)
     (grad_window,) = pullback(adjoint)
 
     interior = new_ends[:, :, HALO : HALO + width]

time: 166 us -> 160 us (0.964)
  other arithmetic: 49.2 us -> 32.3 us
  waiting for transfers between devices: 17.1 us -> 23.4 us
  Pallas kernels: 0 us -> 4.29 us
  local copies, waits for them, and re-layouts: 29.7 us -> 31.5 us
    unnamed x11 -> x0, other arithmetic: 11.3 us -> none
    unnamed x69 -> x62, local copies, waits for them, and re-layouts: 18.5 us -> 8.27 us
    all_to_all x3, waiting for transfers between devices: 0.01 us -> 6.45 us  [to_blocks(): return lax.all_to_all(send_windows(x), 'tm', 0, 0, tiled=True)]
    sub x2 -> x0, other arithmetic: 6.07 us -> none  [the longest x1 4.33 us: on_device(): carried = fine_ends - gain * old]
    concatenate x0 -> x3, local copies, waits for them, and re-layouts: none -> 5.87 us  [send_windows(): return jnp.concatenate([left, main, right], axis=2)]
    pallas_call x0 -> x1, Pallas kernels: none -> 4.29 us  [scans(): pl.pallas_call(scan_kernel, grid=(rows // tile,), in_specs=[stacked, stac...]
    pad x0 -> x6, local copies, waits for them, and re-layouts: none -> 2.7 us  [the longest x3 1.36 us: send_windows(): left = jnp.pad(main[:-1, :, width - HALO:], ((1, 0), (0, 0), (0, 0)))]
    add x1, other arithmetic: 2.95 us -> 0.85 us  [advance(): jnp.maximum(along_rows, 0.0) * (centre - wide[:, :-2, 1:-1])]
  transfers between devices with their start and end apart: 13 -> 13, of which waited for: 4 -> 5; matrix products, arithmetic and copies ran while one was open for 42% -> 33% of each run, Pallas kernels for 0% -> 0%
where the time goes in v3:
time: 160 us; the launch traced here: 159 us
  starting transfers between devices  66.4 us (42%)
  other arithmetic  32.3 us (20%)
  local copies, waits for them, and re-layouts  31.5 us (20%)
  waiting for transfers between devices  23.4 us (15%)
  Pallas kernels  4.29 us (3%)
    ppermute x4, starting transfers between devices, with_halo(): lax.ppermute(head, axis, [((i + 1) % count, i) for i in range(ends)])  25.7 us
    all_to_all x3, starting transfers between devices, to_blocks(): return lax.all_to_all(send_windows(x), 'tm', 0, 0, tiled=True)  18.2 us
    select_n x4, other arithmetic, fine(): jnp.where(inside, advance(field, kappa, along_rows, along_cols), 0.0)  12.1 us
    ppermute x4, starting transfers between devices, with_halo(): lax.ppermute(tail, axis, [(i, (i + 1) % count) for i in range(ends)])  12 us
    reduce_sum x3, other arithmetic, advance(): return centre + time_step * (kappa * spread - transport)  8.98 us
    unnamed x62, local copies, waits for them, and re-layouts  8.27 us
    ppermute x4, waiting for transfers between devices, with_halo(): lax.ppermute(head, axis, [((i + 1) % count, i) for i in range(ends)])  7.76 us
    all_to_all x1, waiting for transfers between devices, on_device(): gradient = lax.all_to_all(copies, 'tm', 0, 2, tiled=True)[0]  7.73 us
  transfers between devices with their start and end apart: 13, of which 5 were waited for; matrix products, arithmetic and copies ran while one was open for 33% of the time, Pallas kernels for 0%

profile of v3, /device:TPU:160, one launch (start us, length us, event | category | flops | bytes accessed | tf_op | source)
XLA Modules:
  0.0 159.2 jit_solution(14108383063688180437)
XLA Ops:
  0.6 1.6 %pad_dynamic-slice_fusion.5 = (f32[4,1040]{1,0:T(4,128)}, f32[4,1040]{1,0:T(4,128)}) fusion(s32[]{:T(128)S(6)} %add.269, s32[]{:T(128)S(6)} %select_n.31, f32[32,8192]{1,0:T(8,128)} %param.8), kind=kLoop, calls=%fused_computation.193 | loop fusion | bytes 1081864 | tf_op jit(solution)/shard_map/jvp()/slice | solution.py:18
  2.3 1.9 %collective-permute-start.2 = (f32[4,1040]{1,0:T(4,128)}, f32[4,1040]{1,0:T(4,128)}, u32[]{:S(2)}, u32[]{:S(2)}) collective-permute-start(f32[4,1040]{1,0:T(4,128)} %get-tuple-element.56), channel_id=1, source_target_pairs={{0,8},{8,16},{16,24},{24,32},{32,40},{40,48},{48,56},{56,64},{64,7... | collective-permute-start | bytes 49928 | tf_op jit(solution)/shard_map/jvp()/ppermute | solution.py:21
  4.2 7.9 %collective-permute-start.3 = (f32[4,1040]{1,0:T(4,128)}, f32[4,1040]{1,0:T(4,128)}, u32[]{:S(2)}, u32[]{:S(2)}) collective-permute-start(f32[4,1040]{1,0:T(4,128)} %get-tuple-element.57), channel_id=1, source_target_pairs={{8,0},{16,8},{24,16},{32,24},{40,32},{48,40},{56,48},{64,56},{72,6... | collective-permute-start | bytes 49928 | tf_op jit(solution)/shard_map/jvp()/ppermute | solution.py:23
  12.0 1.7 %pad_dynamic-slice_fusion.1 = (f32[2,4,1040]{2,1,0:T(4,128)}, f32[2,4,1040]{2,1,0:T(4,128)}) fusion(s32[]{:T(128)S(6)} %add.269, s32[]{:T(128)S(6)} %select_n.31, f32[2,32,8192]{2,1,0:T(8,128)} %param.9), kind=kLoop, calls=%fused_computation.28 | loop fusion | bytes 2163720 | tf_op jit(solution)/shard_map/slice | solution.py:18
  13.7 1.9 %collective-permute-start.4 = (f32[2,4,1040]{2,1,0:T(4,128)}, f32[2,4,1040]{2,1,0:T(4,128)S(1)}, u32[]{:S(2)}, u32[]{:S(2)}) collective-permute-start(f32[2,4,1040]{2,1,0:T(4,128)} %get-tuple-element.22), channel_id=1, source_target_pairs={{0,8},{8,16},{16,24},{24,32},{32,40},{40,48},{48,56},{56,64},{64,7... | collective-permute-start | bytes 99848 | tf_op jit(solution)/shard_map/ppermute | solution.py:21
  15.6 7.9 %collective-permute-start.5 = (f32[2,4,1040]{2,1,0:T(4,128)}, f32[2,4,1040]{2,1,0:T(4,128)}, u32[]{:S(2)}, u32[]{:S(2)}) collective-permute-start(f32[2,4,1040]{2,1,0:T(4,128)} %get-tuple-element.23), channel_id=1, source_target_pairs={{8,0},{16,8},{24,16},{32,24},{40,32},{48,40},{56,48},{64,56},{72,6... | collective-permute-start | bytes 99848 | tf_op jit(solution)/shard_map/ppermute | solution.py:23
  26.3 6.1 %all-to-all-start = ((f32[8,32,1040]{2,1,0:T(8,128)}), f32[8,32,1040]{2,1,0:T(8,128)S(1)}, u32[]{:S(2)}, u32[]{:S(2)}) async-start(f32[8,32,1040]{2,1,0:T(8,128)} %concatenate.18), calls=%async_computation | async-start | bytes 2359296 | tf_op jit(solution)/shard_map/all_to_all | solution.py:111
  41.2 2.2 %concatenate.22 = f32[8,32,1040]{2,1,0:T(8,128)} concatenate(f32[8,32,8]{2,1,0:T(8,128)} %pad.165, f32[8,32,1024]{2,1,0:T(8,128)S(1)} %bitcast.40, f32[8,32,8]{2,1,0:T(8,128)} %pad.166), dimensions={2} | concatenate | bytes 2129920 | tf_op jit(solution)/shard_map/concatenate | solution.py:108
  43.4 2.3 %concatenate.23 = f32[8,32,1040]{2,1,0:T(8,128)} concatenate(f32[8,32,8]{2,1,0:T(8,128)} %pad.167, f32[8,32,1024]{2,1,0:T(8,128)S(1)} %bitcast.42, f32[8,32,8]{2,1,0:T(8,128)} %pad.168), dimensions={2} | concatenate | bytes 2129920 | tf_op jit(solution)/shard_map/concatenate | solution.py:108
  48.7 5.7 %all-to-all-start.1 = ((f32[8,32,1040]{2,1,0:T(8,128)}), f32[8,32,1040]{2,1,0:T(8,128)}, u32[]{:S(2)}, u32[]{:S(2)}) async-start(f32[8,32,1040]{2,1,0:T(8,128)} %concatenate.22), calls=%async_computation.1 | async-start | bytes 2359296 | tf_op jit(solution)/shard_map/all_to_all | solution.py:111
  54.5 1.9 %collective-permute-start = (f32[8,4,1040]{2,1,0:T(4,128)S(1)}, f32[8,4,1040]{2,1,0:T(4,128)S(1)}, u32[]{:S(2)}, u32[]{:S(2)}) collective-permute-start(f32[8,4,1040]{2,1,0:T(4,128)S(1)} %get-tuple-element.50), channel_id=1, source_target_pairs={{0,8},{8,16},{16,24},{24,32},{32,40},{40,48},{48,56},{56,64},{64,7... | collective-permute-start | bytes 399368 | tf_op jit(solution)/shard_map/ppermute | solution.py:21
  56.4 8.0 %collective-permute-start.1 = (f32[8,4,1040]{2,1,0:T(4,128)S(1)}, f32[8,4,1040]{2,1,0:T(4,128)S(1)}, u32[]{:S(2)}, u32[]{:S(2)}) collective-permute-start(f32[8,4,1040]{2,1,0:T(4,128)S(1)} %get-tuple-element.51), channel_id=1, source_target_pairs={{8,0},{16,8},{24,16},{32,24},{40,32},{48,40},{56,48},{64,56},{72,6... | collective-permute-start | bytes 399368 | tf_op jit(solution)/shard_map/ppermute | solution.py:23
  67.7 3.4 %fusion.24 = (f32[8,40,1040]{2,1,0:T(8,128)S(1)}, f32[8,40,1040]{2,1,0:T(8,128)}) fusion(f32[8,40,1040]{2,1,0:T(8,128)S(1)} %pad_maximum_fusion, f32[40,1040]{1,0:T(8,128)S(1)} %get-tuple-element.62, f32[40,1040]{1,0:T(8,128)S(1)} %get-tuple-element.63, f32[40,1040]{1,0:T(8,128)S(1)} %get-tuple-element.61, f32[40,1040]{1,0:T(8,128)S(1)} %get-tuple-element.60, ...), kind=kLoop, calls=%fused_computation.60 | loop fusion | flops 6988800 | bytes 11523200 | tf_op jit(solution)/shard_map/jvp(jit(_where))/select_n | solution.py:56
  72.3 3.4 %fusion.39 = (f32[8,40,1040]{2,1,0:T(8,128)S(1)}, f32[8,40,1040]{2,1,0:T(8,128)}) fusion(f32[8,40,1040]{2,1,0:T(8,128)S(1)} %get-tuple-element.20, f32[40,1040]{1,0:T(8,128)S(1)} %get-tuple-element.62, f32[40,1040]{1,0:T(8,128)S(1)} %get-tuple-element.63, f32[40,1040]{1,0:T(8,128)S(1)} %get-tuple-element.61, f32[40,1040]{1,0:T(8,128)S(1)} %get-tuple-element.60, ...), kind=kLoop, calls=%fused_computation.75 | loop fusion | flops 6988800 | bytes 11523200 | tf_op jit(solution)/shard_map/jvp(jit(_where))/select_n | solution.py:56
  76.9 3.4 %fusion.55 = (f32[8,40,1040]{2,1,0:T(8,128)S(1)}, f32[8,40,1040]{2,1,0:T(8,128)}) fusion(f32[8,40,1040]{2,1,0:T(8,128)S(1)} %get-tuple-element.18, f32[40,1040]{1,0:T(8,128)S(1)} %get-tuple-element.62, f32[40,1040]{1,0:T(8,128)S(1)} %get-tuple-element.63, f32[40,1040]{1,0:T(8,128)S(1)} %get-tuple-element.61, f32[40,1040]{1,0:T(8,128)S(1)} %get-tuple-element.60, ...), kind=kLoop, calls=%fused_computation.91 | loop fusion | flops 6988800 | bytes 11523200 | tf_op jit(solution)/shard_map/jvp(jit(_where))/select_n | solution.py:56
  80.8 6.4 %all-to-all-start.2 = ((f32[8,32,1040]{2,1,0:T(8,128)}), f32[8,32,1040]{2,1,0:T(8,128)}, u32[]{:S(2)}, u32[]{:S(2)}) async-start(f32[8,32,1040]{2,1,0:T(8,128)} %concatenate.23), calls=%async_computation.2 | async-start | bytes 2359296 | tf_op jit(solution)/shard_map/all_to_all | solution.py:111
  87.2 1.6 fusion.84
  89.8 1.8 %fusion.97.fine_ref = f32[8,32,1040]{2,1,0:T(8,128)} fusion(f32[8,40,1040]{2,1,0:T(8,128)S(1)} %get-tuple-element.16, f32[8,40,1040]{2,1,0:T(8,128)S(1)} %fusion.84, f32[8,40,1040]{2,1,0:T(8,128)S(1)} %get-tuple-element.39, f32[8,40,1040]{2,1,0:T(8,128)S(1)} %get-tuple-element.40, f32[8,40,1040]{2,1,0:T(8,128)S(1)} %get-tuple-element.38, ...), kind=kLoop, calls=%fused_computation.181 | loop fusion | flops 2129920 | bytes 6689280 | tf_op jit(solution)/shard_map/jvp(jit(_where))/select_n | solution.py:56
  91.6 6.4 %all-to-all-done.2.target_ref = f32[8,32,1040]{2,1,0:T(8,128)} async-done(((f32[8,32,1040]{2,1,0:T(8,128)}), f32[8,32,1040]{2,1,0:T(8,128)}, u32[]{:S(2)}, u32[]{:S(2)}) %all-to-all-start.2) | async-done | bytes 1064992 | tf_op jit(solution)/shard_map/all_to_all | solution.py:111
  98.1 4.3 %shard_map.77 = (f32[8,32,1040]{2,1,0:T(8,128)}, f32[8,32,1040]{2,1,0:T(8,128)}) custom-call(f32[8,32,1040]{2,1,0:T(8,128)} %fusion.97.fine_ref, f32[8,32,1040]{2,1,0:T(8,128)} %copy-done.4, f32[8,32,1040]{2,1,0:T(8,128)} %all-to-all-done.1.gain_ref, f32[8,32,1040]{2,1,0:T(8,128)} %all-to-all-done.2.target_ref, f32[32,1040]{1,0:T(8,128)} %pad_dynamic-slice_fusion.3.begin_ref), custom_call_target="tpu_custom_call" | custom-call | tf_op jit(solution)/shard_map/pallas_call | solution.py:88
  102.4 2.6 %slice.217 = f32[8,32,1024]{2,1,0:T(8,128)} slice(f32[8,32,1040]{2,1,0:T(8,128)} %get-tuple-element.4), slice={[0:8], [0:32], [8:1032]} | slice | bytes 2097152 | tf_op jit(solution)/shard_map/slice | solution.py:134
  104.9 4.7 %all-to-all-start.3 = ((f32[8,32,1024]{2,1,0:T(8,128)}), f32[8,32,1024]{2,1,0:T(8,128)}, u32[]{:S(2)}, u32[]{:S(2)}) async-start(f32[8,32,1024]{2,1,0:T(8,128)} %slice.217), calls=%async_computation.3 | async-start | bytes 2097152 | tf_op jit(solution)/shard_map/all_to_all | solution.py:135
  109.7 2.4 %fusion.96 = (f32[8,40,1040]{2,1,0:T(8,128)S(1)}, f32[8,40,1040]{2,1,0:T(8,128)S(1)}, f32[8,40,1040]{2,1,0:T(8,128)S(1)}, f32[8,40,1040]{2,1,0:T(8,128)S(1)}, f3...) fusion(f32[8,32,1040]{2,1,0:T(8,128)} %get-tuple-element.5, ...), kind=kLoop, calls=%fused_computation.179 | loop fusion | flops 5990400 | bytes 11256960 | tf_op jit(solution)/shard_map/transpose(jvp())/mul | solution.py:48
  112.2 2.7 %multiply_reduce_fusion.1 = (f32[40,1040]{1,0:T(8,128)S(1)}, f32[8,40,1040]{2,1,0:T(8,128)S(1)}) fusion(f32[8,40,1040]{2,1,0:T(8,128)S(1)} %copy-done.15, f32[8,40,1040]{2,1,0:T(8,128)S(1)} %get-tuple-element.16, f32[8,40,1040]{2,1,0:T(8,128)S(1)} %get-tuple-element.48, f32[8,40,1040]{2,1,0:T(8,128)S(1)} %get-tuple-element.49, ...), kind=kLoop, calls=%fused_computation.158 | loop fusion | flops 6281600 | bytes 13520000 | tf_op jit(solution)/shard_map/transpose(jvp())/reduce_sum | solution.py:50
  116.8 2.8 %multiply_reduce_fusion = (f32[40,1040]{1,0:T(8,128)S(1)}, f32[8,40,1040]{2,1,0:T(8,128)S(1)}) fusion(f32[8,40,1040]{2,1,0:T(8,128)S(1)} %copy-done.14, f32[8,40,1040]{2,1,0:T(8,128)S(1)} %copy-done.1, f32[8,40,1040]{2,1,0:T(8,128)S(1)} %get-tuple-element.37, f32[8,40,1040]{2,1,0:T(8,128)S(1)} %get-tuple-element.36, ...), kind=kLoop, calls=%fused_computation.155 | loop fusion | flops 6281600 | bytes 13520000 | tf_op jit(solution)/shard_map/transpose(jvp())/reduce_sum | solution.py:50
  121.7 3.5 %multiply_reduce_fusion.2 = (f32[40,1040]{1,0:T(8,128)S(1)}, f32[40,1040]{1,0:T(8,128)S(1)}) fusion(f32[8,32,1040]{2,1,0:T(8,128)S(1)} %copy-done.17, pred[40,1040]{1,0:T(8,128)(4,1)S(1)} %and_and_fusion, f32[8,40,1040]{2,1,0:T(8,128)S(1)} %copy-done.16, f32[8,40,1040]{2,1,0:T(8,128)S(1)} %copy-done.3, f32[8,40,1040]{2,1,0:T(8,128)S(1)} %get-tuple-element.35, ...), kind=kLoop, calls=%fused_computation.161 | loop fusion | flops 9235200 | bytes 20076160 | tf_op jit(solution)/shard_map/transpose(jvp())/reduce_sum | solution.py:50
  125.3 6.3 %collective-permute-start.6 = (f32[4,1040]{1,0:T(4,128)S(1)}, f32[4,1040]{1,0:T(4,128)S(1)}, u32[]{:S(2)}, u32[]{:S(2)}) collective-permute-start(f32[4,1040]{1,0:T(4,128)S(1)} %get-tuple-element.64), channel_id=1, source_target_pairs={{8,0},{16,8},{24,16},{32,24},{40,32},{48,40},{56,48},{64,56},{72,6... | collective-permute-start | bytes 49928 | tf_op jit(solution)/shard_map/transpose(jvp())/ppermute | solution.py:21
  131.6 1.9 %collective-permute-start.7 = (f32[4,1040]{1,0:T(4,128)S(1)}, f32[4,1040]{1,0:T(4,128)S(1)}, u32[]{:S(2)}, u32[]{:S(2)}) collective-permute-start(f32[4,1040]{1,0:T(4,128)S(1)} %get-tuple-element.65), channel_id=1, source_target_pairs={{0,8},{8,16},{16,24},{24,32},{32,40},{40,48},{48,56},{56,64},{64,7... | collective-permute-start | bytes 49928 | tf_op jit(solution)/shard_map/transpose(jvp())/ppermute | solution.py:23
  133.5 7.5 %collective-permute-done.7 = f32[4,1040]{1,0:T(4,128)S(1)} collective-permute-done((f32[4,1040]{1,0:T(4,128)S(1)}, f32[4,1040]{1,0:T(4,128)S(1)}, u32[]{:S(2)}, u32[]{:S(2)}) %collective-permute-start.7) | collective-permute-done | bytes 16672 | tf_op jit(solution)/shard_map/transpose(jvp())/ppermute | solution.py:23
  142.3 5.8 %all-to-all-start.4 = ((f32[8,32,1024]{2,1,0:T(8,128)}), f32[8,32,1024]{2,1,0:T(8,128)S(1)}, u32[]{:S(2)}, u32[]{:S(2)}) async-start(f32[8,32,1024]{2,1,0:T(8,128)} %broadcast_in_dim.33), calls=%async_computation.4 | async-start | bytes 2097152 | tf_op jit(solution)/shard_map/all_to_all | solution.py:138
  148.1 2.3 %copy.21 = f32[1,8,4,8,1024]{4,3,1,2,0:T(8,128)} copy(f32[1,8,4,8,1024]{4,3,2,1,0:T(8,128)} %bitcast.13) | data formatting | bytes 2097152 | tf_op jit(solution)/shard_map/all_to_all | solution.py:135
  150.4 7.7 %all-to-all-done.4 = f32[8,32,1024]{2,1,0:T(8,128)S(1)} async-done(((f32[8,32,1024]{2,1,0:T(8,128)}), f32[8,32,1024]{2,1,0:T(8,128)S(1)}, u32[]{:S(2)}, u32[]{:S(2)}) %all-to-all-start.4) | async-done | bytes 1048608 | tf_op jit(solution)/shard_map/all_to_all | solution.py:138
  (111 shorter events, 27.8 us)
Async XLA Ops:
  0.6 22.9 %copy-start.23 = (f32[1,32,8192]{2,1,0:T(8,128)S(1)}, f32[1,32,8192]{2,1,0:T(8,128)}, u32[]{:S(2)}) copy-start(f32[1,32,8192]{2,1,0:T(8,128)} %param.7) | copy-start | bytes 3145732
  2.3 43.4 %collective-permute-start.2 = (f32[4,1040]{1,0:T(4,128)}, f32[4,1040]{1,0:T(4,128)}, u32[]{:S(2)}, u32[]{:S(2)}) collective-permute-start(f32[4,1040]{1,0:T(4,128)} %get-tuple-element.56), channel_id=1, source_target_pairs={{0,8},{8,16},{16,24},{24,32},{32,40},{40,48},{48,56},{56,64},{64,7... | collective-permute-start | bytes 49928 | tf_op jit(solution)/shard_map/jvp()/ppermute | solution.py:21
  4.2 41.5 %collective-permute-start.3 = (f32[4,1040]{1,0:T(4,128)}, f32[4,1040]{1,0:T(4,128)}, u32[]{:S(2)}, u32[]{:S(2)}) collective-permute-start(f32[4,1040]{1,0:T(4,128)} %get-tuple-element.57), channel_id=1, source_target_pairs={{8,0},{16,8},{24,16},{32,24},{40,32},{48,40},{56,48},{64,56},{72,6... | collective-permute-start | bytes 49928 | tf_op jit(solution)/shard_map/jvp()/ppermute | solution.py:23
  13.7 34.2 %collective-permute-start.4 = (f32[2,4,1040]{2,1,0:T(4,128)}, f32[2,4,1040]{2,1,0:T(4,128)S(1)}, u32[]{:S(2)}, u32[]{:S(2)}) collective-permute-start(f32[2,4,1040]{2,1,0:T(4,128)} %get-tuple-element.22), channel_id=1, source_target_pairs={{0,8},{8,16},{16,24},{24,32},{32,40},{40,48},{48,56},{56,64},{64,7... | collective-permute-start | bytes 99848 | tf_op jit(solution)/shard_map/ppermute | solution.py:21
  15.6 32.3 %collective-permute-start.5 = (f32[2,4,1040]{2,1,0:T(4,128)}, f32[2,4,1040]{2,1,0:T(4,128)}, u32[]{:S(2)}, u32[]{:S(2)}) collective-permute-start(f32[2,4,1040]{2,1,0:T(4,128)} %get-tuple-element.23), channel_id=1, source_target_pairs={{8,0},{16,8},{24,16},{32,24},{40,32},{48,40},{56,48},{64,56},{72,6... | collective-permute-start | bytes 99848 | tf_op jit(solution)/shard_map/ppermute | solution.py:23
  26.3 6.1 %copy-start.24 = (f32[1,32,8192]{2,1,0:T(8,128)S(1)}, f32[1,32,8192]{2,1,0:T(8,128)}, u32[]{:S(2)}) copy-start(f32[1,32,8192]{2,1,0:T(8,128)} %param.10) | copy-start | bytes 3145732
  26.3 22.4 %all-to-all-start = ((f32[8,32,1040]{2,1,0:T(8,128)}), f32[8,32,1040]{2,1,0:T(8,128)S(1)}, u32[]{:S(2)}, u32[]{:S(2)}) async-start(f32[8,32,1040]{2,1,0:T(8,128)} %concatenate.18), calls=%async_computation | async-start | bytes 2359296 | tf_op jit(solution)/shard_map/all_to_all | solution.py:111
  34.9 1.9 %copy-start.13 = (f32[2,32,8192]{2,1,0:T(8,128)S(1)}, f32[2,32,8192]{2,1,0:T(8,128)}, u32[]{:S(2)}) copy-start(f32[2,32,8192]{2,1,0:T(8,128)} %param.9) | copy-start | bytes 6291460
  43.4 4.5 %copy-start.22 = (f32[2,32,1040]{2,1,0:T(8,128)S(1)}, f32[2,32,1040]{2,1,0:T(8,128)}, u32[]{:S(2)}) copy-start(f32[2,32,1040]{2,1,0:T(8,128)} %pad_dynamic-slice_fusion.2) | copy-start | bytes 798724
  47.2 24.6 %copy-start.18 = (f32[40,1040]{1,0:T(8,128)}, f32[40,1040]{1,0:T(8,128)S(1)}, u32[]{:S(2)}) copy-start(f32[40,1040]{1,0:T(8,128)S(1)} %get-tuple-element.67) | copy-start | bytes 499204
  48.7 18.3 %copy-start.4 = (f32[8,32,1040]{2,1,0:T(8,128)}, f32[8,32,1040]{2,1,0:T(8,128)S(1)}, u32[]{:S(2)}) copy-start(f32[8,32,1040]{2,1,0:T(8,128)S(1)} %all-to-all-done.old_ref) | copy-start | bytes 3194884
  48.7 32.1 %all-to-all-start.1 = ((f32[8,32,1040]{2,1,0:T(8,128)}), f32[8,32,1040]{2,1,0:T(8,128)}, u32[]{:S(2)}, u32[]{:S(2)}) async-start(f32[8,32,1040]{2,1,0:T(8,128)} %concatenate.22), calls=%async_computation.1 | async-start | bytes 2359296 | tf_op jit(solution)/shard_map/all_to_all | solution.py:111
  54.5 12.3 %collective-permute-start = (f32[8,4,1040]{2,1,0:T(4,128)S(1)}, f32[8,4,1040]{2,1,0:T(4,128)S(1)}, u32[]{:S(2)}, u32[]{:S(2)}) collective-permute-start(f32[8,4,1040]{2,1,0:T(4,128)S(1)} %get-tuple-element.50), channel_id=1, source_target_pairs={{0,8},{8,16},{16,24},{24,32},{32,40},{40,48},{48,56},{56,64},{64,7... | collective-permute-start | bytes 399368 | tf_op jit(solution)/shard_map/ppermute | solution.py:21
  56.4 10.6 %collective-permute-start.1 = (f32[8,4,1040]{2,1,0:T(4,128)S(1)}, f32[8,4,1040]{2,1,0:T(4,128)S(1)}, u32[]{:S(2)}, u32[]{:S(2)}) collective-permute-start(f32[8,4,1040]{2,1,0:T(4,128)S(1)} %get-tuple-element.51), channel_id=1, source_target_pairs={{8,0},{16,8},{24,16},{32,24},{40,32},{48,40},{56,48},{64,56},{72,6... | collective-permute-start | bytes 399368 | tf_op jit(solution)/shard_map/ppermute | solution.py:23
  64.6 11.7 %copy-start.5 = (f32[40,1040]{1,0:T(8,128)}, f32[40,1040]{1,0:T(8,128)S(1)}, u32[]{:S(2)}) copy-start(f32[40,1040]{1,0:T(8,128)S(1)} %get-tuple-element.61) | copy-start | bytes 499204
  64.6 11.7 %copy-start.8 = (f32[40,1040]{1,0:T(8,128)}, f32[40,1040]{1,0:T(8,128)S(1)}, u32[]{:S(2)}) copy-start(f32[40,1040]{1,0:T(8,128)S(1)} %get-tuple-element.63) | copy-start | bytes 499204
  64.6 11.7 %copy-start.11 = (f32[40,1040]{1,0:T(8,128)}, f32[40,1040]{1,0:T(8,128)S(1)}, u32[]{:S(2)}) copy-start(f32[40,1040]{1,0:T(8,128)S(1)} %get-tuple-element.62) | copy-start | bytes 499204
  80.8 17.2 %all-to-all-start.2 = ((f32[8,32,1040]{2,1,0:T(8,128)}), f32[8,32,1040]{2,1,0:T(8,128)}, u32[]{:S(2)}, u32[]{:S(2)}) async-start(f32[8,32,1040]{2,1,0:T(8,128)} %concatenate.23), calls=%async_computation.2 | async-start | bytes 2359296 | tf_op jit(solution)/shard_map/all_to_all | solution.py:111
  87.2 1.6 %copy-start.6 = (f32[40,1040]{1,0:T(8,128)S(1)}, f32[40,1040]{1,0:T(8,128)}, u32[]{:S(2)}) copy-start(f32[40,1040]{1,0:T(8,128)} %copy-done.5) | copy-start | bytes 499204
  87.2 1.6 %copy-start.9 = (f32[40,1040]{1,0:T(8,128)S(1)}, f32[40,1040]{1,0:T(8,128)}, u32[]{:S(2)}) copy-start(f32[40,1040]{1,0:T(8,128)} %copy-done.8) | copy-start | bytes 499204
  104.9 36.3 %all-to-all-start.3 = ((f32[8,32,1024]{2,1,0:T(8,128)}), f32[8,32,1024]{2,1,0:T(8,128)}, u32[]{:S(2)}, u32[]{:S(2)}) async-start(f32[8,32,1024]{2,1,0:T(8,128)} %slice.217), calls=%async_computation.3 | async-start | bytes 2097152 | tf_op jit(solution)/shard_map/all_to_all | solution.py:135
  109.7 2.4 %copy-start.15 = (f32[8,40,1040]{2,1,0:T(8,128)S(1)}, f32[8,40,1040]{2,1,0:T(8,128)}, u32[]{:S(2)}) copy-start(f32[8,40,1040]{2,1,0:T(8,128)} %get-tuple-element.17) | copy-start | bytes 3993604
  112.1 2.8 %copy-start.7 = (f32[40,1040]{1,0:T(8,128)S(1)}, f32[40,1040]{1,0:T(8,128)}, u32[]{:S(2)}) copy-start(f32[40,1040]{1,0:T(8,128)} %copy-done.5) | copy-start | bytes 499204
  112.1 2.8 %copy-start.10 = (f32[40,1040]{1,0:T(8,128)S(1)}, f32[40,1040]{1,0:T(8,128)}, u32[]{:S(2)}) copy-start(f32[40,1040]{1,0:T(8,128)} %copy-done.8) | copy-start | bytes 499204
  112.1 2.8 %copy-start.12 = (f32[40,1040]{1,0:T(8,128)S(1)}, f32[40,1040]{1,0:T(8,128)}, u32[]{:S(2)}) copy-start(f32[40,1040]{1,0:T(8,128)} %copy-done.11) | copy-start | bytes 499204
  112.1 2.8 %copy-start.21 = (f32[40,1040]{1,0:T(8,128)S(1)}, f32[40,1040]{1,0:T(8,128)}, u32[]{:S(2)}) copy-start(f32[40,1040]{1,0:T(8,128)} %get-tuple-element.66) | copy-start | bytes 499204
  115.0 1.8 %copy-start.14 = (f32[8,40,1040]{2,1,0:T(8,128)S(1)}, f32[8,40,1040]{2,1,0:T(8,128)}, u32[]{:S(2)}) copy-start(f32[8,40,1040]{2,1,0:T(8,128)} %get-tuple-element.19) | copy-start | bytes 3993604
  119.6 1.8 %copy-start.16 = (f32[8,40,1040]{2,1,0:T(8,128)S(1)}, f32[8,40,1040]{2,1,0:T(8,128)}, u32[]{:S(2)}) copy-start(f32[8,40,1040]{2,1,0:T(8,128)} %get-tuple-element.21) | copy-start | bytes 3993604
  119.6 2.1 %copy-start.17 = (f32[8,32,1040]{2,1,0:T(8,128)S(1)}, f32[8,32,1040]{2,1,0:T(8,128)}, u32[]{:S(2)}) copy-start(f32[8,32,1040]{2,1,0:T(8,128)} %get-tuple-element.5) | copy-start | bytes 3194884
  125.3 8.3 %collective-permute-start.6 = (f32[4,1040]{1,0:T(4,128)S(1)}, f32[4,1040]{1,0:T(4,128)S(1)}, u32[]{:S(2)}, u32[]{:S(2)}) collective-permute-start(f32[4,1040]{1,0:T(4,128)S(1)} %get-tuple-element.64), channel_id=1, source_target_pairs={{8,0},{16,8},{24,16},{32,24},{40,32},{48,40},{56,48},{64,56},{72,6... | collective-permute-start | bytes 49928 | tf_op jit(solution)/shard_map/transpose(jvp())/ppermute | solution.py:21
  131.6 9.5 %collective-permute-start.7 = (f32[4,1040]{1,0:T(4,128)S(1)}, f32[4,1040]{1,0:T(4,128)S(1)}, u32[]{:S(2)}, u32[]{:S(2)}) collective-permute-start(f32[4,1040]{1,0:T(4,128)S(1)} %get-tuple-element.65), channel_id=1, source_target_pairs={{0,8},{8,16},{16,24},{24,32},{32,40},{40,48},{48,56},{56,64},{64,7... | collective-permute-start | bytes 49928 | tf_op jit(solution)/shard_map/transpose(jvp())/ppermute | solution.py:23
  142.3 15.8 %all-to-all-start.4 = ((f32[8,32,1024]{2,1,0:T(8,128)}), f32[8,32,1024]{2,1,0:T(8,128)S(1)}, u32[]{:S(2)}, u32[]{:S(2)}) async-start(f32[8,32,1024]{2,1,0:T(8,128)} %broadcast_in_dim.33), calls=%async_computation.4 | async-start | bytes 2097152 | tf_op jit(solution)/shard_map/all_to_all | solution.py:138
  (10 other events, 12.1 us)

commit v4 on v3

--- a/solution.py
+++ b/solution.py
@@ -111,8 +111,15 @@
         return lax.all_to_all(send_windows(x), "tm", 0, 0, tiled=True)
 
     old = to_blocks(old_starts[0])
-    gain = to_blocks(coarse_gain[0])
-    target = to_blocks(targets[0])
+    pair = lax.all_to_all(
+        jnp.stack([send_windows(coarse_gain[0]), send_windows(targets[0])], axis=1),
+        "tm", 0, 0, tiled=True,
+    )
+    gain = pair[:, 0]
+    target = pair[:, 1]
+    old, conductivity, velocity, start_state = lax.optimization_barrier(
+        (old, conductivity, velocity, start_state)
+    )
 
     first = block * width
     kappa = own_window(conductivity, first, wide)

time: 160 us -> 152 us (0.950)
  starting transfers between devices: 66.4 us -> 61.5 us
  waiting for transfers between devices: 23.4 us -> 21.2 us
    all_to_all x3 -> x1, starting transfers between devices: 18.2 us -> 6.06 us  [to_blocks(): return lax.all_to_all(send_windows(x), 'tm', 0, 0, tiled=True)]
    all_to_all x0 -> x1, starting transfers between devices: none -> 4.83 us  [on_device(): lax.all_to_all(jnp.stack([send_windows(coarse_gain[0]), send_windows(targ...]
    squeeze x0 -> x1, local copies, waits for them, and re-layouts: none -> 3.24 us  [on_device(): target = pair[:, 1]]
    slice x3, local copies, waits for them, and re-layouts: 3.33 us -> 0.26 us  [with_halo(): lax.slice_in_dim(cells, cells.shape[dim] - width, cells.shape[dim], axis=...]
    all_to_all x3 -> x1, waiting for transfers between devices: 6.45 us -> 4.02 us  [to_blocks(): return lax.all_to_all(send_windows(x), 'tm', 0, 0, tiled=True)]
    another operation x0 -> x1, local copies, waits for them, and re-layouts: none -> 1.87 us  [on_device(): jnp.stack([send_windows(coarse_gain[0]), send_windows(targets[0])], axis=1)]
    another operation x0 -> x1, other arithmetic: none -> 1.78 us  [on_device(): jnp.stack([send_windows(coarse_gain[0]), send_windows(targets[0])], axis=1)]
    unnamed x62 -> x46, local copies, waits for them, and re-layouts: 8.27 us -> 9.13 us
  transfers between devices with their start and end apart: 13 -> 12, of which waited for: 5 -> 5; matrix products, arithmetic and copies ran while one was open for 33% -> 30% of each run, Pallas kernels for 0% -> 0%
where the time goes in v4:
time: 152 us; the launch traced here: 151 us
  starting transfers between devices  61.5 us (40%)
  other arithmetic  32.5 us (21%)
  local copies, waits for them, and re-layouts  30.3 us (20%)
  waiting for transfers between devices  21.2 us (14%)
  Pallas kernels  4.33 us (3%)
    ppermute x4, starting transfers between devices, with_halo(): lax.ppermute(head, axis, [((i + 1) % count, i) for i in range(ends)])  25.7 us
    ppermute x4, starting transfers between devices, with_halo(): lax.ppermute(tail, axis, [(i, (i + 1) % count) for i in range(ends)])  13.5 us
    select_n x4, other arithmetic, fine(): jnp.where(inside, advance(field, kappa, along_rows, along_cols), 0.0)  12 us
    unnamed x46, local copies, waits for them, and re-layouts  9.13 us
    reduce_sum x3, other arithmetic, advance(): return centre + time_step * (kappa * spread - transport)  8.98 us
    ppermute x4, waiting for transfers between devices, with_halo(): lax.ppermute(head, axis, [((i + 1) % count, i) for i in range(ends)])  8.54 us
    all_to_all x1, waiting for transfers between devices, on_device(): gradient = lax.all_to_all(copies, 'tm', 0, 2, tiled=True)[0]  7.73 us
    all_to_all x1, starting transfers between devices, to_blocks(): return lax.all_to_all(send_windows(x), 'tm', 0, 0, tiled=True)  6.06 us
  transfers between devices with their start and end apart: 12, of which 5 were waited for; matrix products, arithmetic and copies ran while one was open for 30% of the time, Pallas kernels for 0%

profile of v4, /device:TPU:160, one launch (start us, length us, event | category | flops | bytes accessed | tf_op | source)
XLA Modules:
  0.0 151.1 jit_solution(3861608185259760571)
XLA Ops:
  0.6 1.8 %copy.26 = f32[4,8,8,1024]{3,2,1,0:T(8,128)S(1)} copy(f32[4,8,8,1024]{3,1,2,0:T(8,128)} %bitcast.57) | data formatting | bytes 2097152
  4.6 6.1 %all-to-all-start = ((f32[8,32,1040]{2,1,0:T(8,128)}), f32[8,32,1040]{2,1,0:T(8,128)S(1)}, u32[]{:S(2)}, u32[]{:S(2)}) async-start(f32[8,32,1040]{2,1,0:T(8,128)} %concatenate.18), calls=%async_computation | async-start | bytes 2359296 | tf_op jit(solution)/shard_map/all_to_all | solution.py:111
  14.4 2.1 %concatenate.22 = f32[8,32,1040]{2,0,1:T(8,128)} concatenate(f32[8,32,8]{2,0,1:T(8,128)} %pad.165, f32[8,32,1024]{2,0,1:T(8,128)S(1)} %bitcast.48, f32[8,32,8]{2,0,1:T(8,128)S(1)} %pad.166), dimensions={2} | concatenate | bytes 2129920 | tf_op jit(solution)/shard_map/concatenate | solution.py:108
  16.5 2.2 %concatenate.23 = f32[8,32,1040]{2,0,1:T(8,128)} concatenate(f32[8,32,8]{2,0,1:T(8,128)} %pad.167, f32[8,32,1024]{2,0,1:T(8,128)S(1)} %bitcast.50, f32[8,32,8]{2,0,1:T(8,128)} %pad.168), dimensions={2} | concatenate | bytes 2129920 | tf_op jit(solution)/shard_map/concatenate | solution.py:108
  18.7 1.8 %pad_maximum_fusion = f32[8,2,32,1040]{3,0,2,1:T(8,128)S(1)} fusion(f32[8,1,32,1040]{3,0,2,1:T(8,128)} %bitcast.54, f32[8,1,32,1040]{3,0,2,1:T(8,128)} %bitcast.53), kind=kLoop, calls=%fused_computation | loop fusion | flops 532480 | bytes 4259840 | tf_op jit(solution)/shard_map/stack | solution.py:115
  20.5 1.9 %copy.18 = f32[8,2,32,1040]{3,2,1,0:T(8,128)} copy(f32[8,2,32,1040]{3,0,2,1:T(8,128)S(1)} %pad_maximum_fusion) | data formatting | bytes 4259840 | tf_op jit(solution)/shard_map/stack | solution.py:115
  22.3 4.0 %all-to-all-done.old_ref = f32[8,32,1040]{2,1,0:T(8,128)S(1)} async-done(((f32[8,32,1040]{2,1,0:T(8,128)}), f32[8,32,1040]{2,1,0:T(8,128)S(1)}, u32[]{:S(2)}, u32[]{:S(2)}) %all-to-all-start) | async-done | bytes 1064992 | tf_op jit(solution)/shard_map/all_to_all | solution.py:111
  26.3 4.8 %all-to-all-start.1 = ((f32[8,2,32,1040]{3,2,1,0:T(8,128)}), f32[8,2,32,1040]{3,2,1,0:T(8,128)}, u32[]{:S(2)}, u32[]{:S(2)}) async-start(f32[8,2,32,1040]{3,2,1,0:T(8,128)} %copy.18), calls=%async_computation.1 | async-start | bytes 4718592 | tf_op jit(solution)/shard_map/all_to_all | solution.py:114
  33.1 2.1 %collective-permute-start.2 = (f32[4,1040]{1,0:T(4,128)S(1)}, f32[4,1040]{1,0:T(4,128)S(1)}, u32[]{:S(2)}, u32[]{:S(2)}) collective-permute-start(f32[4,1040]{1,0:T(4,128)S(1)} %get-tuple-element.66), channel_id=1, source_target_pairs={{0,8},{8,16},{16,24},{24,32},{32,40},{40,48},{48,56},{56,64},{64,7... | collective-permute-start | bytes 49928 | tf_op jit(solution)/shard_map/jvp()/ppermute | solution.py:21
  35.1 7.9 %collective-permute-start.3 = (f32[4,1040]{1,0:T(4,128)S(1)}, f32[4,1040]{1,0:T(4,128)S(1)}, u32[]{:S(2)}, u32[]{:S(2)}) collective-permute-start(f32[4,1040]{1,0:T(4,128)S(1)} %get-tuple-element.67), channel_id=1, source_target_pairs={{8,0},{16,8},{24,16},{32,24},{40,32},{48,40},{56,48},{64,56},{72,6... | collective-permute-start | bytes 49928 | tf_op jit(solution)/shard_map/jvp()/ppermute | solution.py:23
  43.0 1.9 %collective-permute-start.4 = (f32[2,4,1040]{2,1,0:T(4,128)S(1)}, f32[2,4,1040]{2,1,0:T(4,128)S(1)}, u32[]{:S(2)}, u32[]{:S(2)}) collective-permute-start(f32[2,4,1040]{2,1,0:T(4,128)S(1)} %get-tuple-element.32), channel_id=1, source_target_pairs={{0,8},{8,16},{16,24},{24,32},{32,40},{40,48},{48,56},{56,64},{64,7... | collective-permute-start | bytes 99848 | tf_op jit(solution)/shard_map/ppermute | solution.py:21
  44.9 7.9 %collective-permute-start.5 = (f32[2,4,1040]{2,1,0:T(4,128)S(1)}, f32[2,4,1040]{2,1,0:T(4,128)S(1)}, u32[]{:S(2)}, u32[]{:S(2)}) collective-permute-start(f32[2,4,1040]{2,1,0:T(4,128)S(1)} %get-tuple-element.33), channel_id=1, source_target_pairs={{8,0},{16,8},{24,16},{32,24},{40,32},{48,40},{56,48},{64,56},{72,6... | collective-permute-start | bytes 99848 | tf_op jit(solution)/shard_map/ppermute | solution.py:23
  53.6 1.9 %collective-permute-start = (f32[8,4,1040]{2,1,0:T(4,128)S(1)}, f32[8,4,1040]{2,1,0:T(4,128)S(1)}, u32[]{:S(2)}, u32[]{:S(2)}) collective-permute-start(f32[8,4,1040]{2,1,0:T(4,128)S(1)} %get-tuple-element.60), channel_id=1, source_target_pairs={{0,8},{8,16},{16,24},{24,32},{32,40},{40,48},{48,56},{56,64},{64,7... | collective-permute-start | bytes 399368 | tf_op jit(solution)/shard_map/ppermute | solution.py:21
  55.6 8.0 %collective-permute-start.1 = (f32[8,4,1040]{2,1,0:T(4,128)S(1)}, f32[8,4,1040]{2,1,0:T(4,128)S(1)}, u32[]{:S(2)}, u32[]{:S(2)}) collective-permute-start(f32[8,4,1040]{2,1,0:T(4,128)S(1)} %get-tuple-element.61), channel_id=1, source_target_pairs={{8,0},{16,8},{24,16},{32,24},{40,32},{48,40},{56,48},{64,56},{72,6... | collective-permute-start | bytes 399368 | tf_op jit(solution)/shard_map/ppermute | solution.py:23
  67.3 3.4 %fusion.24 = (f32[8,40,1040]{2,1,0:T(8,128)S(1)}, f32[8,40,1040]{2,1,0:T(8,128)}) fusion(f32[8,40,1040]{2,1,0:T(8,128)S(1)} %pad_maximum_fusion.1, f32[40,1040]{1,0:T(8,128)S(1)} %get-tuple-element.72, f32[40,1040]{1,0:T(8,128)S(1)} %get-tuple-element.73, f32[40,1040]{1,0:T(8,128)S(1)} %get-tuple-element.71, f32[40,1040]{1,0:T(8,128)S(1)} %get-tuple-element.70, ...), kind=kLoop, calls=%fused_computation.61 | loop fusion | flops 6988800 | bytes 11523200 | tf_op jit(solution)/shard_map/jvp(jit(_where))/select_n | solution.py:56
  71.8 3.4 %fusion.39 = (f32[8,40,1040]{2,1,0:T(8,128)S(1)}, f32[8,40,1040]{2,1,0:T(8,128)}) fusion(f32[8,40,1040]{2,1,0:T(8,128)S(1)} %get-tuple-element.28, f32[40,1040]{1,0:T(8,128)S(1)} %get-tuple-element.72, f32[40,1040]{1,0:T(8,128)S(1)} %get-tuple-element.73, f32[40,1040]{1,0:T(8,128)S(1)} %get-tuple-element.71, f32[40,1040]{1,0:T(8,128)S(1)} %get-tuple-element.70, ...), kind=kLoop, calls=%fused_computation.76 | loop fusion | flops 6988800 | bytes 11523200 | tf_op jit(solution)/shard_map/jvp(jit(_where))/select_n | solution.py:56
  76.4 3.4 %fusion.55 = (f32[8,40,1040]{2,1,0:T(8,128)S(1)}, f32[8,40,1040]{2,1,0:T(8,128)}) fusion(f32[8,40,1040]{2,1,0:T(8,128)S(1)} %get-tuple-element.26, f32[40,1040]{1,0:T(8,128)S(1)} %get-tuple-element.72, f32[40,1040]{1,0:T(8,128)S(1)} %get-tuple-element.73, f32[40,1040]{1,0:T(8,128)S(1)} %get-tuple-element.71, f32[40,1040]{1,0:T(8,128)S(1)} %get-tuple-element.70, ...), kind=kLoop, calls=%fused_computation.92 | loop fusion | flops 6988800 | bytes 11523200 | tf_op jit(solution)/shard_map/jvp(jit(_where))/select_n | solution.py:56
  82.8 1.8 %fusion.97.fine_ref = f32[8,32,1040]{2,1,0:T(8,128)} fusion(f32[8,40,1040]{2,1,0:T(8,128)S(1)} %get-tuple-element.24, f32[8,40,1040]{2,1,0:T(8,128)S(1)} %fusion.84, f32[8,40,1040]{2,1,0:T(8,128)S(1)} %get-tuple-element.49, f32[8,40,1040]{2,1,0:T(8,128)S(1)} %get-tuple-element.50, f32[8,40,1040]{2,1,0:T(8,128)S(1)} %get-tuple-element.48, ...), kind=kLoop, calls=%fused_computation.184 | loop fusion | flops 2129920 | bytes 6689280 | tf_op jit(solution)/shard_map/jvp(jit(_where))/select_n | solution.py:56
  84.5 3.2 %slice_bitcast_fusion = (f32[8,32,1040]{2,1,0:T(8,128)}, f32[8,32,1040]{2,1,0:T(8,128)}) fusion(f32[8,2,32,1040]{3,2,1,0:T(8,128)} %all-to-all-done.1), kind=kLoop, calls=%fused_computation.181 | loop fusion | bytes 4259840 | tf_op jit(solution)/shard_map/squeeze | solution.py:119
  87.8 4.3 %shard_map.77 = (f32[8,32,1040]{2,1,0:T(8,128)}, f32[8,32,1040]{2,1,0:T(8,128)}) custom-call(f32[8,32,1040]{2,1,0:T(8,128)} %fusion.97.fine_ref, f32[8,32,1040]{2,1,0:T(8,128)} %copy-done.4, f32[8,32,1040]{2,1,0:T(8,128)} %get-tuple-element.31.gain_ref, f32[8,32,1040]{2,1,0:T(8,128)} %get-tuple-element.30.target_ref, ...), custom_call_target="tpu_custom_call" | custom-call | tf_op jit(solution)/shard_map/pallas_call | solution.py:88
  92.1 2.6 %slice.225 = f32[8,32,1024]{2,1,0:T(8,128)} slice(f32[8,32,1040]{2,1,0:T(8,128)} %get-tuple-element.12), slice={[0:8], [0:32], [8:1032]} | slice | bytes 2097152 | tf_op jit(solution)/shard_map/slice | solution.py:141
  94.7 5.7 %all-to-all-start.2 = ((f32[8,32,1024]{2,1,0:T(8,128)}), f32[8,32,1024]{2,1,0:T(8,128)}, u32[]{:S(2)}, u32[]{:S(2)}) async-start(f32[8,32,1024]{2,1,0:T(8,128)} %slice.225), calls=%async_computation.2 | async-start | bytes 2097152 | tf_op jit(solution)/shard_map/all_to_all | solution.py:142
  100.4 2.4 %fusion.96 = (f32[8,40,1040]{2,1,0:T(8,128)S(1)}, f32[8,40,1040]{2,1,0:T(8,128)S(1)}, f32[8,40,1040]{2,1,0:T(8,128)S(1)}, f32[8,40,1040]{2,1,0:T(8,128)S(1)}, f3...) fusion(f32[8,32,1040]{2,1,0:T(8,128)} %get-tuple-element.13, ...), kind=kLoop, calls=%fused_computation.180 | loop fusion | flops 5990400 | bytes 11256960 | tf_op jit(solution)/shard_map/transpose(jvp())/mul | solution.py:48
  102.9 2.7 %multiply_reduce_fusion.1 = (f32[40,1040]{1,0:T(8,128)S(1)}, f32[8,40,1040]{2,1,0:T(8,128)S(1)}) fusion(f32[8,40,1040]{2,1,0:T(8,128)S(1)} %copy-done.13, f32[8,40,1040]{2,1,0:T(8,128)S(1)} %get-tuple-element.24, f32[8,40,1040]{2,1,0:T(8,128)S(1)} %get-tuple-element.58, f32[8,40,1040]{2,1,0:T(8,128)S(1)} %get-tuple-element.59, ...), kind=kLoop, calls=%fused_computation.159 | loop fusion | flops 6281600 | bytes 13520000 | tf_op jit(solution)/shard_map/transpose(jvp())/reduce_sum | solution.py:50
  107.5 2.8 %multiply_reduce_fusion = (f32[40,1040]{1,0:T(8,128)S(1)}, f32[8,40,1040]{2,1,0:T(8,128)S(1)}) fusion(f32[8,40,1040]{2,1,0:T(8,128)S(1)} %copy-done.12, f32[8,40,1040]{2,1,0:T(8,128)S(1)} %copy-done.1, f32[8,40,1040]{2,1,0:T(8,128)S(1)} %get-tuple-element.47, f32[8,40,1040]{2,1,0:T(8,128)S(1)} %get-tuple-element.46, ...), kind=kLoop, calls=%fused_computation.156 | loop fusion | flops 6281600 | bytes 13520000 | tf_op jit(solution)/shard_map/transpose(jvp())/reduce_sum | solution.py:50
  112.4 3.5 %multiply_reduce_fusion.2 = (f32[40,1040]{1,0:T(8,128)S(1)}, f32[40,1040]{1,0:T(8,128)S(1)}) fusion(f32[8,32,1040]{2,1,0:T(8,128)S(1)} %copy-done.15, pred[40,1040]{1,0:T(8,128)(4,1)S(1)} %and_and_fusion, f32[8,40,1040]{2,1,0:T(8,128)S(1)} %copy-done.14, f32[8,40,1040]{2,1,0:T(8,128)S(1)} %copy-done.3, f32[8,40,1040]{2,1,0:T(8,128)S(1)} %get-tuple-element.45, ...), kind=kLoop, calls=%fused_computation.162 | loop fusion | flops 9235200 | bytes 20076160 | tf_op jit(solution)/shard_map/transpose(jvp())/reduce_sum | solution.py:50
  116.0 7.6 %collective-permute-start.6 = (f32[4,1040]{1,0:T(4,128)S(1)}, f32[4,1040]{1,0:T(4,128)S(1)}, u32[]{:S(2)}, u32[]{:S(2)}) collective-permute-start(f32[4,1040]{1,0:T(4,128)S(1)} %get-tuple-element.74), channel_id=1, source_target_pairs={{8,0},{16,8},{24,16},{32,24},{40,32},{48,40},{56,48},{64,56},{72,6... | collective-permute-start | bytes 49928 | tf_op jit(solution)/shard_map/transpose(jvp())/ppermute | solution.py:21
  123.7 1.9 %collective-permute-start.7 = (f32[4,1040]{1,0:T(4,128)S(1)}, f32[4,1040]{1,0:T(4,128)S(1)}, u32[]{:S(2)}, u32[]{:S(2)}) collective-permute-start(f32[4,1040]{1,0:T(4,128)S(1)} %get-tuple-element.75), channel_id=1, source_target_pairs={{0,8},{8,16},{16,24},{24,32},{32,40},{40,48},{48,56},{56,64},{64,7... | collective-permute-start | bytes 49928 | tf_op jit(solution)/shard_map/transpose(jvp())/ppermute | solution.py:23
  125.6 7.4 %collective-permute-done.7 = f32[4,1040]{1,0:T(4,128)S(1)} collective-permute-done((f32[4,1040]{1,0:T(4,128)S(1)}, f32[4,1040]{1,0:T(4,128)S(1)}, u32[]{:S(2)}, u32[]{:S(2)}) %collective-permute-start.7) | collective-permute-done | bytes 16672 | tf_op jit(solution)/shard_map/transpose(jvp())/ppermute | solution.py:23
  134.3 5.7 %all-to-all-start.3 = ((f32[8,32,1024]{2,1,0:T(8,128)}), f32[8,32,1024]{2,1,0:T(8,128)S(1)}, u32[]{:S(2)}, u32[]{:S(2)}) async-start(f32[8,32,1024]{2,1,0:T(8,128)} %broadcast_in_dim.33), calls=%async_computation.3 | async-start | bytes 2097152 | tf_op jit(solution)/shard_map/all_to_all | solution.py:145
  140.0 2.3 %copy.25 = f32[1,8,4,8,1024]{4,3,1,2,0:T(8,128)} copy(f32[1,8,4,8,1024]{4,3,2,1,0:T(8,128)} %bitcast.21) | data formatting | bytes 2097152 | tf_op jit(solution)/shard_map/all_to_all | solution.py:142
  142.3 7.7 %all-to-all-done.3 = f32[8,32,1024]{2,1,0:T(8,128)S(1)} async-done(((f32[8,32,1024]{2,1,0:T(8,128)}), f32[8,32,1024]{2,1,0:T(8,128)S(1)}, u32[]{:S(2)}, u32[]{:S(2)}) %all-to-all-start.3) | async-done | bytes 1048608 | tf_op jit(solution)/shard_map/all_to_all | solution.py:145
  (94 shorter events, 23.5 us)
Async XLA Ops:
  4.6 6.2 %copy-start.18 = (f32[1,32,8192]{2,1,0:T(8,128)S(1)}, f32[1,32,8192]{2,1,0:T(8,128)}, u32[]{:S(2)}) copy-start(f32[1,32,8192]{2,1,0:T(8,128)} %param.10) | copy-start | bytes 3145732
  4.6 21.7 %all-to-all-start = ((f32[8,32,1040]{2,1,0:T(8,128)}), f32[8,32,1040]{2,1,0:T(8,128)S(1)}, u32[]{:S(2)}, u32[]{:S(2)}) async-start(f32[8,32,1040]{2,1,0:T(8,128)} %concatenate.18), calls=%async_computation | async-start | bytes 2359296 | tf_op jit(solution)/shard_map/all_to_all | solution.py:111
  10.9 1.4 copy-start.19
  22.3 8.9 %copy-start.16 = (f32[32,8192]{1,0:T(8,128)S(1)}, f32[32,8192]{1,0:T(8,128)}, u32[]{:S(2)}) copy-start(f32[32,8192]{1,0:T(8,128)} %param.8) | copy-start | bytes 3145732
  26.3 40.2 %copy-start.4 = (f32[8,32,1040]{2,1,0:T(8,128)}, f32[8,32,1040]{2,1,0:T(8,128)S(1)}, u32[]{:S(2)}) copy-start(f32[8,32,1040]{2,1,0:T(8,128)S(1)} %all-to-all-done.old_ref) | copy-start | bytes 3194884
  26.3 58.2 %all-to-all-start.1 = ((f32[8,2,32,1040]{3,2,1,0:T(8,128)}), f32[8,2,32,1040]{3,2,1,0:T(8,128)}, u32[]{:S(2)}, u32[]{:S(2)}) async-start(f32[8,2,32,1040]{3,2,1,0:T(8,128)} %copy.18), calls=%async_computation.1 | async-start | bytes 4718592 | tf_op jit(solution)/shard_map/all_to_all | solution.py:114
  31.2 1.6 %copy-start.11 = (f32[2,32,8192]{2,1,0:T(8,128)S(1)}, f32[2,32,8192]{2,1,0:T(8,128)}, u32[]{:S(2)}) copy-start(f32[2,32,8192]{2,1,0:T(8,128)} %param.9) | copy-start | bytes 6291460
  32.9 20.0 %copy-start.20 = (f32[32,8192]{1,0:T(8,128)S(1)}, f32[32,8192]{1,0:T(8,128)}, u32[]{:S(2)}) copy-start(f32[32,8192]{1,0:T(8,128)} %param.6) | copy-start | bytes 3145732
  33.1 22.5 %collective-permute-start.2 = (f32[4,1040]{1,0:T(4,128)S(1)}, f32[4,1040]{1,0:T(4,128)S(1)}, u32[]{:S(2)}, u32[]{:S(2)}) collective-permute-start(f32[4,1040]{1,0:T(4,128)S(1)} %get-tuple-element.66), channel_id=1, source_target_pairs={{0,8},{8,16},{16,24},{24,32},{32,40},{40,48},{48,56},{56,64},{64,7... | collective-permute-start | bytes 49928 | tf_op jit(solution)/shard_map/jvp()/ppermute | solution.py:21
  35.1 28.5 %collective-permute-start.3 = (f32[4,1040]{1,0:T(4,128)S(1)}, f32[4,1040]{1,0:T(4,128)S(1)}, u32[]{:S(2)}, u32[]{:S(2)}) collective-permute-start(f32[4,1040]{1,0:T(4,128)S(1)} %get-tuple-element.67), channel_id=1, source_target_pairs={{8,0},{16,8},{24,16},{32,24},{40,32},{48,40},{56,48},{64,56},{72,6... | collective-permute-start | bytes 49928 | tf_op jit(solution)/shard_map/jvp()/ppermute | solution.py:23
  43.0 21.4 %collective-permute-start.4 = (f32[2,4,1040]{2,1,0:T(4,128)S(1)}, f32[2,4,1040]{2,1,0:T(4,128)S(1)}, u32[]{:S(2)}, u32[]{:S(2)}) collective-permute-start(f32[2,4,1040]{2,1,0:T(4,128)S(1)} %get-tuple-element.32), channel_id=1, source_target_pairs={{0,8},{8,16},{16,24},{24,32},{32,40},{40,48},{48,56},{56,64},{64,7... | collective-permute-start | bytes 99848 | tf_op jit(solution)/shard_map/ppermute | solution.py:21
  44.9 19.4 %collective-permute-start.5 = (f32[2,4,1040]{2,1,0:T(4,128)S(1)}, f32[2,4,1040]{2,1,0:T(4,128)S(1)}, u32[]{:S(2)}, u32[]{:S(2)}) collective-permute-start(f32[2,4,1040]{2,1,0:T(4,128)S(1)} %get-tuple-element.33), channel_id=1, source_target_pairs={{8,0},{16,8},{24,16},{32,24},{40,32},{48,40},{56,48},{64,56},{72,6... | collective-permute-start | bytes 99848 | tf_op jit(solution)/shard_map/ppermute | solution.py:23
  53.6 11.8 %collective-permute-start = (f32[8,4,1040]{2,1,0:T(4,128)S(1)}, f32[8,4,1040]{2,1,0:T(4,128)S(1)}, u32[]{:S(2)}, u32[]{:S(2)}) collective-permute-start(f32[8,4,1040]{2,1,0:T(4,128)S(1)} %get-tuple-element.60), channel_id=1, source_target_pairs={{0,8},{8,16},{16,24},{24,32},{32,40},{40,48},{48,56},{56,64},{64,7... | collective-permute-start | bytes 399368 | tf_op jit(solution)/shard_map/ppermute | solution.py:21
  55.6 11.0 %collective-permute-start.1 = (f32[8,4,1040]{2,1,0:T(4,128)S(1)}, f32[8,4,1040]{2,1,0:T(4,128)S(1)}, u32[]{:S(2)}, u32[]{:S(2)}) collective-permute-start(f32[8,4,1040]{2,1,0:T(4,128)S(1)} %get-tuple-element.61), channel_id=1, source_target_pairs={{8,0},{16,8},{24,16},{32,24},{40,32},{48,40},{56,48},{64,56},{72,6... | collective-permute-start | bytes 399368 | tf_op jit(solution)/shard_map/ppermute | solution.py:23
  64.5 11.3 %copy-start.9 = (f32[40,1040]{1,0:T(8,128)}, f32[40,1040]{1,0:T(8,128)S(1)}, u32[]{:S(2)}) copy-start(f32[40,1040]{1,0:T(8,128)S(1)} %get-tuple-element.72) | copy-start | bytes 499204
  64.5 17.4 %copy-start.5 = (f32[40,1040]{1,0:T(8,128)}, f32[40,1040]{1,0:T(8,128)S(1)}, u32[]{:S(2)}) copy-start(f32[40,1040]{1,0:T(8,128)S(1)} %get-tuple-element.71) | copy-start | bytes 499204
  64.5 17.4 %copy-start.7 = (f32[40,1040]{1,0:T(8,128)}, f32[40,1040]{1,0:T(8,128)S(1)}, u32[]{:S(2)}) copy-start(f32[40,1040]{1,0:T(8,128)S(1)} %get-tuple-element.73) | copy-start | bytes 499204
  70.7 1.1 copy-start.2
  94.7 38.5 %all-to-all-start.2 = ((f32[8,32,1024]{2,1,0:T(8,128)}), f32[8,32,1024]{2,1,0:T(8,128)}, u32[]{:S(2)}, u32[]{:S(2)}) async-start(f32[8,32,1024]{2,1,0:T(8,128)} %slice.225), calls=%async_computation.2 | async-start | bytes 2097152 | tf_op jit(solution)/shard_map/all_to_all | solution.py:142
  100.4 2.4 %copy-start.13 = (f32[8,40,1040]{2,1,0:T(8,128)S(1)}, f32[8,40,1040]{2,1,0:T(8,128)}, u32[]{:S(2)}) copy-start(f32[8,40,1040]{2,1,0:T(8,128)} %get-tuple-element.25) | copy-start | bytes 3993604
  102.9 2.8 %copy-start.6 = (f32[40,1040]{1,0:T(8,128)S(1)}, f32[40,1040]{1,0:T(8,128)}, u32[]{:S(2)}) copy-start(f32[40,1040]{1,0:T(8,128)} %copy-done.5) | copy-start | bytes 499204
  102.9 2.8 %copy-start.8 = (f32[40,1040]{1,0:T(8,128)S(1)}, f32[40,1040]{1,0:T(8,128)}, u32[]{:S(2)}) copy-start(f32[40,1040]{1,0:T(8,128)} %copy-done.7) | copy-start | bytes 499204
  102.9 2.8 %copy-start.10 = (f32[40,1040]{1,0:T(8,128)S(1)}, f32[40,1040]{1,0:T(8,128)}, u32[]{:S(2)}) copy-start(f32[40,1040]{1,0:T(8,128)} %copy-done.9) | copy-start | bytes 499204
  102.9 2.8 %copy-start.17 = (f32[40,1040]{1,0:T(8,128)S(1)}, f32[40,1040]{1,0:T(8,128)}, u32[]{:S(2)}) copy-start(f32[40,1040]{1,0:T(8,128)} %get-tuple-element.76) | copy-start | bytes 499204
  105.7 1.4 copy-start.1
  105.7 1.8 %copy-start.12 = (f32[8,40,1040]{2,1,0:T(8,128)S(1)}, f32[8,40,1040]{2,1,0:T(8,128)}, u32[]{:S(2)}) copy-start(f32[8,40,1040]{2,1,0:T(8,128)} %get-tuple-element.27) | copy-start | bytes 3993604
  110.3 1.4 copy-start.3
  110.3 1.8 %copy-start.14 = (f32[8,40,1040]{2,1,0:T(8,128)S(1)}, f32[8,40,1040]{2,1,0:T(8,128)}, u32[]{:S(2)}) copy-start(f32[8,40,1040]{2,1,0:T(8,128)} %get-tuple-element.29) | copy-start | bytes 3993604
  110.3 2.1 %copy-start.15 = (f32[8,32,1040]{2,1,0:T(8,128)S(1)}, f32[8,32,1040]{2,1,0:T(8,128)}, u32[]{:S(2)}) copy-start(f32[8,32,1040]{2,1,0:T(8,128)} %get-tuple-element.13) | copy-start | bytes 3194884
  116.0 9.6 %collective-permute-start.6 = (f32[4,1040]{1,0:T(4,128)S(1)}, f32[4,1040]{1,0:T(4,128)S(1)}, u32[]{:S(2)}, u32[]{:S(2)}) collective-permute-start(f32[4,1040]{1,0:T(4,128)S(1)} %get-tuple-element.74), channel_id=1, source_target_pairs={{8,0},{16,8},{24,16},{32,24},{40,32},{48,40},{56,48},{64,56},{72,6... | collective-permute-start | bytes 49928 | tf_op jit(solution)/shard_map/transpose(jvp())/ppermute | solution.py:21
  123.7 9.4 %collective-permute-start.7 = (f32[4,1040]{1,0:T(4,128)S(1)}, f32[4,1040]{1,0:T(4,128)S(1)}, u32[]{:S(2)}, u32[]{:S(2)}) collective-permute-start(f32[4,1040]{1,0:T(4,128)S(1)} %get-tuple-element.75), channel_id=1, source_target_pairs={{0,8},{8,16},{16,24},{24,32},{32,40},{40,48},{48,56},{56,64},{64,7... | collective-permute-start | bytes 49928 | tf_op jit(solution)/shard_map/transpose(jvp())/ppermute | solution.py:23
  134.3 15.7 %all-to-all-start.3 = ((f32[8,32,1024]{2,1,0:T(8,128)}), f32[8,32,1024]{2,1,0:T(8,128)S(1)}, u32[]{:S(2)}, u32[]{:S(2)}) async-start(f32[8,32,1024]{2,1,0:T(8,128)} %broadcast_in_dim.33), calls=%async_computation.3 | async-start | bytes 2097152 | tf_op jit(solution)/shard_map/all_to_all | solution.py:145
  (1 other events, 1.1 us)

commit v5 on v4

--- a/solution.py
+++ b/solution.py
@@ -51,7 +51,6 @@
 
 
 def fine(field, kappa, along_rows, along_cols, inside):
-    kappa = with_halo(kappa, "space", 0, STEPS)
     for step in range(STEPS):
         field = jnp.where(inside, advance(field, kappa, along_rows, along_cols), 0.0)
     return field[:, STEPS:-STEPS]
@@ -65,33 +64,34 @@
     return lax.dynamic_slice_in_dim(pad_cols(x), start, width, axis=x.ndim - 1)
 
 
-def scan_kernel(fine_ref, old_ref, gain_ref, target_ref, begin_ref, ends_ref, adjoint_ref):
+def scan_kernel(fine_ref, old_ref, pair_ref, begin_ref, ends_ref, adjoint_ref):
     slabs = fine_ref.shape[0]
     begin = begin_ref[...]
     for slab in range(slabs):
-        carried = fine_ref[slab] - gain_ref[slab] * old_ref[slab]
-        begin = gain_ref[slab] * begin + carried
+        carried = fine_ref[slab] - pair_ref[slab, 0] * old_ref[slab]
+        begin = pair_ref[slab, 0] * begin + carried
         ends_ref[slab] = begin
-    adjoint = ends_ref[slabs - 1] - target_ref[slabs - 1]
+    adjoint = ends_ref[slabs - 1] - pair_ref[slabs - 1, 1]
     adjoint_ref[slabs - 1] = adjoint
     for slab in range(slabs - 2, -1, -1):
-        adjoint = (ends_ref[slab] - target_ref[slab]) + gain_ref[slab + 1] * adjoint
+        adjoint = (ends_ref[slab] - pair_ref[slab, 1]) + pair_ref[slab + 1, 0] * adjoint
         adjoint_ref[slab] = adjoint
 
 
-def scans(fine_ends, old, gain, target, begin):
+def scans(fine_ends, old, pair, begin):
     slabs, rows, wide = fine_ends.shape
     tile = 8
     stacked = pl.BlockSpec((slabs, tile, wide), lambda i: (0, i, 0))
+    both = pl.BlockSpec((slabs, 2, tile, wide), lambda i: (0, 0, i, 0))
     single = pl.BlockSpec((tile, wide), lambda i: (i, 0))
     shape = jax.ShapeDtypeStruct(fine_ends.shape, fine_ends.dtype)
     return pl.pallas_call(
         scan_kernel,
         grid=(rows // tile,),
-        in_specs=[stacked, stacked, stacked, stacked, single],
+        in_specs=[stacked, stacked, both, single],
         out_specs=[stacked, stacked],
         out_shape=[shape, shape],
-    )(fine_ends, old, gain, target, begin)
+    )(fine_ends, old, pair, begin)
 
 
 def on_device(start_state, old_starts, conductivity, velocity, coarse_gain, targets):
@@ -115,8 +115,6 @@
         jnp.stack([send_windows(coarse_gain[0]), send_windows(targets[0])], axis=1),
         "tm", 0, 0, tiled=True,
     )
-    gain = pair[:, 0]
-    target = pair[:, 1]
     old, conductivity, velocity, start_state = lax.optimization_barrier(
         (old, conductivity, velocity, start_state)
     )
@@ -129,14 +127,24 @@
     strip = lax.axis_index("space")
     row = strip * rows - STEPS + lax.broadcasted_iota(jnp.int32, (1, rows + 2 * STEPS, 1), 1)
     inside = (column >= 0) & (column < cols) & (row >= 0) & (row < rows * lax.axis_size("space"))
-    old_rows = with_halo(old, "space", 1, STEPS)
-    flow_rows = with_halo(flow, "space", 1, STEPS)
+    slabs = old.shape[0]
+    fields = jnp.concatenate([old, kappa[None], flow], axis=0)
+    fields = with_halo(fields, "space", 1, STEPS)
+    old_rows = fields[:slabs]
+    kappa_rows = fields[slabs]
+    flow_rows = fields[slabs + 1 :]
 
     fine_ends, pullback = jax.vjp(
-        lambda k: fine(old_rows, k, flow_rows[0], flow_rows[1], inside), kappa
+        lambda k: fine(old_rows, k, flow_rows[0], flow_rows[1], inside), kappa_rows
     )
-    new_ends, adjoint = scans(fine_ends, old, gain, target, begin)
-    (grad_window,) = pullback(adjoint)
+    new_ends, adjoint = scans(fine_ends, old, pair, begin)
+    (grad_rows,) = pullback(adjoint)
+    count = lax.axis_size("space")
+    ends = count - 1
+    from_below = lax.ppermute(grad_rows[:STEPS], "space", [((i + 1) % count, i) for i in range(ends)])
+    from_above = lax.ppermute(grad_rows[-STEPS:], "space", [(i, (i + 1) % count) for i in range(ends)])
+    grad_window = grad_rows[STEPS:-STEPS]
+    grad_window = grad_window.at[-STEPS:].add(from_below).at[:STEPS].add(from_above)
 
     interior = new_ends[:, :, HALO : HALO + width]
     new_end = lax.all_to_all(interior, "tm", 0, 2, tiled=True)

time: 152 us -> 144 us (0.947)
  starting transfers between devices: 61.5 us -> 42 us
  waiting for transfers between devices: 21.2 us -> 37.3 us
  local copies, waits for them, and re-layouts: 30.3 us -> 24.8 us
    ppermute x4 -> x1, starting transfers between devices: 25.7 us -> 8.04 us  [with_halo(): lax.ppermute(head, axis, [((i + 1) % count, i) for i in range(ends)])]
    ppermute x4 -> x1, starting transfers between devices: 13.5 us -> 2.05 us  [with_halo(): lax.ppermute(tail, axis, [(i, (i + 1) % count) for i in range(ends)])]
    ppermute x4 -> x1, waiting for transfers between devices: 8.54 us -> 16.9 us  [with_halo(): lax.ppermute(head, axis, [((i + 1) % count, i) for i in range(ends)])]
    ppermute x0 -> x2, waiting for transfers between devices: none -> 7.44 us  [the longest x1 7.44 us: on_device(): lax.ppermute(grad_rows[-STEPS:], 'space', [(i, (i + 1) % count) for i in...]
    ppermute x0 -> x2, starting transfers between devices: none -> 7.15 us  [the longest x1 5.23 us: on_device(): lax.ppermute(grad_rows[:STEPS], 'space', [((i + 1) % count, i) for i in r...]
    squeeze x1 -> x0, local copies, waits for them, and re-layouts: 3.24 us -> none  [on_device(): target = pair[:, 1]]
    all_to_all x1, starting transfers between devices: 5.7 us -> 7.96 us  [on_device(): new_end = lax.all_to_all(interior, 'tm', 0, 2, tiled=True)]
    another operation x1 -> x0, local copies, waits for them, and re-layouts: 1.87 us -> none  [on_device(): jnp.stack([send_windows(coarse_gain[0]), send_windows(targets[0])], axis=1)]
  transfers between devices with their start and end apart: 12 -> 8, of which waited for: 5 -> 5; matrix products, arithmetic and copies ran while one was open for 30% -> 31% of each run, Pallas kernels for 0% -> 0%
where the time goes in v5:
time: 144 us; the launch traced here: 143 us
  starting transfers between devices  42 us (29%)
  waiting for transfers between devices  37.3 us (26%)
  other arithmetic  33.7 us (23%)
  local copies, waits for them, and re-layouts  24.8 us (17%)
  Pallas kernels  4.4 us (3%)
    ppermute x1, waiting for transfers between devices, with_halo(): lax.ppermute(head, axis, [((i + 1) % count, i) for i in range(ends)])  16.9 us
    select_n x4, other arithmetic, fine(): jnp.where(inside, advance(field, kappa, along_rows, along_cols), 0.0)  12 us
    unnamed x48, local copies, waits for them, and re-layouts  9.15 us
    reduce_sum x3, other arithmetic, advance(): return centre + time_step * (kappa * spread - transport)  8.98 us
    ppermute x1, starting transfers between devices, with_halo(): lax.ppermute(head, axis, [((i + 1) % count, i) for i in range(ends)])  8.04 us
    all_to_all x1, starting transfers between devices, on_device(): new_end = lax.all_to_all(interior, 'tm', 0, 2, tiled=True)  7.96 us
    all_to_all x1, waiting for transfers between devices, on_device(): gradient = lax.all_to_all(copies, 'tm', 0, 2, tiled=True)[0]  7.73 us
    ppermute x1, waiting for transfers between devices, on_device(): lax.ppermute(grad_rows[-STEPS:], 'space', [(i, (i + 1) % count) for i in...  7.44 us
  transfers between devices with their start and end apart: 8, of which 5 were waited for; matrix products, arithmetic and copies ran while one was open for 31% of the time, Pallas kernels for 0%

profile of v5, /device:TPU:160, one launch (start us, length us, event | category | flops | bytes accessed | tf_op | source)
XLA Modules:
  0.0 143.5 jit_solution(15341840121640761918)
XLA Ops:
  0.6 1.8 %copy.22 = f32[4,8,8,1024]{3,2,1,0:T(8,128)S(1)} copy(f32[4,8,8,1024]{3,1,2,0:T(8,128)} %bitcast.58) | data formatting | bytes 2097152
  3.2 1.4 concatenate.19
  4.7 6.1 %all-to-all-start = ((f32[8,32,1040]{2,1,0:T(8,128)}), f32[8,32,1040]{2,1,0:T(8,128)S(1)}, u32[]{:S(2)}, u32[]{:S(2)}) async-start(f32[8,32,1040]{2,1,0:T(8,128)} %concatenate.19), calls=%async_computation | async-start | bytes 2359296 | tf_op jit(solution)/shard_map/all_to_all | solution.py:111
  15.1 1.4 concatenate.22
  16.5 2.4 %concatenate.23 = f32[8,32,1040]{2,1,0:T(8,128)} concatenate(f32[8,32,8]{2,1,0:T(8,128)S(1)} %pad.165, f32[8,32,1024]{2,1,0:T(8,128)} %bitcast.49, f32[8,32,8]{2,1,0:T(8,128)S(1)} %pad.166), dimensions={2} | concatenate | bytes 2129920 | tf_op jit(solution)/shard_map/concatenate | solution.py:108
  18.9 2.9 %pad_maximum_fusion = f32[8,2,32,1040]{3,2,1,0:T(8,128)} fusion(f32[8,1,32,1040]{3,2,1,0:T(8,128)} %bitcast.53, f32[8,1,32,1040]{3,2,1,0:T(8,128)S(1)} %bitcast.52), kind=kLoop, calls=%fused_computation | loop fusion | flops 532480 | bytes 4259840 | tf_op jit(solution)/shard_map/stack | solution.py:115
  21.8 4.6 %all-to-all-done.old_ref = f32[8,32,1040]{2,1,0:T(8,128)S(1)} async-done(((f32[8,32,1040]{2,1,0:T(8,128)}), f32[8,32,1040]{2,1,0:T(8,128)S(1)}, u32[]{:S(2)}, u32[]{:S(2)}) %all-to-all-start) | async-done | bytes 1064992 | tf_op jit(solution)/shard_map/all_to_all | solution.py:111
  26.4 4.8 %all-to-all-start.1 = ((f32[8,2,32,1040]{3,2,1,0:T(8,128)}), f32[8,2,32,1040]{3,2,1,0:T(8,128)}, u32[]{:S(2)}, u32[]{:S(2)}) async-start(f32[8,2,32,1040]{3,2,1,0:T(8,128)} %pad_maximum_fusion), calls=%async_computation.1 | async-start | bytes 4718592 | tf_op jit(solution)/shard_map/all_to_all | solution.py:114
  31.3 1.1 pad_dynamic-slice_fusion
  32.5 2.1 %collective-permute-start = (f32[11,4,1040]{2,1,0:T(4,128)S(1)}, f32[11,4,1040]{2,1,0:T(4,128)S(1)}, u32[]{:S(2)}, u32[]{:S(2)}) collective-permute-start(f32[11,4,1040]{2,1,0:T(4,128)S(1)} %get-tuple-element.72), channel_id=1, source_target_pairs={{0,8},{8,16},{16,24},{24,32},{32,40},{40,48},{48,56},{56,64},{64,7... | collective-permute-start | bytes 549128 | tf_op jit(solution)/shard_map/ppermute | solution.py:21
  34.6 8.0 %collective-permute-start.1 = (f32[11,4,1040]{2,1,0:T(4,128)S(1)}, f32[11,4,1040]{2,1,0:T(4,128)S(1)}, u32[]{:S(2)}, u32[]{:S(2)}) collective-permute-start(f32[11,4,1040]{2,1,0:T(4,128)S(1)} %get-tuple-element.73), channel_id=1, source_target_pairs={{8,0},{16,8},{24,16},{32,24},{40,32},{48,40},{56,48},{64,56},{72,6... | collective-permute-start | bytes 549128 | tf_op jit(solution)/shard_map/ppermute | solution.py:23
  44.0 16.9 %collective-permute-done.1 = f32[11,4,1040]{2,1,0:T(4,128)S(1)} collective-permute-done((f32[11,4,1040]{2,1,0:T(4,128)S(1)}, f32[11,4,1040]{2,1,0:T(4,128)S(1)}, u32[]{:S(2)}, u32[]{:S(2)}) %collective-permute-start.1) | collective-permute-done | bytes 183072 | tf_op jit(solution)/shard_map/ppermute | solution.py:23
  62.8 3.4 %fusion.24 = (f32[8,40,1040]{2,1,0:T(8,128)S(1)}, f32[8,40,1040]{2,1,0:T(8,128)}) fusion(f32[8,40,1040]{2,1,0:T(8,128)S(1)} %slice.269, f32[40,1040]{1,0:T(8,128)S(1)} %get-tuple-element.98, f32[40,1040]{1,0:T(8,128)S(1)} %get-tuple-element.60, f32[40,1040]{1,0:T(8,128)S(1)} %get-tuple-element.99, f32[40,1040]{1,0:T(8,128)S(1)} %get-tuple-element.56, ...), kind=kLoop, calls=%fused_computation.60 | loop fusion | flops 6988800 | bytes 11523200 | tf_op jit(solution)/shard_map/jvp(jit(_where))/select_n | solution.py:55
  67.3 3.4 %fusion.39 = (f32[8,40,1040]{2,1,0:T(8,128)S(1)}, f32[8,40,1040]{2,1,0:T(8,128)}) fusion(f32[8,40,1040]{2,1,0:T(8,128)S(1)} %get-tuple-element.54, f32[40,1040]{1,0:T(8,128)S(1)} %get-tuple-element.98, f32[40,1040]{1,0:T(8,128)S(1)} %get-tuple-element.60, f32[40,1040]{1,0:T(8,128)S(1)} %get-tuple-element.99, f32[40,1040]{1,0:T(8,128)S(1)} %get-tuple-element.56, ...), kind=kLoop, calls=%fused_computation.75 | loop fusion | flops 6988800 | bytes 11523200 | tf_op jit(solution)/shard_map/jvp(jit(_where))/select_n | solution.py:55
  71.9 3.4 %fusion.55 = (f32[8,40,1040]{2,1,0:T(8,128)S(1)}, f32[8,40,1040]{2,1,0:T(8,128)}) fusion(f32[8,40,1040]{2,1,0:T(8,128)S(1)} %get-tuple-element.52, f32[40,1040]{1,0:T(8,128)S(1)} %get-tuple-element.98, f32[40,1040]{1,0:T(8,128)S(1)} %get-tuple-element.60, f32[40,1040]{1,0:T(8,128)S(1)} %get-tuple-element.99, f32[40,1040]{1,0:T(8,128)S(1)} %get-tuple-element.56, ...), kind=kLoop, calls=%fused_computation.91 | loop fusion | flops 6988800 | bytes 11523200 | tf_op jit(solution)/shard_map/jvp(jit(_where))/select_n | solution.py:55
  75.8 1.6 %fusion.84 = f32[8,40,1040]{2,1,0:T(8,128)S(1)} fusion(f32[8,42,1042]{2,1,0:T(8,128)S(1)} %pad_add_fusion), kind=kLoop, calls=%fused_computation.133 | loop fusion | flops 1664000 | bytes 7987200 | tf_op jit(solution)/shard_map/jvp()/sub | solution.py:38
  78.3 1.7 %fusion.97.fine_ref = f32[8,32,1040]{2,1,0:T(8,128)} fusion(f32[8,40,1040]{2,1,0:T(8,128)S(1)} %get-tuple-element.50, f32[8,40,1040]{2,1,0:T(8,128)S(1)} %fusion.84, f32[8,40,1040]{2,1,0:T(8,128)S(1)} %get-tuple-element.79, f32[8,40,1040]{2,1,0:T(8,128)S(1)} %get-tuple-element.80, f32[8,40,1040]{2,1,0:T(8,128)S(1)} %get-tuple-element.78, ...), kind=kLoop, calls=%fused_computation.180 | loop fusion | flops 2129920 | bytes 6689280 | tf_op jit(solution)/shard_map/jvp(jit(_where))/select_n | solution.py:55
  80.1 4.4 %shard_map.77 = (f32[8,32,1040]{2,1,0:T(8,128)}, f32[8,32,1040]{2,1,0:T(8,128)}) custom-call(f32[8,32,1040]{2,1,0:T(8,128)} %fusion.97.fine_ref, f32[8,32,1040]{2,1,0:T(8,128)} %copy-done, f32[8,2,32,1040]{3,2,1,0:T(8,128)} %all-to-all-done.1.pair_ref, f32[32,1040]{1,0:T(8,128)} %pad_dynamic-slice_fusion.1.begin_ref), custom_call_target="tpu_custom_call" | custom-call | tf_op jit(solution)/shard_map/pallas_call | solution.py:88
  84.5 2.6 %slice.260 = f32[8,32,1024]{2,1,0:T(8,128)} slice(f32[8,32,1040]{2,1,0:T(8,128)} %get-tuple-element.36), slice={[0:8], [0:32], [8:1032]} | slice | bytes 2097152 | tf_op jit(solution)/shard_map/slice | solution.py:149
  87.0 8.0 %all-to-all-start.2 = ((f32[8,32,1024]{2,1,0:T(8,128)}), f32[8,32,1024]{2,1,0:T(8,128)}, u32[]{:S(2)}, u32[]{:S(2)}) async-start(f32[8,32,1024]{2,1,0:T(8,128)} %slice.260), calls=%async_computation.2 | async-start | bytes 2097152 | tf_op jit(solution)/shard_map/all_to_all | solution.py:150
  95.0 2.4 %fusion.96 = (f32[8,40,1040]{2,1,0:T(8,128)S(1)}, f32[8,40,1040]{2,1,0:T(8,128)S(1)}, f32[8,40,1040]{2,1,0:T(8,128)S(1)}, f32[8,40,1040]{2,1,0:T(8,128)S(1)}, f3...) fusion(f32[8,32,1040]{2,1,0:T(8,128)} %get-tuple-element.37, ...), kind=kLoop, calls=%fused_computation.178 | loop fusion | flops 5990400 | bytes 11256960 | tf_op jit(solution)/shard_map/transpose(jvp())/mul | solution.py:48
  97.5 2.7 %multiply_reduce_fusion.1 = (f32[40,1040]{1,0:T(8,128)S(1)}, f32[8,40,1040]{2,1,0:T(8,128)S(1)}) fusion(f32[8,40,1040]{2,1,0:T(8,128)S(1)} %copy-done.12, f32[8,40,1040]{2,1,0:T(8,128)S(1)} %get-tuple-element.50, f32[8,40,1040]{2,1,0:T(8,128)S(1)} %get-tuple-element.88, f32[8,40,1040]{2,1,0:T(8,128)S(1)} %get-tuple-element.89, ...), kind=kLoop, calls=%fused_computation.157 | loop fusion | flops 6281600 | bytes 13520000 | tf_op jit(solution)/shard_map/transpose(jvp())/reduce_sum | solution.py:50
  102.1 2.8 %multiply_reduce_fusion = (f32[40,1040]{1,0:T(8,128)S(1)}, f32[8,40,1040]{2,1,0:T(8,128)S(1)}) fusion(f32[8,40,1040]{2,1,0:T(8,128)S(1)} %copy-done.11, f32[8,40,1040]{2,1,0:T(8,128)S(1)} %copy-done.2, f32[8,40,1040]{2,1,0:T(8,128)S(1)} %get-tuple-element.77, f32[8,40,1040]{2,1,0:T(8,128)S(1)} %get-tuple-element.76, ...), kind=kLoop, calls=%fused_computation.154 | loop fusion | flops 6281600 | bytes 13520000 | tf_op jit(solution)/shard_map/transpose(jvp())/reduce_sum | solution.py:50
  107.0 3.5 %multiply_reduce_fusion.2 = (f32[40,1040]{1,0:T(8,128)S(1)}, f32[40,1040]{1,0:T(8,128)S(1)}) fusion(f32[8,32,1040]{2,1,0:T(8,128)S(1)} %copy-done.16, pred[40,1040]{1,0:T(8,128)(4,1)S(1)} %and_and_fusion, f32[8,40,1040]{2,1,0:T(8,128)S(1)} %copy-done.13, f32[8,40,1040]{2,1,0:T(8,128)S(1)} %copy-done.4, f32[8,40,1040]{2,1,0:T(8,128)S(1)} %get-tuple-element.75, ...), kind=kLoop, calls=%fused_computation.160 | loop fusion | flops 9235200 | bytes 20076160 | tf_op jit(solution)/shard_map/transpose(jvp())/reduce_sum | solution.py:50
  110.6 5.2 %collective-permute-start.2 = (f32[4,1040]{1,0:T(4,128)S(1)}, f32[4,1040]{1,0:T(4,128)S(1)}, u32[]{:S(2)}, u32[]{:S(2)}) collective-permute-start(f32[4,1040]{1,0:T(4,128)S(1)} %get-tuple-element.97), channel_id=1, source_target_pairs={{8,0},{16,8},{24,16},{32,24},{40,32},{48,40},{56,48},{64,56},{72,6... | collective-permute-start | bytes 49928 | tf_op jit(solution)/shard_map/ppermute | solution.py:144
  115.9 1.9 %collective-permute-start.3 = (f32[4,1040]{1,0:T(4,128)S(1)}, f32[4,1040]{1,0:T(4,128)S(1)}, u32[]{:S(2)}, u32[]{:S(2)}) collective-permute-start(f32[4,1040]{1,0:T(4,128)S(1)} %get-tuple-element.96), channel_id=1, source_target_pairs={{0,8},{8,16},{16,24},{24,32},{32,40},{40,48},{48,56},{56,64},{64,7... | collective-permute-start | bytes 49928 | tf_op jit(solution)/shard_map/ppermute | solution.py:145
  117.8 7.4 %collective-permute-done.3 = f32[4,1040]{1,0:T(4,128)S(1)} collective-permute-done((f32[4,1040]{1,0:T(4,128)S(1)}, f32[4,1040]{1,0:T(4,128)S(1)}, u32[]{:S(2)}, u32[]{:S(2)}) %collective-permute-start.3) | collective-permute-done | bytes 16672 | tf_op jit(solution)/shard_map/ppermute | solution.py:145
  125.4 1.1 broadcast_in_dim.57
  126.5 5.9 %all-to-all-start.3 = ((f32[8,32,1024]{2,1,0:T(8,128)}), f32[8,32,1024]{2,1,0:T(8,128)S(1)}, u32[]{:S(2)}, u32[]{:S(2)}) async-start(f32[8,32,1024]{2,1,0:T(8,128)} %broadcast_in_dim.57), calls=%async_computation.3 | async-start | bytes 2097152 | tf_op jit(solution)/shard_map/all_to_all | solution.py:153
  132.4 2.3 %copy.21 = f32[1,8,4,8,1024]{4,3,1,2,0:T(8,128)} copy(f32[1,8,4,8,1024]{4,3,2,1,0:T(8,128)} %bitcast.17) | data formatting | bytes 2097152 | tf_op jit(solution)/shard_map/all_to_all | solution.py:150
  134.7 7.7 %all-to-all-done.3 = f32[8,32,1024]{2,1,0:T(8,128)S(1)} async-done(((f32[8,32,1024]{2,1,0:T(8,128)}), f32[8,32,1024]{2,1,0:T(8,128)S(1)}, u32[]{:S(2)}, u32[]{:S(2)}) %all-to-all-start.3) | async-done | bytes 1048608 | tf_op jit(solution)/shard_map/all_to_all | solution.py:153
  142.4 1.0 copy.25
  (89 shorter events, 16.1 us)
Async XLA Ops:
  4.7 6.2 %copy-start.18 = (f32[1,32,8192]{2,1,0:T(8,128)S(1)}, f32[1,32,8192]{2,1,0:T(8,128)}, u32[]{:S(2)}) copy-start(f32[1,32,8192]{2,1,0:T(8,128)} %param.14) | copy-start | bytes 3145732
  4.7 21.7 %all-to-all-start = ((f32[8,32,1040]{2,1,0:T(8,128)}), f32[8,32,1040]{2,1,0:T(8,128)S(1)}, u32[]{:S(2)}, u32[]{:S(2)}) async-start(f32[8,32,1040]{2,1,0:T(8,128)} %concatenate.19), calls=%async_computation | async-start | bytes 2359296 | tf_op jit(solution)/shard_map/all_to_all | solution.py:111
  11.5 1.2 copy-start.19
  14.0 1.0 copy-start.14
  16.5 2.4 %copy-start.15 = (f32[8,32,1040]{2,1,0:T(8,128)S(1)}, f32[8,32,1040]{2,1,0:T(8,128)}, u32[]{:S(2)}) copy-start(f32[8,32,1040]{2,1,0:T(8,128)} %concatenate.22) | copy-start | bytes 3194884
  21.8 9.4 %copy-start.20 = (f32[32,8192]{1,0:T(8,128)S(1)}, f32[32,8192]{1,0:T(8,128)}, u32[]{:S(2)}) copy-start(f32[32,8192]{1,0:T(8,128)} %param.12) | copy-start | bytes 3145732
  26.4 35.6 %copy-start = (f32[8,32,1040]{2,1,0:T(8,128)}, f32[8,32,1040]{2,1,0:T(8,128)S(1)}, u32[]{:S(2)}) copy-start(f32[8,32,1040]{2,1,0:T(8,128)S(1)} %all-to-all-done.old_ref) | copy-start | bytes 3194884
  26.4 53.7 %all-to-all-start.1 = ((f32[8,2,32,1040]{3,2,1,0:T(8,128)}), f32[8,2,32,1040]{3,2,1,0:T(8,128)}, u32[]{:S(2)}, u32[]{:S(2)}) async-start(f32[8,2,32,1040]{3,2,1,0:T(8,128)} %pad_maximum_fusion), calls=%async_computation.1 | async-start | bytes 4718592 | tf_op jit(solution)/shard_map/all_to_all | solution.py:114
  32.4 10.2 %copy-start.21 = (f32[32,8192]{1,0:T(8,128)S(1)}, f32[32,8192]{1,0:T(8,128)}, u32[]{:S(2)}) copy-start(f32[32,8192]{1,0:T(8,128)} %param.10) | copy-start | bytes 3145732
  32.5 11.5 %collective-permute-start = (f32[11,4,1040]{2,1,0:T(4,128)S(1)}, f32[11,4,1040]{2,1,0:T(4,128)S(1)}, u32[]{:S(2)}, u32[]{:S(2)}) collective-permute-start(f32[11,4,1040]{2,1,0:T(4,128)S(1)} %get-tuple-element.72), channel_id=1, source_target_pairs={{0,8},{8,16},{16,24},{24,32},{32,40},{40,48},{48,56},{56,64},{64,7... | collective-permute-start | bytes 549128 | tf_op jit(solution)/shard_map/ppermute | solution.py:21
  34.6 26.4 %collective-permute-start.1 = (f32[11,4,1040]{2,1,0:T(4,128)S(1)}, f32[11,4,1040]{2,1,0:T(4,128)S(1)}, u32[]{:S(2)}, u32[]{:S(2)}) collective-permute-start(f32[11,4,1040]{2,1,0:T(4,128)S(1)} %get-tuple-element.73), channel_id=1, source_target_pairs={{8,0},{16,8},{24,16},{32,24},{40,32},{48,40},{56,48},{64,56},{72,6... | collective-permute-start | bytes 549128 | tf_op jit(solution)/shard_map/ppermute | solution.py:23
  61.9 15.5 %copy-start.5 = (f32[40,1040]{1,0:T(8,128)}, f32[40,1040]{1,0:T(8,128)S(1)}, u32[]{:S(2)}) copy-start(f32[40,1040]{1,0:T(8,128)S(1)} %get-tuple-element.56) | copy-start | bytes 499204
  62.0 15.5 %copy-start.7 = (f32[40,1040]{1,0:T(8,128)}, f32[40,1040]{1,0:T(8,128)S(1)}, u32[]{:S(2)}) copy-start(f32[40,1040]{1,0:T(8,128)S(1)} %get-tuple-element.60) | copy-start | bytes 499204
  62.0 9.3 %copy-start.9 = (f32[40,1040]{1,0:T(8,128)}, f32[40,1040]{1,0:T(8,128)S(1)}, u32[]{:S(2)}) copy-start(f32[40,1040]{1,0:T(8,128)S(1)} %get-tuple-element.98) | copy-start | bytes 499204
  66.2 1.1 copy-start.3
  70.8 1.1 copy-start.1
  87.0 38.3 %all-to-all-start.2 = ((f32[8,32,1024]{2,1,0:T(8,128)}), f32[8,32,1024]{2,1,0:T(8,128)}, u32[]{:S(2)}, u32[]{:S(2)}) async-start(f32[8,32,1024]{2,1,0:T(8,128)} %slice.260), calls=%async_computation.2 | async-start | bytes 2097152 | tf_op jit(solution)/shard_map/all_to_all | solution.py:150
  95.0 2.4 %copy-start.12 = (f32[8,40,1040]{2,1,0:T(8,128)S(1)}, f32[8,40,1040]{2,1,0:T(8,128)}, u32[]{:S(2)}) copy-start(f32[8,40,1040]{2,1,0:T(8,128)} %get-tuple-element.51) | copy-start | bytes 3993604
  97.4 2.8 %copy-start.6 = (f32[40,1040]{1,0:T(8,128)S(1)}, f32[40,1040]{1,0:T(8,128)}, u32[]{:S(2)}) copy-start(f32[40,1040]{1,0:T(8,128)} %copy-done.5) | copy-start | bytes 499204
  97.5 2.8 %copy-start.8 = (f32[40,1040]{1,0:T(8,128)S(1)}, f32[40,1040]{1,0:T(8,128)}, u32[]{:S(2)}) copy-start(f32[40,1040]{1,0:T(8,128)} %copy-done.7) | copy-start | bytes 499204
  97.5 2.8 %copy-start.10 = (f32[40,1040]{1,0:T(8,128)S(1)}, f32[40,1040]{1,0:T(8,128)}, u32[]{:S(2)}) copy-start(f32[40,1040]{1,0:T(8,128)} %copy-done.9) | copy-start | bytes 499204
  97.5 2.8 %copy-start.17 = (f32[40,1040]{1,0:T(8,128)S(1)}, f32[40,1040]{1,0:T(8,128)}, u32[]{:S(2)}) copy-start(f32[40,1040]{1,0:T(8,128)} %get-tuple-element.48) | copy-start | bytes 499204
  100.3 1.4 copy-start.2
  100.3 1.8 %copy-start.11 = (f32[8,40,1040]{2,1,0:T(8,128)S(1)}, f32[8,40,1040]{2,1,0:T(8,128)}, u32[]{:S(2)}) copy-start(f32[8,40,1040]{2,1,0:T(8,128)} %get-tuple-element.53) | copy-start | bytes 3993604
  104.9 1.4 copy-start.4
  104.9 1.8 %copy-start.13 = (f32[8,40,1040]{2,1,0:T(8,128)S(1)}, f32[8,40,1040]{2,1,0:T(8,128)}, u32[]{:S(2)}) copy-start(f32[8,40,1040]{2,1,0:T(8,128)} %get-tuple-element.55) | copy-start | bytes 3993604
  104.9 2.1 %copy-start.16 = (f32[8,32,1040]{2,1,0:T(8,128)S(1)}, f32[8,32,1040]{2,1,0:T(8,128)}, u32[]{:S(2)}) copy-start(f32[8,32,1040]{2,1,0:T(8,128)} %get-tuple-element.37) | copy-start | bytes 3194884
  110.6 7.2 %collective-permute-start.2 = (f32[4,1040]{1,0:T(4,128)S(1)}, f32[4,1040]{1,0:T(4,128)S(1)}, u32[]{:S(2)}, u32[]{:S(2)}) collective-permute-start(f32[4,1040]{1,0:T(4,128)S(1)} %get-tuple-element.97), channel_id=1, source_target_pairs={{8,0},{16,8},{24,16},{32,24},{40,32},{48,40},{56,48},{64,56},{72,6... | collective-permute-start | bytes 49928 | tf_op jit(solution)/shard_map/ppermute | solution.py:144
  115.9 9.4 %collective-permute-start.3 = (f32[4,1040]{1,0:T(4,128)S(1)}, f32[4,1040]{1,0:T(4,128)S(1)}, u32[]{:S(2)}, u32[]{:S(2)}) collective-permute-start(f32[4,1040]{1,0:T(4,128)S(1)} %get-tuple-element.96), channel_id=1, source_target_pairs={{0,8},{8,16},{16,24},{24,32},{32,40},{40,48},{48,56},{56,64},{64,7... | collective-permute-start | bytes 49928 | tf_op jit(solution)/shard_map/ppermute | solution.py:145
  126.5 15.9 %all-to-all-start.3 = ((f32[8,32,1024]{2,1,0:T(8,128)}), f32[8,32,1024]{2,1,0:T(8,128)S(1)}, u32[]{:S(2)}, u32[]{:S(2)}) async-start(f32[8,32,1024]{2,1,0:T(8,128)} %broadcast_in_dim.57), calls=%async_computation.3 | async-start | bytes 2097152 | tf_op jit(solution)/shard_map/all_to_all | solution.py:153

commit v6 on v5

--- a/solution.py
+++ b/solution.py
@@ -66,31 +66,37 @@
 
 def scan_kernel(fine_ref, old_ref, pair_ref, begin_ref, ends_ref, adjoint_ref):
     slabs = fine_ref.shape[0]
+    width = ends_ref.shape[2]
     begin = begin_ref[...]
+    ends = []
     for slab in range(slabs):
         carried = fine_ref[slab] - pair_ref[slab, 0] * old_ref[slab]
         begin = pair_ref[slab, 0] * begin + carried
-        ends_ref[slab] = begin
-    adjoint = ends_ref[slabs - 1] - pair_ref[slabs - 1, 1]
+        ends.append(begin)
+        ends_ref[slab] = begin[:, HALO : HALO + width]
+    adjoint = ends[slabs - 1] - pair_ref[slabs - 1, 1]
     adjoint_ref[slabs - 1] = adjoint
     for slab in range(slabs - 2, -1, -1):
-        adjoint = (ends_ref[slab] - pair_ref[slab, 1]) + pair_ref[slab + 1, 0] * adjoint
+        adjoint = (ends[slab] - pair_ref[slab, 1]) + pair_ref[slab + 1, 0] * adjoint
         adjoint_ref[slab] = adjoint
 
 
-def scans(fine_ends, old, pair, begin):
+def scans(fine_ends, old, pair, begin, width):
     slabs, rows, wide = fine_ends.shape
     tile = 8
     stacked = pl.BlockSpec((slabs, tile, wide), lambda i: (0, i, 0))
+    inner = pl.BlockSpec((slabs, tile, width), lambda i: (0, i, 0))
     both = pl.BlockSpec((slabs, 2, tile, wide), lambda i: (0, 0, i, 0))
     single = pl.BlockSpec((tile, wide), lambda i: (i, 0))
-    shape = jax.ShapeDtypeStruct(fine_ends.shape, fine_ends.dtype)
     return pl.pallas_call(
         scan_kernel,
         grid=(rows // tile,),
         in_specs=[stacked, stacked, both, single],
-        out_specs=[stacked, stacked],
-        out_shape=[shape, shape],
+        out_specs=[inner, stacked],
+        out_shape=[
+            jax.ShapeDtypeStruct((slabs, rows, width), fine_ends.dtype),
+            jax.ShapeDtypeStruct(fine_ends.shape, fine_ends.dtype),
+        ],
     )(fine_ends, old, pair, begin)
 
 
@@ -137,7 +143,7 @@
     fine_ends, pullback = jax.vjp(
         lambda k: fine(old_rows, k, flow_rows[0], flow_rows[1], inside), kappa_rows
     )
-    new_ends, adjoint = scans(fine_ends, old, pair, begin)
+    interior, adjoint = scans(fine_ends, old, pair, begin, width)
     (grad_rows,) = pullback(adjoint)
     count = lax.axis_size("space")
     ends = count - 1
@@ -146,7 +152,6 @@
     grad_window = grad_rows[STEPS:-STEPS]
     grad_window = grad_window.at[-STEPS:].add(from_below).at[:STEPS].add(from_above)
 
-    interior = new_ends[:, :, HALO : HALO + width]
     new_end = lax.all_to_all(interior, "tm", 0, 2, tiled=True)
     own = grad_window[:, HALO : HALO + width]
     copies = jnp.broadcast_to(own[None], (blocks,) + own.shape)

time: 144 us -> 142 us (0.986)
  local copies, waits for them, and re-layouts: 24.8 us -> 22.2 us
    slice x1 -> x0, local copies, waits for them, and re-layouts: 2.58 us -> none  [on_device(): interior = new_ends[:, :, HALO:HALO + width]]
  transfers between devices with their start and end apart: 8 -> 8, of which waited for: 5 -> 5; matrix products, arithmetic and copies ran while one was open for 31% -> 32% of each run, Pallas kernels for 0% -> 0%
where the time goes in v6:
time: 142 us; the launch traced here: 141 us
  starting transfers between devices  42 us (30%)
  waiting for transfers between devices  37.3 us (26%)
  other arithmetic  33.7 us (24%)
  local copies, waits for them, and re-layouts  22.2 us (16%)
  Pallas kernels  4.38 us (3%)
    ppermute x1, waiting for transfers between devices, with_halo(): lax.ppermute(head, axis, [((i + 1) % count, i) for i in range(ends)])  16.9 us
    select_n x4, other arithmetic, fine(): jnp.where(inside, advance(field, kappa, along_rows, along_cols), 0.0)  12 us
    unnamed x48, local copies, waits for them, and re-layouts  9.15 us
    reduce_sum x3, other arithmetic, advance(): return centre + time_step * (kappa * spread - transport)  8.98 us
    ppermute x1, starting transfers between devices, with_halo(): lax.ppermute(head, axis, [((i + 1) % count, i) for i in range(ends)])  8.04 us
    all_to_all x1, starting transfers between devices, on_device(): new_end = lax.all_to_all(interior, 'tm', 0, 2, tiled=True)  7.96 us
    all_to_all x1, waiting for transfers between devices, on_device(): gradient = lax.all_to_all(copies, 'tm', 0, 2, tiled=True)[0]  7.73 us
    ppermute x1, waiting for transfers between devices, on_device(): lax.ppermute(grad_rows[-STEPS:], 'space', [(i, (i + 1) % count) for i in...  7.44 us
  transfers between devices with their start and end apart: 8, of which 5 were waited for; matrix products, arithmetic and copies ran while one was open for 32% of the time, Pallas kernels for 0%

profile of v6, /device:TPU:160, one launch (start us, length us, event | category | flops | bytes accessed | tf_op | source)
XLA Modules:
  0.0 140.9 jit_solution(7120619209420173734)
XLA Ops:
  0.6 1.8 %copy.22 = f32[4,8,8,1024]{3,2,1,0:T(8,128)S(1)} copy(f32[4,8,8,1024]{3,1,2,0:T(8,128)} %bitcast.58) | data formatting | bytes 2097152
  3.2 1.4 concatenate.19
  4.6 6.1 %all-to-all-start = ((f32[8,32,1040]{2,1,0:T(8,128)}), f32[8,32,1040]{2,1,0:T(8,128)S(1)}, u32[]{:S(2)}, u32[]{:S(2)}) async-start(f32[8,32,1040]{2,1,0:T(8,128)} %concatenate.19), calls=%async_computation | async-start | bytes 2359296 | tf_op jit(solution)/shard_map/all_to_all | solution.py:117
  13.9 1.0 copy-done.14
  15.0 1.4 %concatenate.22 = f32[8,32,1040]{2,1,0:T(8,128)} concatenate(f32[8,32,8]{2,1,0:T(8,128)S(1)} %pad.163, f32[8,32,1024]{2,1,0:T(8,128)S(1)} %bitcast.47, f32[8,32,8]{2,1,0:T(8,128)S(1)} %pad.164), dimensions={2} | concatenate | bytes 2129920 | tf_op jit(solution)/shard_map/concatenate | solution.py:114
  16.5 2.4 %concatenate.23 = f32[8,32,1040]{2,1,0:T(8,128)} concatenate(f32[8,32,8]{2,1,0:T(8,128)S(1)} %pad.165, f32[8,32,1024]{2,1,0:T(8,128)} %bitcast.49, f32[8,32,8]{2,1,0:T(8,128)S(1)} %pad.166), dimensions={2} | concatenate | bytes 2129920 | tf_op jit(solution)/shard_map/concatenate | solution.py:114
  18.9 2.9 %pad_maximum_fusion = f32[8,2,32,1040]{3,2,1,0:T(8,128)} fusion(f32[8,1,32,1040]{3,2,1,0:T(8,128)} %bitcast.53, f32[8,1,32,1040]{3,2,1,0:T(8,128)S(1)} %bitcast.52), kind=kLoop, calls=%fused_computation | loop fusion | flops 532480 | bytes 4259840 | tf_op jit(solution)/shard_map/stack | solution.py:121
  21.8 4.6 %all-to-all-done.old_ref = f32[8,32,1040]{2,1,0:T(8,128)S(1)} async-done(((f32[8,32,1040]{2,1,0:T(8,128)}), f32[8,32,1040]{2,1,0:T(8,128)S(1)}, u32[]{:S(2)}, u32[]{:S(2)}) %all-to-all-start) | async-done | bytes 1064992 | tf_op jit(solution)/shard_map/all_to_all | solution.py:117
  26.3 4.9 %all-to-all-start.1 = ((f32[8,2,32,1040]{3,2,1,0:T(8,128)}), f32[8,2,32,1040]{3,2,1,0:T(8,128)}, u32[]{:S(2)}, u32[]{:S(2)}) async-start(f32[8,2,32,1040]{3,2,1,0:T(8,128)} %pad_maximum_fusion), calls=%async_computation.1 | async-start | bytes 4718592 | tf_op jit(solution)/shard_map/all_to_all | solution.py:120
  31.3 1.1 pad_dynamic-slice_fusion
  32.5 2.1 %collective-permute-start = (f32[11,4,1040]{2,1,0:T(4,128)S(1)}, f32[11,4,1040]{2,1,0:T(4,128)S(1)}, u32[]{:S(2)}, u32[]{:S(2)}) collective-permute-start(f32[11,4,1040]{2,1,0:T(4,128)S(1)} %get-tuple-element.72), channel_id=1, source_target_pairs={{0,8},{8,16},{16,24},{24,32},{32,40},{40,48},{48,56},{56,64},{64,7... | collective-permute-start | bytes 549128 | tf_op jit(solution)/shard_map/ppermute | solution.py:21
  34.6 8.0 %collective-permute-start.1 = (f32[11,4,1040]{2,1,0:T(4,128)S(1)}, f32[11,4,1040]{2,1,0:T(4,128)S(1)}, u32[]{:S(2)}, u32[]{:S(2)}) collective-permute-start(f32[11,4,1040]{2,1,0:T(4,128)S(1)} %get-tuple-element.73), channel_id=1, source_target_pairs={{8,0},{16,8},{24,16},{32,24},{40,32},{48,40},{56,48},{64,56},{72,6... | collective-permute-start | bytes 549128 | tf_op jit(solution)/shard_map/ppermute | solution.py:23
  44.0 16.9 %collective-permute-done.1 = f32[11,4,1040]{2,1,0:T(4,128)S(1)} collective-permute-done((f32[11,4,1040]{2,1,0:T(4,128)S(1)}, f32[11,4,1040]{2,1,0:T(4,128)S(1)}, u32[]{:S(2)}, u32[]{:S(2)}) %collective-permute-start.1) | collective-permute-done | bytes 183072 | tf_op jit(solution)/shard_map/ppermute | solution.py:23
  62.8 3.4 %fusion.24 = (f32[8,40,1040]{2,1,0:T(8,128)S(1)}, f32[8,40,1040]{2,1,0:T(8,128)}) fusion(f32[8,40,1040]{2,1,0:T(8,128)S(1)} %slice.265, f32[40,1040]{1,0:T(8,128)S(1)} %get-tuple-element.98, f32[40,1040]{1,0:T(8,128)S(1)} %get-tuple-element.60, f32[40,1040]{1,0:T(8,128)S(1)} %get-tuple-element.99, f32[40,1040]{1,0:T(8,128)S(1)} %get-tuple-element.56, ...), kind=kLoop, calls=%fused_computation.60 | loop fusion | flops 6988800 | bytes 11523200 | tf_op jit(solution)/shard_map/jvp(jit(_where))/select_n | solution.py:55
  67.3 3.4 %fusion.39 = (f32[8,40,1040]{2,1,0:T(8,128)S(1)}, f32[8,40,1040]{2,1,0:T(8,128)}) fusion(f32[8,40,1040]{2,1,0:T(8,128)S(1)} %get-tuple-element.54, f32[40,1040]{1,0:T(8,128)S(1)} %get-tuple-element.98, f32[40,1040]{1,0:T(8,128)S(1)} %get-tuple-element.60, f32[40,1040]{1,0:T(8,128)S(1)} %get-tuple-element.99, f32[40,1040]{1,0:T(8,128)S(1)} %get-tuple-element.56, ...), kind=kLoop, calls=%fused_computation.75 | loop fusion | flops 6988800 | bytes 11523200 | tf_op jit(solution)/shard_map/jvp(jit(_where))/select_n | solution.py:55
  71.9 3.4 %fusion.55 = (f32[8,40,1040]{2,1,0:T(8,128)S(1)}, f32[8,40,1040]{2,1,0:T(8,128)}) fusion(f32[8,40,1040]{2,1,0:T(8,128)S(1)} %get-tuple-element.52, f32[40,1040]{1,0:T(8,128)S(1)} %get-tuple-element.98, f32[40,1040]{1,0:T(8,128)S(1)} %get-tuple-element.60, f32[40,1040]{1,0:T(8,128)S(1)} %get-tuple-element.99, f32[40,1040]{1,0:T(8,128)S(1)} %get-tuple-element.56, ...), kind=kLoop, calls=%fused_computation.91 | loop fusion | flops 6988800 | bytes 11523200 | tf_op jit(solution)/shard_map/jvp(jit(_where))/select_n | solution.py:55
  75.8 1.6 %fusion.84 = f32[8,40,1040]{2,1,0:T(8,128)S(1)} fusion(f32[8,42,1042]{2,1,0:T(8,128)S(1)} %pad_add_fusion), kind=kLoop, calls=%fused_computation.133 | loop fusion | flops 1664000 | bytes 7987200 | tf_op jit(solution)/shard_map/jvp()/sub | solution.py:38
  78.3 1.7 %fusion.97.fine_ref = f32[8,32,1040]{2,1,0:T(8,128)} fusion(f32[8,40,1040]{2,1,0:T(8,128)S(1)} %get-tuple-element.50, f32[8,40,1040]{2,1,0:T(8,128)S(1)} %fusion.84, f32[8,40,1040]{2,1,0:T(8,128)S(1)} %get-tuple-element.79, f32[8,40,1040]{2,1,0:T(8,128)S(1)} %get-tuple-element.80, f32[8,40,1040]{2,1,0:T(8,128)S(1)} %get-tuple-element.78, ...), kind=kLoop, calls=%fused_computation.180 | loop fusion | flops 2129920 | bytes 6689280 | tf_op jit(solution)/shard_map/jvp(jit(_where))/select_n | solution.py:55
  80.1 4.4 %shard_map.77 = (f32[8,32,1024]{2,1,0:T(8,128)}, f32[8,32,1040]{2,1,0:T(8,128)}) custom-call(f32[8,32,1040]{2,1,0:T(8,128)} %fusion.97.fine_ref, f32[8,32,1040]{2,1,0:T(8,128)} %copy-done, f32[8,2,32,1040]{3,2,1,0:T(8,128)} %all-to-all-done.1.pair_ref, f32[32,1040]{1,0:T(8,128)} %pad_dynamic-slice_fusion.1.begin_ref), custom_call_target="tpu_custom_call" | custom-call | tf_op jit(solution)/shard_map/pallas_call | solution.py:91
  84.4 8.0 %all-to-all-start.2 = ((f32[8,32,1024]{2,1,0:T(8,128)}), f32[8,32,1024]{2,1,0:T(8,128)}, u32[]{:S(2)}, u32[]{:S(2)}) async-start(f32[8,32,1024]{2,1,0:T(8,128)} %get-tuple-element.36), calls=%async_computation.2 | async-start | bytes 2097152 | tf_op jit(solution)/shard_map/all_to_all | solution.py:155
  92.4 2.4 %fusion.96 = (f32[8,40,1040]{2,1,0:T(8,128)S(1)}, f32[8,40,1040]{2,1,0:T(8,128)S(1)}, f32[8,40,1040]{2,1,0:T(8,128)S(1)}, f32[8,40,1040]{2,1,0:T(8,128)S(1)}, f3...) fusion(f32[8,32,1040]{2,1,0:T(8,128)} %get-tuple-element.37, ...), kind=kLoop, calls=%fused_computation.178 | loop fusion | flops 5990400 | bytes 11256960 | tf_op jit(solution)/shard_map/transpose(jvp())/mul | solution.py:48
  94.9 2.7 %multiply_reduce_fusion.1 = (f32[40,1040]{1,0:T(8,128)S(1)}, f32[8,40,1040]{2,1,0:T(8,128)S(1)}) fusion(f32[8,40,1040]{2,1,0:T(8,128)S(1)} %copy-done.12, f32[8,40,1040]{2,1,0:T(8,128)S(1)} %get-tuple-element.50, f32[8,40,1040]{2,1,0:T(8,128)S(1)} %get-tuple-element.88, f32[8,40,1040]{2,1,0:T(8,128)S(1)} %get-tuple-element.89, ...), kind=kLoop, calls=%fused_computation.157 | loop fusion | flops 6281600 | bytes 13520000 | tf_op jit(solution)/shard_map/transpose(jvp())/reduce_sum | solution.py:50
  99.5 2.8 %multiply_reduce_fusion = (f32[40,1040]{1,0:T(8,128)S(1)}, f32[8,40,1040]{2,1,0:T(8,128)S(1)}) fusion(f32[8,40,1040]{2,1,0:T(8,128)S(1)} %copy-done.11, f32[8,40,1040]{2,1,0:T(8,128)S(1)} %copy-done.2, f32[8,40,1040]{2,1,0:T(8,128)S(1)} %get-tuple-element.77, f32[8,40,1040]{2,1,0:T(8,128)S(1)} %get-tuple-element.76, ...), kind=kLoop, calls=%fused_computation.154 | loop fusion | flops 6281600 | bytes 13520000 | tf_op jit(solution)/shard_map/transpose(jvp())/reduce_sum | solution.py:50
  104.4 3.5 %multiply_reduce_fusion.2 = (f32[40,1040]{1,0:T(8,128)S(1)}, f32[40,1040]{1,0:T(8,128)S(1)}) fusion(f32[8,32,1040]{2,1,0:T(8,128)S(1)} %copy-done.16, pred[40,1040]{1,0:T(8,128)(4,1)S(1)} %and_and_fusion, f32[8,40,1040]{2,1,0:T(8,128)S(1)} %copy-done.13, f32[8,40,1040]{2,1,0:T(8,128)S(1)} %copy-done.4, f32[8,40,1040]{2,1,0:T(8,128)S(1)} %get-tuple-element.75, ...), kind=kLoop, calls=%fused_computation.160 | loop fusion | flops 9235200 | bytes 20076160 | tf_op jit(solution)/shard_map/transpose(jvp())/reduce_sum | solution.py:50
  108.0 5.2 %collective-permute-start.2 = (f32[4,1040]{1,0:T(4,128)S(1)}, f32[4,1040]{1,0:T(4,128)S(1)}, u32[]{:S(2)}, u32[]{:S(2)}) collective-permute-start(f32[4,1040]{1,0:T(4,128)S(1)} %get-tuple-element.97), channel_id=1, source_target_pairs={{8,0},{16,8},{24,16},{32,24},{40,32},{48,40},{56,48},{64,56},{72,6... | collective-permute-start | bytes 49928 | tf_op jit(solution)/shard_map/ppermute | solution.py:150
  113.3 1.9 %collective-permute-start.3 = (f32[4,1040]{1,0:T(4,128)S(1)}, f32[4,1040]{1,0:T(4,128)S(1)}, u32[]{:S(2)}, u32[]{:S(2)}) collective-permute-start(f32[4,1040]{1,0:T(4,128)S(1)} %get-tuple-element.96), channel_id=1, source_target_pairs={{0,8},{8,16},{16,24},{24,32},{32,40},{40,48},{48,56},{56,64},{64,7... | collective-permute-start | bytes 49928 | tf_op jit(solution)/shard_map/ppermute | solution.py:151
  115.2 7.4 %collective-permute-done.3 = f32[4,1040]{1,0:T(4,128)S(1)} collective-permute-done((f32[4,1040]{1,0:T(4,128)S(1)}, f32[4,1040]{1,0:T(4,128)S(1)}, u32[]{:S(2)}, u32[]{:S(2)}) %collective-permute-start.3) | collective-permute-done | bytes 16672 | tf_op jit(solution)/shard_map/ppermute | solution.py:151
  122.8 1.1 broadcast_in_dim.57
  123.9 5.9 %all-to-all-start.3 = ((f32[8,32,1024]{2,1,0:T(8,128)}), f32[8,32,1024]{2,1,0:T(8,128)S(1)}, u32[]{:S(2)}, u32[]{:S(2)}) async-start(f32[8,32,1024]{2,1,0:T(8,128)} %broadcast_in_dim.57), calls=%async_computation.3 | async-start | bytes 2097152 | tf_op jit(solution)/shard_map/all_to_all | solution.py:158
  129.8 2.3 %copy.21 = f32[1,8,4,8,1024]{4,3,1,2,0:T(8,128)} copy(f32[1,8,4,8,1024]{4,3,2,1,0:T(8,128)} %bitcast.17) | data formatting | bytes 2097152 | tf_op jit(solution)/shard_map/all_to_all | solution.py:155
  132.1 7.7 %all-to-all-done.3 = f32[8,32,1024]{2,1,0:T(8,128)S(1)} async-done(((f32[8,32,1024]{2,1,0:T(8,128)}), f32[8,32,1024]{2,1,0:T(8,128)S(1)}, u32[]{:S(2)}, u32[]{:S(2)}) %all-to-all-start.3) | async-done | bytes 1048608 | tf_op jit(solution)/shard_map/all_to_all | solution.py:158
  139.8 1.0 copy.25
  (88 shorter events, 15.1 us)
Async XLA Ops:
  4.6 6.2 %copy-start.18 = (f32[1,32,8192]{2,1,0:T(8,128)S(1)}, f32[1,32,8192]{2,1,0:T(8,128)}, u32[]{:S(2)}) copy-start(f32[1,32,8192]{2,1,0:T(8,128)} %param.14) | copy-start | bytes 3145732
  4.6 21.7 %all-to-all-start = ((f32[8,32,1040]{2,1,0:T(8,128)}), f32[8,32,1040]{2,1,0:T(8,128)S(1)}, u32[]{:S(2)}, u32[]{:S(2)}) async-start(f32[8,32,1040]{2,1,0:T(8,128)} %concatenate.19), calls=%async_computation | async-start | bytes 2359296 | tf_op jit(solution)/shard_map/all_to_all | solution.py:117
  11.5 1.2 copy-start.19
  13.9 1.0 copy-start.14
  16.5 2.4 %copy-start.15 = (f32[8,32,1040]{2,1,0:T(8,128)S(1)}, f32[8,32,1040]{2,1,0:T(8,128)}, u32[]{:S(2)}) copy-start(f32[8,32,1040]{2,1,0:T(8,128)} %concatenate.22) | copy-start | bytes 3194884
  21.8 9.4 %copy-start.20 = (f32[32,8192]{1,0:T(8,128)S(1)}, f32[32,8192]{1,0:T(8,128)}, u32[]{:S(2)}) copy-start(f32[32,8192]{1,0:T(8,128)} %param.12) | copy-start | bytes 3145732
  26.3 35.7 %copy-start = (f32[8,32,1040]{2,1,0:T(8,128)}, f32[8,32,1040]{2,1,0:T(8,128)S(1)}, u32[]{:S(2)}) copy-start(f32[8,32,1040]{2,1,0:T(8,128)S(1)} %all-to-all-done.old_ref) | copy-start | bytes 3194884
  26.3 53.7 %all-to-all-start.1 = ((f32[8,2,32,1040]{3,2,1,0:T(8,128)}), f32[8,2,32,1040]{3,2,1,0:T(8,128)}, u32[]{:S(2)}, u32[]{:S(2)}) async-start(f32[8,2,32,1040]{3,2,1,0:T(8,128)} %pad_maximum_fusion), calls=%async_computation.1 | async-start | bytes 4718592 | tf_op jit(solution)/shard_map/all_to_all | solution.py:120
  32.4 10.2 %copy-start.21 = (f32[32,8192]{1,0:T(8,128)S(1)}, f32[32,8192]{1,0:T(8,128)}, u32[]{:S(2)}) copy-start(f32[32,8192]{1,0:T(8,128)} %param.10) | copy-start | bytes 3145732
  32.5 11.5 %collective-permute-start = (f32[11,4,1040]{2,1,0:T(4,128)S(1)}, f32[11,4,1040]{2,1,0:T(4,128)S(1)}, u32[]{:S(2)}, u32[]{:S(2)}) collective-permute-start(f32[11,4,1040]{2,1,0:T(4,128)S(1)} %get-tuple-element.72), channel_id=1, source_target_pairs={{0,8},{8,16},{16,24},{24,32},{32,40},{40,48},{48,56},{56,64},{64,7... | collective-permute-start | bytes 549128 | tf_op jit(solution)/shard_map/ppermute | solution.py:21
  34.6 26.4 %collective-permute-start.1 = (f32[11,4,1040]{2,1,0:T(4,128)S(1)}, f32[11,4,1040]{2,1,0:T(4,128)S(1)}, u32[]{:S(2)}, u32[]{:S(2)}) collective-permute-start(f32[11,4,1040]{2,1,0:T(4,128)S(1)} %get-tuple-element.73), channel_id=1, source_target_pairs={{8,0},{16,8},{24,16},{32,24},{40,32},{48,40},{56,48},{64,56},{72,6... | collective-permute-start | bytes 549128 | tf_op jit(solution)/shard_map/ppermute | solution.py:23
  61.9 15.5 %copy-start.5 = (f32[40,1040]{1,0:T(8,128)}, f32[40,1040]{1,0:T(8,128)S(1)}, u32[]{:S(2)}) copy-start(f32[40,1040]{1,0:T(8,128)S(1)} %get-tuple-element.56) | copy-start | bytes 499204
  62.0 15.5 %copy-start.7 = (f32[40,1040]{1,0:T(8,128)}, f32[40,1040]{1,0:T(8,128)S(1)}, u32[]{:S(2)}) copy-start(f32[40,1040]{1,0:T(8,128)S(1)} %get-tuple-element.60) | copy-start | bytes 499204
  62.0 9.3 %copy-start.9 = (f32[40,1040]{1,0:T(8,128)}, f32[40,1040]{1,0:T(8,128)S(1)}, u32[]{:S(2)}) copy-start(f32[40,1040]{1,0:T(8,128)S(1)} %get-tuple-element.98) | copy-start | bytes 499204
  66.2 1.1 copy-start.3
  70.8 1.1 copy-start.1
  84.4 38.3 %all-to-all-start.2 = ((f32[8,32,1024]{2,1,0:T(8,128)}), f32[8,32,1024]{2,1,0:T(8,128)}, u32[]{:S(2)}, u32[]{:S(2)}) async-start(f32[8,32,1024]{2,1,0:T(8,128)} %get-tuple-element.36), calls=%async_computation.2 | async-start | bytes 2097152 | tf_op jit(solution)/shard_map/all_to_all | solution.py:155
  92.4 2.4 %copy-start.12 = (f32[8,40,1040]{2,1,0:T(8,128)S(1)}, f32[8,40,1040]{2,1,0:T(8,128)}, u32[]{:S(2)}) copy-start(f32[8,40,1040]{2,1,0:T(8,128)} %get-tuple-element.51) | copy-start | bytes 3993604
  94.9 2.8 %copy-start.6 = (f32[40,1040]{1,0:T(8,128)S(1)}, f32[40,1040]{1,0:T(8,128)}, u32[]{:S(2)}) copy-start(f32[40,1040]{1,0:T(8,128)} %copy-done.5) | copy-start | bytes 499204
  94.9 2.8 %copy-start.8 = (f32[40,1040]{1,0:T(8,128)S(1)}, f32[40,1040]{1,0:T(8,128)}, u32[]{:S(2)}) copy-start(f32[40,1040]{1,0:T(8,128)} %copy-done.7) | copy-start | bytes 499204
  94.9 2.8 %copy-start.10 = (f32[40,1040]{1,0:T(8,128)S(1)}, f32[40,1040]{1,0:T(8,128)}, u32[]{:S(2)}) copy-start(f32[40,1040]{1,0:T(8,128)} %copy-done.9) | copy-start | bytes 499204
  94.9 2.8 %copy-start.17 = (f32[40,1040]{1,0:T(8,128)S(1)}, f32[40,1040]{1,0:T(8,128)}, u32[]{:S(2)}) copy-start(f32[40,1040]{1,0:T(8,128)} %get-tuple-element.48) | copy-start | bytes 499204
  97.7 1.4 copy-start.2
  97.7 1.8 %copy-start.11 = (f32[8,40,1040]{2,1,0:T(8,128)S(1)}, f32[8,40,1040]{2,1,0:T(8,128)}, u32[]{:S(2)}) copy-start(f32[8,40,1040]{2,1,0:T(8,128)} %get-tuple-element.53) | copy-start | bytes 3993604
  102.3 1.4 copy-start.4
  102.3 1.8 %copy-start.13 = (f32[8,40,1040]{2,1,0:T(8,128)S(1)}, f32[8,40,1040]{2,1,0:T(8,128)}, u32[]{:S(2)}) copy-start(f32[8,40,1040]{2,1,0:T(8,128)} %get-tuple-element.55) | copy-start | bytes 3993604
  102.3 2.1 %copy-start.16 = (f32[8,32,1040]{2,1,0:T(8,128)S(1)}, f32[8,32,1040]{2,1,0:T(8,128)}, u32[]{:S(2)}) copy-start(f32[8,32,1040]{2,1,0:T(8,128)} %get-tuple-element.37) | copy-start | bytes 3194884
  108.0 7.2 %collective-permute-start.2 = (f32[4,1040]{1,0:T(4,128)S(1)}, f32[4,1040]{1,0:T(4,128)S(1)}, u32[]{:S(2)}, u32[]{:S(2)}) collective-permute-start(f32[4,1040]{1,0:T(4,128)S(1)} %get-tuple-element.97), channel_id=1, source_target_pairs={{8,0},{16,8},{24,16},{32,24},{40,32},{48,40},{56,48},{64,56},{72,6... | collective-permute-start | bytes 49928 | tf_op jit(solution)/shard_map/ppermute | solution.py:150
  113.3 9.4 %collective-permute-start.3 = (f32[4,1040]{1,0:T(4,128)S(1)}, f32[4,1040]{1,0:T(4,128)S(1)}, u32[]{:S(2)}, u32[]{:S(2)}) collective-permute-start(f32[4,1040]{1,0:T(4,128)S(1)} %get-tuple-element.96), channel_id=1, source_target_pairs={{0,8},{8,16},{16,24},{24,32},{32,40},{40,48},{48,56},{56,64},{64,7... | collective-permute-start | bytes 49928 | tf_op jit(solution)/shard_map/ppermute | solution.py:151
  123.9 15.9 %all-to-all-start.3 = ((f32[8,32,1024]{2,1,0:T(8,128)}), f32[8,32,1024]{2,1,0:T(8,128)S(1)}, u32[]{:S(2)}, u32[]{:S(2)}) async-start(f32[8,32,1024]{2,1,0:T(8,128)} %broadcast_in_dim.57), calls=%async_computation.3 | async-start | bytes 2097152 | tf_op jit(solution)/shard_map/all_to_all | solution.py:158

commit v7 on v6

--- a/solution.py
+++ b/solution.py
@@ -117,10 +117,7 @@
         return lax.all_to_all(send_windows(x), "tm", 0, 0, tiled=True)
 
     old = to_blocks(old_starts[0])
-    pair = lax.all_to_all(
-        jnp.stack([send_windows(coarse_gain[0]), send_windows(targets[0])], axis=1),
-        "tm", 0, 0, tiled=True,
-    )
+    pair = jnp.stack([send_windows(coarse_gain[0]), send_windows(targets[0])], axis=1)
     old, conductivity, velocity, start_state = lax.optimization_barrier(
         (old, conductivity, velocity, start_state)
     )
@@ -136,6 +133,8 @@
     slabs = old.shape[0]
     fields = jnp.concatenate([old, kappa[None], flow], axis=0)
     fields = with_halo(fields, "space", 1, STEPS)
+    fields, pair = lax.optimization_barrier((fields, pair))
+    pair = lax.all_to_all(pair, "tm", 0, 0, tiled=True)
     old_rows = fields[:slabs]
     kappa_rows = fields[slabs]
     flow_rows = fields[slabs + 1 :]

time: 142 us -> 131 us (0.923)
  waiting for transfers between devices: 37.3 us -> 25.3 us
  local copies, waits for them, and re-layouts: 22.2 us -> 25.3 us
  starting transfers between devices: 42 us -> 38.9 us
  other arithmetic: 33.7 us -> 35.2 us
    ppermute x1, waiting for transfers between devices: 16.9 us -> 0.72 us  [with_halo(): lax.ppermute(head, axis, [((i + 1) % count, i) for i in range(ends)])]
    all_to_all x1, waiting for transfers between devices: 0.01 us -> 4.58 us  [on_device(): pair = lax.all_to_all(pair, 'tm', 0, 0, tiled=True)]
    all_to_all x1, starting transfers between devices: 7.96 us -> 4.69 us  [on_device(): new_end = lax.all_to_all(interior, 'tm', 0, 2, tiled=True)]
    all_to_all x1, starting transfers between devices: 4.86 us -> 6.8 us  [on_device(): pair = lax.all_to_all(pair, 'tm', 0, 0, tiled=True)]
    ppermute x1, starting transfers between devices: 5.23 us -> 3.62 us  [on_device(): lax.ppermute(grad_rows[:STEPS], 'space', [((i + 1) % count, i) for i in r...]
    unnamed x48 -> x56, local copies, waits for them, and re-layouts: 9.15 us -> 9.48 us
    mul x4 -> x3, other arithmetic: 3.9 us -> 3.88 us  [advance(): jnp.minimum(along_cols, 0.0) * (wide[:, 1:-1, 2:] - centre)]
  transfers between devices with their start and end apart: 8 -> 8, of which waited for: 5 -> 6; matrix products, arithmetic and copies ran while one was open for 32% -> 36% of each run, Pallas kernels for 0% -> 0%
where the time goes in v7:
time: 131 us; the launch traced here: 130 us
  starting transfers between devices  38.9 us (30%)
  other arithmetic  35.2 us (27%)
  local copies, waits for them, and re-layouts  25.3 us (19%)
  waiting for transfers between devices  25.3 us (19%)
  Pallas kernels  4.38 us (3%)
    select_n x4, other arithmetic, fine(): jnp.where(inside, advance(field, kappa, along_rows, along_cols), 0.0)  12.1 us
    unnamed x56, local copies, waits for them, and re-layouts  9.48 us
    reduce_sum x3, other arithmetic, advance(): return centre + time_step * (kappa * spread - transport)  9.09 us
    ppermute x1, starting transfers between devices, with_halo(): lax.ppermute(head, axis, [((i + 1) % count, i) for i in range(ends)])  7.86 us
    all_to_all x1, waiting for transfers between devices, on_device(): gradient = lax.all_to_all(copies, 'tm', 0, 2, tiled=True)[0]  7.73 us
    ppermute x1, waiting for transfers between devices, on_device(): lax.ppermute(grad_rows[-STEPS:], 'space', [(i, (i + 1) % count) for i in...  7.34 us
    all_to_all x1, starting transfers between devices, on_device(): pair = lax.all_to_all(pair, 'tm', 0, 0, tiled=True)  6.8 us
    all_to_all x1, starting transfers between devices, to_blocks(): return lax.all_to_all(send_windows(x), 'tm', 0, 0, tiled=True)  6.06 us
  transfers between devices with their start and end apart: 8, of which 6 were waited for; matrix products, arithmetic and copies ran while one was open for 36% of the time, Pallas kernels for 0%

profile of v7, /device:TPU:160, one launch (start us, length us, event | category | flops | bytes accessed | tf_op | source)
XLA Modules:
  0.0 130.3 jit_solution(798421096917608530)
XLA Ops:
  0.6 1.8 %copy.22 = f32[4,8,8,1024]{3,2,1,0:T(8,128)S(1)} copy(f32[4,8,8,1024]{3,1,2,0:T(8,128)} %bitcast.59) | data formatting | bytes 2097152
  3.2 1.4 %concatenate.19 = f32[8,32,1040]{2,1,0:T(8,128)} concatenate(f32[8,32,8]{2,1,0:T(8,128)S(1)} %pad.155, f32[8,32,1024]{2,1,0:T(8,128)S(1)} %bitcast.52, f32[8,32,8]{2,1,0:T(8,128)S(1)} %pad.156), dimensions={2} | concatenate | bytes 2129920 | tf_op jit(solution)/shard_map/concatenate | solution.py:114
  4.6 6.1 %all-to-all-start = ((f32[8,32,1040]{2,1,0:T(8,128)}), f32[8,32,1040]{2,1,0:T(8,128)S(1)}, u32[]{:S(2)}, u32[]{:S(2)}) async-start(f32[8,32,1040]{2,1,0:T(8,128)} %concatenate.19), calls=%async_computation | async-start | bytes 2359296 | tf_op jit(solution)/shard_map/all_to_all | solution.py:117
  15.6 2.1 %concatenate.22 = f32[8,32,1040]{2,1,0:T(8,128)} concatenate(f32[8,32,8]{2,1,0:T(8,128)} %pad.159, f32[8,32,1024]{2,1,0:T(8,128)S(1)} %bitcast.48, f32[8,32,8]{2,1,0:T(8,128)S(1)} %pad.160), dimensions={2} | concatenate | bytes 2129920 | tf_op jit(solution)/shard_map/concatenate | solution.py:114
  17.7 2.2 %concatenate.23 = f32[8,32,1040]{2,1,0:T(8,128)} concatenate(f32[8,32,8]{2,1,0:T(8,128)} %pad.161, f32[8,32,1024]{2,1,0:T(8,128)S(1)} %bitcast.50, f32[8,32,8]{2,1,0:T(8,128)} %pad.162), dimensions={2} | concatenate | bytes 2129920 | tf_op jit(solution)/shard_map/concatenate | solution.py:114
  19.9 3.3 %pad_maximum_fusion = f32[8,2,32,1040]{3,2,1,0:T(8,128)} fusion(f32[8,1,32,1040]{3,2,1,0:T(8,128)} %bitcast.54, f32[8,1,32,1040]{3,2,1,0:T(8,128)} %bitcast.53), kind=kLoop, calls=%fused_computation | loop fusion | flops 532480 | bytes 4259840 | tf_op jit(solution)/shard_map/stack | solution.py:120
  23.2 3.1 %all-to-all-done.old_ref = f32[8,32,1040]{2,1,0:T(8,128)S(1)} async-done(((f32[8,32,1040]{2,1,0:T(8,128)}), f32[8,32,1040]{2,1,0:T(8,128)S(1)}, u32[]{:S(2)}, u32[]{:S(2)}) %all-to-all-start) | async-done | bytes 1064992 | tf_op jit(solution)/shard_map/all_to_all | solution.py:117
  26.5 1.4 %pad_dynamic-slice_fusion = f32[2,32,1040]{2,1,0:T(8,128)S(1)} fusion(s32[]{:T(128)S(6)} %select_n.31, f32[2,32,8192]{2,1,0:T(8,128)} %param.13), kind=kLoop, calls=%fused_computation.1 | loop fusion | bytes 2363396 | tf_op jit(solution)/shard_map/dynamic_slice | solution.py:64
  28.0 2.1 %collective-permute-start = (f32[11,4,1040]{2,1,0:T(4,128)S(1)}, f32[11,4,1040]{2,1,0:T(4,128)S(1)}, u32[]{:S(2)}, u32[]{:S(2)}) collective-permute-start(f32[11,4,1040]{2,1,0:T(4,128)S(1)} %get-tuple-element.73), channel_id=1, source_target_pairs={{0,8},{8,16},{16,24},{24,32},{32,40},{40,48},{48,56},{56,64},{64,7... | collective-permute-start | bytes 549128 | tf_op jit(solution)/shard_map/ppermute | solution.py:21
  30.0 7.9 %collective-permute-start.1 = (f32[11,4,1040]{2,1,0:T(4,128)S(1)}, f32[11,4,1040]{2,1,0:T(4,128)S(1)}, u32[]{:S(2)}, u32[]{:S(2)}) collective-permute-start(f32[11,4,1040]{2,1,0:T(4,128)S(1)} %get-tuple-element.74), channel_id=1, source_target_pairs={{8,0},{16,8},{24,16},{32,24},{40,32},{48,40},{56,48},{64,56},{72,6... | collective-permute-start | bytes 549128 | tf_op jit(solution)/shard_map/ppermute | solution.py:23
  38.7 1.8 %collective-permute-done = f32[11,4,1040]{2,1,0:T(4,128)S(1)} collective-permute-done((f32[11,4,1040]{2,1,0:T(4,128)S(1)}, f32[11,4,1040]{2,1,0:T(4,128)S(1)}, u32[]{:S(2)}, u32[]{:S(2)}) %collective-permute-start) | collective-permute-done | bytes 183072 | tf_op jit(solution)/shard_map/ppermute | solution.py:21
  41.5 1.2 copy-done.14
  42.9 6.8 %all-to-all-start.1 = ((f32[8,2,32,1040]{3,2,1,0:T(8,128)}), f32[8,2,32,1040]{3,2,1,0:T(8,128)}, u32[]{:S(2)}, u32[]{:S(2)}) async-start(f32[8,2,32,1040]{3,2,1,0:T(8,128)} %pad_maximum_fusion), calls=%async_computation.1 | async-start | bytes 4718592 | tf_op jit(solution)/shard_map/all_to_all | solution.py:137
  50.3 3.5 %fusion.24 = (f32[8,40,1040]{2,1,0:T(8,128)S(1)}, f32[8,40,1040]{2,1,0:T(8,128)}) fusion(f32[8,40,1040]{2,1,0:T(8,128)S(1)} %slice.216, f32[40,1040]{1,0:T(8,128)S(1)} %get-tuple-element.60, f32[40,1040]{1,0:T(8,128)S(1)} %get-tuple-element.61, f32[40,1040]{1,0:T(8,128)S(1)} %get-tuple-element.59, f32[40,1040]{1,0:T(8,128)S(1)} %get-tuple-element.62, ...), kind=kLoop, calls=%fused_computation.60 | loop fusion | flops 6988800 | bytes 11523200 | tf_op jit(solution)/shard_map/jvp(jit(_where))/select_n | solution.py:55
  54.9 3.4 %fusion.39 = (f32[8,40,1040]{2,1,0:T(8,128)S(1)}, f32[8,40,1040]{2,1,0:T(8,128)}) fusion(f32[8,40,1040]{2,1,0:T(8,128)S(1)} %get-tuple-element.56, f32[40,1040]{1,0:T(8,128)S(1)} %get-tuple-element.60, f32[40,1040]{1,0:T(8,128)S(1)} %get-tuple-element.61, f32[40,1040]{1,0:T(8,128)S(1)} %get-tuple-element.59, f32[40,1040]{1,0:T(8,128)S(1)} %get-tuple-element.62, ...), kind=kLoop, calls=%fused_computation.75 | loop fusion | flops 6988800 | bytes 11523200 | tf_op jit(solution)/shard_map/jvp(jit(_where))/select_n | solution.py:55
  59.9 3.4 %fusion.55 = (f32[8,40,1040]{2,1,0:T(8,128)S(1)}, f32[8,40,1040]{2,1,0:T(8,128)}) fusion(f32[8,40,1040]{2,1,0:T(8,128)S(1)} %get-tuple-element.54, f32[40,1040]{1,0:T(8,128)S(1)} %copy-done.12, f32[40,1040]{1,0:T(8,128)S(1)} %get-tuple-element.61, f32[40,1040]{1,0:T(8,128)S(1)} %get-tuple-element.59, f32[40,1040]{1,0:T(8,128)S(1)} %copy-done.9, ...), kind=kLoop, calls=%fused_computation.91 | loop fusion | flops 6988800 | bytes 11523200 | tf_op jit(solution)/shard_map/jvp(jit(_where))/select_n | solution.py:55
  63.9 1.6 %broadcast_multiply_fusion.2 = f32[40,1040]{1,0:T(8,128)} fusion(f32[11,40,1040]{2,1,0:T(8,128)} %copy-done.14), kind=kLoop, calls=%fused_computation.205 | loop fusion | flops 41600 | bytes 332800 | tf_op jit(solution)/shard_map/transpose(jvp())/mul | solution.py:50
  65.5 1.6 %fusion.84 = f32[8,40,1040]{2,1,0:T(8,128)S(1)} fusion(f32[8,42,1042]{2,1,0:T(8,128)S(1)} %pad_add_fusion), kind=kLoop, calls=%fused_computation.133 | loop fusion | flops 1664000 | bytes 7987200 | tf_op jit(solution)/shard_map/jvp()/sub | solution.py:38
  68.0 1.8 %fusion.97.fine_ref = f32[8,32,1040]{2,1,0:T(8,128)} fusion(f32[8,40,1040]{2,1,0:T(8,128)S(1)} %get-tuple-element.52, f32[8,40,1040]{2,1,0:T(8,128)S(1)} %fusion.84, f32[8,40,1040]{2,1,0:T(8,128)S(1)} %get-tuple-element.80, f32[8,40,1040]{2,1,0:T(8,128)S(1)} %get-tuple-element.81, f32[8,40,1040]{2,1,0:T(8,128)S(1)} %get-tuple-element.79, ...), kind=kLoop, calls=%fused_computation.180 | loop fusion | flops 2129920 | bytes 6689280 | tf_op jit(solution)/shard_map/jvp(jit(_where))/select_n | solution.py:55
  69.7 4.6 %all-to-all-done.1.pair_ref = f32[8,2,32,1040]{3,2,1,0:T(8,128)} async-done(((f32[8,2,32,1040]{3,2,1,0:T(8,128)}), f32[8,2,32,1040]{3,2,1,0:T(8,128)}, u32[]{:S(2)}, u32[]{:S(2)}) %all-to-all-start.1) | async-done | bytes 2129952 | tf_op jit(solution)/shard_map/all_to_all | solution.py:137
  74.3 4.4 %shard_map.77 = (f32[8,32,1024]{2,1,0:T(8,128)}, f32[8,32,1040]{2,1,0:T(8,128)}) custom-call(f32[8,32,1040]{2,1,0:T(8,128)} %fusion.97.fine_ref, f32[8,32,1040]{2,1,0:T(8,128)} %copy-done.4, f32[8,2,32,1040]{3,2,1,0:T(8,128)} %all-to-all-done.1.pair_ref, f32[32,1040]{1,0:T(8,128)} %pad_dynamic-slice_fusion.1.begin_ref), custom_call_target="tpu_custom_call" | custom-call | tf_op jit(solution)/shard_map/pallas_call | solution.py:91
  78.7 4.7 %all-to-all-start.2 = ((f32[8,32,1024]{2,1,0:T(8,128)}), f32[8,32,1024]{2,1,0:T(8,128)}, u32[]{:S(2)}, u32[]{:S(2)}) async-start(f32[8,32,1024]{2,1,0:T(8,128)} %get-tuple-element.40), calls=%async_computation.2 | async-start | bytes 2097152 | tf_op jit(solution)/shard_map/all_to_all | solution.py:154
  83.4 2.4 %fusion.96 = (f32[8,40,1040]{2,1,0:T(8,128)S(1)}, f32[8,40,1040]{2,1,0:T(8,128)S(1)}, f32[8,40,1040]{2,1,0:T(8,128)S(1)}, f32[8,40,1040]{2,1,0:T(8,128)S(1)}, f3...) fusion(f32[8,32,1040]{2,1,0:T(8,128)} %get-tuple-element.41, ...), kind=kLoop, calls=%fused_computation.178 | loop fusion | flops 5990400 | bytes 11256960 | tf_op jit(solution)/shard_map/transpose(jvp())/mul | solution.py:48
  85.9 2.8 %multiply_reduce_fusion.1 = (f32[40,1040]{1,0:T(8,128)S(1)}, f32[8,40,1040]{2,1,0:T(8,128)S(1)}) fusion(f32[8,40,1040]{2,1,0:T(8,128)S(1)} %copy-done.16, f32[8,40,1040]{2,1,0:T(8,128)S(1)} %get-tuple-element.52, f32[8,40,1040]{2,1,0:T(8,128)S(1)} %get-tuple-element.89, f32[8,40,1040]{2,1,0:T(8,128)S(1)} %get-tuple-element.90, ...), kind=kLoop, calls=%fused_computation.157 | loop fusion | flops 6281600 | bytes 13520000 | tf_op jit(solution)/shard_map/transpose(jvp())/reduce_sum | solution.py:50
  90.5 2.7 %multiply_reduce_fusion = (f32[40,1040]{1,0:T(8,128)S(1)}, f32[8,40,1040]{2,1,0:T(8,128)S(1)}) fusion(f32[8,40,1040]{2,1,0:T(8,128)S(1)} %copy-done.15, f32[8,40,1040]{2,1,0:T(8,128)S(1)} %copy-done.1, f32[8,40,1040]{2,1,0:T(8,128)S(1)} %get-tuple-element.78, f32[8,40,1040]{2,1,0:T(8,128)S(1)} %get-tuple-element.77, ...), kind=kLoop, calls=%fused_computation.154 | loop fusion | flops 6281600 | bytes 13520000 | tf_op jit(solution)/shard_map/transpose(jvp())/reduce_sum | solution.py:50
  95.4 3.6 %multiply_reduce_fusion.2 = (f32[40,1040]{1,0:T(8,128)S(1)}, f32[40,1040]{1,0:T(8,128)S(1)}) fusion(f32[8,32,1040]{2,1,0:T(8,128)S(1)} %copy-done.18, pred[40,1040]{1,0:T(8,128)(4,1)S(1)} %and_and_fusion, f32[8,40,1040]{2,1,0:T(8,128)S(1)} %copy-done.17, f32[8,40,1040]{2,1,0:T(8,128)S(1)} %copy-done.3, f32[8,40,1040]{2,1,0:T(8,128)S(1)} %get-tuple-element.76, ...), kind=kLoop, calls=%fused_computation.160 | loop fusion | flops 9235200 | bytes 20076160 | tf_op jit(solution)/shard_map/transpose(jvp())/reduce_sum | solution.py:50
  99.1 3.6 %collective-permute-start.2 = (f32[4,1040]{1,0:T(4,128)S(1)}, f32[4,1040]{1,0:T(4,128)S(1)}, u32[]{:S(2)}, u32[]{:S(2)}) collective-permute-start(f32[4,1040]{1,0:T(4,128)S(1)} %get-tuple-element.98), channel_id=1, source_target_pairs={{8,0},{16,8},{24,16},{32,24},{40,32},{48,40},{56,48},{64,56},{72,6... | collective-permute-start | bytes 49928 | tf_op jit(solution)/shard_map/ppermute | solution.py:149
  102.8 1.9 %collective-permute-start.3 = (f32[4,1040]{1,0:T(4,128)S(1)}, f32[4,1040]{1,0:T(4,128)S(1)}, u32[]{:S(2)}, u32[]{:S(2)}) collective-permute-start(f32[4,1040]{1,0:T(4,128)S(1)} %get-tuple-element.97), channel_id=1, source_target_pairs={{0,8},{8,16},{16,24},{24,32},{32,40},{40,48},{48,56},{56,64},{64,7... | collective-permute-start | bytes 49928 | tf_op jit(solution)/shard_map/ppermute | solution.py:150
  104.7 7.3 %collective-permute-done.3 = f32[4,1040]{1,0:T(4,128)S(1)} collective-permute-done((f32[4,1040]{1,0:T(4,128)S(1)}, f32[4,1040]{1,0:T(4,128)S(1)}, u32[]{:S(2)}, u32[]{:S(2)}) %collective-permute-start.3) | collective-permute-done | bytes 16672 | tf_op jit(solution)/shard_map/ppermute | solution.py:150
  113.3 5.9 %all-to-all-start.3 = ((f32[8,32,1024]{2,1,0:T(8,128)}), f32[8,32,1024]{2,1,0:T(8,128)S(1)}, u32[]{:S(2)}, u32[]{:S(2)}) async-start(f32[8,32,1024]{2,1,0:T(8,128)} %broadcast_in_dim.57), calls=%async_computation.3 | async-start | bytes 2097152 | tf_op jit(solution)/shard_map/all_to_all | solution.py:157
  119.2 2.3 %copy.21 = f32[1,8,4,8,1024]{4,3,1,2,0:T(8,128)} copy(f32[1,8,4,8,1024]{4,3,2,1,0:T(8,128)} %bitcast.17) | data formatting | bytes 2097152 | tf_op jit(solution)/shard_map/all_to_all | solution.py:154
  121.5 7.7 %all-to-all-done.3 = f32[8,32,1024]{2,1,0:T(8,128)S(1)} async-done(((f32[8,32,1024]{2,1,0:T(8,128)}), f32[8,32,1024]{2,1,0:T(8,128)S(1)}, u32[]{:S(2)}, u32[]{:S(2)}) %all-to-all-start.3) | async-done | bytes 1048608 | tf_op jit(solution)/shard_map/all_to_all | solution.py:157
  (95 shorter events, 18.6 us)
Async XLA Ops:
  4.6 6.2 %copy-start.22 = (f32[1,32,8192]{2,1,0:T(8,128)S(1)}, f32[1,32,8192]{2,1,0:T(8,128)}, u32[]{:S(2)}) copy-start(f32[1,32,8192]{2,1,0:T(8,128)} %param.14) | copy-start | bytes 3145732
  4.6 21.7 %all-to-all-start = ((f32[8,32,1040]{2,1,0:T(8,128)}), f32[8,32,1040]{2,1,0:T(8,128)S(1)}, u32[]{:S(2)}, u32[]{:S(2)}) async-start(f32[8,32,1040]{2,1,0:T(8,128)} %concatenate.19), calls=%async_computation | async-start | bytes 2359296 | tf_op jit(solution)/shard_map/all_to_all | solution.py:117
  11.5 1.4 %copy-start.23 = (f32[1,32,8192]{2,1,0:T(8,128)S(1)}, f32[1,32,8192]{2,1,0:T(8,128)}, u32[]{:S(2)}) copy-start(f32[1,32,8192]{2,1,0:T(8,128)} %param.15) | copy-start | bytes 3145732
  19.9 6.4 %copy-start.24 = (f32[32,8192]{1,0:T(8,128)S(1)}, f32[32,8192]{1,0:T(8,128)}, u32[]{:S(2)}) copy-start(f32[32,8192]{1,0:T(8,128)} %param.12) | copy-start | bytes 3145732
  26.4 14.9 %copy-start.4 = (f32[8,32,1040]{2,1,0:T(8,128)}, f32[8,32,1040]{2,1,0:T(8,128)S(1)}, u32[]{:S(2)}) copy-start(f32[8,32,1040]{2,1,0:T(8,128)S(1)} %all-to-all-done.old_ref) | copy-start | bytes 3194884
  27.9 10.0 %copy-start.25 = (f32[32,8192]{1,0:T(8,128)S(1)}, f32[32,8192]{1,0:T(8,128)}, u32[]{:S(2)}) copy-start(f32[32,8192]{1,0:T(8,128)} %param.10) | copy-start | bytes 3145732
  28.0 12.5 %collective-permute-start = (f32[11,4,1040]{2,1,0:T(4,128)S(1)}, f32[11,4,1040]{2,1,0:T(4,128)S(1)}, u32[]{:S(2)}, u32[]{:S(2)}) collective-permute-start(f32[11,4,1040]{2,1,0:T(4,128)S(1)} %get-tuple-element.73), channel_id=1, source_target_pairs={{0,8},{8,16},{16,24},{24,32},{32,40},{40,48},{48,56},{56,64},{64,7... | collective-permute-start | bytes 549128 | tf_op jit(solution)/shard_map/ppermute | solution.py:21
  30.0 11.2 %collective-permute-start.1 = (f32[11,4,1040]{2,1,0:T(4,128)S(1)}, f32[11,4,1040]{2,1,0:T(4,128)S(1)}, u32[]{:S(2)}, u32[]{:S(2)}) collective-permute-start(f32[11,4,1040]{2,1,0:T(4,128)S(1)} %get-tuple-element.74), channel_id=1, source_target_pairs={{8,0},{16,8},{24,16},{32,24},{40,32},{48,40},{56,48},{64,56},{72,6... | collective-permute-start | bytes 549128 | tf_op jit(solution)/shard_map/ppermute | solution.py:23
  41.4 1.3 %copy-start.14 = (f32[11,40,1040]{2,1,0:T(8,128)}, f32[11,40,1040]{2,1,0:T(8,128)S(1)}, u32[]{:S(2)}) copy-start(f32[11,40,1040]{2,1,0:T(8,128)S(1)} %pad_maximum_fusion.1) | copy-start | bytes 5491204
  42.8 11.6 %copy-start.8 = (f32[40,1040]{1,0:T(8,128)}, f32[40,1040]{1,0:T(8,128)S(1)}, u32[]{:S(2)}) copy-start(f32[40,1040]{1,0:T(8,128)S(1)} %get-tuple-element.62) | copy-start | bytes 499204
  42.8 11.6 %copy-start.11 = (f32[40,1040]{1,0:T(8,128)}, f32[40,1040]{1,0:T(8,128)S(1)}, u32[]{:S(2)}) copy-start(f32[40,1040]{1,0:T(8,128)S(1)} %get-tuple-element.60) | copy-start | bytes 499204
  42.8 11.6 %copy-start.19 = (f32[40,1040]{1,0:T(8,128)}, f32[40,1040]{1,0:T(8,128)S(1)}, u32[]{:S(2)}) copy-start(f32[40,1040]{1,0:T(8,128)S(1)} %get-tuple-element.58) | copy-start | bytes 499204
  42.8 16.1 %copy-start.5 = (f32[40,1040]{1,0:T(8,128)}, f32[40,1040]{1,0:T(8,128)S(1)}, u32[]{:S(2)}) copy-start(f32[40,1040]{1,0:T(8,128)S(1)} %get-tuple-element.61) | copy-start | bytes 499204
  42.9 31.4 %all-to-all-start.1 = ((f32[8,2,32,1040]{3,2,1,0:T(8,128)}), f32[8,2,32,1040]{3,2,1,0:T(8,128)}, u32[]{:S(2)}, u32[]{:S(2)}) async-start(f32[8,2,32,1040]{3,2,1,0:T(8,128)} %pad_maximum_fusion), calls=%async_computation.1 | async-start | bytes 4718592 | tf_op jit(solution)/shard_map/all_to_all | solution.py:137
  58.3 1.2 copy-start.9
  58.3 1.4 %copy-start.12 = (f32[40,1040]{1,0:T(8,128)S(1)}, f32[40,1040]{1,0:T(8,128)}, u32[]{:S(2)}) copy-start(f32[40,1040]{1,0:T(8,128)} %copy-done.11) | copy-start | bytes 499204
  58.3 1.6 %copy-start.20 = (f32[40,1040]{1,0:T(8,128)S(1)}, f32[40,1040]{1,0:T(8,128)}, u32[]{:S(2)}) copy-start(f32[40,1040]{1,0:T(8,128)} %copy-done.19) | copy-start | bytes 499204
  65.5 1.6 %copy-start.6 = (f32[40,1040]{1,0:T(8,128)S(1)}, f32[40,1040]{1,0:T(8,128)}, u32[]{:S(2)}) copy-start(f32[40,1040]{1,0:T(8,128)} %copy-done.5) | copy-start | bytes 499204
  78.7 33.5 %all-to-all-start.2 = ((f32[8,32,1024]{2,1,0:T(8,128)}), f32[8,32,1024]{2,1,0:T(8,128)}, u32[]{:S(2)}, u32[]{:S(2)}) async-start(f32[8,32,1024]{2,1,0:T(8,128)} %get-tuple-element.40), calls=%async_computation.2 | async-start | bytes 2097152 | tf_op jit(solution)/shard_map/all_to_all | solution.py:154
  83.4 2.4 %copy-start.16 = (f32[8,40,1040]{2,1,0:T(8,128)S(1)}, f32[8,40,1040]{2,1,0:T(8,128)}, u32[]{:S(2)}) copy-start(f32[8,40,1040]{2,1,0:T(8,128)} %get-tuple-element.53) | copy-start | bytes 3993604
  85.8 2.8 %copy-start.7 = (f32[40,1040]{1,0:T(8,128)S(1)}, f32[40,1040]{1,0:T(8,128)}, u32[]{:S(2)}) copy-start(f32[40,1040]{1,0:T(8,128)} %copy-done.5) | copy-start | bytes 499204
  85.8 2.8 %copy-start.10 = (f32[40,1040]{1,0:T(8,128)S(1)}, f32[40,1040]{1,0:T(8,128)}, u32[]{:S(2)}) copy-start(f32[40,1040]{1,0:T(8,128)} %copy-done.8) | copy-start | bytes 499204
  85.9 2.8 %copy-start.13 = (f32[40,1040]{1,0:T(8,128)S(1)}, f32[40,1040]{1,0:T(8,128)}, u32[]{:S(2)}) copy-start(f32[40,1040]{1,0:T(8,128)} %copy-done.11) | copy-start | bytes 499204
  85.9 2.8 %copy-start.21 = (f32[40,1040]{1,0:T(8,128)S(1)}, f32[40,1040]{1,0:T(8,128)}, u32[]{:S(2)}) copy-start(f32[40,1040]{1,0:T(8,128)} %broadcast_multiply_fusion.2) | copy-start | bytes 499204
  88.7 1.4 %copy-start.1 = (f32[8,40,1040]{2,1,0:T(8,128)S(1)}, f32[8,40,1040]{2,1,0:T(8,128)}, u32[]{:S(2)}) copy-start(f32[8,40,1040]{2,1,0:T(8,128)} %copy-done) | copy-start | bytes 3993604
  88.7 1.8 %copy-start.15 = (f32[8,40,1040]{2,1,0:T(8,128)S(1)}, f32[8,40,1040]{2,1,0:T(8,128)}, u32[]{:S(2)}) copy-start(f32[8,40,1040]{2,1,0:T(8,128)} %get-tuple-element.55) | copy-start | bytes 3993604
  93.2 1.4 %copy-start.3 = (f32[8,40,1040]{2,1,0:T(8,128)S(1)}, f32[8,40,1040]{2,1,0:T(8,128)}, u32[]{:S(2)}) copy-start(f32[8,40,1040]{2,1,0:T(8,128)} %copy-done.2) | copy-start | bytes 3993604
  93.2 1.8 %copy-start.17 = (f32[8,40,1040]{2,1,0:T(8,128)S(1)}, f32[8,40,1040]{2,1,0:T(8,128)}, u32[]{:S(2)}) copy-start(f32[8,40,1040]{2,1,0:T(8,128)} %get-tuple-element.57) | copy-start | bytes 3993604
  93.3 2.1 %copy-start.18 = (f32[8,32,1040]{2,1,0:T(8,128)S(1)}, f32[8,32,1040]{2,1,0:T(8,128)}, u32[]{:S(2)}) copy-start(f32[8,32,1040]{2,1,0:T(8,128)} %get-tuple-element.41) | copy-start | bytes 3194884
  99.1 5.6 %collective-permute-start.2 = (f32[4,1040]{1,0:T(4,128)S(1)}, f32[4,1040]{1,0:T(4,128)S(1)}, u32[]{:S(2)}, u32[]{:S(2)}) collective-permute-start(f32[4,1040]{1,0:T(4,128)S(1)} %get-tuple-element.98), channel_id=1, source_target_pairs={{8,0},{16,8},{24,16},{32,24},{40,32},{48,40},{56,48},{64,56},{72,6... | collective-permute-start | bytes 49928 | tf_op jit(solution)/shard_map/ppermute | solution.py:149
  102.8 9.3 %collective-permute-start.3 = (f32[4,1040]{1,0:T(4,128)S(1)}, f32[4,1040]{1,0:T(4,128)S(1)}, u32[]{:S(2)}, u32[]{:S(2)}) collective-permute-start(f32[4,1040]{1,0:T(4,128)S(1)} %get-tuple-element.97), channel_id=1, source_target_pairs={{0,8},{8,16},{16,24},{24,32},{32,40},{40,48},{48,56},{56,64},{64,7... | collective-permute-start | bytes 49928 | tf_op jit(solution)/shard_map/ppermute | solution.py:150
  113.3 15.9 %all-to-all-start.3 = ((f32[8,32,1024]{2,1,0:T(8,128)}), f32[8,32,1024]{2,1,0:T(8,128)S(1)}, u32[]{:S(2)}, u32[]{:S(2)}) async-start(f32[8,32,1024]{2,1,0:T(8,128)} %broadcast_in_dim.57), calls=%async_computation.3 | async-start | bytes 2097152 | tf_op jit(solution)/shard_map/all_to_all | solution.py:157
  (2 other events, 2.3 us)

commit v8 on v7

--- a/solution.py
+++ b/solution.py
@@ -144,6 +144,8 @@
     )
     interior, adjoint = scans(fine_ends, old, pair, begin, width)
     (grad_rows,) = pullback(adjoint)
+    new_end = lax.all_to_all(interior, "tm", 0, 2, tiled=True)
+    new_end, grad_rows = lax.optimization_barrier((new_end, grad_rows))
     count = lax.axis_size("space")
     ends = count - 1
     from_below = lax.ppermute(grad_rows[:STEPS], "space", [((i + 1) % count, i) for i in range(ends)])
@@ -151,7 +153,6 @@
     grad_window = grad_rows[STEPS:-STEPS]
     grad_window = grad_window.at[-STEPS:].add(from_below).at[:STEPS].add(from_above)
 
-    new_end = lax.all_to_all(interior, "tm", 0, 2, tiled=True)
     own = grad_window[:, HALO : HALO + width]
     copies = jnp.broadcast_to(own[None], (blocks,) + own.shape)
     gradient = lax.all_to_all(copies, "tm", 0, 2, tiled=True)[0]

time: 131 us -> 133 us (1.015)
  blocking collectives: 0 us -> 15.7 us
  waiting for transfers between devices: 25.3 us -> 17.6 us
  starting transfers between devices: 38.9 us -> 33 us
    all_to_all x0 -> x1, blocking collectives: none -> 15.7 us  [on_device(): gradient = lax.all_to_all(copies, 'tm', 0, 2, tiled=True)[0]]
    all_to_all x1 -> x0, waiting for transfers between devices: 7.73 us -> none  [on_device(): gradient = lax.all_to_all(copies, 'tm', 0, 2, tiled=True)[0]]
    all_to_all x1 -> x0, starting transfers between devices: 5.9 us -> none  [on_device(): gradient = lax.all_to_all(copies, 'tm', 0, 2, tiled=True)[0]]
  transfers between devices with their start and end apart: 8 -> 7, of which waited for: 6 -> 5; matrix products, arithmetic and copies ran while one was open for 36% -> 34% of each run, Pallas kernels for 0% -> 0%
where the time goes in v8:
time: 133 us; the launch traced here: 131 us
  other arithmetic  35.2 us (26%)
  starting transfers between devices  33 us (25%)
  local copies, waits for them, and re-layouts  24.4 us (18%)
  waiting for transfers between devices  17.6 us (13%)
  blocking collectives  15.7 us (12%)
  Pallas kernels  4.38 us (3%)
    all_to_all x1, blocking collectives, on_device(): gradient = lax.all_to_all(copies, 'tm', 0, 2, tiled=True)[0]  15.7 us
    select_n x4, other arithmetic, fine(): jnp.where(inside, advance(field, kappa, along_rows, along_cols), 0.0)  12 us
    unnamed x56, local copies, waits for them, and re-layouts  9.53 us
    reduce_sum x3, other arithmetic, advance(): return centre + time_step * (kappa * spread - transport)  9.09 us
    ppermute x1, starting transfers between devices, with_halo(): lax.ppermute(head, axis, [((i + 1) % count, i) for i in range(ends)])  7.86 us
    ppermute x1, waiting for transfers between devices, on_device(): lax.ppermute(grad_rows[-STEPS:], 'space', [(i, (i + 1) % count) for i in...  7.34 us
    all_to_all x1, starting transfers between devices, on_device(): pair = lax.all_to_all(pair, 'tm', 0, 0, tiled=True)  6.8 us
    all_to_all x1, starting transfers between devices, to_blocks(): return lax.all_to_all(send_windows(x), 'tm', 0, 0, tiled=True)  6.06 us
  transfers between devices with their start and end apart: 7, of which 5 were waited for; matrix products, arithmetic and copies ran while one was open for 34% of the time, Pallas kernels for 0%

profile of v8, /device:TPU:160, one launch (start us, length us, event | category | flops | bytes accessed | tf_op | source)
XLA Modules:
  0.0 131.4 jit_solution(11693098049423568921)
XLA Ops:
  0.6 1.8 %copy.22 = f32[4,8,8,1024]{3,2,1,0:T(8,128)S(1)} copy(f32[4,8,8,1024]{3,1,2,0:T(8,128)} %bitcast.59) | data formatting | bytes 2097152
  3.2 1.4 %concatenate.19 = f32[8,32,1040]{2,1,0:T(8,128)} concatenate(f32[8,32,8]{2,1,0:T(8,128)S(1)} %pad.155, f32[8,32,1024]{2,1,0:T(8,128)S(1)} %bitcast.52, f32[8,32,8]{2,1,0:T(8,128)S(1)} %pad.156), dimensions={2} | concatenate | bytes 2129920 | tf_op jit(solution)/shard_map/concatenate | solution.py:114
  4.7 6.1 %all-to-all-start = ((f32[8,32,1040]{2,1,0:T(8,128)}), f32[8,32,1040]{2,1,0:T(8,128)S(1)}, u32[]{:S(2)}, u32[]{:S(2)}) async-start(f32[8,32,1040]{2,1,0:T(8,128)} %concatenate.19), calls=%async_computation | async-start | bytes 2359296 | tf_op jit(solution)/shard_map/all_to_all | solution.py:117
  15.6 2.1 %concatenate.22 = f32[8,32,1040]{2,1,0:T(8,128)} concatenate(f32[8,32,8]{2,1,0:T(8,128)} %pad.159, f32[8,32,1024]{2,1,0:T(8,128)S(1)} %bitcast.48, f32[8,32,8]{2,1,0:T(8,128)S(1)} %pad.160), dimensions={2} | concatenate | bytes 2129920 | tf_op jit(solution)/shard_map/concatenate | solution.py:114
  17.7 2.2 %concatenate.23 = f32[8,32,1040]{2,1,0:T(8,128)} concatenate(f32[8,32,8]{2,1,0:T(8,128)} %pad.161, f32[8,32,1024]{2,1,0:T(8,128)S(1)} %bitcast.50, f32[8,32,8]{2,1,0:T(8,128)} %pad.162), dimensions={2} | concatenate | bytes 2129920 | tf_op jit(solution)/shard_map/concatenate | solution.py:114
  19.9 3.3 %pad_maximum_fusion = f32[8,2,32,1040]{3,2,1,0:T(8,128)} fusion(f32[8,1,32,1040]{3,2,1,0:T(8,128)} %bitcast.54, f32[8,1,32,1040]{3,2,1,0:T(8,128)} %bitcast.53), kind=kLoop, calls=%fused_computation | loop fusion | flops 532480 | bytes 4259840 | tf_op jit(solution)/shard_map/stack | solution.py:120
  23.2 3.1 %all-to-all-done.old_ref = f32[8,32,1040]{2,1,0:T(8,128)S(1)} async-done(((f32[8,32,1040]{2,1,0:T(8,128)}), f32[8,32,1040]{2,1,0:T(8,128)S(1)}, u32[]{:S(2)}, u32[]{:S(2)}) %all-to-all-start) | async-done | bytes 1064992 | tf_op jit(solution)/shard_map/all_to_all | solution.py:117
  26.5 1.4 %pad_dynamic-slice_fusion = f32[2,32,1040]{2,1,0:T(8,128)S(1)} fusion(s32[]{:T(128)S(6)} %select_n.31, f32[2,32,8192]{2,1,0:T(8,128)} %param.13), kind=kLoop, calls=%fused_computation.1 | loop fusion | bytes 2363396 | tf_op jit(solution)/shard_map/dynamic_slice | solution.py:64
  28.0 2.1 %collective-permute-start = (f32[11,4,1040]{2,1,0:T(4,128)S(1)}, f32[11,4,1040]{2,1,0:T(4,128)S(1)}, u32[]{:S(2)}, u32[]{:S(2)}) collective-permute-start(f32[11,4,1040]{2,1,0:T(4,128)S(1)} %get-tuple-element.77), channel_id=1, source_target_pairs={{0,8},{8,16},{16,24},{24,32},{32,40},{40,48},{48,56},{56,64},{64,7... | collective-permute-start | bytes 549128 | tf_op jit(solution)/shard_map/ppermute | solution.py:21
  30.0 7.9 %collective-permute-start.1 = (f32[11,4,1040]{2,1,0:T(4,128)S(1)}, f32[11,4,1040]{2,1,0:T(4,128)S(1)}, u32[]{:S(2)}, u32[]{:S(2)}) collective-permute-start(f32[11,4,1040]{2,1,0:T(4,128)S(1)} %get-tuple-element.78), channel_id=1, source_target_pairs={{8,0},{16,8},{24,16},{32,24},{40,32},{48,40},{56,48},{64,56},{72,6... | collective-permute-start | bytes 549128 | tf_op jit(solution)/shard_map/ppermute | solution.py:23
  38.7 1.8 %collective-permute-done = f32[11,4,1040]{2,1,0:T(4,128)S(1)} collective-permute-done((f32[11,4,1040]{2,1,0:T(4,128)S(1)}, f32[11,4,1040]{2,1,0:T(4,128)S(1)}, u32[]{:S(2)}, u32[]{:S(2)}) %collective-permute-start) | collective-permute-done | bytes 183072 | tf_op jit(solution)/shard_map/ppermute | solution.py:21
  41.5 1.2 copy-done.14
  42.9 6.8 %all-to-all-start.1 = ((f32[8,2,32,1040]{3,2,1,0:T(8,128)}), f32[8,2,32,1040]{3,2,1,0:T(8,128)}, u32[]{:S(2)}, u32[]{:S(2)}) async-start(f32[8,2,32,1040]{3,2,1,0:T(8,128)} %pad_maximum_fusion), calls=%async_computation.1 | async-start | bytes 4718592 | tf_op jit(solution)/shard_map/all_to_all | solution.py:137
  50.3 3.5 %fusion.24 = (f32[8,40,1040]{2,1,0:T(8,128)S(1)}, f32[8,40,1040]{2,1,0:T(8,128)}) fusion(f32[8,40,1040]{2,1,0:T(8,128)S(1)} %slice.216, f32[40,1040]{1,0:T(8,128)S(1)} %get-tuple-element.64, f32[40,1040]{1,0:T(8,128)S(1)} %get-tuple-element.65, f32[40,1040]{1,0:T(8,128)S(1)} %get-tuple-element.63, f32[40,1040]{1,0:T(8,128)S(1)} %get-tuple-element.66, ...), kind=kLoop, calls=%fused_computation.60 | loop fusion | flops 6988800 | bytes 11523200 | tf_op jit(solution)/shard_map/jvp(jit(_where))/select_n | solution.py:55
  54.9 3.4 %fusion.39 = (f32[8,40,1040]{2,1,0:T(8,128)S(1)}, f32[8,40,1040]{2,1,0:T(8,128)}) fusion(f32[8,40,1040]{2,1,0:T(8,128)S(1)} %get-tuple-element.60, f32[40,1040]{1,0:T(8,128)S(1)} %get-tuple-element.64, f32[40,1040]{1,0:T(8,128)S(1)} %get-tuple-element.65, f32[40,1040]{1,0:T(8,128)S(1)} %get-tuple-element.63, f32[40,1040]{1,0:T(8,128)S(1)} %get-tuple-element.66, ...), kind=kLoop, calls=%fused_computation.75 | loop fusion | flops 6988800 | bytes 11523200 | tf_op jit(solution)/shard_map/jvp(jit(_where))/select_n | solution.py:55
  59.9 3.4 %fusion.55 = (f32[8,40,1040]{2,1,0:T(8,128)S(1)}, f32[8,40,1040]{2,1,0:T(8,128)}) fusion(f32[8,40,1040]{2,1,0:T(8,128)S(1)} %get-tuple-element.58, f32[40,1040]{1,0:T(8,128)S(1)} %copy-done.12, f32[40,1040]{1,0:T(8,128)S(1)} %get-tuple-element.65, f32[40,1040]{1,0:T(8,128)S(1)} %get-tuple-element.63, f32[40,1040]{1,0:T(8,128)S(1)} %copy-done.9, ...), kind=kLoop, calls=%fused_computation.91 | loop fusion | flops 6988800 | bytes 11523200 | tf_op jit(solution)/shard_map/jvp(jit(_where))/select_n | solution.py:55
  63.9 1.6 %broadcast_multiply_fusion.2 = f32[40,1040]{1,0:T(8,128)} fusion(f32[11,40,1040]{2,1,0:T(8,128)} %copy-done.14), kind=kLoop, calls=%fused_computation.205 | loop fusion | flops 41600 | bytes 332800 | tf_op jit(solution)/shard_map/transpose(jvp())/mul | solution.py:50
  65.5 1.6 %fusion.84 = f32[8,40,1040]{2,1,0:T(8,128)S(1)} fusion(f32[8,42,1042]{2,1,0:T(8,128)S(1)} %pad_add_fusion), kind=kLoop, calls=%fused_computation.133 | loop fusion | flops 1664000 | bytes 7987200 | tf_op jit(solution)/shard_map/jvp()/sub | solution.py:38
  68.0 1.8 %fusion.97.fine_ref = f32[8,32,1040]{2,1,0:T(8,128)} fusion(f32[8,40,1040]{2,1,0:T(8,128)S(1)} %get-tuple-element.56, f32[8,40,1040]{2,1,0:T(8,128)S(1)} %fusion.84, f32[8,40,1040]{2,1,0:T(8,128)S(1)} %get-tuple-element.84, f32[8,40,1040]{2,1,0:T(8,128)S(1)} %get-tuple-element.85, f32[8,40,1040]{2,1,0:T(8,128)S(1)} %get-tuple-element.83, ...), kind=kLoop, calls=%fused_computation.180 | loop fusion | flops 2129920 | bytes 6689280 | tf_op jit(solution)/shard_map/jvp(jit(_where))/select_n | solution.py:55
  69.7 4.6 %all-to-all-done.1.pair_ref = f32[8,2,32,1040]{3,2,1,0:T(8,128)} async-done(((f32[8,2,32,1040]{3,2,1,0:T(8,128)}), f32[8,2,32,1040]{3,2,1,0:T(8,128)}, u32[]{:S(2)}, u32[]{:S(2)}) %all-to-all-start.1) | async-done | bytes 2129952 | tf_op jit(solution)/shard_map/all_to_all | solution.py:137
  74.3 4.4 %shard_map.77 = (f32[8,32,1024]{2,1,0:T(8,128)}, f32[8,32,1040]{2,1,0:T(8,128)}) custom-call(f32[8,32,1040]{2,1,0:T(8,128)} %fusion.97.fine_ref, f32[8,32,1040]{2,1,0:T(8,128)} %copy-done.4, f32[8,2,32,1040]{3,2,1,0:T(8,128)} %all-to-all-done.1.pair_ref, f32[32,1040]{1,0:T(8,128)} %pad_dynamic-slice_fusion.1.begin_ref), custom_call_target="tpu_custom_call" | custom-call | tf_op jit(solution)/shard_map/pallas_call | solution.py:91
  78.7 4.7 %all-to-all-start.2 = ((f32[8,32,1024]{2,1,0:T(8,128)}), f32[8,32,1024]{2,1,0:T(8,128)}, u32[]{:S(2)}, u32[]{:S(2)}) async-start(f32[8,32,1024]{2,1,0:T(8,128)} %get-tuple-element.42), calls=%async_computation.2 | async-start | bytes 2097152 | tf_op jit(solution)/shard_map/all_to_all | solution.py:147
  83.4 2.4 %fusion.96 = (f32[8,40,1040]{2,1,0:T(8,128)S(1)}, f32[8,40,1040]{2,1,0:T(8,128)S(1)}, f32[8,40,1040]{2,1,0:T(8,128)S(1)}, f32[8,40,1040]{2,1,0:T(8,128)S(1)}, f3...) fusion(f32[8,32,1040]{2,1,0:T(8,128)} %get-tuple-element.43, ...), kind=kLoop, calls=%fused_computation.178 | loop fusion | flops 5990400 | bytes 11256960 | tf_op jit(solution)/shard_map/transpose(jvp())/mul | solution.py:48
  85.9 2.8 %multiply_reduce_fusion.1 = (f32[40,1040]{1,0:T(8,128)S(1)}, f32[8,40,1040]{2,1,0:T(8,128)S(1)}) fusion(f32[8,40,1040]{2,1,0:T(8,128)S(1)} %copy-done.16, f32[8,40,1040]{2,1,0:T(8,128)S(1)} %get-tuple-element.56, f32[8,40,1040]{2,1,0:T(8,128)S(1)} %get-tuple-element.93, f32[8,40,1040]{2,1,0:T(8,128)S(1)} %get-tuple-element.94, ...), kind=kLoop, calls=%fused_computation.157 | loop fusion | flops 6281600 | bytes 13520000 | tf_op jit(solution)/shard_map/transpose(jvp())/reduce_sum | solution.py:50
  90.5 2.7 %multiply_reduce_fusion = (f32[40,1040]{1,0:T(8,128)S(1)}, f32[8,40,1040]{2,1,0:T(8,128)S(1)}) fusion(f32[8,40,1040]{2,1,0:T(8,128)S(1)} %copy-done.15, f32[8,40,1040]{2,1,0:T(8,128)S(1)} %copy-done.1, f32[8,40,1040]{2,1,0:T(8,128)S(1)} %get-tuple-element.82, f32[8,40,1040]{2,1,0:T(8,128)S(1)} %get-tuple-element.81, ...), kind=kLoop, calls=%fused_computation.154 | loop fusion | flops 6281600 | bytes 13520000 | tf_op jit(solution)/shard_map/transpose(jvp())/reduce_sum | solution.py:50
  95.4 3.6 %multiply_reduce_fusion.2 = (f32[40,1040]{1,0:T(8,128)S(1)}, f32[40,1040]{1,0:T(8,128)S(1)}) fusion(f32[8,32,1040]{2,1,0:T(8,128)S(1)} %copy-done.18, pred[40,1040]{1,0:T(8,128)(4,1)S(1)} %and_and_fusion, f32[8,40,1040]{2,1,0:T(8,128)S(1)} %copy-done.17, f32[8,40,1040]{2,1,0:T(8,128)S(1)} %copy-done.3, f32[8,40,1040]{2,1,0:T(8,128)S(1)} %get-tuple-element.80, ...), kind=kLoop, calls=%fused_computation.160 | loop fusion | flops 9235200 | bytes 20076160 | tf_op jit(solution)/shard_map/transpose(jvp())/reduce_sum | solution.py:50
  99.1 2.3 %copy.21 = f32[1,8,4,8,1024]{4,3,1,2,0:T(8,128)} copy(f32[1,8,4,8,1024]{4,3,2,1,0:T(8,128)} %bitcast.17) | data formatting | bytes 2097152 | tf_op jit(solution)/shard_map/all_to_all | solution.py:147
  101.4 3.6 %collective-permute-start.2 = (f32[4,1040]{1,0:T(4,128)S(1)}, f32[4,1040]{1,0:T(4,128)S(1)}, u32[]{:S(2)}, u32[]{:S(2)}) collective-permute-start(f32[4,1040]{1,0:T(4,128)S(1)} %get-tuple-element.102), channel_id=1, source_target_pairs={{8,0},{16,8},{24,16},{32,24},{40,32},{48,40},{56,48},{64,56},{72,6... | collective-permute-start | bytes 49928 | tf_op jit(solution)/shard_map/ppermute | solution.py:151
  105.1 1.9 %collective-permute-start.3 = (f32[4,1040]{1,0:T(4,128)S(1)}, f32[4,1040]{1,0:T(4,128)S(1)}, u32[]{:S(2)}, u32[]{:S(2)}) collective-permute-start(f32[4,1040]{1,0:T(4,128)S(1)} %get-tuple-element.101), channel_id=1, source_target_pairs={{0,8},{8,16},{16,24},{24,32},{32,40},{40,48},{48,56},{56,64},{64,7... | collective-permute-start | bytes 49928 | tf_op jit(solution)/shard_map/ppermute | solution.py:152
  107.0 7.3 %collective-permute-done.3 = f32[4,1040]{1,0:T(4,128)S(1)} collective-permute-done((f32[4,1040]{1,0:T(4,128)S(1)}, f32[4,1040]{1,0:T(4,128)S(1)}, u32[]{:S(2)}, u32[]{:S(2)}) %collective-permute-start.3) | collective-permute-done | bytes 16672 | tf_op jit(solution)/shard_map/ppermute | solution.py:152
  114.6 15.7 %all_to_all.43 = f32[8,32,1024]{2,1,0:T(8,128)S(1)} all-to-all(f32[8,32,1024]{2,1,0:T(8,128)S(1)} %broadcast_in_dim.57), channel_id=1, replica_groups=mesh['space'=32,'tm'=8] {'tm'}, dimensions={0} | all-to-all | bytes 2097152 | tf_op jit(solution)/shard_map/all_to_all | solution.py:158
  130.3 1.1 copy.25
  (94 shorter events, 16.6 us)
Async XLA Ops:
  4.7 6.2 %copy-start.22 = (f32[1,32,8192]{2,1,0:T(8,128)S(1)}, f32[1,32,8192]{2,1,0:T(8,128)}, u32[]{:S(2)}) copy-start(f32[1,32,8192]{2,1,0:T(8,128)} %param.14) | copy-start | bytes 3145732
  4.7 21.7 %all-to-all-start = ((f32[8,32,1040]{2,1,0:T(8,128)}), f32[8,32,1040]{2,1,0:T(8,128)S(1)}, u32[]{:S(2)}, u32[]{:S(2)}) async-start(f32[8,32,1040]{2,1,0:T(8,128)} %concatenate.19), calls=%async_computation | async-start | bytes 2359296 | tf_op jit(solution)/shard_map/all_to_all | solution.py:117
  11.5 1.4 %copy-start.23 = (f32[1,32,8192]{2,1,0:T(8,128)S(1)}, f32[1,32,8192]{2,1,0:T(8,128)}, u32[]{:S(2)}) copy-start(f32[1,32,8192]{2,1,0:T(8,128)} %param.15) | copy-start | bytes 3145732
  19.9 6.5 %copy-start.24 = (f32[32,8192]{1,0:T(8,128)S(1)}, f32[32,8192]{1,0:T(8,128)}, u32[]{:S(2)}) copy-start(f32[32,8192]{1,0:T(8,128)} %param.12) | copy-start | bytes 3145732
  26.4 14.9 %copy-start.4 = (f32[8,32,1040]{2,1,0:T(8,128)}, f32[8,32,1040]{2,1,0:T(8,128)S(1)}, u32[]{:S(2)}) copy-start(f32[8,32,1040]{2,1,0:T(8,128)S(1)} %all-to-all-done.old_ref) | copy-start | bytes 3194884
  27.9 10.0 %copy-start.25 = (f32[32,8192]{1,0:T(8,128)S(1)}, f32[32,8192]{1,0:T(8,128)}, u32[]{:S(2)}) copy-start(f32[32,8192]{1,0:T(8,128)} %param.10) | copy-start | bytes 3145732
  28.0 12.5 %collective-permute-start = (f32[11,4,1040]{2,1,0:T(4,128)S(1)}, f32[11,4,1040]{2,1,0:T(4,128)S(1)}, u32[]{:S(2)}, u32[]{:S(2)}) collective-permute-start(f32[11,4,1040]{2,1,0:T(4,128)S(1)} %get-tuple-element.77), channel_id=1, source_target_pairs={{0,8},{8,16},{16,24},{24,32},{32,40},{40,48},{48,56},{56,64},{64,7... | collective-permute-start | bytes 549128 | tf_op jit(solution)/shard_map/ppermute | solution.py:21
  30.0 11.2 %collective-permute-start.1 = (f32[11,4,1040]{2,1,0:T(4,128)S(1)}, f32[11,4,1040]{2,1,0:T(4,128)S(1)}, u32[]{:S(2)}, u32[]{:S(2)}) collective-permute-start(f32[11,4,1040]{2,1,0:T(4,128)S(1)} %get-tuple-element.78), channel_id=1, source_target_pairs={{8,0},{16,8},{24,16},{32,24},{40,32},{48,40},{56,48},{64,56},{72,6... | collective-permute-start | bytes 549128 | tf_op jit(solution)/shard_map/ppermute | solution.py:23
  41.5 1.3 %copy-start.14 = (f32[11,40,1040]{2,1,0:T(8,128)}, f32[11,40,1040]{2,1,0:T(8,128)S(1)}, u32[]{:S(2)}) copy-start(f32[11,40,1040]{2,1,0:T(8,128)S(1)} %pad_maximum_fusion.1) | copy-start | bytes 5491204
  42.8 11.5 %copy-start.8 = (f32[40,1040]{1,0:T(8,128)}, f32[40,1040]{1,0:T(8,128)S(1)}, u32[]{:S(2)}) copy-start(f32[40,1040]{1,0:T(8,128)S(1)} %get-tuple-element.66) | copy-start | bytes 499204
  42.8 11.5 %copy-start.11 = (f32[40,1040]{1,0:T(8,128)}, f32[40,1040]{1,0:T(8,128)S(1)}, u32[]{:S(2)}) copy-start(f32[40,1040]{1,0:T(8,128)S(1)} %get-tuple-element.64) | copy-start | bytes 499204
  42.8 11.6 %copy-start.19 = (f32[40,1040]{1,0:T(8,128)}, f32[40,1040]{1,0:T(8,128)S(1)}, u32[]{:S(2)}) copy-start(f32[40,1040]{1,0:T(8,128)S(1)} %get-tuple-element.62) | copy-start | bytes 499204
  42.8 16.0 %copy-start.5 = (f32[40,1040]{1,0:T(8,128)}, f32[40,1040]{1,0:T(8,128)S(1)}, u32[]{:S(2)}) copy-start(f32[40,1040]{1,0:T(8,128)S(1)} %get-tuple-element.65) | copy-start | bytes 499204
  42.9 31.4 %all-to-all-start.1 = ((f32[8,2,32,1040]{3,2,1,0:T(8,128)}), f32[8,2,32,1040]{3,2,1,0:T(8,128)}, u32[]{:S(2)}, u32[]{:S(2)}) async-start(f32[8,2,32,1040]{3,2,1,0:T(8,128)} %pad_maximum_fusion), calls=%async_computation.1 | async-start | bytes 4718592 | tf_op jit(solution)/shard_map/all_to_all | solution.py:137
  58.3 1.2 copy-start
  58.3 1.2 copy-start.9
  58.3 1.4 %copy-start.12 = (f32[40,1040]{1,0:T(8,128)S(1)}, f32[40,1040]{1,0:T(8,128)}, u32[]{:S(2)}) copy-start(f32[40,1040]{1,0:T(8,128)} %copy-done.11) | copy-start | bytes 499204
  58.3 1.6 %copy-start.20 = (f32[40,1040]{1,0:T(8,128)S(1)}, f32[40,1040]{1,0:T(8,128)}, u32[]{:S(2)}) copy-start(f32[40,1040]{1,0:T(8,128)} %copy-done.19) | copy-start | bytes 499204
  65.5 1.6 %copy-start.6 = (f32[40,1040]{1,0:T(8,128)S(1)}, f32[40,1040]{1,0:T(8,128)}, u32[]{:S(2)}) copy-start(f32[40,1040]{1,0:T(8,128)} %copy-done.5) | copy-start | bytes 499204
  78.7 20.4 %all-to-all-start.2 = ((f32[8,32,1024]{2,1,0:T(8,128)}), f32[8,32,1024]{2,1,0:T(8,128)}, u32[]{:S(2)}, u32[]{:S(2)}) async-start(f32[8,32,1024]{2,1,0:T(8,128)} %get-tuple-element.42), calls=%async_computation.2 | async-start | bytes 2097152 | tf_op jit(solution)/shard_map/all_to_all | solution.py:147
  83.4 2.4 %copy-start.16 = (f32[8,40,1040]{2,1,0:T(8,128)S(1)}, f32[8,40,1040]{2,1,0:T(8,128)}, u32[]{:S(2)}) copy-start(f32[8,40,1040]{2,1,0:T(8,128)} %get-tuple-element.57) | copy-start | bytes 3993604
  85.8 2.8 %copy-start.7 = (f32[40,1040]{1,0:T(8,128)S(1)}, f32[40,1040]{1,0:T(8,128)}, u32[]{:S(2)}) copy-start(f32[40,1040]{1,0:T(8,128)} %copy-done.5) | copy-start | bytes 499204
  85.9 2.8 %copy-start.10 = (f32[40,1040]{1,0:T(8,128)S(1)}, f32[40,1040]{1,0:T(8,128)}, u32[]{:S(2)}) copy-start(f32[40,1040]{1,0:T(8,128)} %copy-done.8) | copy-start | bytes 499204
  85.9 2.8 %copy-start.13 = (f32[40,1040]{1,0:T(8,128)S(1)}, f32[40,1040]{1,0:T(8,128)}, u32[]{:S(2)}) copy-start(f32[40,1040]{1,0:T(8,128)} %copy-done.11) | copy-start | bytes 499204
  85.9 2.8 %copy-start.21 = (f32[40,1040]{1,0:T(8,128)S(1)}, f32[40,1040]{1,0:T(8,128)}, u32[]{:S(2)}) copy-start(f32[40,1040]{1,0:T(8,128)} %broadcast_multiply_fusion.2) | copy-start | bytes 499204
  88.7 1.4 %copy-start.1 = (f32[8,40,1040]{2,1,0:T(8,128)S(1)}, f32[8,40,1040]{2,1,0:T(8,128)}, u32[]{:S(2)}) copy-start(f32[8,40,1040]{2,1,0:T(8,128)} %copy-done) | copy-start | bytes 3993604
  88.7 1.8 %copy-start.15 = (f32[8,40,1040]{2,1,0:T(8,128)S(1)}, f32[8,40,1040]{2,1,0:T(8,128)}, u32[]{:S(2)}) copy-start(f32[8,40,1040]{2,1,0:T(8,128)} %get-tuple-element.59) | copy-start | bytes 3993604
  93.2 1.4 %copy-start.3 = (f32[8,40,1040]{2,1,0:T(8,128)S(1)}, f32[8,40,1040]{2,1,0:T(8,128)}, u32[]{:S(2)}) copy-start(f32[8,40,1040]{2,1,0:T(8,128)} %copy-done.2) | copy-start | bytes 3993604
  93.2 1.8 %copy-start.17 = (f32[8,40,1040]{2,1,0:T(8,128)S(1)}, f32[8,40,1040]{2,1,0:T(8,128)}, u32[]{:S(2)}) copy-start(f32[8,40,1040]{2,1,0:T(8,128)} %get-tuple-element.61) | copy-start | bytes 3993604
  93.3 2.1 %copy-start.18 = (f32[8,32,1040]{2,1,0:T(8,128)S(1)}, f32[8,32,1040]{2,1,0:T(8,128)}, u32[]{:S(2)}) copy-start(f32[8,32,1040]{2,1,0:T(8,128)} %get-tuple-element.43) | copy-start | bytes 3194884
  101.4 5.6 %collective-permute-start.2 = (f32[4,1040]{1,0:T(4,128)S(1)}, f32[4,1040]{1,0:T(4,128)S(1)}, u32[]{:S(2)}, u32[]{:S(2)}) collective-permute-start(f32[4,1040]{1,0:T(4,128)S(1)} %get-tuple-element.102), channel_id=1, source_target_pairs={{8,0},{16,8},{24,16},{32,24},{40,32},{48,40},{56,48},{64,56},{72,6... | collective-permute-start | bytes 49928 | tf_op jit(solution)/shard_map/ppermute | solution.py:151
  105.1 9.3 %collective-permute-start.3 = (f32[4,1040]{1,0:T(4,128)S(1)}, f32[4,1040]{1,0:T(4,128)S(1)}, u32[]{:S(2)}, u32[]{:S(2)}) collective-permute-start(f32[4,1040]{1,0:T(4,128)S(1)} %get-tuple-element.101), channel_id=1, source_target_pairs={{0,8},{8,16},{16,24},{24,32},{32,40},{40,48},{48,56},{56,64},{64,7... | collective-permute-start | bytes 49928 | tf_op jit(solution)/shard_map/ppermute | solution.py:152
  (1 other events, 1.1 us)

commit v9 on v7

--- a/solution.py
+++ b/solution.py
@@ -64,40 +64,39 @@
     return lax.dynamic_slice_in_dim(pad_cols(x), start, width, axis=x.ndim - 1)
 
 
-def scan_kernel(fine_ref, old_ref, pair_ref, begin_ref, ends_ref, adjoint_ref):
+def scan_kernel(fine_ref, old_ref, gain_ref, target_ref, begin_ref, ends_ref, adjoint_ref):
     slabs = fine_ref.shape[0]
     width = ends_ref.shape[2]
     begin = begin_ref[...]
     ends = []
     for slab in range(slabs):
-        carried = fine_ref[slab] - pair_ref[slab, 0] * old_ref[slab]
-        begin = pair_ref[slab, 0] * begin + carried
+        carried = fine_ref[slab] - gain_ref[slab] * old_ref[slab]
+        begin = gain_ref[slab] * begin + carried
         ends.append(begin)
         ends_ref[slab] = begin[:, HALO : HALO + width]
-    adjoint = ends[slabs - 1] - pair_ref[slabs - 1, 1]
+    adjoint = ends[slabs - 1] - target_ref[slabs - 1]
     adjoint_ref[slabs - 1] = adjoint
     for slab in range(slabs - 2, -1, -1):
-        adjoint = (ends[slab] - pair_ref[slab, 1]) + pair_ref[slab + 1, 0] * adjoint
+        adjoint = (ends[slab] - target_ref[slab]) + gain_ref[slab + 1] * adjoint
         adjoint_ref[slab] = adjoint
 
 
-def scans(fine_ends, old, pair, begin, width):
+def scans(fine_ends, old, gain, target, begin, width):
     slabs, rows, wide = fine_ends.shape
     tile = 8
     stacked = pl.BlockSpec((slabs, tile, wide), lambda i: (0, i, 0))
     inner = pl.BlockSpec((slabs, tile, width), lambda i: (0, i, 0))
-    both = pl.BlockSpec((slabs, 2, tile, wide), lambda i: (0, 0, i, 0))
     single = pl.BlockSpec((tile, wide), lambda i: (i, 0))
     return pl.pallas_call(
         scan_kernel,
         grid=(rows // tile,),
-        in_specs=[stacked, stacked, both, single],
+        in_specs=[stacked, stacked, stacked, stacked, single],
         out_specs=[inner, stacked],
         out_shape=[
             jax.ShapeDtypeStruct((slabs, rows, width), fine_ends.dtype),
             jax.ShapeDtypeStruct(fine_ends.shape, fine_ends.dtype),
         ],
-    )(fine_ends, old, pair, begin)
+    )(fine_ends, old, gain, target, begin)
 
 
 def on_device(start_state, old_starts, conductivity, velocity, coarse_gain, targets):
@@ -117,7 +116,13 @@
         return lax.all_to_all(send_windows(x), "tm", 0, 0, tiled=True)
 
     old = to_blocks(old_starts[0])
-    pair = jnp.stack([send_windows(coarse_gain[0]), send_windows(targets[0])], axis=1)
+    target_out = send_windows(targets[0])
+    pieces = [lax.dynamic_index_in_dim(target_out, block, 0, keepdims=False)]
+    for shift in range(1, blocks):
+        piece = lax.dynamic_index_in_dim(target_out, (block + shift) % blocks, 0, keepdims=False)
+        pieces.append(lax.ppermute(piece, "tm", [(i, (i + shift) % blocks) for i in range(blocks)]))
+    target = jnp.take(jnp.stack(pieces), (block - jnp.arange(blocks)) % blocks, axis=0)
+    gain_out = send_windows(coarse_gain[0])
     old, conductivity, velocity, start_state = lax.optimization_barrier(
         (old, conductivity, velocity, start_state)
     )
@@ -133,8 +138,8 @@
     slabs = old.shape[0]
     fields = jnp.concatenate([old, kappa[None], flow], axis=0)
     fields = with_halo(fields, "space", 1, STEPS)
-    fields, pair = lax.optimization_barrier((fields, pair))
-    pair = lax.all_to_all(pair, "tm", 0, 0, tiled=True)
+    fields, gain_out = lax.optimization_barrier((fields, gain_out))
+    gain = lax.all_to_all(gain_out, "tm", 0, 0, tiled=True)
     old_rows = fields[:slabs]
     kappa_rows = fields[slabs]
     flow_rows = fields[slabs + 1 :]
@@ -142,7 +147,7 @@
     fine_ends, pullback = jax.vjp(
         lambda k: fine(old_rows, k, flow_rows[0], flow_rows[1], inside), kappa_rows
     )
-    interior, adjoint = scans(fine_ends, old, pair, begin, width)
+    interior, adjoint = scans(fine_ends, old, gain, target, begin, width)
     (grad_rows,) = pullback(adjoint)
     count = lax.axis_size("space")
     ends = count - 1

time: 131 us -> 161 us (1.23)
  starting transfers between devices: 38.9 us -> 56.4 us
  waiting for transfers between devices: 25.3 us -> 32.5 us
  local copies, waits for them, and re-layouts: 25.3 us -> 32.4 us
  other arithmetic: 35.2 us -> 33.2 us
    ppermute x0 -> x7, waiting for transfers between devices: none -> 14.8 us  [on_device(): lax.ppermute(piece, 'tm', [(i, (i + shift) % blocks) for i in range(block...]
    ppermute x0 -> x7, starting transfers between devices: none -> 12.2 us  [on_device(): lax.ppermute(piece, 'tm', [(i, (i + shift) % blocks) for i in range(block...]
    unnamed x56 -> x66, local copies, waits for them, and re-layouts: 9.48 us -> 15.7 us
    all_to_all x1, waiting for transfers between devices: 4.58 us -> 0.01 us  [on_device(): gain = lax.all_to_all(gain_out, 'tm', 0, 0, tiled=True)]
    ppermute x1, starting transfers between devices: 3.62 us -> 7.21 us  [on_device(): lax.ppermute(grad_rows[:STEPS], 'space', [((i + 1) % count, i) for i in r...]
    another operation x1 -> x0, other arithmetic: 3.3 us -> none  [on_device(): jnp.stack([send_windows(coarse_gain[0]), send_windows(targets[0])], axis=1)]
    all_to_all x1, waiting for transfers between devices: 3.14 us -> 0.01 us  [to_blocks(): return lax.all_to_all(send_windows(x), 'tm', 0, 0, tiled=True)]
    gather x0 -> x1, local copies, waits for them, and re-layouts: none -> 1.89 us  [on_device(): jnp.take(jnp.stack(pieces), (block - jnp.arange(blocks)) % blocks, axis=0)]
  transfers between devices with their start and end apart: 8 -> 15, of which waited for: 6 -> 7; matrix products, arithmetic and copies ran while one was open for 36% -> 32% of each run, Pallas kernels for 0% -> 0%
where the time goes in v9:
time: 161 us; the launch traced here: 160 us
  starting transfers between devices  56.4 us (35%)
  other arithmetic  33.2 us (21%)
  waiting for transfers between devices  32.5 us (20%)
  local copies, waits for them, and re-layouts  32.4 us (20%)
  Pallas kernels  4.35 us (3%)
    unnamed x66, local copies, waits for them, and re-layouts  15.7 us
    ppermute x7, waiting for transfers between devices, on_device(): lax.ppermute(piece, 'tm', [(i, (i + shift) % blocks) for i in range(block...  14.8 us
    ppermute x7, starting transfers between devices, on_device(): lax.ppermute(piece, 'tm', [(i, (i + shift) % blocks) for i in range(block...  12.2 us
    select_n x4, other arithmetic, fine(): jnp.where(inside, advance(field, kappa, along_rows, along_cols), 0.0)  12.2 us
    reduce_sum x3, other arithmetic, advance(): return centre + time_step * (kappa * spread - transport)  9.09 us
    ppermute x1, starting transfers between devices, with_halo(): lax.ppermute(head, axis, [((i + 1) % count, i) for i in range(ends)])  7.86 us
    all_to_all x1, waiting for transfers between devices, on_device(): gradient = lax.all_to_all(copies, 'tm', 0, 2, tiled=True)[0]  7.73 us
    all_to_all x1, starting transfers between devices, on_device(): gain = lax.all_to_all(gain_out, 'tm', 0, 0, tiled=True)  7.44 us
  transfers between devices with their start and end apart: 15, of which 7 were waited for; matrix products, arithmetic and copies ran while one was open for 32% of the time, Pallas kernels for 0%

profile of v9, /device:TPU:160, one launch (start us, length us, event | category | flops | bytes accessed | tf_op | source)
XLA Modules:
  0.0 160.1 jit_solution(16874110963879702029)
XLA Ops:
  0.6 1.8 %copy.25 = f32[4,8,8,1024]{3,2,1,0:T(8,128)S(1)} copy(f32[4,8,8,1024]{3,1,2,0:T(8,128)} %bitcast.85) | data formatting | bytes 2097152
  4.6 6.1 %all-to-all-start = ((f32[8,32,1040]{2,1,0:T(8,128)}), f32[8,32,1040]{2,1,0:T(8,128)S(1)}, u32[]{:S(2)}, u32[]{:S(2)}) async-start(f32[8,32,1040]{2,1,0:T(8,128)} %concatenate.19), calls=%async_computation | async-start | bytes 2359296 | tf_op jit(solution)/shard_map/all_to_all | solution.py:116
  15.3 2.7 %collective-permute-start.8 = (f32[32,1040]{1,0:T(8,128)}, f32[32,1040]{1,0:T(8,128)S(1)}, u32[]{:S(2)}, u32[]{:S(2)}) collective-permute-start(f32[32,1040]{1,0:T(8,128)} %get-tuple-element.91), channel_id=1, source_target_pairs={{0,7},{1,0},{2,1},{3,2},{4,3},{5,4},{6,5},{7,6},{8,15},{9,8},{10,9... | collective-permute-start | bytes 399368 | tf_op jit(solution)/shard_map/ppermute | solution.py:123
  18.8 1.8 %collective-permute-start.6 = (f32[32,1040]{1,0:T(8,128)}, f32[32,1040]{1,0:T(8,128)S(1)}, u32[]{:S(2)}, u32[]{:S(2)}) collective-permute-start(f32[32,1040]{1,0:T(8,128)} %get-tuple-element.93), channel_id=1, source_target_pairs={{0,5},{1,6},{2,7},{3,0},{4,1},{5,2},{6,3},{7,4},{8,13},{9,14},{10,... | collective-permute-start | bytes 399368 | tf_op jit(solution)/shard_map/ppermute | solution.py:123
  21.1 1.8 %collective-permute-start.2 = (f32[32,1040]{1,0:T(8,128)}, f32[32,1040]{1,0:T(8,128)}, u32[]{:S(2)}, u32[]{:S(2)}) collective-permute-start(f32[32,1040]{1,0:T(8,128)} %get-tuple-element.97), channel_id=1, source_target_pairs={{0,1},{1,2},{2,3},{3,4},{4,5},{5,6},{6,7},{7,0},{8,9},{9,10},{10,1... | collective-permute-start | bytes 399368 | tf_op jit(solution)/shard_map/ppermute | solution.py:123
  26.0 8.1 %collective-permute-done.2 = f32[32,1040]{1,0:T(8,128)} collective-permute-done((f32[32,1040]{1,0:T(8,128)}, f32[32,1040]{1,0:T(8,128)}, u32[]{:S(2)}, u32[]{:S(2)}) %collective-permute-start.2) | collective-permute-done | bytes 133152 | tf_op jit(solution)/shard_map/ppermute | solution.py:123
  34.0 2.7 %collective-permute-start.3 = (f32[32,1040]{1,0:T(8,128)S(1)}, f32[32,1040]{1,0:T(8,128)S(1)}, u32[]{:S(2)}, u32[]{:S(2)}) collective-permute-start(f32[32,1040]{1,0:T(8,128)S(1)} %copy-done.27), channel_id=1, source_target_pairs={{0,2},{1,3},{2,4},{3,5},{4,6},{5,7},{6,0},{7,1},{8,10},{9,11},{10,... | collective-permute-start | bytes 399368 | tf_op jit(solution)/shard_map/ppermute | solution.py:123
  38.4 3.2 %collective-permute-done.3 = f32[32,1040]{1,0:T(8,128)S(1)} collective-permute-done((f32[32,1040]{1,0:T(8,128)S(1)}, f32[32,1040]{1,0:T(8,128)S(1)}, u32[]{:S(2)}, u32[]{:S(2)}) %collective-permute-start.3) | collective-permute-done | bytes 133152 | tf_op jit(solution)/shard_map/ppermute | solution.py:123
  41.6 1.9 %collective-permute-start.4 = (f32[32,1040]{1,0:T(8,128)S(1)}, f32[32,1040]{1,0:T(8,128)S(1)}, u32[]{:S(2)}, u32[]{:S(2)}) collective-permute-start(f32[32,1040]{1,0:T(8,128)S(1)} %copy-done.26), channel_id=1, source_target_pairs={{0,3},{1,4},{2,5},{3,6},{4,7},{5,0},{6,1},{7,2},{8,11},{9,12},{10,... | collective-permute-start | bytes 399368 | tf_op jit(solution)/shard_map/ppermute | solution.py:123
  44.1 3.5 %collective-permute-done.4 = f32[32,1040]{1,0:T(8,128)S(1)} collective-permute-done((f32[32,1040]{1,0:T(8,128)S(1)}, f32[32,1040]{1,0:T(8,128)S(1)}, u32[]{:S(2)}, u32[]{:S(2)}) %collective-permute-start.4) | collective-permute-done | bytes 133152 | tf_op jit(solution)/shard_map/ppermute | solution.py:123
  51.9 1.9 %gather_fusion = f32[8,32,1040]{2,1,0:T(8,128)S(1)} fusion(f32[8,32,1040]{2,1,0:T(8,128)} %bitcast_dynamic-update-slice_fusion, s32[1024]{0:T(1024)S(1)} %pad_clamp_fusion), kind=kCustom, calls=%fused_computation | custom fusion | bytes 2129952 | tf_op jit(solution)/shard_map/jit(_take)/gather | solution.py:124
  57.0 2.1 %collective-permute-start = (f32[11,4,1040]{2,1,0:T(4,128)S(1)}, f32[11,4,1040]{2,1,0:T(4,128)S(1)}, u32[]{:S(2)}, u32[]{:S(2)}) collective-permute-start(f32[11,4,1040]{2,1,0:T(4,128)S(1)} %get-tuple-element.73), channel_id=1, source_target_pairs={{0,8},{8,16},{16,24},{24,32},{32,40},{40,48},{48,56},{56,64},{64,7... | collective-permute-start | bytes 549128 | tf_op jit(solution)/shard_map/ppermute | solution.py:21
  59.1 7.9 %collective-permute-start.1 = (f32[11,4,1040]{2,1,0:T(4,128)S(1)}, f32[11,4,1040]{2,1,0:T(4,128)S(1)}, u32[]{:S(2)}, u32[]{:S(2)}) collective-permute-start(f32[11,4,1040]{2,1,0:T(4,128)S(1)} %get-tuple-element.74), channel_id=1, source_target_pairs={{8,0},{16,8},{24,16},{32,24},{40,32},{48,40},{56,48},{64,56},{72,6... | collective-permute-start | bytes 549128 | tf_op jit(solution)/shard_map/ppermute | solution.py:23
  67.7 1.8 %collective-permute-done = f32[11,4,1040]{2,1,0:T(4,128)S(1)} collective-permute-done((f32[11,4,1040]{2,1,0:T(4,128)S(1)}, f32[11,4,1040]{2,1,0:T(4,128)S(1)}, u32[]{:S(2)}, u32[]{:S(2)}) %collective-permute-start) | collective-permute-done | bytes 183072 | tf_op jit(solution)/shard_map/ppermute | solution.py:21
  71.9 7.4 %all-to-all-start.1 = ((f32[8,32,1040]{2,1,0:T(8,128)}), f32[8,32,1040]{2,1,0:T(8,128)}, u32[]{:S(2)}, u32[]{:S(2)}) async-start(f32[8,32,1040]{2,1,0:T(8,128)} %concatenate.22), calls=%async_computation.1 | async-start | bytes 2359296 | tf_op jit(solution)/shard_map/all_to_all | solution.py:142
  79.9 3.5 %fusion.24 = (f32[8,40,1040]{2,1,0:T(8,128)S(1)}, f32[8,40,1040]{2,1,0:T(8,128)}) fusion(f32[8,40,1040]{2,1,0:T(8,128)S(1)} %slice.214, f32[40,1040]{1,0:T(8,128)S(1)} %get-tuple-element.60, f32[40,1040]{1,0:T(8,128)S(1)} %get-tuple-element.61, f32[40,1040]{1,0:T(8,128)S(1)} %get-tuple-element.59, f32[40,1040]{1,0:T(8,128)S(1)} %get-tuple-element.62, ...), kind=kLoop, calls=%fused_computation.60 | loop fusion | flops 6988800 | bytes 11523200 | tf_op jit(solution)/shard_map/jvp(jit(_where))/select_n | solution.py:55
  84.5 3.4 %fusion.39 = (f32[8,40,1040]{2,1,0:T(8,128)S(1)}, f32[8,40,1040]{2,1,0:T(8,128)}) fusion(f32[8,40,1040]{2,1,0:T(8,128)S(1)} %get-tuple-element.56, f32[40,1040]{1,0:T(8,128)S(1)} %get-tuple-element.60, f32[40,1040]{1,0:T(8,128)S(1)} %get-tuple-element.61, f32[40,1040]{1,0:T(8,128)S(1)} %get-tuple-element.59, f32[40,1040]{1,0:T(8,128)S(1)} %get-tuple-element.62, ...), kind=kLoop, calls=%fused_computation.75 | loop fusion | flops 6988800 | bytes 11523200 | tf_op jit(solution)/shard_map/jvp(jit(_where))/select_n | solution.py:55
  89.6 3.5 %fusion.55 = (f32[8,40,1040]{2,1,0:T(8,128)S(1)}, f32[8,40,1040]{2,1,0:T(8,128)}) fusion(f32[8,40,1040]{2,1,0:T(8,128)S(1)} %get-tuple-element.54, f32[40,1040]{1,0:T(8,128)S(1)} %copy-done.12, f32[40,1040]{1,0:T(8,128)S(1)} %get-tuple-element.61, f32[40,1040]{1,0:T(8,128)S(1)} %get-tuple-element.59, f32[40,1040]{1,0:T(8,128)S(1)} %copy-done.9, ...), kind=kLoop, calls=%fused_computation.91 | loop fusion | flops 6988800 | bytes 11523200 | tf_op jit(solution)/shard_map/jvp(jit(_where))/select_n | solution.py:55
  95.2 1.6 %broadcast_multiply_fusion.2 = f32[40,1040]{1,0:T(8,128)} fusion(f32[11,40,1040]{2,1,0:T(8,128)} %copy-done.14), kind=kLoop, calls=%fused_computation.221 | loop fusion | flops 41600 | bytes 332800 | tf_op jit(solution)/shard_map/transpose(jvp())/mul | solution.py:50
  97.7 1.8 %fusion.97.fine_ref = f32[8,32,1040]{2,1,0:T(8,128)} fusion(f32[8,40,1040]{2,1,0:T(8,128)S(1)} %get-tuple-element.52, f32[8,40,1040]{2,1,0:T(8,128)S(1)} %fusion.84, f32[8,40,1040]{2,1,0:T(8,128)S(1)} %get-tuple-element.80, f32[8,40,1040]{2,1,0:T(8,128)S(1)} %get-tuple-element.81, f32[8,40,1040]{2,1,0:T(8,128)S(1)} %get-tuple-element.79, ...), kind=kLoop, calls=%fused_computation.180 | loop fusion | flops 2129920 | bytes 6689280 | tf_op jit(solution)/shard_map/jvp(jit(_where))/select_n | solution.py:55
  99.5 4.4 %shard_map.77 = (f32[8,32,1024]{2,1,0:T(8,128)}, f32[8,32,1040]{2,1,0:T(8,128)}) custom-call(f32[8,32,1040]{2,1,0:T(8,128)} %fusion.97.fine_ref, f32[8,32,1040]{2,1,0:T(8,128)} %copy-done.4, f32[8,32,1040]{2,1,0:T(8,128)} %all-to-all-done.1.gain_ref, f32[8,32,1040]{2,1,0:T(8,128)} %broadcast_select_fusion.target_ref, ...), custom_call_target="tpu_custom_call" | custom-call | tf_op jit(solution)/shard_map/pallas_call | solution.py:90
  103.9 5.7 %all-to-all-start.2 = ((f32[8,32,1024]{2,1,0:T(8,128)}), f32[8,32,1024]{2,1,0:T(8,128)}, u32[]{:S(2)}, u32[]{:S(2)}) async-start(f32[8,32,1024]{2,1,0:T(8,128)} %get-tuple-element.40), calls=%async_computation.2 | async-start | bytes 2097152 | tf_op jit(solution)/shard_map/all_to_all | solution.py:159
  109.6 2.4 %fusion.96 = (f32[8,40,1040]{2,1,0:T(8,128)S(1)}, f32[8,40,1040]{2,1,0:T(8,128)S(1)}, f32[8,40,1040]{2,1,0:T(8,128)S(1)}, f32[8,40,1040]{2,1,0:T(8,128)S(1)}, f3...) fusion(f32[8,32,1040]{2,1,0:T(8,128)} %get-tuple-element.41, ...), kind=kLoop, calls=%fused_computation.178 | loop fusion | flops 5990400 | bytes 11256960 | tf_op jit(solution)/shard_map/transpose(jvp())/mul | solution.py:48
  112.1 2.8 %multiply_reduce_fusion.1 = (f32[40,1040]{1,0:T(8,128)S(1)}, f32[8,40,1040]{2,1,0:T(8,128)S(1)}) fusion(f32[8,40,1040]{2,1,0:T(8,128)S(1)} %copy-done.16, f32[8,40,1040]{2,1,0:T(8,128)S(1)} %get-tuple-element.52, f32[8,40,1040]{2,1,0:T(8,128)S(1)} %get-tuple-element.89, f32[8,40,1040]{2,1,0:T(8,128)S(1)} %get-tuple-element.90, ...), kind=kLoop, calls=%fused_computation.157 | loop fusion | flops 6281600 | bytes 13520000 | tf_op jit(solution)/shard_map/transpose(jvp())/reduce_sum | solution.py:50
  116.7 2.7 %multiply_reduce_fusion = (f32[40,1040]{1,0:T(8,128)S(1)}, f32[8,40,1040]{2,1,0:T(8,128)S(1)}) fusion(f32[8,40,1040]{2,1,0:T(8,128)S(1)} %copy-done.15, f32[8,40,1040]{2,1,0:T(8,128)S(1)} %copy-done.1, f32[8,40,1040]{2,1,0:T(8,128)S(1)} %get-tuple-element.78, f32[8,40,1040]{2,1,0:T(8,128)S(1)} %get-tuple-element.77, ...), kind=kLoop, calls=%fused_computation.154 | loop fusion | flops 6281600 | bytes 13520000 | tf_op jit(solution)/shard_map/transpose(jvp())/reduce_sum | solution.py:50
  121.6 3.6 %multiply_reduce_fusion.2 = (f32[40,1040]{1,0:T(8,128)S(1)}, f32[40,1040]{1,0:T(8,128)S(1)}) fusion(f32[8,32,1040]{2,1,0:T(8,128)S(1)} %copy-done.18, pred[40,1040]{1,0:T(8,128)(4,1)S(1)} %and_and_fusion, f32[8,40,1040]{2,1,0:T(8,128)S(1)} %copy-done.17, f32[8,40,1040]{2,1,0:T(8,128)S(1)} %copy-done.3, f32[8,40,1040]{2,1,0:T(8,128)S(1)} %get-tuple-element.76, ...), kind=kLoop, calls=%fused_computation.160 | loop fusion | flops 9235200 | bytes 20076160 | tf_op jit(solution)/shard_map/transpose(jvp())/reduce_sum | solution.py:50
  125.3 7.2 %collective-permute-start.9 = (f32[4,1040]{1,0:T(4,128)S(1)}, f32[4,1040]{1,0:T(4,128)S(1)}, u32[]{:S(2)}, u32[]{:S(2)}) collective-permute-start(f32[4,1040]{1,0:T(4,128)S(1)} %get-tuple-element.106), channel_id=1, source_target_pairs={{8,0},{16,8},{24,16},{32,24},{40,32},{48,40},{56,48},{64,56},{72,6... | collective-permute-start | bytes 49928 | tf_op jit(solution)/shard_map/ppermute | solution.py:154
  132.5 1.9 %collective-permute-start.10 = (f32[4,1040]{1,0:T(4,128)S(1)}, f32[4,1040]{1,0:T(4,128)S(1)}, u32[]{:S(2)}, u32[]{:S(2)}) collective-permute-start(f32[4,1040]{1,0:T(4,128)S(1)} %get-tuple-element.105), channel_id=1, source_target_pairs={{0,8},{8,16},{16,24},{24,32},{32,40},{40,48},{48,56},{56,64},{64,7... | collective-permute-start | bytes 49928 | tf_op jit(solution)/shard_map/ppermute | solution.py:155
  134.5 7.4 %collective-permute-done.10 = f32[4,1040]{1,0:T(4,128)S(1)} collective-permute-done((f32[4,1040]{1,0:T(4,128)S(1)}, f32[4,1040]{1,0:T(4,128)S(1)}, u32[]{:S(2)}, u32[]{:S(2)}) %collective-permute-start.10) | collective-permute-done | bytes 16672 | tf_op jit(solution)/shard_map/ppermute | solution.py:155
  143.1 5.9 %all-to-all-start.3 = ((f32[8,32,1024]{2,1,0:T(8,128)}), f32[8,32,1024]{2,1,0:T(8,128)S(1)}, u32[]{:S(2)}, u32[]{:S(2)}) async-start(f32[8,32,1024]{2,1,0:T(8,128)} %broadcast_in_dim.69), calls=%async_computation.3 | async-start | bytes 2097152 | tf_op jit(solution)/shard_map/all_to_all | solution.py:162
  149.0 2.3 %copy.24 = f32[1,8,4,8,1024]{4,3,1,2,0:T(8,128)} copy(f32[1,8,4,8,1024]{4,3,2,1,0:T(8,128)} %bitcast.30) | data formatting | bytes 2097152 | tf_op jit(solution)/shard_map/all_to_all | solution.py:159
  151.3 7.7 %all-to-all-done.3 = f32[8,32,1024]{2,1,0:T(8,128)S(1)} async-done(((f32[8,32,1024]{2,1,0:T(8,128)}), f32[8,32,1024]{2,1,0:T(8,128)S(1)}, u32[]{:S(2)}, u32[]{:S(2)}) %all-to-all-start.3) | async-done | bytes 1048608 | tf_op jit(solution)/shard_map/all_to_all | solution.py:162
  (125 shorter events, 36.4 us)
Async XLA Ops:
  4.6 6.1 %copy-start.22 = (f32[1,32,8192]{2,1,0:T(8,128)S(1)}, f32[1,32,8192]{2,1,0:T(8,128)}, u32[]{:S(2)}) copy-start(f32[1,32,8192]{2,1,0:T(8,128)} %param.15) | copy-start | bytes 3145732
  4.6 50.4 %all-to-all-start = ((f32[8,32,1040]{2,1,0:T(8,128)}), f32[8,32,1040]{2,1,0:T(8,128)S(1)}, u32[]{:S(2)}, u32[]{:S(2)}) async-start(f32[8,32,1040]{2,1,0:T(8,128)} %concatenate.19), calls=%async_computation | async-start | bytes 2359296 | tf_op jit(solution)/shard_map/all_to_all | solution.py:116
  14.2 8.7 %copy-start.23 = (f32[1,32,8192]{2,1,0:T(8,128)S(1)}, f32[1,32,8192]{2,1,0:T(8,128)}, u32[]{:S(2)}) copy-start(f32[1,32,8192]{2,1,0:T(8,128)} %param.14) | copy-start | bytes 3145732
  15.3 36.0 %collective-permute-start.8 = (f32[32,1040]{1,0:T(8,128)}, f32[32,1040]{1,0:T(8,128)S(1)}, u32[]{:S(2)}, u32[]{:S(2)}) collective-permute-start(f32[32,1040]{1,0:T(8,128)} %get-tuple-element.91), channel_id=1, source_target_pairs={{0,7},{1,0},{2,1},{3,2},{4,3},{5,4},{6,5},{7,6},{8,15},{9,8},{10,9... | collective-permute-start | bytes 399368 | tf_op jit(solution)/shard_map/ppermute | solution.py:123
  18.0 32.6 %collective-permute-start.7 = (f32[32,1040]{1,0:T(8,128)}, f32[32,1040]{1,0:T(8,128)S(1)}, u32[]{:S(2)}, u32[]{:S(2)}) collective-permute-start(f32[32,1040]{1,0:T(8,128)} %get-tuple-element.92), channel_id=1, source_target_pairs={{0,6},{1,7},{2,0},{3,1},{4,2},{5,3},{6,4},{7,5},{8,14},{9,15},{10,... | collective-permute-start | bytes 399368 | tf_op jit(solution)/shard_map/ppermute | solution.py:123
  18.8 31.1 %collective-permute-start.6 = (f32[32,1040]{1,0:T(8,128)}, f32[32,1040]{1,0:T(8,128)S(1)}, u32[]{:S(2)}, u32[]{:S(2)}) collective-permute-start(f32[32,1040]{1,0:T(8,128)} %get-tuple-element.93), channel_id=1, source_target_pairs={{0,5},{1,6},{2,7},{3,0},{4,1},{5,2},{6,3},{7,4},{8,13},{9,14},{10,... | collective-permute-start | bytes 399368 | tf_op jit(solution)/shard_map/ppermute | solution.py:123
  20.6 27.7 %collective-permute-start.5 = (f32[32,1040]{1,0:T(8,128)}, f32[32,1040]{1,0:T(8,128)}, u32[]{:S(2)}, u32[]{:S(2)}) collective-permute-start(f32[32,1040]{1,0:T(8,128)} %get-tuple-element.94), channel_id=1, source_target_pairs={{0,4},{1,5},{2,6},{3,7},{4,0},{5,1},{6,2},{7,3},{8,12},{9,13},{10,... | collective-permute-start | bytes 399368 | tf_op jit(solution)/shard_map/ppermute | solution.py:123
  21.1 12.9 %collective-permute-start.2 = (f32[32,1040]{1,0:T(8,128)}, f32[32,1040]{1,0:T(8,128)}, u32[]{:S(2)}, u32[]{:S(2)}) collective-permute-start(f32[32,1040]{1,0:T(8,128)} %get-tuple-element.97), channel_id=1, source_target_pairs={{0,1},{1,2},{2,3},{3,4},{4,5},{5,6},{6,7},{7,0},{8,9},{9,10},{10,1... | collective-permute-start | bytes 399368 | tf_op jit(solution)/shard_map/ppermute | solution.py:123
  24.5 9.6 %copy-start.27 = (f32[32,1040]{1,0:T(8,128)S(1)}, f32[32,1040]{1,0:T(8,128)}, u32[]{:S(2)}) copy-start(f32[32,1040]{1,0:T(8,128)} %get-tuple-element.96) | copy-start | bytes 399364
  24.5 17.1 %copy-start.26 = (f32[32,1040]{1,0:T(8,128)S(1)}, f32[32,1040]{1,0:T(8,128)}, u32[]{:S(2)}) copy-start(f32[32,1040]{1,0:T(8,128)} %get-tuple-element.95) | copy-start | bytes 399364
  34.0 7.5 %collective-permute-start.3 = (f32[32,1040]{1,0:T(8,128)S(1)}, f32[32,1040]{1,0:T(8,128)S(1)}, u32[]{:S(2)}, u32[]{:S(2)}) collective-permute-start(f32[32,1040]{1,0:T(8,128)S(1)} %copy-done.27), channel_id=1, source_target_pairs={{0,2},{1,3},{2,4},{3,5},{4,6},{5,7},{6,0},{7,1},{8,10},{9,11},{10,... | collective-permute-start | bytes 399368 | tf_op jit(solution)/shard_map/ppermute | solution.py:123
  41.6 6.0 %collective-permute-start.4 = (f32[32,1040]{1,0:T(8,128)S(1)}, f32[32,1040]{1,0:T(8,128)S(1)}, u32[]{:S(2)}, u32[]{:S(2)}) collective-permute-start(f32[32,1040]{1,0:T(8,128)S(1)} %copy-done.26), channel_id=1, source_target_pairs={{0,3},{1,4},{2,5},{3,6},{4,7},{5,0},{6,1},{7,2},{8,11},{9,12},{10,... | collective-permute-start | bytes 399368 | tf_op jit(solution)/shard_map/ppermute | solution.py:123
  55.4 14.9 %copy-start.4 = (f32[8,32,1040]{2,1,0:T(8,128)}, f32[8,32,1040]{2,1,0:T(8,128)S(1)}, u32[]{:S(2)}) copy-start(f32[8,32,1040]{2,1,0:T(8,128)S(1)} %all-to-all-done.old_ref) | copy-start | bytes 3194884
  56.9 10.0 %copy-start.25 = (f32[32,8192]{1,0:T(8,128)S(1)}, f32[32,8192]{1,0:T(8,128)}, u32[]{:S(2)}) copy-start(f32[32,8192]{1,0:T(8,128)} %param.10) | copy-start | bytes 3145732
  57.0 12.5 %collective-permute-start = (f32[11,4,1040]{2,1,0:T(4,128)S(1)}, f32[11,4,1040]{2,1,0:T(4,128)S(1)}, u32[]{:S(2)}, u32[]{:S(2)}) collective-permute-start(f32[11,4,1040]{2,1,0:T(4,128)S(1)} %get-tuple-element.73), channel_id=1, source_target_pairs={{0,8},{8,16},{16,24},{24,32},{32,40},{40,48},{48,56},{56,64},{64,7... | collective-permute-start | bytes 549128 | tf_op jit(solution)/shard_map/ppermute | solution.py:21
  59.1 11.2 %collective-permute-start.1 = (f32[11,4,1040]{2,1,0:T(4,128)S(1)}, f32[11,4,1040]{2,1,0:T(4,128)S(1)}, u32[]{:S(2)}, u32[]{:S(2)}) collective-permute-start(f32[11,4,1040]{2,1,0:T(4,128)S(1)} %get-tuple-element.74), channel_id=1, source_target_pairs={{8,0},{16,8},{24,16},{32,24},{40,32},{48,40},{56,48},{64,56},{72,6... | collective-permute-start | bytes 549128 | tf_op jit(solution)/shard_map/ppermute | solution.py:23
  71.8 12.2 %copy-start.8 = (f32[40,1040]{1,0:T(8,128)}, f32[40,1040]{1,0:T(8,128)S(1)}, u32[]{:S(2)}) copy-start(f32[40,1040]{1,0:T(8,128)S(1)} %get-tuple-element.62) | copy-start | bytes 499204
  71.8 12.2 %copy-start.11 = (f32[40,1040]{1,0:T(8,128)}, f32[40,1040]{1,0:T(8,128)S(1)}, u32[]{:S(2)}) copy-start(f32[40,1040]{1,0:T(8,128)S(1)} %get-tuple-element.60) | copy-start | bytes 499204
  71.8 12.2 %copy-start.19 = (f32[40,1040]{1,0:T(8,128)}, f32[40,1040]{1,0:T(8,128)S(1)}, u32[]{:S(2)}) copy-start(f32[40,1040]{1,0:T(8,128)S(1)} %get-tuple-element.58) | copy-start | bytes 499204
  71.8 16.7 %copy-start.5 = (f32[40,1040]{1,0:T(8,128)}, f32[40,1040]{1,0:T(8,128)S(1)}, u32[]{:S(2)}) copy-start(f32[40,1040]{1,0:T(8,128)S(1)} %get-tuple-element.61) | copy-start | bytes 499204
  71.9 27.6 %all-to-all-start.1 = ((f32[8,32,1040]{2,1,0:T(8,128)}), f32[8,32,1040]{2,1,0:T(8,128)}, u32[]{:S(2)}, u32[]{:S(2)}) async-start(f32[8,32,1040]{2,1,0:T(8,128)} %concatenate.22), calls=%async_computation.1 | async-start | bytes 2359296 | tf_op jit(solution)/shard_map/all_to_all | solution.py:142
  93.6 3.2 %copy-start.6 = (f32[40,1040]{1,0:T(8,128)S(1)}, f32[40,1040]{1,0:T(8,128)}, u32[]{:S(2)}) copy-start(f32[40,1040]{1,0:T(8,128)} %copy-done.5) | copy-start | bytes 499204
  103.9 38.2 %all-to-all-start.2 = ((f32[8,32,1024]{2,1,0:T(8,128)}), f32[8,32,1024]{2,1,0:T(8,128)}, u32[]{:S(2)}, u32[]{:S(2)}) async-start(f32[8,32,1024]{2,1,0:T(8,128)} %get-tuple-element.40), calls=%async_computation.2 | async-start | bytes 2097152 | tf_op jit(solution)/shard_map/all_to_all | solution.py:159
  109.6 2.4 %copy-start.16 = (f32[8,40,1040]{2,1,0:T(8,128)S(1)}, f32[8,40,1040]{2,1,0:T(8,128)}, u32[]{:S(2)}) copy-start(f32[8,40,1040]{2,1,0:T(8,128)} %get-tuple-element.53) | copy-start | bytes 3993604
  112.0 2.8 %copy-start.7 = (f32[40,1040]{1,0:T(8,128)S(1)}, f32[40,1040]{1,0:T(8,128)}, u32[]{:S(2)}) copy-start(f32[40,1040]{1,0:T(8,128)} %copy-done.5) | copy-start | bytes 499204
  112.0 2.8 %copy-start.10 = (f32[40,1040]{1,0:T(8,128)S(1)}, f32[40,1040]{1,0:T(8,128)}, u32[]{:S(2)}) copy-start(f32[40,1040]{1,0:T(8,128)} %copy-done.8) | copy-start | bytes 499204
  112.0 2.8 %copy-start.13 = (f32[40,1040]{1,0:T(8,128)S(1)}, f32[40,1040]{1,0:T(8,128)}, u32[]{:S(2)}) copy-start(f32[40,1040]{1,0:T(8,128)} %copy-done.11) | copy-start | bytes 499204
  112.1 2.8 %copy-start.21 = (f32[40,1040]{1,0:T(8,128)S(1)}, f32[40,1040]{1,0:T(8,128)}, u32[]{:S(2)}) copy-start(f32[40,1040]{1,0:T(8,128)} %broadcast_multiply_fusion.2) | copy-start | bytes 499204
  119.4 2.1 %copy-start.18 = (f32[8,32,1040]{2,1,0:T(8,128)S(1)}, f32[8,32,1040]{2,1,0:T(8,128)}, u32[]{:S(2)}) copy-start(f32[8,32,1040]{2,1,0:T(8,128)} %get-tuple-element.41) | copy-start | bytes 3194884
  125.3 9.2 %collective-permute-start.9 = (f32[4,1040]{1,0:T(4,128)S(1)}, f32[4,1040]{1,0:T(4,128)S(1)}, u32[]{:S(2)}, u32[]{:S(2)}) collective-permute-start(f32[4,1040]{1,0:T(4,128)S(1)} %get-tuple-element.106), channel_id=1, source_target_pairs={{8,0},{16,8},{24,16},{32,24},{40,32},{48,40},{56,48},{64,56},{72,6... | collective-permute-start | bytes 49928 | tf_op jit(solution)/shard_map/ppermute | solution.py:154
  132.5 9.4 %collective-permute-start.10 = (f32[4,1040]{1,0:T(4,128)S(1)}, f32[4,1040]{1,0:T(4,128)S(1)}, u32[]{:S(2)}, u32[]{:S(2)}) collective-permute-start(f32[4,1040]{1,0:T(4,128)S(1)} %get-tuple-element.105), channel_id=1, source_target_pairs={{0,8},{8,16},{16,24},{24,32},{32,40},{40,48},{48,56},{56,64},{64,7... | collective-permute-start | bytes 49928 | tf_op jit(solution)/shard_map/ppermute | solution.py:155
  143.1 15.9 %all-to-all-start.3 = ((f32[8,32,1024]{2,1,0:T(8,128)}), f32[8,32,1024]{2,1,0:T(8,128)S(1)}, u32[]{:S(2)}, u32[]{:S(2)}) async-start(f32[8,32,1024]{2,1,0:T(8,128)} %broadcast_in_dim.69), calls=%async_computation.3 | async-start | bytes 2097152 | tf_op jit(solution)/shard_map/all_to_all | solution.py:162
  (11 other events, 15.8 us)

commit v10 on v7

--- a/solution.py
+++ b/solution.py
@@ -83,7 +83,7 @@
 
 def scans(fine_ends, old, pair, begin, width):
     slabs, rows, wide = fine_ends.shape
-    tile = 8
+    tile = 16
     stacked = pl.BlockSpec((slabs, tile, wide), lambda i: (0, i, 0))
     inner = pl.BlockSpec((slabs, tile, width), lambda i: (0, i, 0))
     both = pl.BlockSpec((slabs, 2, tile, wide), lambda i: (0, 0, i, 0))

time: 131 us -> 130 us (level)
  no operation moved by 1% of the time
where the time goes in v10:
time: 130 us
  starting transfers between devices  38.9 us (30%)
  other arithmetic  35.2 us (27%)
  local copies, waits for them, and re-layouts  25.3 us (19%)
  waiting for transfers between devices  25.3 us (19%)
  Pallas kernels  3.67 us (3%)
    select_n x4, other arithmetic, fine(): jnp.where(inside, advance(field, kappa, along_rows, along_cols), 0.0)  12.1 us
    unnamed x56, local copies, waits for them, and re-layouts  9.48 us
    reduce_sum x3, other arithmetic, advance(): return centre + time_step * (kappa * spread - transport)  9.09 us
    ppermute x1, starting transfers between devices, with_halo(): lax.ppermute(head, axis, [((i + 1) % count, i) for i in range(ends)])  7.86 us
    all_to_all x1, waiting for transfers between devices, on_device(): gradient = lax.all_to_all(copies, 'tm', 0, 2, tiled=True)[0]  7.73 us
    ppermute x1, waiting for transfers between devices, on_device(): lax.ppermute(grad_rows[-STEPS:], 'space', [(i, (i + 1) % count) for i in...  7.34 us
    all_to_all x1, starting transfers between devices, on_device(): pair = lax.all_to_all(pair, 'tm', 0, 0, tiled=True)  6.8 us
    all_to_all x1, starting transfers between devices, to_blocks(): return lax.all_to_all(send_windows(x), 'tm', 0, 0, tiled=True)  6.06 us
  transfers between devices with their start and end apart: 8, of which 6 were waited for; matrix products, arithmetic and copies ran while one was open for 36% of the time, Pallas kernels for 0%

profile of v10, /device:TPU:160, one launch (start us, length us, event | category | flops | bytes accessed | tf_op | source)
XLA Modules:
  0.0 129.6 jit_solution(11315846975799802238)
XLA Ops:
  0.6 1.8 %copy.22 = f32[4,8,8,1024]{3,2,1,0:T(8,128)S(1)} copy(f32[4,8,8,1024]{3,1,2,0:T(8,128)} %bitcast.59) | data formatting | bytes 2097152
  3.2 1.4 %concatenate.19 = f32[8,32,1040]{2,1,0:T(8,128)} concatenate(f32[8,32,8]{2,1,0:T(8,128)S(1)} %pad.155, f32[8,32,1024]{2,1,0:T(8,128)S(1)} %bitcast.52, f32[8,32,8]{2,1,0:T(8,128)S(1)} %pad.156), dimensions={2} | concatenate | bytes 2129920 | tf_op jit(solution)/shard_map/concatenate | solution.py:114
  4.6 6.1 %all-to-all-start = ((f32[8,32,1040]{2,1,0:T(8,128)}), f32[8,32,1040]{2,1,0:T(8,128)S(1)}, u32[]{:S(2)}, u32[]{:S(2)}) async-start(f32[8,32,1040]{2,1,0:T(8,128)} %concatenate.19), calls=%async_computation | async-start | bytes 2359296 | tf_op jit(solution)/shard_map/all_to_all | solution.py:117
  15.6 2.1 %concatenate.22 = f32[8,32,1040]{2,1,0:T(8,128)} concatenate(f32[8,32,8]{2,1,0:T(8,128)} %pad.159, f32[8,32,1024]{2,1,0:T(8,128)S(1)} %bitcast.48, f32[8,32,8]{2,1,0:T(8,128)S(1)} %pad.160), dimensions={2} | concatenate | bytes 2129920 | tf_op jit(solution)/shard_map/concatenate | solution.py:114
  17.7 2.2 %concatenate.23 = f32[8,32,1040]{2,1,0:T(8,128)} concatenate(f32[8,32,8]{2,1,0:T(8,128)} %pad.161, f32[8,32,1024]{2,1,0:T(8,128)S(1)} %bitcast.50, f32[8,32,8]{2,1,0:T(8,128)} %pad.162), dimensions={2} | concatenate | bytes 2129920 | tf_op jit(solution)/shard_map/concatenate | solution.py:114
  19.9 3.3 %pad_maximum_fusion = f32[8,2,32,1040]{3,2,1,0:T(8,128)} fusion(f32[8,1,32,1040]{3,2,1,0:T(8,128)} %bitcast.54, f32[8,1,32,1040]{3,2,1,0:T(8,128)} %bitcast.53), kind=kLoop, calls=%fused_computation | loop fusion | flops 532480 | bytes 4259840 | tf_op jit(solution)/shard_map/stack | solution.py:120
  23.2 3.1 %all-to-all-done.old_ref = f32[8,32,1040]{2,1,0:T(8,128)S(1)} async-done(((f32[8,32,1040]{2,1,0:T(8,128)}), f32[8,32,1040]{2,1,0:T(8,128)S(1)}, u32[]{:S(2)}, u32[]{:S(2)}) %all-to-all-start) | async-done | bytes 1064992 | tf_op jit(solution)/shard_map/all_to_all | solution.py:117
  26.5 1.4 %pad_dynamic-slice_fusion = f32[2,32,1040]{2,1,0:T(8,128)S(1)} fusion(s32[]{:T(128)S(6)} %select_n.31, f32[2,32,8192]{2,1,0:T(8,128)} %param.13), kind=kLoop, calls=%fused_computation.1 | loop fusion | bytes 2363396 | tf_op jit(solution)/shard_map/dynamic_slice | solution.py:64
  28.0 2.1 %collective-permute-start = (f32[11,4,1040]{2,1,0:T(4,128)S(1)}, f32[11,4,1040]{2,1,0:T(4,128)S(1)}, u32[]{:S(2)}, u32[]{:S(2)}) collective-permute-start(f32[11,4,1040]{2,1,0:T(4,128)S(1)} %get-tuple-element.73), channel_id=1, source_target_pairs={{0,8},{8,16},{16,24},{24,32},{32,40},{40,48},{48,56},{56,64},{64,7... | collective-permute-start | bytes 549128 | tf_op jit(solution)/shard_map/ppermute | solution.py:21
  30.0 7.9 %collective-permute-start.1 = (f32[11,4,1040]{2,1,0:T(4,128)S(1)}, f32[11,4,1040]{2,1,0:T(4,128)S(1)}, u32[]{:S(2)}, u32[]{:S(2)}) collective-permute-start(f32[11,4,1040]{2,1,0:T(4,128)S(1)} %get-tuple-element.74), channel_id=1, source_target_pairs={{8,0},{16,8},{24,16},{32,24},{40,32},{48,40},{56,48},{64,56},{72,6... | collective-permute-start | bytes 549128 | tf_op jit(solution)/shard_map/ppermute | solution.py:23
  38.7 1.8 %collective-permute-done = f32[11,4,1040]{2,1,0:T(4,128)S(1)} collective-permute-done((f32[11,4,1040]{2,1,0:T(4,128)S(1)}, f32[11,4,1040]{2,1,0:T(4,128)S(1)}, u32[]{:S(2)}, u32[]{:S(2)}) %collective-permute-start) | collective-permute-done | bytes 183072 | tf_op jit(solution)/shard_map/ppermute | solution.py:21
  41.5 1.2 copy-done.14
  42.9 6.8 %all-to-all-start.1 = ((f32[8,2,32,1040]{3,2,1,0:T(8,128)}), f32[8,2,32,1040]{3,2,1,0:T(8,128)}, u32[]{:S(2)}, u32[]{:S(2)}) async-start(f32[8,2,32,1040]{3,2,1,0:T(8,128)} %pad_maximum_fusion), calls=%async_computation.1 | async-start | bytes 4718592 | tf_op jit(solution)/shard_map/all_to_all | solution.py:137
  50.3 3.5 %fusion.24 = (f32[8,40,1040]{2,1,0:T(8,128)S(1)}, f32[8,40,1040]{2,1,0:T(8,128)}) fusion(f32[8,40,1040]{2,1,0:T(8,128)S(1)} %slice.216, f32[40,1040]{1,0:T(8,128)S(1)} %get-tuple-element.60, f32[40,1040]{1,0:T(8,128)S(1)} %get-tuple-element.61, f32[40,1040]{1,0:T(8,128)S(1)} %get-tuple-element.59, f32[40,1040]{1,0:T(8,128)S(1)} %get-tuple-element.62, ...), kind=kLoop, calls=%fused_computation.60 | loop fusion | flops 6988800 | bytes 11523200 | tf_op jit(solution)/shard_map/jvp(jit(_where))/select_n | solution.py:55
  54.9 3.4 %fusion.39 = (f32[8,40,1040]{2,1,0:T(8,128)S(1)}, f32[8,40,1040]{2,1,0:T(8,128)}) fusion(f32[8,40,1040]{2,1,0:T(8,128)S(1)} %get-tuple-element.56, f32[40,1040]{1,0:T(8,128)S(1)} %get-tuple-element.60, f32[40,1040]{1,0:T(8,128)S(1)} %get-tuple-element.61, f32[40,1040]{1,0:T(8,128)S(1)} %get-tuple-element.59, f32[40,1040]{1,0:T(8,128)S(1)} %get-tuple-element.62, ...), kind=kLoop, calls=%fused_computation.75 | loop fusion | flops 6988800 | bytes 11523200 | tf_op jit(solution)/shard_map/jvp(jit(_where))/select_n | solution.py:55
  59.9 3.4 %fusion.55 = (f32[8,40,1040]{2,1,0:T(8,128)S(1)}, f32[8,40,1040]{2,1,0:T(8,128)}) fusion(f32[8,40,1040]{2,1,0:T(8,128)S(1)} %get-tuple-element.54, f32[40,1040]{1,0:T(8,128)S(1)} %copy-done.12, f32[40,1040]{1,0:T(8,128)S(1)} %get-tuple-element.61, f32[40,1040]{1,0:T(8,128)S(1)} %get-tuple-element.59, f32[40,1040]{1,0:T(8,128)S(1)} %copy-done.9, ...), kind=kLoop, calls=%fused_computation.91 | loop fusion | flops 6988800 | bytes 11523200 | tf_op jit(solution)/shard_map/jvp(jit(_where))/select_n | solution.py:55
  63.9 1.6 %broadcast_multiply_fusion.2 = f32[40,1040]{1,0:T(8,128)} fusion(f32[11,40,1040]{2,1,0:T(8,128)} %copy-done.14), kind=kLoop, calls=%fused_computation.205 | loop fusion | flops 41600 | bytes 332800 | tf_op jit(solution)/shard_map/transpose(jvp())/mul | solution.py:50
  65.5 1.6 %fusion.84 = f32[8,40,1040]{2,1,0:T(8,128)S(1)} fusion(f32[8,42,1042]{2,1,0:T(8,128)S(1)} %pad_add_fusion), kind=kLoop, calls=%fused_computation.133 | loop fusion | flops 1664000 | bytes 7987200 | tf_op jit(solution)/shard_map/jvp()/sub | solution.py:38
  68.0 1.8 %fusion.97.fine_ref = f32[8,32,1040]{2,1,0:T(8,128)} fusion(f32[8,40,1040]{2,1,0:T(8,128)S(1)} %get-tuple-element.52, f32[8,40,1040]{2,1,0:T(8,128)S(1)} %fusion.84, f32[8,40,1040]{2,1,0:T(8,128)S(1)} %get-tuple-element.80, f32[8,40,1040]{2,1,0:T(8,128)S(1)} %get-tuple-element.81, f32[8,40,1040]{2,1,0:T(8,128)S(1)} %get-tuple-element.79, ...), kind=kLoop, calls=%fused_computation.180 | loop fusion | flops 2129920 | bytes 6689280 | tf_op jit(solution)/shard_map/jvp(jit(_where))/select_n | solution.py:55
  69.7 4.6 %all-to-all-done.1.pair_ref = f32[8,2,32,1040]{3,2,1,0:T(8,128)} async-done(((f32[8,2,32,1040]{3,2,1,0:T(8,128)}), f32[8,2,32,1040]{3,2,1,0:T(8,128)}, u32[]{:S(2)}, u32[]{:S(2)}) %all-to-all-start.1) | async-done | bytes 2129952 | tf_op jit(solution)/shard_map/all_to_all | solution.py:137
  74.3 3.7 %shard_map.77 = (f32[8,32,1024]{2,1,0:T(8,128)}, f32[8,32,1040]{2,1,0:T(8,128)}) custom-call(f32[8,32,1040]{2,1,0:T(8,128)} %fusion.97.fine_ref, f32[8,32,1040]{2,1,0:T(8,128)} %copy-done.4, f32[8,2,32,1040]{3,2,1,0:T(8,128)} %all-to-all-done.1.pair_ref, f32[32,1040]{1,0:T(8,128)} %pad_dynamic-slice_fusion.1.begin_ref), custom_call_target="tpu_custom_call" | custom-call | tf_op jit(solution)/shard_map/pallas_call | solution.py:91
  78.0 4.7 %all-to-all-start.2 = ((f32[8,32,1024]{2,1,0:T(8,128)}), f32[8,32,1024]{2,1,0:T(8,128)}, u32[]{:S(2)}, u32[]{:S(2)}) async-start(f32[8,32,1024]{2,1,0:T(8,128)} %get-tuple-element.40), calls=%async_computation.2 | async-start | bytes 2097152 | tf_op jit(solution)/shard_map/all_to_all | solution.py:154
  82.7 2.4 %fusion.96 = (f32[8,40,1040]{2,1,0:T(8,128)S(1)}, f32[8,40,1040]{2,1,0:T(8,128)S(1)}, f32[8,40,1040]{2,1,0:T(8,128)S(1)}, f32[8,40,1040]{2,1,0:T(8,128)S(1)}, f3...) fusion(f32[8,32,1040]{2,1,0:T(8,128)} %get-tuple-element.41, ...), kind=kLoop, calls=%fused_computation.178 | loop fusion | flops 5990400 | bytes 11256960 | tf_op jit(solution)/shard_map/transpose(jvp())/mul | solution.py:48
  85.2 2.8 %multiply_reduce_fusion.1 = (f32[40,1040]{1,0:T(8,128)S(1)}, f32[8,40,1040]{2,1,0:T(8,128)S(1)}) fusion(f32[8,40,1040]{2,1,0:T(8,128)S(1)} %copy-done.16, f32[8,40,1040]{2,1,0:T(8,128)S(1)} %get-tuple-element.52, f32[8,40,1040]{2,1,0:T(8,128)S(1)} %get-tuple-element.89, f32[8,40,1040]{2,1,0:T(8,128)S(1)} %get-tuple-element.90, ...), kind=kLoop, calls=%fused_computation.157 | loop fusion | flops 6281600 | bytes 13520000 | tf_op jit(solution)/shard_map/transpose(jvp())/reduce_sum | solution.py:50
  89.8 2.7 %multiply_reduce_fusion = (f32[40,1040]{1,0:T(8,128)S(1)}, f32[8,40,1040]{2,1,0:T(8,128)S(1)}) fusion(f32[8,40,1040]{2,1,0:T(8,128)S(1)} %copy-done.15, f32[8,40,1040]{2,1,0:T(8,128)S(1)} %copy-done.1, f32[8,40,1040]{2,1,0:T(8,128)S(1)} %get-tuple-element.78, f32[8,40,1040]{2,1,0:T(8,128)S(1)} %get-tuple-element.77, ...), kind=kLoop, calls=%fused_computation.154 | loop fusion | flops 6281600 | bytes 13520000 | tf_op jit(solution)/shard_map/transpose(jvp())/reduce_sum | solution.py:50
  94.7 3.6 %multiply_reduce_fusion.2 = (f32[40,1040]{1,0:T(8,128)S(1)}, f32[40,1040]{1,0:T(8,128)S(1)}) fusion(f32[8,32,1040]{2,1,0:T(8,128)S(1)} %copy-done.18, pred[40,1040]{1,0:T(8,128)(4,1)S(1)} %and_and_fusion, f32[8,40,1040]{2,1,0:T(8,128)S(1)} %copy-done.17, f32[8,40,1040]{2,1,0:T(8,128)S(1)} %copy-done.3, f32[8,40,1040]{2,1,0:T(8,128)S(1)} %get-tuple-element.76, ...), kind=kLoop, calls=%fused_computation.160 | loop fusion | flops 9235200 | bytes 20076160 | tf_op jit(solution)/shard_map/transpose(jvp())/reduce_sum | solution.py:50
  98.4 3.6 %collective-permute-start.2 = (f32[4,1040]{1,0:T(4,128)S(1)}, f32[4,1040]{1,0:T(4,128)S(1)}, u32[]{:S(2)}, u32[]{:S(2)}) collective-permute-start(f32[4,1040]{1,0:T(4,128)S(1)} %get-tuple-element.98), channel_id=1, source_target_pairs={{8,0},{16,8},{24,16},{32,24},{40,32},{48,40},{56,48},{64,56},{72,6... | collective-permute-start | bytes 49928 | tf_op jit(solution)/shard_map/ppermute | solution.py:149
  102.1 1.9 %collective-permute-start.3 = (f32[4,1040]{1,0:T(4,128)S(1)}, f32[4,1040]{1,0:T(4,128)S(1)}, u32[]{:S(2)}, u32[]{:S(2)}) collective-permute-start(f32[4,1040]{1,0:T(4,128)S(1)} %get-tuple-element.97), channel_id=1, source_target_pairs={{0,8},{8,16},{16,24},{24,32},{32,40},{40,48},{48,56},{56,64},{64,7... | collective-permute-start | bytes 49928 | tf_op jit(solution)/shard_map/ppermute | solution.py:150
  104.0 7.3 %collective-permute-done.3 = f32[4,1040]{1,0:T(4,128)S(1)} collective-permute-done((f32[4,1040]{1,0:T(4,128)S(1)}, f32[4,1040]{1,0:T(4,128)S(1)}, u32[]{:S(2)}, u32[]{:S(2)}) %collective-permute-start.3) | collective-permute-done | bytes 16672 | tf_op jit(solution)/shard_map/ppermute | solution.py:150
  112.6 5.9 %all-to-all-start.3 = ((f32[8,32,1024]{2,1,0:T(8,128)}), f32[8,32,1024]{2,1,0:T(8,128)S(1)}, u32[]{:S(2)}, u32[]{:S(2)}) async-start(f32[8,32,1024]{2,1,0:T(8,128)} %broadcast_in_dim.57), calls=%async_computation.3 | async-start | bytes 2097152 | tf_op jit(solution)/shard_map/all_to_all | solution.py:157
  118.5 2.3 %copy.21 = f32[1,8,4,8,1024]{4,3,1,2,0:T(8,128)} copy(f32[1,8,4,8,1024]{4,3,2,1,0:T(8,128)} %bitcast.17) | data formatting | bytes 2097152 | tf_op jit(solution)/shard_map/all_to_all | solution.py:154
  120.8 7.7 %all-to-all-done.3 = f32[8,32,1024]{2,1,0:T(8,128)S(1)} async-done(((f32[8,32,1024]{2,1,0:T(8,128)}), f32[8,32,1024]{2,1,0:T(8,128)S(1)}, u32[]{:S(2)}, u32[]{:S(2)}) %all-to-all-start.3) | async-done | bytes 1048608 | tf_op jit(solution)/shard_map/all_to_all | solution.py:157
  (95 shorter events, 18.6 us)
Async XLA Ops:
  4.6 6.2 %copy-start.22 = (f32[1,32,8192]{2,1,0:T(8,128)S(1)}, f32[1,32,8192]{2,1,0:T(8,128)}, u32[]{:S(2)}) copy-start(f32[1,32,8192]{2,1,0:T(8,128)} %param.14) | copy-start | bytes 3145732
  4.6 21.7 %all-to-all-start = ((f32[8,32,1040]{2,1,0:T(8,128)}), f32[8,32,1040]{2,1,0:T(8,128)S(1)}, u32[]{:S(2)}, u32[]{:S(2)}) async-start(f32[8,32,1040]{2,1,0:T(8,128)} %concatenate.19), calls=%async_computation | async-start | bytes 2359296 | tf_op jit(solution)/shard_map/all_to_all | solution.py:117
  11.5 1.4 %copy-start.23 = (f32[1,32,8192]{2,1,0:T(8,128)S(1)}, f32[1,32,8192]{2,1,0:T(8,128)}, u32[]{:S(2)}) copy-start(f32[1,32,8192]{2,1,0:T(8,128)} %param.15) | copy-start | bytes 3145732
  19.9 6.4 %copy-start.24 = (f32[32,8192]{1,0:T(8,128)S(1)}, f32[32,8192]{1,0:T(8,128)}, u32[]{:S(2)}) copy-start(f32[32,8192]{1,0:T(8,128)} %param.12) | copy-start | bytes 3145732
  26.4 14.9 %copy-start.4 = (f32[8,32,1040]{2,1,0:T(8,128)}, f32[8,32,1040]{2,1,0:T(8,128)S(1)}, u32[]{:S(2)}) copy-start(f32[8,32,1040]{2,1,0:T(8,128)S(1)} %all-to-all-done.old_ref) | copy-start | bytes 3194884
  27.9 10.0 %copy-start.25 = (f32[32,8192]{1,0:T(8,128)S(1)}, f32[32,8192]{1,0:T(8,128)}, u32[]{:S(2)}) copy-start(f32[32,8192]{1,0:T(8,128)} %param.10) | copy-start | bytes 3145732
  28.0 12.5 %collective-permute-start = (f32[11,4,1040]{2,1,0:T(4,128)S(1)}, f32[11,4,1040]{2,1,0:T(4,128)S(1)}, u32[]{:S(2)}, u32[]{:S(2)}) collective-permute-start(f32[11,4,1040]{2,1,0:T(4,128)S(1)} %get-tuple-element.73), channel_id=1, source_target_pairs={{0,8},{8,16},{16,24},{24,32},{32,40},{40,48},{48,56},{56,64},{64,7... | collective-permute-start | bytes 549128 | tf_op jit(solution)/shard_map/ppermute | solution.py:21
  30.0 11.2 %collective-permute-start.1 = (f32[11,4,1040]{2,1,0:T(4,128)S(1)}, f32[11,4,1040]{2,1,0:T(4,128)S(1)}, u32[]{:S(2)}, u32[]{:S(2)}) collective-permute-start(f32[11,4,1040]{2,1,0:T(4,128)S(1)} %get-tuple-element.74), channel_id=1, source_target_pairs={{8,0},{16,8},{24,16},{32,24},{40,32},{48,40},{56,48},{64,56},{72,6... | collective-permute-start | bytes 549128 | tf_op jit(solution)/shard_map/ppermute | solution.py:23
  41.4 1.3 %copy-start.14 = (f32[11,40,1040]{2,1,0:T(8,128)}, f32[11,40,1040]{2,1,0:T(8,128)S(1)}, u32[]{:S(2)}) copy-start(f32[11,40,1040]{2,1,0:T(8,128)S(1)} %pad_maximum_fusion.1) | copy-start | bytes 5491204
  42.8 11.6 %copy-start.8 = (f32[40,1040]{1,0:T(8,128)}, f32[40,1040]{1,0:T(8,128)S(1)}, u32[]{:S(2)}) copy-start(f32[40,1040]{1,0:T(8,128)S(1)} %get-tuple-element.62) | copy-start | bytes 499204
  42.8 11.6 %copy-start.11 = (f32[40,1040]{1,0:T(8,128)}, f32[40,1040]{1,0:T(8,128)S(1)}, u32[]{:S(2)}) copy-start(f32[40,1040]{1,0:T(8,128)S(1)} %get-tuple-element.60) | copy-start | bytes 499204
  42.8 11.6 %copy-start.19 = (f32[40,1040]{1,0:T(8,128)}, f32[40,1040]{1,0:T(8,128)S(1)}, u32[]{:S(2)}) copy-start(f32[40,1040]{1,0:T(8,128)S(1)} %get-tuple-element.58) | copy-start | bytes 499204
  42.8 16.1 %copy-start.5 = (f32[40,1040]{1,0:T(8,128)}, f32[40,1040]{1,0:T(8,128)S(1)}, u32[]{:S(2)}) copy-start(f32[40,1040]{1,0:T(8,128)S(1)} %get-tuple-element.61) | copy-start | bytes 499204
  42.9 31.4 %all-to-all-start.1 = ((f32[8,2,32,1040]{3,2,1,0:T(8,128)}), f32[8,2,32,1040]{3,2,1,0:T(8,128)}, u32[]{:S(2)}, u32[]{:S(2)}) async-start(f32[8,2,32,1040]{3,2,1,0:T(8,128)} %pad_maximum_fusion), calls=%async_computation.1 | async-start | bytes 4718592 | tf_op jit(solution)/shard_map/all_to_all | solution.py:137
  58.3 1.2 copy-start.9
  58.3 1.4 %copy-start.12 = (f32[40,1040]{1,0:T(8,128)S(1)}, f32[40,1040]{1,0:T(8,128)}, u32[]{:S(2)}) copy-start(f32[40,1040]{1,0:T(8,128)} %copy-done.11) | copy-start | bytes 499204
  58.3 1.6 %copy-start.20 = (f32[40,1040]{1,0:T(8,128)S(1)}, f32[40,1040]{1,0:T(8,128)}, u32[]{:S(2)}) copy-start(f32[40,1040]{1,0:T(8,128)} %copy-done.19) | copy-start | bytes 499204
  65.5 1.6 %copy-start.6 = (f32[40,1040]{1,0:T(8,128)S(1)}, f32[40,1040]{1,0:T(8,128)}, u32[]{:S(2)}) copy-start(f32[40,1040]{1,0:T(8,128)} %copy-done.5) | copy-start | bytes 499204
  78.0 33.5 %all-to-all-start.2 = ((f32[8,32,1024]{2,1,0:T(8,128)}), f32[8,32,1024]{2,1,0:T(8,128)}, u32[]{:S(2)}, u32[]{:S(2)}) async-start(f32[8,32,1024]{2,1,0:T(8,128)} %get-tuple-element.40), calls=%async_computation.2 | async-start | bytes 2097152 | tf_op jit(solution)/shard_map/all_to_all | solution.py:154
  82.7 2.4 %copy-start.16 = (f32[8,40,1040]{2,1,0:T(8,128)S(1)}, f32[8,40,1040]{2,1,0:T(8,128)}, u32[]{:S(2)}) copy-start(f32[8,40,1040]{2,1,0:T(8,128)} %get-tuple-element.53) | copy-start | bytes 3993604
  85.1 2.8 %copy-start.7 = (f32[40,1040]{1,0:T(8,128)S(1)}, f32[40,1040]{1,0:T(8,128)}, u32[]{:S(2)}) copy-start(f32[40,1040]{1,0:T(8,128)} %copy-done.5) | copy-start | bytes 499204
  85.1 2.8 %copy-start.10 = (f32[40,1040]{1,0:T(8,128)S(1)}, f32[40,1040]{1,0:T(8,128)}, u32[]{:S(2)}) copy-start(f32[40,1040]{1,0:T(8,128)} %copy-done.8) | copy-start | bytes 499204
  85.2 2.8 %copy-start.13 = (f32[40,1040]{1,0:T(8,128)S(1)}, f32[40,1040]{1,0:T(8,128)}, u32[]{:S(2)}) copy-start(f32[40,1040]{1,0:T(8,128)} %copy-done.11) | copy-start | bytes 499204
  85.2 2.8 %copy-start.21 = (f32[40,1040]{1,0:T(8,128)S(1)}, f32[40,1040]{1,0:T(8,128)}, u32[]{:S(2)}) copy-start(f32[40,1040]{1,0:T(8,128)} %broadcast_multiply_fusion.2) | copy-start | bytes 499204
  88.0 1.4 %copy-start.1 = (f32[8,40,1040]{2,1,0:T(8,128)S(1)}, f32[8,40,1040]{2,1,0:T(8,128)}, u32[]{:S(2)}) copy-start(f32[8,40,1040]{2,1,0:T(8,128)} %copy-done) | copy-start | bytes 3993604
  88.0 1.8 %copy-start.15 = (f32[8,40,1040]{2,1,0:T(8,128)S(1)}, f32[8,40,1040]{2,1,0:T(8,128)}, u32[]{:S(2)}) copy-start(f32[8,40,1040]{2,1,0:T(8,128)} %get-tuple-element.55) | copy-start | bytes 3993604
  92.5 1.4 %copy-start.3 = (f32[8,40,1040]{2,1,0:T(8,128)S(1)}, f32[8,40,1040]{2,1,0:T(8,128)}, u32[]{:S(2)}) copy-start(f32[8,40,1040]{2,1,0:T(8,128)} %copy-done.2) | copy-start | bytes 3993604
  92.5 1.8 %copy-start.17 = (f32[8,40,1040]{2,1,0:T(8,128)S(1)}, f32[8,40,1040]{2,1,0:T(8,128)}, u32[]{:S(2)}) copy-start(f32[8,40,1040]{2,1,0:T(8,128)} %get-tuple-element.57) | copy-start | bytes 3993604
  92.5 2.1 %copy-start.18 = (f32[8,32,1040]{2,1,0:T(8,128)S(1)}, f32[8,32,1040]{2,1,0:T(8,128)}, u32[]{:S(2)}) copy-start(f32[8,32,1040]{2,1,0:T(8,128)} %get-tuple-element.41) | copy-start | bytes 3194884
  98.4 5.6 %collective-permute-start.2 = (f32[4,1040]{1,0:T(4,128)S(1)}, f32[4,1040]{1,0:T(4,128)S(1)}, u32[]{:S(2)}, u32[]{:S(2)}) collective-permute-start(f32[4,1040]{1,0:T(4,128)S(1)} %get-tuple-element.98), channel_id=1, source_target_pairs={{8,0},{16,8},{24,16},{32,24},{40,32},{48,40},{56,48},{64,56},{72,6... | collective-permute-start | bytes 49928 | tf_op jit(solution)/shard_map/ppermute | solution.py:149
  102.1 9.3 %collective-permute-start.3 = (f32[4,1040]{1,0:T(4,128)S(1)}, f32[4,1040]{1,0:T(4,128)S(1)}, u32[]{:S(2)}, u32[]{:S(2)}) collective-permute-start(f32[4,1040]{1,0:T(4,128)S(1)} %get-tuple-element.97), channel_id=1, source_target_pairs={{0,8},{8,16},{16,24},{24,32},{32,40},{40,48},{48,56},{56,64},{64,7... | collective-permute-start | bytes 49928 | tf_op jit(solution)/shard_map/ppermute | solution.py:150
  112.6 15.9 %all-to-all-start.3 = ((f32[8,32,1024]{2,1,0:T(8,128)}), f32[8,32,1024]{2,1,0:T(8,128)S(1)}, u32[]{:S(2)}, u32[]{:S(2)}) async-start(f32[8,32,1024]{2,1,0:T(8,128)} %broadcast_in_dim.57), calls=%async_computation.3 | async-start | bytes 2097152 | tf_op jit(solution)/shard_map/all_to_all | solution.py:157
  (2 other events, 2.3 us)

commit v11 on v10

--- a/solution.py
+++ b/solution.py
@@ -83,7 +83,7 @@
 
 def scans(fine_ends, old, pair, begin, width):
     slabs, rows, wide = fine_ends.shape
-    tile = 16
+    tile = 32
     stacked = pl.BlockSpec((slabs, tile, wide), lambda i: (0, i, 0))
     inner = pl.BlockSpec((slabs, tile, width), lambda i: (0, i, 0))
     both = pl.BlockSpec((slabs, 2, tile, wide), lambda i: (0, 0, i, 0))

time: 130 us -> 131 us (level)
  no operation moved by 1% of the time
where the time goes in v11:
time: 131 us; the launch traced here: 130 us
  starting transfers between devices  38.9 us (30%)
  other arithmetic  35.2 us (27%)
  local copies, waits for them, and re-layouts  25.3 us (19%)
  waiting for transfers between devices  25.3 us (19%)
  Pallas kernels  4.17 us (3%)
    select_n x4, other arithmetic, fine(): jnp.where(inside, advance(field, kappa, along_rows, along_cols), 0.0)  12.1 us
    unnamed x56, local copies, waits for them, and re-layouts  9.48 us
    reduce_sum x3, other arithmetic, advance(): return centre + time_step * (kappa * spread - transport)  9.09 us
    ppermute x1, starting transfers between devices, with_halo(): lax.ppermute(head, axis, [((i + 1) % count, i) for i in range(ends)])  7.86 us
    all_to_all x1, waiting for transfers between devices, on_device(): gradient = lax.all_to_all(copies, 'tm', 0, 2, tiled=True)[0]  7.73 us
    ppermute x1, waiting for transfers between devices, on_device(): lax.ppermute(grad_rows[-STEPS:], 'space', [(i, (i + 1) % count) for i in...  7.34 us
    all_to_all x1, starting transfers between devices, on_device(): pair = lax.all_to_all(pair, 'tm', 0, 0, tiled=True)  6.8 us
    all_to_all x1, starting transfers between devices, to_blocks(): return lax.all_to_all(send_windows(x), 'tm', 0, 0, tiled=True)  6.06 us
  transfers between devices with their start and end apart: 8, of which 6 were waited for; matrix products, arithmetic and copies ran while one was open for 36% of the time, Pallas kernels for 0%

profile of v11, /device:TPU:160, one launch (start us, length us, event | category | flops | bytes accessed | tf_op | source)
XLA Modules:
  0.0 130.0 jit_solution(9868726663147022743)
XLA Ops:
  0.6 1.8 %copy.22 = f32[4,8,8,1024]{3,2,1,0:T(8,128)S(1)} copy(f32[4,8,8,1024]{3,1,2,0:T(8,128)} %bitcast.59) | data formatting | bytes 2097152
  3.2 1.4 %concatenate.19 = f32[8,32,1040]{2,1,0:T(8,128)} concatenate(f32[8,32,8]{2,1,0:T(8,128)S(1)} %pad.155, f32[8,32,1024]{2,1,0:T(8,128)S(1)} %bitcast.52, f32[8,32,8]{2,1,0:T(8,128)S(1)} %pad.156), dimensions={2} | concatenate | bytes 2129920 | tf_op jit(solution)/shard_map/concatenate | solution.py:114
  4.6 6.1 %all-to-all-start = ((f32[8,32,1040]{2,1,0:T(8,128)}), f32[8,32,1040]{2,1,0:T(8,128)S(1)}, u32[]{:S(2)}, u32[]{:S(2)}) async-start(f32[8,32,1040]{2,1,0:T(8,128)} %concatenate.19), calls=%async_computation | async-start | bytes 2359296 | tf_op jit(solution)/shard_map/all_to_all | solution.py:117
  15.6 2.1 %concatenate.22 = f32[8,32,1040]{2,1,0:T(8,128)} concatenate(f32[8,32,8]{2,1,0:T(8,128)} %pad.159, f32[8,32,1024]{2,1,0:T(8,128)S(1)} %bitcast.48, f32[8,32,8]{2,1,0:T(8,128)S(1)} %pad.160), dimensions={2} | concatenate | bytes 2129920 | tf_op jit(solution)/shard_map/concatenate | solution.py:114
  17.7 2.2 %concatenate.23 = f32[8,32,1040]{2,1,0:T(8,128)} concatenate(f32[8,32,8]{2,1,0:T(8,128)} %pad.161, f32[8,32,1024]{2,1,0:T(8,128)S(1)} %bitcast.50, f32[8,32,8]{2,1,0:T(8,128)} %pad.162), dimensions={2} | concatenate | bytes 2129920 | tf_op jit(solution)/shard_map/concatenate | solution.py:114
  19.9 3.3 %pad_maximum_fusion = f32[8,2,32,1040]{3,2,1,0:T(8,128)} fusion(f32[8,1,32,1040]{3,2,1,0:T(8,128)} %bitcast.54, f32[8,1,32,1040]{3,2,1,0:T(8,128)} %bitcast.53), kind=kLoop, calls=%fused_computation | loop fusion | flops 532480 | bytes 4259840 | tf_op jit(solution)/shard_map/stack | solution.py:120
  23.2 3.1 %all-to-all-done.old_ref = f32[8,32,1040]{2,1,0:T(8,128)S(1)} async-done(((f32[8,32,1040]{2,1,0:T(8,128)}), f32[8,32,1040]{2,1,0:T(8,128)S(1)}, u32[]{:S(2)}, u32[]{:S(2)}) %all-to-all-start) | async-done | bytes 1064992 | tf_op jit(solution)/shard_map/all_to_all | solution.py:117
  26.5 1.4 %pad_dynamic-slice_fusion = f32[2,32,1040]{2,1,0:T(8,128)S(1)} fusion(s32[]{:T(128)S(6)} %select_n.31, f32[2,32,8192]{2,1,0:T(8,128)} %param.13), kind=kLoop, calls=%fused_computation.1 | loop fusion | bytes 2363396 | tf_op jit(solution)/shard_map/dynamic_slice | solution.py:64
  28.0 2.1 %collective-permute-start = (f32[11,4,1040]{2,1,0:T(4,128)S(1)}, f32[11,4,1040]{2,1,0:T(4,128)S(1)}, u32[]{:S(2)}, u32[]{:S(2)}) collective-permute-start(f32[11,4,1040]{2,1,0:T(4,128)S(1)} %get-tuple-element.73), channel_id=1, source_target_pairs={{0,8},{8,16},{16,24},{24,32},{32,40},{40,48},{48,56},{56,64},{64,7... | collective-permute-start | bytes 549128 | tf_op jit(solution)/shard_map/ppermute | solution.py:21
  30.0 7.9 %collective-permute-start.1 = (f32[11,4,1040]{2,1,0:T(4,128)S(1)}, f32[11,4,1040]{2,1,0:T(4,128)S(1)}, u32[]{:S(2)}, u32[]{:S(2)}) collective-permute-start(f32[11,4,1040]{2,1,0:T(4,128)S(1)} %get-tuple-element.74), channel_id=1, source_target_pairs={{8,0},{16,8},{24,16},{32,24},{40,32},{48,40},{56,48},{64,56},{72,6... | collective-permute-start | bytes 549128 | tf_op jit(solution)/shard_map/ppermute | solution.py:23
  38.7 1.8 %collective-permute-done = f32[11,4,1040]{2,1,0:T(4,128)S(1)} collective-permute-done((f32[11,4,1040]{2,1,0:T(4,128)S(1)}, f32[11,4,1040]{2,1,0:T(4,128)S(1)}, u32[]{:S(2)}, u32[]{:S(2)}) %collective-permute-start) | collective-permute-done | bytes 183072 | tf_op jit(solution)/shard_map/ppermute | solution.py:21
  41.5 1.2 copy-done.14
  42.9 6.8 %all-to-all-start.1 = ((f32[8,2,32,1040]{3,2,1,0:T(8,128)}), f32[8,2,32,1040]{3,2,1,0:T(8,128)}, u32[]{:S(2)}, u32[]{:S(2)}) async-start(f32[8,2,32,1040]{3,2,1,0:T(8,128)} %pad_maximum_fusion), calls=%async_computation.1 | async-start | bytes 4718592 | tf_op jit(solution)/shard_map/all_to_all | solution.py:137
  50.3 3.5 %fusion.24 = (f32[8,40,1040]{2,1,0:T(8,128)S(1)}, f32[8,40,1040]{2,1,0:T(8,128)}) fusion(f32[8,40,1040]{2,1,0:T(8,128)S(1)} %slice.216, f32[40,1040]{1,0:T(8,128)S(1)} %get-tuple-element.60, f32[40,1040]{1,0:T(8,128)S(1)} %get-tuple-element.61, f32[40,1040]{1,0:T(8,128)S(1)} %get-tuple-element.59, f32[40,1040]{1,0:T(8,128)S(1)} %get-tuple-element.62, ...), kind=kLoop, calls=%fused_computation.60 | loop fusion | flops 6988800 | bytes 11523200 | tf_op jit(solution)/shard_map/jvp(jit(_where))/select_n | solution.py:55
  54.9 3.4 %fusion.39 = (f32[8,40,1040]{2,1,0:T(8,128)S(1)}, f32[8,40,1040]{2,1,0:T(8,128)}) fusion(f32[8,40,1040]{2,1,0:T(8,128)S(1)} %get-tuple-element.56, f32[40,1040]{1,0:T(8,128)S(1)} %get-tuple-element.60, f32[40,1040]{1,0:T(8,128)S(1)} %get-tuple-element.61, f32[40,1040]{1,0:T(8,128)S(1)} %get-tuple-element.59, f32[40,1040]{1,0:T(8,128)S(1)} %get-tuple-element.62, ...), kind=kLoop, calls=%fused_computation.75 | loop fusion | flops 6988800 | bytes 11523200 | tf_op jit(solution)/shard_map/jvp(jit(_where))/select_n | solution.py:55
  59.9 3.4 %fusion.55 = (f32[8,40,1040]{2,1,0:T(8,128)S(1)}, f32[8,40,1040]{2,1,0:T(8,128)}) fusion(f32[8,40,1040]{2,1,0:T(8,128)S(1)} %get-tuple-element.54, f32[40,1040]{1,0:T(8,128)S(1)} %copy-done.12, f32[40,1040]{1,0:T(8,128)S(1)} %get-tuple-element.61, f32[40,1040]{1,0:T(8,128)S(1)} %get-tuple-element.59, f32[40,1040]{1,0:T(8,128)S(1)} %copy-done.9, ...), kind=kLoop, calls=%fused_computation.91 | loop fusion | flops 6988800 | bytes 11523200 | tf_op jit(solution)/shard_map/jvp(jit(_where))/select_n | solution.py:55
  63.9 1.6 %broadcast_multiply_fusion.2 = f32[40,1040]{1,0:T(8,128)} fusion(f32[11,40,1040]{2,1,0:T(8,128)} %copy-done.14), kind=kLoop, calls=%fused_computation.205 | loop fusion | flops 41600 | bytes 332800 | tf_op jit(solution)/shard_map/transpose(jvp())/mul | solution.py:50
  65.5 1.6 %fusion.84 = f32[8,40,1040]{2,1,0:T(8,128)S(1)} fusion(f32[8,42,1042]{2,1,0:T(8,128)S(1)} %pad_add_fusion), kind=kLoop, calls=%fused_computation.133 | loop fusion | flops 1664000 | bytes 7987200 | tf_op jit(solution)/shard_map/jvp()/sub | solution.py:38
  68.0 1.8 %fusion.97.fine_ref = f32[8,32,1040]{2,1,0:T(8,128)} fusion(f32[8,40,1040]{2,1,0:T(8,128)S(1)} %get-tuple-element.52, f32[8,40,1040]{2,1,0:T(8,128)S(1)} %fusion.84, f32[8,40,1040]{2,1,0:T(8,128)S(1)} %get-tuple-element.80, f32[8,40,1040]{2,1,0:T(8,128)S(1)} %get-tuple-element.81, f32[8,40,1040]{2,1,0:T(8,128)S(1)} %get-tuple-element.79, ...), kind=kLoop, calls=%fused_computation.180 | loop fusion | flops 2129920 | bytes 6689280 | tf_op jit(solution)/shard_map/jvp(jit(_where))/select_n | solution.py:55
  69.7 4.6 %all-to-all-done.1.pair_ref = f32[8,2,32,1040]{3,2,1,0:T(8,128)} async-done(((f32[8,2,32,1040]{3,2,1,0:T(8,128)}), f32[8,2,32,1040]{3,2,1,0:T(8,128)}, u32[]{:S(2)}, u32[]{:S(2)}) %all-to-all-start.1) | async-done | bytes 2129952 | tf_op jit(solution)/shard_map/all_to_all | solution.py:137
  74.3 4.2 %shard_map.77 = (f32[8,32,1024]{2,1,0:T(8,128)}, f32[8,32,1040]{2,1,0:T(8,128)}) custom-call(f32[8,32,1040]{2,1,0:T(8,128)} %fusion.97.fine_ref, f32[8,32,1040]{2,1,0:T(8,128)} %copy-done.4, f32[8,2,32,1040]{3,2,1,0:T(8,128)} %all-to-all-done.1.pair_ref, f32[32,1040]{1,0:T(8,128)} %pad_dynamic-slice_fusion.1.begin_ref), custom_call_target="tpu_custom_call" | custom-call | tf_op jit(solution)/shard_map/pallas_call | solution.py:91
  78.5 4.7 %all-to-all-start.2 = ((f32[8,32,1024]{2,1,0:T(8,128)}), f32[8,32,1024]{2,1,0:T(8,128)}, u32[]{:S(2)}, u32[]{:S(2)}) async-start(f32[8,32,1024]{2,1,0:T(8,128)} %get-tuple-element.40), calls=%async_computation.2 | async-start | bytes 2097152 | tf_op jit(solution)/shard_map/all_to_all | solution.py:154
  83.2 2.4 %fusion.96 = (f32[8,40,1040]{2,1,0:T(8,128)S(1)}, f32[8,40,1040]{2,1,0:T(8,128)S(1)}, f32[8,40,1040]{2,1,0:T(8,128)S(1)}, f32[8,40,1040]{2,1,0:T(8,128)S(1)}, f3...) fusion(f32[8,32,1040]{2,1,0:T(8,128)} %get-tuple-element.41, ...), kind=kLoop, calls=%fused_computation.178 | loop fusion | flops 5990400 | bytes 11256960 | tf_op jit(solution)/shard_map/transpose(jvp())/mul | solution.py:48
  85.7 2.8 %multiply_reduce_fusion.1 = (f32[40,1040]{1,0:T(8,128)S(1)}, f32[8,40,1040]{2,1,0:T(8,128)S(1)}) fusion(f32[8,40,1040]{2,1,0:T(8,128)S(1)} %copy-done.16, f32[8,40,1040]{2,1,0:T(8,128)S(1)} %get-tuple-element.52, f32[8,40,1040]{2,1,0:T(8,128)S(1)} %get-tuple-element.89, f32[8,40,1040]{2,1,0:T(8,128)S(1)} %get-tuple-element.90, ...), kind=kLoop, calls=%fused_computation.157 | loop fusion | flops 6281600 | bytes 13520000 | tf_op jit(solution)/shard_map/transpose(jvp())/reduce_sum | solution.py:50
  90.3 2.7 %multiply_reduce_fusion = (f32[40,1040]{1,0:T(8,128)S(1)}, f32[8,40,1040]{2,1,0:T(8,128)S(1)}) fusion(f32[8,40,1040]{2,1,0:T(8,128)S(1)} %copy-done.15, f32[8,40,1040]{2,1,0:T(8,128)S(1)} %copy-done.1, f32[8,40,1040]{2,1,0:T(8,128)S(1)} %get-tuple-element.78, f32[8,40,1040]{2,1,0:T(8,128)S(1)} %get-tuple-element.77, ...), kind=kLoop, calls=%fused_computation.154 | loop fusion | flops 6281600 | bytes 13520000 | tf_op jit(solution)/shard_map/transpose(jvp())/reduce_sum | solution.py:50
  95.2 3.6 %multiply_reduce_fusion.2 = (f32[40,1040]{1,0:T(8,128)S(1)}, f32[40,1040]{1,0:T(8,128)S(1)}) fusion(f32[8,32,1040]{2,1,0:T(8,128)S(1)} %copy-done.18, pred[40,1040]{1,0:T(8,128)(4,1)S(1)} %and_and_fusion, f32[8,40,1040]{2,1,0:T(8,128)S(1)} %copy-done.17, f32[8,40,1040]{2,1,0:T(8,128)S(1)} %copy-done.3, f32[8,40,1040]{2,1,0:T(8,128)S(1)} %get-tuple-element.76, ...), kind=kLoop, calls=%fused_computation.160 | loop fusion | flops 9235200 | bytes 20076160 | tf_op jit(solution)/shard_map/transpose(jvp())/reduce_sum | solution.py:50
  98.9 3.6 %collective-permute-start.2 = (f32[4,1040]{1,0:T(4,128)S(1)}, f32[4,1040]{1,0:T(4,128)S(1)}, u32[]{:S(2)}, u32[]{:S(2)}) collective-permute-start(f32[4,1040]{1,0:T(4,128)S(1)} %get-tuple-element.98), channel_id=1, source_target_pairs={{8,0},{16,8},{24,16},{32,24},{40,32},{48,40},{56,48},{64,56},{72,6... | collective-permute-start | bytes 49928 | tf_op jit(solution)/shard_map/ppermute | solution.py:149
  102.5 1.9 %collective-permute-start.3 = (f32[4,1040]{1,0:T(4,128)S(1)}, f32[4,1040]{1,0:T(4,128)S(1)}, u32[]{:S(2)}, u32[]{:S(2)}) collective-permute-start(f32[4,1040]{1,0:T(4,128)S(1)} %get-tuple-element.97), channel_id=1, source_target_pairs={{0,8},{8,16},{16,24},{24,32},{32,40},{40,48},{48,56},{56,64},{64,7... | collective-permute-start | bytes 49928 | tf_op jit(solution)/shard_map/ppermute | solution.py:150
  104.5 7.3 %collective-permute-done.3 = f32[4,1040]{1,0:T(4,128)S(1)} collective-permute-done((f32[4,1040]{1,0:T(4,128)S(1)}, f32[4,1040]{1,0:T(4,128)S(1)}, u32[]{:S(2)}, u32[]{:S(2)}) %collective-permute-start.3) | collective-permute-done | bytes 16672 | tf_op jit(solution)/shard_map/ppermute | solution.py:150
  113.1 5.9 %all-to-all-start.3 = ((f32[8,32,1024]{2,1,0:T(8,128)}), f32[8,32,1024]{2,1,0:T(8,128)S(1)}, u32[]{:S(2)}, u32[]{:S(2)}) async-start(f32[8,32,1024]{2,1,0:T(8,128)} %broadcast_in_dim.57), calls=%async_computation.3 | async-start | bytes 2097152 | tf_op jit(solution)/shard_map/all_to_all | solution.py:157
  119.0 2.3 %copy.21 = f32[1,8,4,8,1024]{4,3,1,2,0:T(8,128)} copy(f32[1,8,4,8,1024]{4,3,2,1,0:T(8,128)} %bitcast.17) | data formatting | bytes 2097152 | tf_op jit(solution)/shard_map/all_to_all | solution.py:154
  121.3 7.7 %all-to-all-done.3 = f32[8,32,1024]{2,1,0:T(8,128)S(1)} async-done(((f32[8,32,1024]{2,1,0:T(8,128)}), f32[8,32,1024]{2,1,0:T(8,128)S(1)}, u32[]{:S(2)}, u32[]{:S(2)}) %all-to-all-start.3) | async-done | bytes 1048608 | tf_op jit(solution)/shard_map/all_to_all | solution.py:157
  (95 shorter events, 18.6 us)
Async XLA Ops:
  4.6 6.2 %copy-start.22 = (f32[1,32,8192]{2,1,0:T(8,128)S(1)}, f32[1,32,8192]{2,1,0:T(8,128)}, u32[]{:S(2)}) copy-start(f32[1,32,8192]{2,1,0:T(8,128)} %param.14) | copy-start | bytes 3145732
  4.6 21.7 %all-to-all-start = ((f32[8,32,1040]{2,1,0:T(8,128)}), f32[8,32,1040]{2,1,0:T(8,128)S(1)}, u32[]{:S(2)}, u32[]{:S(2)}) async-start(f32[8,32,1040]{2,1,0:T(8,128)} %concatenate.19), calls=%async_computation | async-start | bytes 2359296 | tf_op jit(solution)/shard_map/all_to_all | solution.py:117
  11.5 1.4 %copy-start.23 = (f32[1,32,8192]{2,1,0:T(8,128)S(1)}, f32[1,32,8192]{2,1,0:T(8,128)}, u32[]{:S(2)}) copy-start(f32[1,32,8192]{2,1,0:T(8,128)} %param.15) | copy-start | bytes 3145732
  19.9 6.4 %copy-start.24 = (f32[32,8192]{1,0:T(8,128)S(1)}, f32[32,8192]{1,0:T(8,128)}, u32[]{:S(2)}) copy-start(f32[32,8192]{1,0:T(8,128)} %param.12) | copy-start | bytes 3145732
  26.4 14.9 %copy-start.4 = (f32[8,32,1040]{2,1,0:T(8,128)}, f32[8,32,1040]{2,1,0:T(8,128)S(1)}, u32[]{:S(2)}) copy-start(f32[8,32,1040]{2,1,0:T(8,128)S(1)} %all-to-all-done.old_ref) | copy-start | bytes 3194884
  27.9 10.0 %copy-start.25 = (f32[32,8192]{1,0:T(8,128)S(1)}, f32[32,8192]{1,0:T(8,128)}, u32[]{:S(2)}) copy-start(f32[32,8192]{1,0:T(8,128)} %param.10) | copy-start | bytes 3145732
  28.0 12.5 %collective-permute-start = (f32[11,4,1040]{2,1,0:T(4,128)S(1)}, f32[11,4,1040]{2,1,0:T(4,128)S(1)}, u32[]{:S(2)}, u32[]{:S(2)}) collective-permute-start(f32[11,4,1040]{2,1,0:T(4,128)S(1)} %get-tuple-element.73), channel_id=1, source_target_pairs={{0,8},{8,16},{16,24},{24,32},{32,40},{40,48},{48,56},{56,64},{64,7... | collective-permute-start | bytes 549128 | tf_op jit(solution)/shard_map/ppermute | solution.py:21
  30.0 11.2 %collective-permute-start.1 = (f32[11,4,1040]{2,1,0:T(4,128)S(1)}, f32[11,4,1040]{2,1,0:T(4,128)S(1)}, u32[]{:S(2)}, u32[]{:S(2)}) collective-permute-start(f32[11,4,1040]{2,1,0:T(4,128)S(1)} %get-tuple-element.74), channel_id=1, source_target_pairs={{8,0},{16,8},{24,16},{32,24},{40,32},{48,40},{56,48},{64,56},{72,6... | collective-permute-start | bytes 549128 | tf_op jit(solution)/shard_map/ppermute | solution.py:23
  41.4 1.3 %copy-start.14 = (f32[11,40,1040]{2,1,0:T(8,128)}, f32[11,40,1040]{2,1,0:T(8,128)S(1)}, u32[]{:S(2)}) copy-start(f32[11,40,1040]{2,1,0:T(8,128)S(1)} %pad_maximum_fusion.1) | copy-start | bytes 5491204
  42.8 11.6 %copy-start.8 = (f32[40,1040]{1,0:T(8,128)}, f32[40,1040]{1,0:T(8,128)S(1)}, u32[]{:S(2)}) copy-start(f32[40,1040]{1,0:T(8,128)S(1)} %get-tuple-element.62) | copy-start | bytes 499204
  42.8 11.6 %copy-start.11 = (f32[40,1040]{1,0:T(8,128)}, f32[40,1040]{1,0:T(8,128)S(1)}, u32[]{:S(2)}) copy-start(f32[40,1040]{1,0:T(8,128)S(1)} %get-tuple-element.60) | copy-start | bytes 499204
  42.8 11.6 %copy-start.19 = (f32[40,1040]{1,0:T(8,128)}, f32[40,1040]{1,0:T(8,128)S(1)}, u32[]{:S(2)}) copy-start(f32[40,1040]{1,0:T(8,128)S(1)} %get-tuple-element.58) | copy-start | bytes 499204
  42.8 16.1 %copy-start.5 = (f32[40,1040]{1,0:T(8,128)}, f32[40,1040]{1,0:T(8,128)S(1)}, u32[]{:S(2)}) copy-start(f32[40,1040]{1,0:T(8,128)S(1)} %get-tuple-element.61) | copy-start | bytes 499204
  42.9 31.4 %all-to-all-start.1 = ((f32[8,2,32,1040]{3,2,1,0:T(8,128)}), f32[8,2,32,1040]{3,2,1,0:T(8,128)}, u32[]{:S(2)}, u32[]{:S(2)}) async-start(f32[8,2,32,1040]{3,2,1,0:T(8,128)} %pad_maximum_fusion), calls=%async_computation.1 | async-start | bytes 4718592 | tf_op jit(solution)/shard_map/all_to_all | solution.py:137
  58.3 1.2 copy-start.9
  58.3 1.4 %copy-start.12 = (f32[40,1040]{1,0:T(8,128)S(1)}, f32[40,1040]{1,0:T(8,128)}, u32[]{:S(2)}) copy-start(f32[40,1040]{1,0:T(8,128)} %copy-done.11) | copy-start | bytes 499204
  58.3 1.6 %copy-start.20 = (f32[40,1040]{1,0:T(8,128)S(1)}, f32[40,1040]{1,0:T(8,128)}, u32[]{:S(2)}) copy-start(f32[40,1040]{1,0:T(8,128)} %copy-done.19) | copy-start | bytes 499204
  65.5 1.6 %copy-start.6 = (f32[40,1040]{1,0:T(8,128)S(1)}, f32[40,1040]{1,0:T(8,128)}, u32[]{:S(2)}) copy-start(f32[40,1040]{1,0:T(8,128)} %copy-done.5) | copy-start | bytes 499204
  78.5 33.5 %all-to-all-start.2 = ((f32[8,32,1024]{2,1,0:T(8,128)}), f32[8,32,1024]{2,1,0:T(8,128)}, u32[]{:S(2)}, u32[]{:S(2)}) async-start(f32[8,32,1024]{2,1,0:T(8,128)} %get-tuple-element.40), calls=%async_computation.2 | async-start | bytes 2097152 | tf_op jit(solution)/shard_map/all_to_all | solution.py:154
  83.2 2.4 %copy-start.16 = (f32[8,40,1040]{2,1,0:T(8,128)S(1)}, f32[8,40,1040]{2,1,0:T(8,128)}, u32[]{:S(2)}) copy-start(f32[8,40,1040]{2,1,0:T(8,128)} %get-tuple-element.53) | copy-start | bytes 3993604
  85.6 2.8 %copy-start.7 = (f32[40,1040]{1,0:T(8,128)S(1)}, f32[40,1040]{1,0:T(8,128)}, u32[]{:S(2)}) copy-start(f32[40,1040]{1,0:T(8,128)} %copy-done.5) | copy-start | bytes 499204
  85.6 2.8 %copy-start.10 = (f32[40,1040]{1,0:T(8,128)S(1)}, f32[40,1040]{1,0:T(8,128)}, u32[]{:S(2)}) copy-start(f32[40,1040]{1,0:T(8,128)} %copy-done.8) | copy-start | bytes 499204
  85.6 2.8 %copy-start.13 = (f32[40,1040]{1,0:T(8,128)S(1)}, f32[40,1040]{1,0:T(8,128)}, u32[]{:S(2)}) copy-start(f32[40,1040]{1,0:T(8,128)} %copy-done.11) | copy-start | bytes 499204
  85.7 2.8 %copy-start.21 = (f32[40,1040]{1,0:T(8,128)S(1)}, f32[40,1040]{1,0:T(8,128)}, u32[]{:S(2)}) copy-start(f32[40,1040]{1,0:T(8,128)} %broadcast_multiply_fusion.2) | copy-start | bytes 499204
  88.5 1.4 %copy-start.1 = (f32[8,40,1040]{2,1,0:T(8,128)S(1)}, f32[8,40,1040]{2,1,0:T(8,128)}, u32[]{:S(2)}) copy-start(f32[8,40,1040]{2,1,0:T(8,128)} %copy-done) | copy-start | bytes 3993604
  88.5 1.8 %copy-start.15 = (f32[8,40,1040]{2,1,0:T(8,128)S(1)}, f32[8,40,1040]{2,1,0:T(8,128)}, u32[]{:S(2)}) copy-start(f32[8,40,1040]{2,1,0:T(8,128)} %get-tuple-element.55) | copy-start | bytes 3993604
  93.0 1.4 %copy-start.3 = (f32[8,40,1040]{2,1,0:T(8,128)S(1)}, f32[8,40,1040]{2,1,0:T(8,128)}, u32[]{:S(2)}) copy-start(f32[8,40,1040]{2,1,0:T(8,128)} %copy-done.2) | copy-start | bytes 3993604
  93.0 1.8 %copy-start.17 = (f32[8,40,1040]{2,1,0:T(8,128)S(1)}, f32[8,40,1040]{2,1,0:T(8,128)}, u32[]{:S(2)}) copy-start(f32[8,40,1040]{2,1,0:T(8,128)} %get-tuple-element.57) | copy-start | bytes 3993604
  93.0 2.1 %copy-start.18 = (f32[8,32,1040]{2,1,0:T(8,128)S(1)}, f32[8,32,1040]{2,1,0:T(8,128)}, u32[]{:S(2)}) copy-start(f32[8,32,1040]{2,1,0:T(8,128)} %get-tuple-element.41) | copy-start | bytes 3194884
  98.9 5.6 %collective-permute-start.2 = (f32[4,1040]{1,0:T(4,128)S(1)}, f32[4,1040]{1,0:T(4,128)S(1)}, u32[]{:S(2)}, u32[]{:S(2)}) collective-permute-start(f32[4,1040]{1,0:T(4,128)S(1)} %get-tuple-element.98), channel_id=1, source_target_pairs={{8,0},{16,8},{24,16},{32,24},{40,32},{48,40},{56,48},{64,56},{72,6... | collective-permute-start | bytes 49928 | tf_op jit(solution)/shard_map/ppermute | solution.py:149
  102.5 9.3 %collective-permute-start.3 = (f32[4,1040]{1,0:T(4,128)S(1)}, f32[4,1040]{1,0:T(4,128)S(1)}, u32[]{:S(2)}, u32[]{:S(2)}) collective-permute-start(f32[4,1040]{1,0:T(4,128)S(1)} %get-tuple-element.97), channel_id=1, source_target_pairs={{0,8},{8,16},{16,24},{24,32},{32,40},{40,48},{48,56},{56,64},{64,7... | collective-permute-start | bytes 49928 | tf_op jit(solution)/shard_map/ppermute | solution.py:150
  113.1 15.9 %all-to-all-start.3 = ((f32[8,32,1024]{2,1,0:T(8,128)}), f32[8,32,1024]{2,1,0:T(8,128)S(1)}, u32[]{:S(2)}, u32[]{:S(2)}) async-start(f32[8,32,1024]{2,1,0:T(8,128)} %broadcast_in_dim.57), calls=%async_computation.3 | async-start | bytes 2097152 | tf_op jit(solution)/shard_map/all_to_all | solution.py:157
  (2 other events, 2.3 us)
